TPU v7x, 128 devices: a whole 4x4x4 slice. The times are simulated.
128 devices in a mesh: site: 4 (over y), term: 32 (over z, x, core).
Axes of the slice: x: 4, y: 4, z: 4, core: 2. Of those that a mesh axis runs over, the one named last changes fastest.
Arguments:
- left_env: float32 [32, 12, 256, 256], P('term'), may hold values from -6 to 6
- right_env: float32 [4, 32, 12, 256, 256], P('site', 'term'), may hold values from -6 to 6
- mps: float32 [4, 2, 12, 256, 256], P('site'), may hold values from -0.375 to 0.375
- psi: float32 [4, 2, 12, 256, 256], P('site'), may hold values from -0.00390625 to 0.00390625
- coef: float32 [4, 32, 4], P('site', 'term'), may hold values from 0.5 to 1.5
- sector_sizes: int32 [12], replicated, may hold values from 128 to 256, as said below
- pattern: int32 [32, 12], P('term'), may hold values 0 or 1
Outputs:
- applied: float32 [4, 2, 3072, 256], P('site', None, 'term')
Inputs may be any that keep to these rules, and one draw needn't show every extreme that they name: `sector_sizes`: every size lies in 128 .. 256, the sizes add up to exactly 2560, and at least one sector has exactly 256.
All inputs are finite; a program needn't handle non-finite values. No bound on the sum of `pattern` on one device may be relied on, other than what follows from the above.
Results may differ from a plain program's by a relative error of at most 0.00018.
Values sent between devices are 32-bit elements; how exact they have to be, the bound alone decides.
No kernel may reach another device: no remote copies, remote signals or barrier semaphores. Data moves between devices by JAX's collectives and lax.ppermute only.
A program may use at most 128 MiB of HBM per device.

v0:
```python
import jax
import jax.numpy as jnp
from jax import lax
from jax.experimental import pallas as pl
from jax.experimental.pallas import tpu as pltpu
from jax.sharding import Mesh, PartitionSpec as P

f32, bf16 = jnp.float32, jnp.bfloat16
W = 256
NQ = 12
ROWS = 32
SITES = 4
LAG = 2


def halves(x):
    high = x.astype(bf16)
    return high, (x - high.astype(f32)).astype(bf16)


def product(a, b, dims):
    (ah, al), (bh, bl) = a, b

    def dot(u, v):
        return lax.dot_general(u, v, (dims, ((), ())), preferred_element_type=f32)

    return dot(ah, bh) + (dot(ah, bl) + dot(al, bh))


def framed(x, rows, columns):
    i = lax.broadcasted_iota(jnp.int32, x.shape, 0)
    j = lax.broadcasted_iota(jnp.int32, x.shape, 1)
    return jnp.where((i < rows) & (j < columns), x, 0.0)


def fetch(q, left, mps, psi, rights, stage, sems, wait):
    below, above = jnp.maximum(q - 1, 0), jnp.minimum(q + 1, NQ - 1)
    sources = (left.at[q], mps.at[0, q], mps.at[1, below], psi.at[0, q], psi.at[1, q], rights.at[q], rights.at[above], left.at[below])
    for i, source in enumerate(sources):
        copy = pltpu.make_async_copy(source, stage.at[i], sems.at[i])
        copy.wait() if wait else copy.start()


def first_kernel(ints, left, mps, psi, rights, stage, sems):
    @pl.when(ints[0] == 0)
    def _():
        fetch(0, left, mps, psi, rights, stage, sems, False)
        fetch(0, left, mps, psi, rights, stage, sems, True)


def sector_kernel(step, ints, floats, arrived, previous, stage, left, mps, psi, rights, *rest):
    environ, staged, keep, send, results, total, sems, stores = rest[-8:]
    site, my_z, my_x, core = ints[0], ints[1], ints[2], ints[3]
    q = step - LAG * site
    below = jnp.maximum(q - 1, 0)
    above = jnp.minimum(q + 1, NQ - 1)
    more = (q >= -1) & (q < NQ - 1) & (step < LAST - 1)

    @pl.when(more)
    def _():
        fetch(q + 1, left, mps, psi, rights, staged, sems, False)

    @pl.when((q >= 0) & (q < NQ))
    def _():
        size, under, over = ints[4 + q], ints[4 + below], ints[4 + above]
        present, present_above = ints[16 + q].astype(f32), ints[16 + above].astype(f32)
        present_above = jnp.where(q < NQ - 1, present_above, 0.0)
        c0 = jnp.where(site == 0, present, 1.0) * floats[0]
        c1 = jnp.where(site == 0, ints[16 + below].astype(f32), 1.0) * floats[1]
        now = jnp.where(site == 0, stage[0], arrived[...])
        before = jnp.where(site == 0, stage[7], previous[...])
        before = jnp.where(q > 0, before, 0.0)
        s = framed(stage[1], size, size)
        u = framed(stage[2], under, size)
        first = c0 * product(halves(now), halves(s), ((1,), (0,)))
        second = c1 * product(halves(before), halves(u), ((1,), (0,)))
        moved = product(halves(s.T), halves(first), ((1,), (0,))) + product(
            halves(u.T), halves(second), ((1,), (0,)))
        environ[...] = moved
        total[...] = moved

        def move(state, i, target, near, far, third):
            return pltpu.make_async_copy(
                results.at[state, pl.ds(ROWS * i, ROWS)], target.at[state, near, far, third], stores)

        def apply(state, _):
            c = jnp.where(state == 0, floats[2] * present, floats[3] * present_above)
            n = jnp.where(state == 0, size, over)
            part = c * product(halves(total[...]), halves(stage[3 + state]), ((1,), (0,)))
            results[state] = product(halves(part), halves(framed(stage[5 + state], n, n)), ((1,), (1,)))

            def place(i, _):
                piece = (W // ROWS) * q + i
                owner, third = piece // 3, piece % 3
                z = (owner // 8 - my_z + 4) % 4
                x = ((owner // 2) % 4 - my_x + 4) % 4
                near = jnp.where(state == 0, x, z)
                far = jnp.where(state == 0, z, x)
                mine = owner % 2 == core

                @pl.when(mine)
                def _():
                    move(state, i, keep, near, far, third).start()

                @pl.when(jnp.logical_not(mine))
                def _():
                    move(state, i, send, near, far, third).start()

                return 0

            return lax.fori_loop(0, W // ROWS, place, 0)

        lax.fori_loop(0, 2, apply, 0)
        pltpu.make_async_copy(results, stage.at[pl.ds(0, 2)], stores).wait()

    @pl.when(more)
    def _():
        fetch(q + 1, left, mps, psi, rights, staged, sems, True)


LAST = NQ + LAG * (SITES - 1)
SCALAR = pl.BlockSpec(memory_space=pltpu.SMEM)
LOCAL = pl.BlockSpec(memory_space=pltpu.VMEM)
FAR = pl.BlockSpec(memory_space=pltpu.HBM)
STAGE = jax.ShapeDtypeStruct((8, W, W), f32)
GRANT = pltpu.CompilerParams(vmem_limit_bytes=53 * 2**20)


def first_stage(ints, left, mps, psi, rights):
    return pl.pallas_call(
        first_kernel, in_specs=[SCALAR] + [FAR] * 4, out_specs=LOCAL, out_shape=STAGE,
        scratch_shapes=[pltpu.SemaphoreType.DMA((8,))], compiler_params=GRANT, name="first",
    )(ints, left, mps, psi, rights)


def sector_step(step, ints, floats, arrived, previous, stage, left, mps, psi, rights, held):
    shape = jax.ShapeDtypeStruct((2, 4, 4, 3, ROWS, W), f32)

    def kernel(*refs):
        sector_kernel(step, *refs)

    return pl.pallas_call(
        kernel,
        in_specs=[SCALAR] * 2 + [LOCAL] * 3 + [FAR] * (4 + len(held)),
        out_specs=[LOCAL, LOCAL, FAR, FAR],
        out_shape=[jax.ShapeDtypeStruct((W, W), f32), STAGE, shape, shape],
        scratch_shapes=[
            pltpu.VMEM((2, W, W), f32),
            pltpu.VMEM((W, W), f32),
            pltpu.SemaphoreType.DMA((8,)),
            pltpu.SemaphoreType.DMA,
        ],
        input_output_aliases={9: 2, 10: 3} if held else {},
        compiler_params=GRANT,
        name=f"sector{step}",
    )(ints, floats, arrived, previous, stage, left, mps, psi, rights, *held)


def turned(x, axis, by):
    return lax.ppermute(x, axis, [(i, (i + by) % 4) for i in range(4)])


def round_far(blocks, axis):
    half = blocks.shape[1] // 2
    up = turned(blocks[2, :half], axis, 1)
    down = turned(blocks[2, half:], axis, -1)
    return blocks[0], jnp.concatenate([blocks[1, :half] + up, blocks[1, half:]]), jnp.concatenate(
        [blocks[3, :half], blocks[3, half:] + down])


def round_near(parts, axis):
    own, ahead, behind = parts
    return own + turned(ahead, axis, 1) + turned(behind, axis, -1)


def reduced(keep, send):
    both = keep + lax.ppermute(send, "core", [(0, 1), (1, 0)])
    both = both.reshape(2, 4, 4, 96, W)
    first, second = round_far(both[0], "x"), round_far(both[1], "z")
    first, second = round_near(first, "x"), round_near(second, "z")
    first, second = round_far(first, "z"), round_far(second, "x")
    return jnp.stack([round_near(first, "z"), round_near(second, "x")])[None]


def shards(left_env, right_env, mps, psi, coef, sector_sizes, pattern):
    place = jnp.stack([lax.axis_index(a) for a in ("site", "z", "x", "core")]).astype(jnp.int32)
    ints = jnp.concatenate([place, sector_sizes, pattern[0]])
    floats = coef[0, 0]
    sources = (left_env[0], mps[0], psi[0], right_env[0, 0])
    nothing = jnp.zeros((W, W), f32)
    arrivals = {}
    held = ()
    stage = first_stage(ints, *sources)
    for step in range(LAST):
        arrived = arrivals.get(step, nothing)
        environ, stage, *held = sector_step(
            step, ints, floats, arrived, arrivals.get(step - 1, nothing), stage, *sources, tuple(held))
        if step + LAG < LAST:
            arrivals[step + LAG] = lax.ppermute(environ, "site", [(0, 1), (1, 2), (2, 3)])
    return reduced(*held)


def solution(mesh):
    fine = Mesh(mesh.devices.reshape(4, 4, 4, 2), ("site", "z", "x", "core"))
    term = ("z", "x", "core")
    return jax.shard_map(
        shards,
        mesh=fine,
        in_specs=(
            P(term, None, None, None),
            P("site", term, None, None, None),
            P("site", None, None, None, None),
            P("site", None, None, None, None),
            P("site", term, None),
            P(),
            P(term, None),
        ),
        out_specs=P("site", None, term, None),
        check_vma=False,
    )
```

profile of v0, /device:TPU:24, one launch (start us, length us, event | category | flops | bytes accessed | tf_op | source)
XLA Modules:
  0.0 198.0 jit_solution(14406426461301090685)
XLA Ops:
  0.8 2.0 %first.1.refs_4_ = f32[8,256,256]{2,1,0:T(8,128)} custom-call(s32[28]{0:T(128)S(1)} %concatenate.27.ints.refs_0_, f32[12,256,256]{2,1,0:T(8,128)} %bitcast.156, f32[2,12,256,256]{3,2,1,0:T(8,128)} %bitcast.118, f32[2,12,256,256]{3,2,1,0:T(8,128)} %bitcast.137, f32[12,256,256]{2,1,0:T(8,128)} %bitcast.175), custom_call_target="tpu_custom_call" | custom-call | tf_op jit(solution)/shard_map/first/pallas_call | solution.py:130
  2.8 3.0 %sector0.1 = (f32[256,256]{1,0:T(8,128)S(1)}, f32[8,256,256]{2,1,0:T(8,128)}, f32[2,4,4,3,32,256]{5,4,3,2,1,0:T(8,128)}, f32[2,4,4,3,32,256]{5,4,3,2,1,0:T(8,128)}) custom-call(s32[28]{0:T(128)S(1)} %concatenate.27.ints.refs_0_, f32[4]{0:T(128)S(1)} %bitcast.100, f32[256,256]{1,0:T(8,128)S(1)} %broadcast_in_dim.6.refs_2_.refs_3_, ...), custom_call_target="tpu_custom_call" | custom-call | tf_op jit(solution)/shard_map/sector0/pallas_call | solution.py:142
  5.8 1.3 collective-permute-start.1
  7.1 3.1 %sector1.1 = (f32[256,256]{1,0:T(8,128)S(1)}, f32[8,256,256]{2,1,0:T(8,128)}, f32[2,4,4,3,32,256]{5,4,3,2,1,0:T(8,128)}, f32[2,4,4,3,32,256]{5,4,3,2,1,0:T(8,128)}) custom-call(s32[28]{0:T(128)S(1)} %concatenate.27.ints.refs_0_, f32[4]{0:T(128)S(1)} %bitcast.101, ...), custom_call_target="tpu_custom_call", output_to_operand_aliasing={{2}: (9, {}), {3}: (10, {})} | custom-call | tf_op jit(solution)/shard_map/sector1/pallas_call | solution.py:142
  10.2 1.3 collective-permute-start
  11.5 4.8 %collective-permute-done.1.refs_2_.refs_3_ = f32[256,256]{1,0:T(8,128)S(1)} collective-permute-done((f32[256,256]{1,0:T(8,128)S(1)}, f32[256,256]{1,0:T(8,128)S(1)}, u32[]{:S(2)}, u32[]{:S(2)}) %collective-permute-start.1) | collective-permute-done | bytes 262176 | tf_op jit(solution)/shard_map/ppermute | solution.py:199
  16.4 3.0 %sector2.1 = (f32[256,256]{1,0:T(8,128)S(1)}, f32[8,256,256]{2,1,0:T(8,128)}, f32[2,4,4,3,32,256]{5,4,3,2,1,0:T(8,128)}, f32[2,4,4,3,32,256]{5,4,3,2,1,0:T(8,128)}) custom-call(s32[28]{0:T(128)S(1)} %concatenate.27.ints.refs_0_, f32[4]{0:T(128)S(1)} %bitcast.102, ...), custom_call_target="tpu_custom_call", output_to_operand_aliasing={{2}: (9, {}), {3}: (10, {})} | custom-call | tf_op jit(solution)/shard_map/sector2/pallas_call | solution.py:142
  19.4 1.3 collective-permute-start.3
  21.4 3.1 %sector3.1 = (f32[256,256]{1,0:T(8,128)S(1)}, f32[8,256,256]{2,1,0:T(8,128)}, f32[2,4,4,3,32,256]{5,4,3,2,1,0:T(8,128)}, f32[2,4,4,3,32,256]{5,4,3,2,1,0:T(8,128)}) custom-call(s32[28]{0:T(128)S(1)} %concatenate.27.ints.refs_0_, f32[4]{0:T(128)S(1)} %bitcast.103, ...), custom_call_target="tpu_custom_call", output_to_operand_aliasing={{2}: (9, {}), {3}: (10, {})} | custom-call | tf_op jit(solution)/shard_map/sector3/pallas_call | solution.py:142
  24.5 1.3 collective-permute-start.2
  25.8 2.1 %collective-permute-done.3.refs_2_.refs_3_ = f32[256,256]{1,0:T(8,128)S(1)} collective-permute-done((f32[256,256]{1,0:T(8,128)S(1)}, f32[256,256]{1,0:T(8,128)S(1)}, u32[]{:S(2)}, u32[]{:S(2)}) %collective-permute-start.3) | collective-permute-done | bytes 262176 | tf_op jit(solution)/shard_map/ppermute | solution.py:199
  27.9 3.0 %sector4.1 = (f32[256,256]{1,0:T(8,128)S(1)}, f32[8,256,256]{2,1,0:T(8,128)}, f32[2,4,4,3,32,256]{5,4,3,2,1,0:T(8,128)}, f32[2,4,4,3,32,256]{5,4,3,2,1,0:T(8,128)}) custom-call(s32[28]{0:T(128)S(1)} %concatenate.27.ints.refs_0_, f32[4]{0:T(128)S(1)} %bitcast.104, ...), custom_call_target="tpu_custom_call", output_to_operand_aliasing={{2}: (9, {}), {3}: (10, {})} | custom-call | tf_op jit(solution)/shard_map/sector4/pallas_call | solution.py:142
  32.2 2.7 %collective-permute-done.2.refs_2_.refs_3_ = f32[256,256]{1,0:T(8,128)S(1)} collective-permute-done((f32[256,256]{1,0:T(8,128)S(1)}, f32[256,256]{1,0:T(8,128)S(1)}, u32[]{:S(2)}, u32[]{:S(2)}) %collective-permute-start.2) | collective-permute-done | bytes 262176 | tf_op jit(solution)/shard_map/ppermute | solution.py:199
  35.0 4.6 %sector5.1 = (f32[256,256]{1,0:T(8,128)S(1)}, f32[8,256,256]{2,1,0:T(8,128)}, f32[2,4,4,3,32,256]{5,4,3,2,1,0:T(8,128)}, f32[2,4,4,3,32,256]{5,4,3,2,1,0:T(8,128)}) custom-call(s32[28]{0:T(128)S(1)} %concatenate.27.ints.refs_0_, f32[4]{0:T(128)S(1)} %bitcast.105, ...), custom_call_target="tpu_custom_call", output_to_operand_aliasing={{2}: (9, {}), {3}: (10, {})} | custom-call | tf_op jit(solution)/shard_map/sector5/pallas_call | solution.py:142
  40.8 4.2 %collective-permute-done.5.refs_2_.refs_3_ = f32[256,256]{1,0:T(8,128)S(1)} collective-permute-done((f32[256,256]{1,0:T(8,128)S(1)}, f32[256,256]{1,0:T(8,128)S(1)}, u32[]{:S(2)}, u32[]{:S(2)}) %collective-permute-start.5) | collective-permute-done | bytes 262176 | tf_op jit(solution)/shard_map/ppermute | solution.py:199
  45.0 6.4 %sector6.1 = (f32[256,256]{1,0:T(8,128)S(1)}, f32[8,256,256]{2,1,0:T(8,128)}, f32[2,4,4,3,32,256]{5,4,3,2,1,0:T(8,128)}, f32[2,4,4,3,32,256]{5,4,3,2,1,0:T(8,128)}) custom-call(s32[28]{0:T(128)S(1)} %concatenate.27.ints.refs_0_, f32[4]{0:T(128)S(1)} %bitcast.106, ...), custom_call_target="tpu_custom_call", output_to_operand_aliasing={{2}: (9, {}), {3}: (10, {})} | custom-call | tf_op jit(solution)/shard_map/sector6/pallas_call | solution.py:142
  51.4 1.3 collective-permute-start.7
  53.5 6.4 %sector7.1 = (f32[256,256]{1,0:T(8,128)S(1)}, f32[8,256,256]{2,1,0:T(8,128)}, f32[2,4,4,3,32,256]{5,4,3,2,1,0:T(8,128)}, f32[2,4,4,3,32,256]{5,4,3,2,1,0:T(8,128)}) custom-call(s32[28]{0:T(128)S(1)} %concatenate.27.ints.refs_0_, f32[4]{0:T(128)S(1)} %bitcast.107, ...), custom_call_target="tpu_custom_call", output_to_operand_aliasing={{2}: (9, {}), {3}: (10, {})} | custom-call | tf_op jit(solution)/shard_map/sector7/pallas_call | solution.py:142
  61.8 6.4 %sector8.1 = (f32[256,256]{1,0:T(8,128)S(1)}, f32[8,256,256]{2,1,0:T(8,128)}, f32[2,4,4,3,32,256]{5,4,3,2,1,0:T(8,128)}, f32[2,4,4,3,32,256]{5,4,3,2,1,0:T(8,128)}) custom-call(s32[28]{0:T(128)S(1)} %concatenate.27.ints.refs_0_, f32[4]{0:T(128)S(1)} %bitcast.108, ...), custom_call_target="tpu_custom_call", output_to_operand_aliasing={{2}: (9, {}), {3}: (10, {})} | custom-call | tf_op jit(solution)/shard_map/sector8/pallas_call | solution.py:142
  70.2 6.6 %sector9.1 = (f32[256,256]{1,0:T(8,128)S(1)}, f32[8,256,256]{2,1,0:T(8,128)}, f32[2,4,4,3,32,256]{5,4,3,2,1,0:T(8,128)}, f32[2,4,4,3,32,256]{5,4,3,2,1,0:T(8,128)}) custom-call(s32[28]{0:T(128)S(1)} %concatenate.27.ints.refs_0_, f32[4]{0:T(128)S(1)} %bitcast.109, ...), custom_call_target="tpu_custom_call", output_to_operand_aliasing={{2}: (9, {}), {3}: (10, {})} | custom-call | tf_op jit(solution)/shard_map/sector9/pallas_call | solution.py:142
  78.5 6.4 %sector10.1 = (f32[256,256]{1,0:T(8,128)S(1)}, f32[8,256,256]{2,1,0:T(8,128)}, f32[2,4,4,3,32,256]{5,4,3,2,1,0:T(8,128)}, f32[2,4,4,3,32,256]{5,4,3,2,1,0:T(8,128)}) custom-call(s32[28]{0:T(128)S(1)} %concatenate.27.ints.refs_0_, f32[4]{0:T(128)S(1)} %bitcast.110, ...), custom_call_target="tpu_custom_call", output_to_operand_aliasing={{2}: (9, {}), {3}: (10, {})} | custom-call | tf_op jit(solution)/shard_map/sector10/pallas_call | solution.py:142
  87.1 6.4 %sector11.1 = (f32[256,256]{1,0:T(8,128)S(1)}, f32[8,256,256]{2,1,0:T(8,128)}, f32[2,4,4,3,32,256]{5,4,3,2,1,0:T(8,128)}, f32[2,4,4,3,32,256]{5,4,3,2,1,0:T(8,128)}) custom-call(s32[28]{0:T(128)S(1)} %concatenate.27.ints.refs_0_, f32[4]{0:T(128)S(1)} %bitcast.111, ...), custom_call_target="tpu_custom_call", output_to_operand_aliasing={{2}: (9, {}), {3}: (10, {})} | custom-call | tf_op jit(solution)/shard_map/sector11/pallas_call | solution.py:142
  93.5 1.3 collective-permute-start.10
  95.4 6.4 %sector12.1 = (f32[256,256]{1,0:T(8,128)S(1)}, f32[8,256,256]{2,1,0:T(8,128)}, f32[2,4,4,3,32,256]{5,4,3,2,1,0:T(8,128)}, f32[2,4,4,3,32,256]{5,4,3,2,1,0:T(8,128)}) custom-call(s32[28]{0:T(128)S(1)} %concatenate.27.ints.refs_0_, f32[4]{0:T(128)S(1)} %bitcast.112, ...), custom_call_target="tpu_custom_call", output_to_operand_aliasing={{2}: (9, {}), {3}: (10, {})} | custom-call | tf_op jit(solution)/shard_map/sector12/pallas_call | solution.py:142
  103.7 6.4 %sector13.1 = (f32[256,256]{1,0:T(8,128)S(1)}, f32[8,256,256]{2,1,0:T(8,128)}, f32[2,4,4,3,32,256]{5,4,3,2,1,0:T(8,128)}, f32[2,4,4,3,32,256]{5,4,3,2,1,0:T(8,128)}) custom-call(s32[28]{0:T(128)S(1)} %concatenate.27.ints.refs_0_, f32[4]{0:T(128)S(1)} %bitcast.113, ...), custom_call_target="tpu_custom_call", output_to_operand_aliasing={{2}: (9, {}), {3}: (10, {})} | custom-call | tf_op jit(solution)/shard_map/sector13/pallas_call | solution.py:142
  112.1 6.5 %sector14.1 = (f32[256,256]{1,0:T(8,128)S(1)}, f32[8,256,256]{2,1,0:T(8,128)}, f32[2,4,4,3,32,256]{5,4,3,2,1,0:T(8,128)}, f32[2,4,4,3,32,256]{5,4,3,2,1,0:T(8,128)}) custom-call(s32[28]{0:T(128)S(1)} %concatenate.27.ints.refs_0_, f32[4]{0:T(128)S(1)} %bitcast.114, ...), custom_call_target="tpu_custom_call", output_to_operand_aliasing={{2}: (9, {}), {3}: (10, {})} | custom-call | tf_op jit(solution)/shard_map/sector14/pallas_call | solution.py:142
  120.4 6.4 %sector15.1 = (f32[256,256]{1,0:T(8,128)S(1)}, f32[8,256,256]{2,1,0:T(8,128)}, f32[2,4,4,3,32,256]{5,4,3,2,1,0:T(8,128)}, f32[2,4,4,3,32,256]{5,4,3,2,1,0:T(8,128)}) custom-call(s32[28]{0:T(128)S(1)} %concatenate.27.ints.refs_0_, f32[4]{0:T(128)S(1)} %bitcast.115, ...), custom_call_target="tpu_custom_call", output_to_operand_aliasing={{2}: (9, {}), {3}: (10, {})} | custom-call | tf_op jit(solution)/shard_map/sector15/pallas_call | solution.py:142
  128.9 6.5 %sector16.1 = (f32[256,256]{1,0:T(8,128)}, f32[8,256,256]{2,1,0:T(8,128)}, f32[2,4,4,3,32,256]{5,4,3,2,1,0:T(8,128)}, f32[2,4,4,3,32,256]{5,4,3,2,1,0:T(8,128)}) custom-call(s32[28]{0:T(128)S(1)} %concatenate.27.ints.refs_0_, f32[4]{0:T(128)S(1)} %bitcast.116, ...), custom_call_target="tpu_custom_call", output_to_operand_aliasing={{2}: (9, {}), {3}: (10, {})} | custom-call | tf_op jit(solution)/shard_map/sector16/pallas_call | solution.py:142
  135.4 1.8 collective-permute-done.14.refs_2_
  137.2 6.4 %sector17.1 = (f32[256,256]{1,0:T(8,128)}, f32[8,256,256]{2,1,0:T(8,128)}, f32[2,4,4,3,32,256]{5,4,3,2,1,0:T(8,128)}, f32[2,4,4,3,32,256]{5,4,3,2,1,0:T(8,128)}) custom-call(s32[28]{0:T(128)S(1)} %concatenate.27.ints.refs_0_, f32[4]{0:T(128)S(1)} %bitcast.117, ...), custom_call_target="tpu_custom_call", output_to_operand_aliasing={{2}: (9, {}), {3}: (10, {})} | custom-call | tf_op jit(solution)/shard_map/sector17/pallas_call | solution.py:142
  143.9 5.9 %collective-permute-done.16 = f32[2,4,4,3,32,256]{5,4,3,2,1,0:T(8,128)S(1)} collective-permute-done((f32[2,4,4,3,32,256]{5,4,3,2,1,0:T(8,128)}, f32[2,4,4,3,32,256]{5,4,3,2,1,0:T(8,128)S(1)}, u32[]{:S(2)}, u32[]{:S(2)}) %collective-permute-start.16) | collective-permute-done | bytes 3145760 | tf_op jit(solution)/shard_map/ppermute | solution.py:177
  149.8 2.8 %add.51 = f32[2,4,4,3,32,256]{5,4,3,2,1,0:T(8,128)S(1)} add(f32[2,4,4,3,32,256]{5,4,3,2,1,0:T(8,128)} %get-tuple-element.141, f32[2,4,4,3,32,256]{5,4,3,2,1,0:T(8,128)S(1)} %collective-permute-done.16) | non-fusion elementwise | flops 786432 | bytes 9437184 | tf_op jit(solution)/shard_map/add | solution.py:177
  153.0 4.2 %collective-permute-start.25 = (f32[2,96,256]{2,1,0:T(8,128)S(1)}, f32[2,96,256]{2,1,0:T(8,128)S(1)}, u32[]{:S(2)}, u32[]{:S(2)}) collective-permute-start(f32[2,96,256]{2,1,0:T(8,128)S(1)} %get-tuple-element.155), channel_id=1, source_target_pairs={{0,8},{8,16},{16,24},{24,0},{1,9},{9,17},{17,25},{25,1},{2,10},{10... | collective-permute-start | bytes 589832 | tf_op jit(solution)/shard_map/ppermute | solution.py:160
  157.3 2.2 %collective-permute-start.27 = (f32[2,96,256]{2,1,0:T(8,128)S(1)}, f32[2,96,256]{2,1,0:T(8,128)S(1)}, u32[]{:S(2)}, u32[]{:S(2)}) collective-permute-start(f32[2,96,256]{2,1,0:T(8,128)S(1)} %get-tuple-element.156), channel_id=1, source_target_pairs={{0,24},{8,0},{16,8},{24,16},{1,25},{9,1},{17,9},{25,17},{2,26},{10... | collective-permute-start | bytes 589832 | tf_op jit(solution)/shard_map/ppermute | solution.py:160
  159.5 1.5 collective-permute-start.17
  161.0 1.8 collective-permute-start.19
  162.9 1.7 collective-permute-done.25
  164.7 3.1 %collective-permute-start.28 = (f32[4,96,256]{2,1,0:T(8,128)S(1)}, f32[4,96,256]{2,1,0:T(8,128)S(1)}, u32[]{:S(2)}, u32[]{:S(2)}) collective-permute-start(f32[4,96,256]{2,1,0:T(8,128)S(1)} %pad_maximum_fusion.3), channel_id=1, source_target_pairs={{0,24},{8,0},{16,8},{24,16},{1,25},{9,1},{17,9},{25,17},{2,26},{10... | collective-permute-start | bytes 1179656 | tf_op jit(solution)/shard_map/ppermute | solution.py:160
  168.0 2.9 %collective-permute-start.20 = (f32[4,96,256]{2,1,0:T(8,128)S(1)}, f32[4,96,256]{2,1,0:T(8,128)S(1)}, u32[]{:S(2)}, u32[]{:S(2)}) collective-permute-start(f32[4,96,256]{2,1,0:T(8,128)S(1)} %pad_maximum_fusion.1), channel_id=1, source_target_pairs={{0,6},{2,0},{4,2},{6,4},{1,7},{3,1},{5,3},{7,5},{8,14},{10,8},{12,... | collective-permute-start | bytes 1179656 | tf_op jit(solution)/shard_map/ppermute | solution.py:160
  171.0 4.6 %collective-permute-done.28 = f32[4,96,256]{2,1,0:T(8,128)S(1)} collective-permute-done((f32[4,96,256]{2,1,0:T(8,128)S(1)}, f32[4,96,256]{2,1,0:T(8,128)S(1)}, u32[]{:S(2)}, u32[]{:S(2)}) %collective-permute-start.28) | collective-permute-done | bytes 393248 | tf_op jit(solution)/shard_map/ppermute | solution.py:160
  175.6 3.5 %collective-permute-done.26 = f32[4,96,256]{2,1,0:T(8,128)S(1)} collective-permute-done((f32[4,96,256]{2,1,0:T(8,128)S(1)}, f32[4,96,256]{2,1,0:T(8,128)S(1)}, u32[]{:S(2)}, u32[]{:S(2)}) %collective-permute-start.26) | collective-permute-done | bytes 393248 | tf_op jit(solution)/shard_map/ppermute | solution.py:160
  179.2 1.5 collective-permute-start.29
  180.7 1.8 collective-permute-start.31
  182.7 3.2 %collective-permute-start.23 = (f32[48,256]{1,0:T(8,128)S(1)}, f32[48,256]{1,0:T(8,128)S(1)}, u32[]{:S(2)}, u32[]{:S(2)}) collective-permute-start(f32[48,256]{1,0:T(8,128)S(1)} %get-tuple-element.162), channel_id=1, source_target_pairs={{0,24},{8,0},{16,8},{24,16},{1,25},{9,1},{17,9},{25,17},{2,26},{10... | collective-permute-start | bytes 147464 | tf_op jit(solution)/shard_map/ppermute | solution.py:160
  186.0 1.9 collective-permute-start.32
  188.2 3.2 %collective-permute-start.24 = (f32[96,256]{1,0:T(8,128)S(1)}, f32[96,256]{1,0:T(8,128)S(1)}, u32[]{:S(2)}, u32[]{:S(2)}) collective-permute-start(f32[96,256]{1,0:T(8,128)S(1)} %pad_maximum_fusion.5), channel_id=1, source_target_pairs={{0,24},{8,0},{16,8},{24,16},{1,25},{9,1},{17,9},{25,17},{2,26},{10... | collective-permute-start | bytes 294920 | tf_op jit(solution)/shard_map/ppermute | solution.py:160
  191.5 2.4 %collective-permute-done.30 = f32[96,256]{1,0:T(8,128)S(1)} collective-permute-done((f32[96,256]{1,0:T(8,128)S(1)}, f32[96,256]{1,0:T(8,128)S(1)}, u32[]{:S(2)}, u32[]{:S(2)}) %collective-permute-start.30) | collective-permute-done | bytes 98336 | tf_op jit(solution)/shard_map/ppermute | solution.py:160
  193.9 3.4 %collective-permute-done.22 = f32[96,256]{1,0:T(8,128)S(1)} collective-permute-done((f32[96,256]{1,0:T(8,128)S(1)}, f32[96,256]{1,0:T(8,128)S(1)}, u32[]{:S(2)}, u32[]{:S(2)}) %collective-permute-start.22) | collective-permute-done | bytes 98336 | tf_op jit(solution)/shard_map/ppermute | solution.py:160
  (65 shorter events, 23.6 us)
Async XLA Ops:
  0.7 2.0 %copy-start = (f32[1,1,4]{2,1,0:T(1,128)S(1)}, f32[1,1,4]{2,1,0:T(1,128)}, u32[]{:S(2)}) copy-start(f32[1,1,4]{2,1,0:T(1,128)} %param.11) | copy-start | bytes 52
  5.8 10.5 %collective-permute-start.1 = (f32[256,256]{1,0:T(8,128)S(1)}, f32[256,256]{1,0:T(8,128)S(1)}, u32[]{:S(2)}, u32[]{:S(2)}) collective-permute-start(f32[256,256]{1,0:T(8,128)S(1)} %get-tuple-element.78), channel_id=1, source_target_pairs={{0,32},{32,64},{64,96},{1,33},{33,65},{65,97},{2,34},{34,66},{66,9... | collective-permute-start | bytes 786440 | tf_op jit(solution)/shard_map/ppermute | solution.py:199
  10.2 11.1 %collective-permute-start = (f32[256,256]{1,0:T(8,128)S(1)}, f32[256,256]{1,0:T(8,128)S(1)}, u32[]{:S(2)}, u32[]{:S(2)}) collective-permute-start(f32[256,256]{1,0:T(8,128)S(1)} %get-tuple-element.77), channel_id=1, source_target_pairs={{0,32},{32,64},{64,96},{1,33},{33,65},{65,97},{2,34},{34,66},{66,9... | collective-permute-start | bytes 786440 | tf_op jit(solution)/shard_map/ppermute | solution.py:199
  19.4 8.5 %collective-permute-start.3 = (f32[256,256]{1,0:T(8,128)S(1)}, f32[256,256]{1,0:T(8,128)S(1)}, u32[]{:S(2)}, u32[]{:S(2)}) collective-permute-start(f32[256,256]{1,0:T(8,128)S(1)} %get-tuple-element.86), channel_id=1, source_target_pairs={{0,32},{32,64},{64,96},{1,33},{33,65},{65,97},{2,34},{34,66},{66,9... | collective-permute-start | bytes 786440 | tf_op jit(solution)/shard_map/ppermute | solution.py:199
  24.5 10.5 %collective-permute-start.2 = (f32[256,256]{1,0:T(8,128)S(1)}, f32[256,256]{1,0:T(8,128)S(1)}, u32[]{:S(2)}, u32[]{:S(2)}) collective-permute-start(f32[256,256]{1,0:T(8,128)S(1)} %get-tuple-element.85), channel_id=1, source_target_pairs={{0,32},{32,64},{64,96},{1,33},{33,65},{65,97},{2,34},{34,66},{66,9... | collective-permute-start | bytes 786440 | tf_op jit(solution)/shard_map/ppermute | solution.py:199
  30.9 14.1 %collective-permute-start.5 = (f32[256,256]{1,0:T(8,128)S(1)}, f32[256,256]{1,0:T(8,128)S(1)}, u32[]{:S(2)}, u32[]{:S(2)}) collective-permute-start(f32[256,256]{1,0:T(8,128)S(1)} %get-tuple-element.94), channel_id=1, source_target_pairs={{0,32},{32,64},{64,96},{1,33},{33,65},{65,97},{2,34},{34,66},{66,9... | collective-permute-start | bytes 786440 | tf_op jit(solution)/shard_map/ppermute | solution.py:199
  39.5 13.9 %collective-permute-start.4 = (f32[256,256]{1,0:T(8,128)S(1)}, f32[256,256]{1,0:T(8,128)S(1)}, u32[]{:S(2)}, u32[]{:S(2)}) collective-permute-start(f32[256,256]{1,0:T(8,128)S(1)} %get-tuple-element.93), channel_id=1, source_target_pairs={{0,32},{32,64},{64,96},{1,33},{33,65},{65,97},{2,34},{34,66},{66,9... | collective-permute-start | bytes 786440 | tf_op jit(solution)/shard_map/ppermute | solution.py:199
  51.4 10.4 %collective-permute-start.7 = (f32[256,256]{1,0:T(8,128)S(1)}, f32[256,256]{1,0:T(8,128)S(1)}, u32[]{:S(2)}, u32[]{:S(2)}) collective-permute-start(f32[256,256]{1,0:T(8,128)S(1)} %get-tuple-element.102), channel_id=1, source_target_pairs={{0,32},{32,64},{64,96},{1,33},{33,65},{65,97},{2,34},{34,66},{66,9... | collective-permute-start | bytes 786440 | tf_op jit(solution)/shard_map/ppermute | solution.py:199
  59.9 10.3 %collective-permute-start.6 = (f32[256,256]{1,0:T(8,128)S(1)}, f32[256,256]{1,0:T(8,128)S(1)}, u32[]{:S(2)}, u32[]{:S(2)}) collective-permute-start(f32[256,256]{1,0:T(8,128)S(1)} %get-tuple-element.101), channel_id=1, source_target_pairs={{0,32},{32,64},{64,96},{1,33},{33,65},{65,97},{2,34},{34,66},{66,9... | collective-permute-start | bytes 786440 | tf_op jit(solution)/shard_map/ppermute | solution.py:199
  68.1 10.3 %collective-permute-start.9 = (f32[256,256]{1,0:T(8,128)S(1)}, f32[256,256]{1,0:T(8,128)S(1)}, u32[]{:S(2)}, u32[]{:S(2)}) collective-permute-start(f32[256,256]{1,0:T(8,128)S(1)} %get-tuple-element.110), channel_id=1, source_target_pairs={{0,32},{32,64},{64,96},{1,33},{33,65},{65,97},{2,34},{34,66},{66,9... | collective-permute-start | bytes 786440 | tf_op jit(solution)/shard_map/ppermute | solution.py:199
  76.8 10.3 %collective-permute-start.8 = (f32[256,256]{1,0:T(8,128)S(1)}, f32[256,256]{1,0:T(8,128)S(1)}, u32[]{:S(2)}, u32[]{:S(2)}) collective-permute-start(f32[256,256]{1,0:T(8,128)S(1)} %get-tuple-element.109), channel_id=1, source_target_pairs={{0,32},{32,64},{64,96},{1,33},{33,65},{65,97},{2,34},{34,66},{66,9... | collective-permute-start | bytes 786440 | tf_op jit(solution)/shard_map/ppermute | solution.py:199
  84.9 10.5 %collective-permute-start.11 = (f32[256,256]{1,0:T(8,128)S(1)}, f32[256,256]{1,0:T(8,128)S(1)}, u32[]{:S(2)}, u32[]{:S(2)}) collective-permute-start(f32[256,256]{1,0:T(8,128)S(1)} %get-tuple-element.118), channel_id=1, source_target_pairs={{0,32},{32,64},{64,96},{1,33},{33,65},{65,97},{2,34},{34,66},{66,9... | collective-permute-start | bytes 786440 | tf_op jit(solution)/shard_map/ppermute | solution.py:199
  93.5 10.3 %collective-permute-start.10 = (f32[256,256]{1,0:T(8,128)S(1)}, f32[256,256]{1,0:T(8,128)S(1)}, u32[]{:S(2)}, u32[]{:S(2)}) collective-permute-start(f32[256,256]{1,0:T(8,128)S(1)} %get-tuple-element.117), channel_id=1, source_target_pairs={{0,32},{32,64},{64,96},{1,33},{33,65},{65,97},{2,34},{34,66},{66,9... | collective-permute-start | bytes 786440 | tf_op jit(solution)/shard_map/ppermute | solution.py:199
  101.7 10.3 %collective-permute-start.13 = (f32[256,256]{1,0:T(8,128)S(1)}, f32[256,256]{1,0:T(8,128)S(1)}, u32[]{:S(2)}, u32[]{:S(2)}) collective-permute-start(f32[256,256]{1,0:T(8,128)S(1)} %get-tuple-element.126), channel_id=1, source_target_pairs={{0,32},{32,64},{64,96},{1,33},{33,65},{65,97},{2,34},{34,66},{66,9... | collective-permute-start | bytes 786440 | tf_op jit(solution)/shard_map/ppermute | solution.py:199
  110.2 10.3 %collective-permute-start.12 = (f32[256,256]{1,0:T(8,128)S(1)}, f32[256,256]{1,0:T(8,128)S(1)}, u32[]{:S(2)}, u32[]{:S(2)}) collective-permute-start(f32[256,256]{1,0:T(8,128)S(1)} %get-tuple-element.125), channel_id=1, source_target_pairs={{0,32},{32,64},{64,96},{1,33},{33,65},{65,97},{2,34},{34,66},{66,9... | collective-permute-start | bytes 786440 | tf_op jit(solution)/shard_map/ppermute | solution.py:199
  118.5 10.3 %collective-permute-start.15 = (f32[256,256]{1,0:T(8,128)S(1)}, f32[256,256]{1,0:T(8,128)S(1)}, u32[]{:S(2)}, u32[]{:S(2)}) collective-permute-start(f32[256,256]{1,0:T(8,128)S(1)} %get-tuple-element.134), channel_id=1, source_target_pairs={{0,32},{32,64},{64,96},{1,33},{33,65},{65,97},{2,34},{34,66},{66,9... | collective-permute-start | bytes 786440 | tf_op jit(solution)/shard_map/ppermute | solution.py:199
  126.8 10.3 %collective-permute-start.14 = (f32[256,256]{1,0:T(8,128)S(1)}, f32[256,256]{1,0:T(8,128)S(1)}, u32[]{:S(2)}, u32[]{:S(2)}) collective-permute-start(f32[256,256]{1,0:T(8,128)S(1)} %get-tuple-element.133), channel_id=1, source_target_pairs={{0,32},{32,64},{64,96},{1,33},{33,65},{65,97},{2,34},{34,66},{66,9... | collective-permute-start | bytes 786440 | tf_op jit(solution)/shard_map/ppermute | solution.py:199
  143.6 6.2 %collective-permute-start.16 = (f32[2,4,4,3,32,256]{5,4,3,2,1,0:T(8,128)}, f32[2,4,4,3,32,256]{5,4,3,2,1,0:T(8,128)S(1)}, u32[]{:S(2)}, u32[]{:S(2)}) collective-permute-start(f32[2,4,4,3,32,256]{5,4,3,2,1,0:T(8,128)} %get-tuple-element.142), channel_id=1, source_target_pairs={{0,1},{1,0},{2,3},{3,2},{4,5},{5,4},{6,7},{7,6},{8,9},{9,8},{10,11... | collective-permute-start | bytes 9437192 | tf_op jit(solution)/shard_map/ppermute | solution.py:177
  153.0 11.5 %collective-permute-start.25 = (f32[2,96,256]{2,1,0:T(8,128)S(1)}, f32[2,96,256]{2,1,0:T(8,128)S(1)}, u32[]{:S(2)}, u32[]{:S(2)}) collective-permute-start(f32[2,96,256]{2,1,0:T(8,128)S(1)} %get-tuple-element.155), channel_id=1, source_target_pairs={{0,8},{8,16},{16,24},{24,0},{1,9},{9,17},{17,25},{25,1},{2,10},{10... | collective-permute-start | bytes 589832 | tf_op jit(solution)/shard_map/ppermute | solution.py:160
  157.3 7.3 %collective-permute-start.27 = (f32[2,96,256]{2,1,0:T(8,128)S(1)}, f32[2,96,256]{2,1,0:T(8,128)S(1)}, u32[]{:S(2)}, u32[]{:S(2)}) collective-permute-start(f32[2,96,256]{2,1,0:T(8,128)S(1)} %get-tuple-element.156), channel_id=1, source_target_pairs={{0,24},{8,0},{16,8},{24,16},{1,25},{9,1},{17,9},{25,17},{2,26},{10... | collective-permute-start | bytes 589832 | tf_op jit(solution)/shard_map/ppermute | solution.py:160
  159.5 8.4 %collective-permute-start.17 = (f32[2,96,256]{2,1,0:T(8,128)S(1)}, f32[2,96,256]{2,1,0:T(8,128)S(1)}, u32[]{:S(2)}, u32[]{:S(2)}) collective-permute-start(f32[2,96,256]{2,1,0:T(8,128)S(1)} %get-tuple-element.149), channel_id=1, source_target_pairs={{0,2},{2,4},{4,6},{6,0},{1,3},{3,5},{5,7},{7,1},{8,10},{10,12},{12... | collective-permute-start | bytes 589832 | tf_op jit(solution)/shard_map/ppermute | solution.py:160
  161.0 6.9 %collective-permute-start.19 = (f32[2,96,256]{2,1,0:T(8,128)S(1)}, f32[2,96,256]{2,1,0:T(8,128)S(1)}, u32[]{:S(2)}, u32[]{:S(2)}) collective-permute-start(f32[2,96,256]{2,1,0:T(8,128)S(1)} %get-tuple-element.150), channel_id=1, source_target_pairs={{0,6},{2,0},{4,2},{6,4},{1,7},{3,1},{5,3},{7,5},{8,14},{10,8},{12,... | collective-permute-start | bytes 589832 | tf_op jit(solution)/shard_map/ppermute | solution.py:160
  164.7 10.9 %collective-permute-start.28 = (f32[4,96,256]{2,1,0:T(8,128)S(1)}, f32[4,96,256]{2,1,0:T(8,128)S(1)}, u32[]{:S(2)}, u32[]{:S(2)}) collective-permute-start(f32[4,96,256]{2,1,0:T(8,128)S(1)} %pad_maximum_fusion.3), channel_id=1, source_target_pairs={{0,24},{8,0},{16,8},{24,16},{1,25},{9,1},{17,9},{25,17},{2,26},{10... | collective-permute-start | bytes 1179656 | tf_op jit(solution)/shard_map/ppermute | solution.py:160
  167.8 11.3 %collective-permute-start.26 = (f32[4,96,256]{2,1,0:T(8,128)S(1)}, f32[4,96,256]{2,1,0:T(8,128)S(1)}, u32[]{:S(2)}, u32[]{:S(2)}) collective-permute-start(f32[4,96,256]{2,1,0:T(8,128)S(1)} %pad_maximum_fusion.2), channel_id=1, source_target_pairs={{0,8},{8,16},{16,24},{24,0},{1,9},{9,17},{17,25},{25,1},{2,10},{10... | collective-permute-start | bytes 1179656 | tf_op jit(solution)/shard_map/ppermute | solution.py:160
  168.0 14.5 %collective-permute-start.20 = (f32[4,96,256]{2,1,0:T(8,128)S(1)}, f32[4,96,256]{2,1,0:T(8,128)S(1)}, u32[]{:S(2)}, u32[]{:S(2)}) collective-permute-start(f32[4,96,256]{2,1,0:T(8,128)S(1)} %pad_maximum_fusion.1), channel_id=1, source_target_pairs={{0,6},{2,0},{4,2},{6,4},{1,7},{3,1},{5,3},{7,5},{8,14},{10,8},{12,... | collective-permute-start | bytes 1179656 | tf_op jit(solution)/shard_map/ppermute | solution.py:160
  170.9 11.6 %collective-permute-start.18 = (f32[4,96,256]{2,1,0:T(8,128)S(1)}, f32[4,96,256]{2,1,0:T(8,128)S(1)}, u32[]{:S(2)}, u32[]{:S(2)}) collective-permute-start(f32[4,96,256]{2,1,0:T(8,128)S(1)} %pad_maximum_fusion), channel_id=1, source_target_pairs={{0,2},{2,4},{4,6},{6,0},{1,3},{3,5},{5,7},{7,1},{8,10},{10,12},{12... | collective-permute-start | bytes 1179656 | tf_op jit(solution)/shard_map/ppermute | solution.py:160
  179.2 6.7 %collective-permute-start.29 = (f32[48,256]{1,0:T(8,128)S(1)}, f32[48,256]{1,0:T(8,128)S(1)}, u32[]{:S(2)}, u32[]{:S(2)}) collective-permute-start(f32[48,256]{1,0:T(8,128)S(1)} %get-tuple-element.167), channel_id=1, source_target_pairs={{0,2},{2,4},{4,6},{6,0},{1,3},{3,5},{5,7},{7,1},{8,10},{10,12},{12... | collective-permute-start | bytes 147464 | tf_op jit(solution)/shard_map/ppermute | solution.py:160
  180.7 5.2 %collective-permute-start.31 = (f32[48,256]{1,0:T(8,128)S(1)}, f32[48,256]{1,0:T(8,128)S(1)}, u32[]{:S(2)}, u32[]{:S(2)}) collective-permute-start(f32[48,256]{1,0:T(8,128)S(1)} %get-tuple-element.168), channel_id=1, source_target_pairs={{0,6},{2,0},{4,2},{6,4},{1,7},{3,1},{5,3},{7,5},{8,14},{10,8},{12,... | collective-permute-start | bytes 147464 | tf_op jit(solution)/shard_map/ppermute | solution.py:160
  182.6 5.5 %collective-permute-start.21 = (f32[48,256]{1,0:T(8,128)S(1)}, f32[48,256]{1,0:T(8,128)S(1)}, u32[]{:S(2)}, u32[]{:S(2)}) collective-permute-start(f32[48,256]{1,0:T(8,128)S(1)} %get-tuple-element.161), channel_id=1, source_target_pairs={{0,8},{8,16},{16,24},{24,0},{1,9},{9,17},{17,25},{25,1},{2,10},{10... | collective-permute-start | bytes 147464 | tf_op jit(solution)/shard_map/ppermute | solution.py:160
  182.7 5.4 %collective-permute-start.23 = (f32[48,256]{1,0:T(8,128)S(1)}, f32[48,256]{1,0:T(8,128)S(1)}, u32[]{:S(2)}, u32[]{:S(2)}) collective-permute-start(f32[48,256]{1,0:T(8,128)S(1)} %get-tuple-element.162), channel_id=1, source_target_pairs={{0,24},{8,0},{16,8},{24,16},{1,25},{9,1},{17,9},{25,17},{2,26},{10... | collective-permute-start | bytes 147464 | tf_op jit(solution)/shard_map/ppermute | solution.py:160
  186.0 5.5 %collective-permute-start.32 = (f32[96,256]{1,0:T(8,128)S(1)}, f32[96,256]{1,0:T(8,128)S(1)}, u32[]{:S(2)}, u32[]{:S(2)}) collective-permute-start(f32[96,256]{1,0:T(8,128)S(1)} %pad_maximum_fusion.7), channel_id=1, source_target_pairs={{0,6},{2,0},{4,2},{6,4},{1,7},{3,1},{5,3},{7,5},{8,14},{10,8},{12,... | collective-permute-start | bytes 294920 | tf_op jit(solution)/shard_map/ppermute | solution.py:160
  187.9 5.9 %collective-permute-start.30 = (f32[96,256]{1,0:T(8,128)S(1)}, f32[96,256]{1,0:T(8,128)S(1)}, u32[]{:S(2)}, u32[]{:S(2)}) collective-permute-start(f32[96,256]{1,0:T(8,128)S(1)} %pad_maximum_fusion.6), channel_id=1, source_target_pairs={{0,2},{2,4},{4,6},{6,0},{1,3},{3,5},{5,7},{7,1},{8,10},{10,12},{12... | collective-permute-start | bytes 294920 | tf_op jit(solution)/shard_map/ppermute | solution.py:160
  188.2 5.7 %collective-permute-start.24 = (f32[96,256]{1,0:T(8,128)S(1)}, f32[96,256]{1,0:T(8,128)S(1)}, u32[]{:S(2)}, u32[]{:S(2)}) collective-permute-start(f32[96,256]{1,0:T(8,128)S(1)} %pad_maximum_fusion.5), channel_id=1, source_target_pairs={{0,24},{8,0},{16,8},{24,16},{1,25},{9,1},{17,9},{25,17},{2,26},{10... | collective-permute-start | bytes 294920 | tf_op jit(solution)/shard_map/ppermute | solution.py:160
  191.4 5.9 %collective-permute-start.22 = (f32[96,256]{1,0:T(8,128)S(1)}, f32[96,256]{1,0:T(8,128)S(1)}, u32[]{:S(2)}, u32[]{:S(2)}) collective-permute-start(f32[96,256]{1,0:T(8,128)S(1)} %pad_maximum_fusion.4), channel_id=1, source_target_pairs={{0,8},{8,16},{16,24},{24,0},{1,9},{9,17},{17,25},{25,1},{2,10},{10... | collective-permute-start | bytes 294920 | tf_op jit(solution)/shard_map/ppermute | solution.py:160
where the time goes:
time: 199 us; the launch traced here: 198 us
  Pallas kernels  98.9 us (50%)
  starting transfers between devices  48.8 us (25%)
  waiting for transfers between devices  44.3 us (22%)
  other arithmetic  4.01 us (2%)
    pallas_call x18, Pallas kernels, sector_step(): pl.pallas_call(kernel, in_specs=[SCALAR] * 2 + [LOCAL] * 3 + [FAR] * (4 +...  96.9 us
    ppermute x16, starting transfers between devices, turned(): return lax.ppermute(x, axis, [(i, (i + by) % 4) for i in range(4)])  27.9 us
    ppermute x16, waiting for transfers between devices, shards(): lax.ppermute(environ, 'site', [(0, 1), (1, 2), (2, 3)])  22.9 us
    ppermute x16, starting transfers between devices, shards(): lax.ppermute(environ, 'site', [(0, 1), (1, 2), (2, 3)])  20.7 us
    ppermute x16, waiting for transfers between devices, turned(): return lax.ppermute(x, axis, [(i, (i + by) % 4) for i in range(4)])  15.6 us
    ppermute x1, waiting for transfers between devices, reduced(): both = keep + lax.ppermute(send, 'core', [(0, 1), (1, 0)])  5.86 us
  transfers between devices with their start and end apart: 33, of which 22 were waited for; matrix products, arithmetic and copies ran while one was open for 0% of the time, Pallas kernels for 44%

commit v1 on v0

--- a/solution.py
+++ b/solution.py
@@ -33,33 +33,12 @@
     return jnp.where((i < rows) & (j < columns), x, 0.0)
 
 
-def fetch(q, left, mps, psi, rights, stage, sems, wait):
-    below, above = jnp.maximum(q - 1, 0), jnp.minimum(q + 1, NQ - 1)
-    sources = (left.at[q], mps.at[0, q], mps.at[1, below], psi.at[0, q], psi.at[1, q], rights.at[q], rights.at[above], left.at[below])
-    for i, source in enumerate(sources):
-        copy = pltpu.make_async_copy(source, stage.at[i], sems.at[i])
-        copy.wait() if wait else copy.start()
-
-
-def first_kernel(ints, left, mps, psi, rights, stage, sems):
-    @pl.when(ints[0] == 0)
-    def _():
-        fetch(0, left, mps, psi, rights, stage, sems, False)
-        fetch(0, left, mps, psi, rights, stage, sems, True)
-
-
-def sector_kernel(step, ints, floats, arrived, previous, stage, left, mps, psi, rights, *rest):
-    environ, staged, keep, send, results, total, sems, stores = rest[-8:]
+def sector_kernel(step, ints, floats, arrived, previous, left, mps, psi, rights, *rest):
+    environ, keep, send, results, total, stores = rest[-6:]
     site, my_z, my_x, core = ints[0], ints[1], ints[2], ints[3]
     q = step - LAG * site
     below = jnp.maximum(q - 1, 0)
     above = jnp.minimum(q + 1, NQ - 1)
-    more = (q >= -1) & (q < NQ - 1) & (step < LAST - 1)
-
-    @pl.when(more)
-    def _():
-        fetch(q + 1, left, mps, psi, rights, staged, sems, False)
-
     @pl.when((q >= 0) & (q < NQ))
     def _():
         size, under, over = ints[4 + q], ints[4 + below], ints[4 + above]
@@ -67,11 +46,11 @@
         present_above = jnp.where(q < NQ - 1, present_above, 0.0)
         c0 = jnp.where(site == 0, present, 1.0) * floats[0]
         c1 = jnp.where(site == 0, ints[16 + below].astype(f32), 1.0) * floats[1]
-        now = jnp.where(site == 0, stage[0], arrived[...])
-        before = jnp.where(site == 0, stage[7], previous[...])
+        now = jnp.where(site == 0, left[q], arrived[...])
+        before = jnp.where(site == 0, left[below], previous[...])
         before = jnp.where(q > 0, before, 0.0)
-        s = framed(stage[1], size, size)
-        u = framed(stage[2], under, size)
+        s = framed(mps[0, q], size, size)
+        u = framed(mps[1, below], under, size)
         first = c0 * product(halves(now), halves(s), ((1,), (0,)))
         second = c1 * product(halves(before), halves(u), ((1,), (0,)))
         moved = product(halves(s.T), halves(first), ((1,), (0,))) + product(
@@ -86,8 +65,8 @@
         def apply(state, _):
             c = jnp.where(state == 0, floats[2] * present, floats[3] * present_above)
             n = jnp.where(state == 0, size, over)
-            part = c * product(halves(total[...]), halves(stage[3 + state]), ((1,), (0,)))
-            results[state] = product(halves(part), halves(framed(stage[5 + state], n, n)), ((1,), (1,)))
+            part = c * product(halves(total[...]), halves(psi[state, q]), ((1,), (0,)))
+            results[state] = product(halves(part), halves(framed(rights[jnp.where(state == 0, q, above)], n, n)), ((1,), (1,)))
 
             def place(i, _):
                 piece = (W // ROWS) * q + i
@@ -111,29 +90,17 @@
             return lax.fori_loop(0, W // ROWS, place, 0)
 
         lax.fori_loop(0, 2, apply, 0)
-        pltpu.make_async_copy(results, stage.at[pl.ds(0, 2)], stores).wait()
-
-    @pl.when(more)
-    def _():
-        fetch(q + 1, left, mps, psi, rights, staged, sems, True)
+        pltpu.make_async_copy(results, psi.at[:, 0], stores).wait()
 
 
 LAST = NQ + LAG * (SITES - 1)
 SCALAR = pl.BlockSpec(memory_space=pltpu.SMEM)
 LOCAL = pl.BlockSpec(memory_space=pltpu.VMEM)
 FAR = pl.BlockSpec(memory_space=pltpu.HBM)
-STAGE = jax.ShapeDtypeStruct((8, W, W), f32)
-GRANT = pltpu.CompilerParams(vmem_limit_bytes=53 * 2**20)
+GRANT = pltpu.CompilerParams(vmem_limit_bytes=8 * 2**20)
 
 
-def first_stage(ints, left, mps, psi, rights):
-    return pl.pallas_call(
-        first_kernel, in_specs=[SCALAR] + [FAR] * 4, out_specs=LOCAL, out_shape=STAGE,
-        scratch_shapes=[pltpu.SemaphoreType.DMA((8,))], compiler_params=GRANT, name="first",
-    )(ints, left, mps, psi, rights)
-
-
-def sector_step(step, ints, floats, arrived, previous, stage, left, mps, psi, rights, held):
+def sector_step(step, ints, floats, arrived, previous, left, mps, psi, rights, held):
     shape = jax.ShapeDtypeStruct((2, 4, 4, 3, ROWS, W), f32)
 
     def kernel(*refs):
@@ -141,19 +108,18 @@
 
     return pl.pallas_call(
         kernel,
-        in_specs=[SCALAR] * 2 + [LOCAL] * 3 + [FAR] * (4 + len(held)),
-        out_specs=[LOCAL, LOCAL, FAR, FAR],
-        out_shape=[jax.ShapeDtypeStruct((W, W), f32), STAGE, shape, shape],
+        in_specs=[SCALAR] * 2 + [LOCAL] * 6 + [FAR] * len(held),
+        out_specs=[LOCAL, FAR, FAR],
+        out_shape=[jax.ShapeDtypeStruct((W, W), f32), shape, shape],
         scratch_shapes=[
             pltpu.VMEM((2, W, W), f32),
             pltpu.VMEM((W, W), f32),
-            pltpu.SemaphoreType.DMA((8,)),
             pltpu.SemaphoreType.DMA,
         ],
-        input_output_aliases={9: 2, 10: 3} if held else {},
+        input_output_aliases={8: 1, 9: 2} if held else {},
         compiler_params=GRANT,
         name=f"sector{step}",
-    )(ints, floats, arrived, previous, stage, left, mps, psi, rights, *held)
+    )(ints, floats, arrived, previous, left, mps, psi, rights, *held)
 
 
 def turned(x, axis, by):
@@ -190,11 +156,10 @@
     nothing = jnp.zeros((W, W), f32)
     arrivals = {}
     held = ()
-    stage = first_stage(ints, *sources)
     for step in range(LAST):
         arrived = arrivals.get(step, nothing)
-        environ, stage, *held = sector_step(
-            step, ints, floats, arrived, arrivals.get(step - 1, nothing), stage, *sources, tuple(held))
+        environ, *held = sector_step(
+            step, ints, floats, arrived, arrivals.get(step - 1, nothing), *sources, tuple(held))
         if step + LAG < LAST:
             arrivals[step + LAG] = lax.ppermute(environ, "site", [(0, 1), (1, 2), (2, 3)])
     return reduced(*held)

time: 199 us -> 174 us (0.87)
  Pallas kernels: 98.9 us -> 53.9 us
  waiting for transfers between devices: 44.3 us -> 59.8 us
  local copies, waits for them, and re-layouts: 1.35 us -> 11.4 us
  starting transfers between devices: 48.8 us -> 46.1 us
  other arithmetic: 4.01 us -> 1.85 us
    pallas_call x19 -> x18, Pallas kernels: 98.9 us -> 53.9 us  [sector_step(): pl.pallas_call(kernel, in_specs=[SCALAR] * 2 + [LOCAL] * 6 + [FAR] * len(...]
    ppermute x16, waiting for transfers between devices: 22.9 us -> 38.2 us  [shards(): lax.ppermute(environ, 'site', [(0, 1), (1, 2), (2, 3)])]
    unnamed x2 -> x20, local copies, waits for them, and re-layouts: 0.01 us -> 10 us
    ppermute x16, starting transfers between devices: 27.9 us -> 25.1 us  [turned(): return lax.ppermute(x, axis, [(i, (i + by) % 4) for i in range(4)])]
    add x1, other arithmetic: 2.85 us -> 0.69 us  [reduced(): both = keep + lax.ppermute(send, 'core', [(0, 1), (1, 0)])]
  transfers between devices with their start and end apart: 33 -> 33, of which waited for: 22 -> 22; matrix products, arithmetic and copies ran while one was open for 0% -> 0% of each run, Pallas kernels for 44% -> 28%
where the time goes in v1:
time: 174 us
  waiting for transfers between devices  59.8 us (34%)
  Pallas kernels  53.9 us (31%)
  starting transfers between devices  46.1 us (26%)
  local copies, waits for them, and re-layouts  11.4 us (7%)
  other arithmetic  1.85 us (1%)
    pallas_call x18, Pallas kernels, sector_step(): pl.pallas_call(kernel, in_specs=[SCALAR] * 2 + [LOCAL] * 6 + [FAR] * len(...  53.9 us
    ppermute x16, waiting for transfers between devices, shards(): lax.ppermute(environ, 'site', [(0, 1), (1, 2), (2, 3)])  38.2 us
    ppermute x16, starting transfers between devices, turned(): return lax.ppermute(x, axis, [(i, (i + by) % 4) for i in range(4)])  25.1 us
    ppermute x16, starting transfers between devices, shards(): lax.ppermute(environ, 'site', [(0, 1), (1, 2), (2, 3)])  20.9 us
    ppermute x16, waiting for transfers between devices, turned(): return lax.ppermute(x, axis, [(i, (i + by) % 4) for i in range(4)])  15.9 us
    unnamed x20, local copies, waits for them, and re-layouts  10 us
    ppermute x1, waiting for transfers between devices, reduced(): both = keep + lax.ppermute(send, 'core', [(0, 1), (1, 0)])  5.65 us
  transfers between devices with their start and end apart: 33, of which 22 were waited for; matrix products, arithmetic and copies ran while one was open for 0% of the time, Pallas kernels for 28%

profile of v1, /device:TPU:24, one launch (start us, length us, event | category | flops | bytes accessed | tf_op | source)
XLA Modules:
  0.0 173.5 jit_solution(9473238346410793071)
XLA Ops:
  0.8 2.8 %copy-done = f32[1,2,12,256,256]{4,3,2,1,0:T(8,128)S(1)} copy-done((f32[1,2,12,256,256]{4,3,2,1,0:T(8,128)S(1)}, f32[1,2,12,256,256]{4,3,2,1,0:T(8,128)}, u32[]{:S(2)}) %copy-start) | copy-done | bytes 6291480
  3.6 2.8 %copy-done.1 = f32[1,2,12,256,256]{4,3,2,1,0:T(8,128)S(1)} copy-done((f32[1,2,12,256,256]{4,3,2,1,0:T(8,128)S(1)}, f32[1,2,12,256,256]{4,3,2,1,0:T(8,128)}, u32[]{:S(2)}) %copy-start.1) | copy-done | bytes 6291480
  6.3 1.9 %copy-done.2 = f32[1,12,256,256]{3,2,1,0:T(8,128)S(1)} copy-done((f32[1,12,256,256]{3,2,1,0:T(8,128)S(1)}, f32[1,12,256,256]{3,2,1,0:T(8,128)}, u32[]{:S(2)}) %copy-start.2) | copy-done | bytes 3145752
  8.2 1.9 %copy-done.3 = f32[1,1,12,256,256]{4,3,2,1,0:T(8,128)S(1)} copy-done((f32[1,1,12,256,256]{4,3,2,1,0:T(8,128)S(1)}, f32[1,1,12,256,256]{4,3,2,1,0:T(8,128)}, u32[]{:S(2)}) %copy-start.3) | copy-done | bytes 3145752
  11.4 1.3 collective-permute-start.1
  13.2 1.3 collective-permute-start
  14.5 7.9 %collective-permute-done.1.refs_2_.refs_3_ = f32[256,256]{1,0:T(8,128)S(1)} collective-permute-done((f32[256,256]{1,0:T(8,128)S(1)}, f32[256,256]{1,0:T(8,128)S(1)}, u32[]{:S(2)}, u32[]{:S(2)}) %collective-permute-start.1) | collective-permute-done | bytes 262176 | tf_op jit(solution)/shard_map/ppermute | solution.py:164
  23.0 1.6 collective-permute-start.3
  24.6 3.5 %collective-permute-done.refs_2_.refs_3_ = f32[256,256]{1,0:T(8,128)S(1)} collective-permute-done((f32[256,256]{1,0:T(8,128)S(1)}, f32[256,256]{1,0:T(8,128)S(1)}, u32[]{:S(2)}, u32[]{:S(2)}) %collective-permute-start) | collective-permute-done | bytes 262176 | tf_op jit(solution)/shard_map/ppermute | solution.py:164
  30.0 4.1 %collective-permute-done.3.refs_2_.refs_3_ = f32[256,256]{1,0:T(8,128)S(1)} collective-permute-done((f32[256,256]{1,0:T(8,128)S(1)}, f32[256,256]{1,0:T(8,128)S(1)}, u32[]{:S(2)}, u32[]{:S(2)}) %collective-permute-start.3) | collective-permute-done | bytes 262176 | tf_op jit(solution)/shard_map/ppermute | solution.py:164
  35.9 2.2 %collective-permute-done.2.refs_2_.refs_3_ = f32[256,256]{1,0:T(8,128)S(1)} collective-permute-done((f32[256,256]{1,0:T(8,128)S(1)}, f32[256,256]{1,0:T(8,128)S(1)}, u32[]{:S(2)}, u32[]{:S(2)}) %collective-permute-start.2) | collective-permute-done | bytes 262176 | tf_op jit(solution)/shard_map/ppermute | solution.py:164
  38.7 1.3 collective-permute-start.4
  40.0 4.8 %collective-permute-done.5.refs_2_.refs_3_ = f32[256,256]{1,0:T(8,128)S(1)} collective-permute-done((f32[256,256]{1,0:T(8,128)S(1)}, f32[256,256]{1,0:T(8,128)S(1)}, u32[]{:S(2)}, u32[]{:S(2)}) %collective-permute-start.5) | collective-permute-done | bytes 262176 | tf_op jit(solution)/shard_map/ppermute | solution.py:164
  44.8 4.1 %sector6.1 = (f32[256,256]{1,0:T(8,128)S(1)}, f32[2,4,4,3,32,256]{5,4,3,2,1,0:T(8,128)S(1)}, f32[2,4,4,3,32,256]{5,4,3,2,1,0:T(8,128)S(1)}) custom-call(s32[28]{0:T(128)S(1)} %concatenate.27.refs_0_, f32[4]{0:T(128)S(1)} %bitcast.182, f32[256,256]{1,0:T(8,128)S(1)} %collective-permute-done.5.refs_2_.refs_3_, ...), custom_call_target="tpu_custom_call", output_to_operand_aliasing={{1}: (8, {}), {2}: (9, {})} | custom-call | tf_op jit(solution)/shard_map/sector6/pallas_call | solution.py:109
  50.9 4.1 %sector7.1 = (f32[256,256]{1,0:T(8,128)S(1)}, f32[2,4,4,3,32,256]{5,4,3,2,1,0:T(8,128)S(1)}, f32[2,4,4,3,32,256]{5,4,3,2,1,0:T(8,128)S(1)}) custom-call(s32[28]{0:T(128)S(1)} %concatenate.27.refs_0_, f32[4]{0:T(128)S(1)} %bitcast.183, f32[256,256]{1,0:T(8,128)S(1)} %collective-permute-done.4.refs_2_.refs_3_, ...), custom_call_target="tpu_custom_call", output_to_operand_aliasing={{1}: (8, {}), {2}: (9, {})} | custom-call | tf_op jit(solution)/shard_map/sector7/pallas_call | solution.py:109
  57.1 4.1 %sector8.1 = (f32[256,256]{1,0:T(8,128)S(1)}, f32[2,4,4,3,32,256]{5,4,3,2,1,0:T(8,128)S(1)}, f32[2,4,4,3,32,256]{5,4,3,2,1,0:T(8,128)S(1)}) custom-call(s32[28]{0:T(128)S(1)} %concatenate.27.refs_0_, f32[4]{0:T(128)S(1)} %bitcast.184, f32[256,256]{1,0:T(8,128)S(1)} %collective-permute-done.7.refs_2_.refs_3_, ...), custom_call_target="tpu_custom_call", output_to_operand_aliasing={{1}: (8, {}), {2}: (9, {})} | custom-call | tf_op jit(solution)/shard_map/sector8/pallas_call | solution.py:109
  63.2 4.3 %sector9.1 = (f32[256,256]{1,0:T(8,128)S(1)}, f32[2,4,4,3,32,256]{5,4,3,2,1,0:T(8,128)S(1)}, f32[2,4,4,3,32,256]{5,4,3,2,1,0:T(8,128)S(1)}) custom-call(s32[28]{0:T(128)S(1)} %concatenate.27.refs_0_, f32[4]{0:T(128)S(1)} %bitcast.185, f32[256,256]{1,0:T(8,128)S(1)} %collective-permute-done.6.refs_2_.refs_3_, ...), custom_call_target="tpu_custom_call", output_to_operand_aliasing={{1}: (8, {}), {2}: (9, {})} | custom-call | tf_op jit(solution)/shard_map/sector9/pallas_call | solution.py:109
  67.5 1.3 collective-permute-start.8
  69.7 4.1 %sector10.1 = (f32[256,256]{1,0:T(8,128)S(1)}, f32[2,4,4,3,32,256]{5,4,3,2,1,0:T(8,128)S(1)}, f32[2,4,4,3,32,256]{5,4,3,2,1,0:T(8,128)S(1)}) custom-call(s32[28]{0:T(128)S(1)} %concatenate.27.refs_0_, f32[4]{0:T(128)S(1)} %bitcast.186, f32[256,256]{1,0:T(8,128)S(1)} %collective-permute-done.9.refs_2_.refs_3_, ...), custom_call_target="tpu_custom_call", output_to_operand_aliasing={{1}: (8, {}), {2}: (9, {})} | custom-call | tf_op jit(solution)/shard_map/sector10/pallas_call | solution.py:109
  75.1 1.5 collective-permute-done.8.refs_2_.refs_3_
  76.6 4.1 %sector11.1 = (f32[256,256]{1,0:T(8,128)S(1)}, f32[2,4,4,3,32,256]{5,4,3,2,1,0:T(8,128)S(1)}, f32[2,4,4,3,32,256]{5,4,3,2,1,0:T(8,128)S(1)}) custom-call(s32[28]{0:T(128)S(1)} %concatenate.27.refs_0_, f32[4]{0:T(128)S(1)} %bitcast.187, f32[256,256]{1,0:T(8,128)S(1)} %collective-permute-done.8.refs_2_.refs_3_, ...), custom_call_target="tpu_custom_call", output_to_operand_aliasing={{1}: (8, {}), {2}: (9, {})} | custom-call | tf_op jit(solution)/shard_map/sector11/pallas_call | solution.py:109
  83.0 4.1 %sector12.1 = (f32[256,256]{1,0:T(8,128)S(1)}, f32[2,4,4,3,32,256]{5,4,3,2,1,0:T(8,128)S(1)}, f32[2,4,4,3,32,256]{5,4,3,2,1,0:T(8,128)S(1)}) custom-call(s32[28]{0:T(128)S(1)} %concatenate.27.refs_0_, f32[4]{0:T(128)S(1)} %bitcast.188, f32[256,256]{1,0:T(8,128)S(1)} %collective-permute-done.11.refs_2_.refs_3_, ...), custom_call_target="tpu_custom_call", output_to_operand_aliasing={{1}: (8, {}), {2}: (9, {})} | custom-call | tf_op jit(solution)/shard_map/sector12/pallas_call | solution.py:109
  88.4 3.2 %collective-permute-done.10.refs_2_.refs_3_ = f32[256,256]{1,0:T(8,128)S(1)} collective-permute-done((f32[256,256]{1,0:T(8,128)S(1)}, f32[256,256]{1,0:T(8,128)S(1)}, u32[]{:S(2)}, u32[]{:S(2)}) %collective-permute-start.10) | collective-permute-done | bytes 262176 | tf_op jit(solution)/shard_map/ppermute | solution.py:164
  91.5 4.1 %sector13.1 = (f32[256,256]{1,0:T(8,128)S(1)}, f32[2,4,4,3,32,256]{5,4,3,2,1,0:T(8,128)S(1)}, f32[2,4,4,3,32,256]{5,4,3,2,1,0:T(8,128)S(1)}) custom-call(s32[28]{0:T(128)S(1)} %concatenate.27.refs_0_, f32[4]{0:T(128)S(1)} %bitcast.189, f32[256,256]{1,0:T(8,128)S(1)} %collective-permute-done.10.refs_2_.refs_3_, ...), custom_call_target="tpu_custom_call", output_to_operand_aliasing={{1}: (8, {}), {2}: (9, {})} | custom-call | tf_op jit(solution)/shard_map/sector13/pallas_call | solution.py:109
  97.6 4.1 %sector14.1 = (f32[256,256]{1,0:T(8,128)S(1)}, f32[2,4,4,3,32,256]{5,4,3,2,1,0:T(8,128)S(1)}, f32[2,4,4,3,32,256]{5,4,3,2,1,0:T(8,128)S(1)}) custom-call(s32[28]{0:T(128)S(1)} %concatenate.27.refs_0_, f32[4]{0:T(128)S(1)} %bitcast.190, f32[256,256]{1,0:T(8,128)S(1)} %collective-permute-done.13.refs_2_.refs_3_, ...), custom_call_target="tpu_custom_call", output_to_operand_aliasing={{1}: (8, {}), {2}: (9, {})} | custom-call | tf_op jit(solution)/shard_map/sector14/pallas_call | solution.py:109
  101.6 1.3 collective-permute-start.15
  102.9 4.1 %collective-permute-done.12.refs_2_.refs_3_ = f32[256,256]{1,0:T(8,128)S(1)} collective-permute-done((f32[256,256]{1,0:T(8,128)S(1)}, f32[256,256]{1,0:T(8,128)S(1)}, u32[]{:S(2)}, u32[]{:S(2)}) %collective-permute-start.12) | collective-permute-done | bytes 262176 | tf_op jit(solution)/shard_map/ppermute | solution.py:164
  107.1 4.1 %sector15.1 = (f32[256,256]{1,0:T(8,128)S(1)}, f32[2,4,4,3,32,256]{5,4,3,2,1,0:T(8,128)S(1)}, f32[2,4,4,3,32,256]{5,4,3,2,1,0:T(8,128)S(1)}) custom-call(s32[28]{0:T(128)S(1)} %concatenate.27.refs_0_, f32[4]{0:T(128)S(1)} %bitcast.191, f32[256,256]{1,0:T(8,128)S(1)} %collective-permute-done.12.refs_2_.refs_3_, ...), custom_call_target="tpu_custom_call", output_to_operand_aliasing={{1}: (8, {}), {2}: (9, {})} | custom-call | tf_op jit(solution)/shard_map/sector15/pallas_call | solution.py:109
  113.1 4.8 %sector16.1 = (f32[256,256]{1,0:T(8,128)}, f32[2,4,4,3,32,256]{5,4,3,2,1,0:T(8,128)S(1)}, f32[2,4,4,3,32,256]{5,4,3,2,1,0:T(8,128)S(1)}) custom-call(s32[28]{0:T(128)S(1)} %concatenate.27.refs_0_, f32[4]{0:T(128)S(1)} %bitcast.192, f32[256,256]{1,0:T(8,128)S(1)} %collective-permute-done.15.refs_2_.refs_3_, ...), custom_call_target="tpu_custom_call", output_to_operand_aliasing={{1}: (8, {}), {2}: (9, {})} | custom-call | tf_op jit(solution)/shard_map/sector16/pallas_call | solution.py:109
  117.9 1.5 collective-permute-done.14.refs_2_
  119.4 4.8 %sector17.1 = (f32[256,256]{1,0:T(8,128)}, f32[2,4,4,3,32,256]{5,4,3,2,1,0:T(8,128)S(1)}, f32[2,4,4,3,32,256]{5,4,3,2,1,0:T(8,128)S(1)}) custom-call(s32[28]{0:T(128)S(1)} %concatenate.27.refs_0_, f32[4]{0:T(128)S(1)} %bitcast.193, f32[256,256]{1,0:T(8,128)S(1)} %collective-permute-done.14.refs_2_, ...), custom_call_target="tpu_custom_call", output_to_operand_aliasing={{1}: (8, {}), {2}: (9, {})} | custom-call | tf_op jit(solution)/shard_map/sector17/pallas_call | solution.py:109
  124.3 5.6 %collective-permute-done.16 = f32[2,4,4,3,32,256]{5,4,3,2,1,0:T(8,128)S(1)} collective-permute-done((f32[2,4,4,3,32,256]{5,4,3,2,1,0:T(8,128)S(1)}, f32[2,4,4,3,32,256]{5,4,3,2,1,0:T(8,128)S(1)}, u32[]{:S(2)}, u32[]{:S(2)}) %collective-permute-start.16) | collective-permute-done | bytes 3145760 | tf_op jit(solution)/shard_map/ppermute | solution.py:143
  131.1 1.9 %collective-permute-start.25 = (f32[2,96,256]{2,1,0:T(8,128)S(1)}, f32[2,96,256]{2,1,0:T(8,128)S(1)}, u32[]{:S(2)}, u32[]{:S(2)}) collective-permute-start(f32[2,96,256]{2,1,0:T(8,128)S(1)} %get-tuple-element.121), channel_id=1, source_target_pairs={{0,8},{8,16},{16,24},{24,0},{1,9},{9,17},{17,25},{25,1},{2,10},{10... | collective-permute-start | bytes 589832 | tf_op jit(solution)/shard_map/ppermute | solution.py:126
  132.9 2.1 %collective-permute-start.27 = (f32[2,96,256]{2,1,0:T(8,128)S(1)}, f32[2,96,256]{2,1,0:T(8,128)S(1)}, u32[]{:S(2)}, u32[]{:S(2)}) collective-permute-start(f32[2,96,256]{2,1,0:T(8,128)S(1)} %get-tuple-element.122), channel_id=1, source_target_pairs={{0,24},{8,0},{16,8},{24,16},{1,25},{9,1},{17,9},{25,17},{2,26},{10... | collective-permute-start | bytes 589832 | tf_op jit(solution)/shard_map/ppermute | solution.py:126
  135.1 1.4 collective-permute-start.17
  136.5 1.9 %collective-permute-start.19 = (f32[2,96,256]{2,1,0:T(8,128)S(1)}, f32[2,96,256]{2,1,0:T(8,128)S(1)}, u32[]{:S(2)}, u32[]{:S(2)}) collective-permute-start(f32[2,96,256]{2,1,0:T(8,128)S(1)} %get-tuple-element.116), channel_id=1, source_target_pairs={{0,6},{2,0},{4,2},{6,4},{1,7},{3,1},{5,3},{7,5},{8,14},{10,8},{12,... | collective-permute-start | bytes 589832 | tf_op jit(solution)/shard_map/ppermute | solution.py:126
  138.5 1.7 collective-permute-done.25
  140.3 3.1 %collective-permute-start.28 = (f32[4,96,256]{2,1,0:T(8,128)S(1)}, f32[4,96,256]{2,1,0:T(8,128)S(1)}, u32[]{:S(2)}, u32[]{:S(2)}) collective-permute-start(f32[4,96,256]{2,1,0:T(8,128)S(1)} %pad_maximum_fusion.3), channel_id=1, source_target_pairs={{0,24},{8,0},{16,8},{24,16},{1,25},{9,1},{17,9},{25,17},{2,26},{10... | collective-permute-start | bytes 1179656 | tf_op jit(solution)/shard_map/ppermute | solution.py:126
  143.6 2.6 %collective-permute-start.20 = (f32[4,96,256]{2,1,0:T(8,128)S(1)}, f32[4,96,256]{2,1,0:T(8,128)S(1)}, u32[]{:S(2)}, u32[]{:S(2)}) collective-permute-start(f32[4,96,256]{2,1,0:T(8,128)S(1)} %pad_maximum_fusion.1), channel_id=1, source_target_pairs={{0,6},{2,0},{4,2},{6,4},{1,7},{3,1},{5,3},{7,5},{8,14},{10,8},{12,... | collective-permute-start | bytes 1179656 | tf_op jit(solution)/shard_map/ppermute | solution.py:126
  146.3 4.9 %collective-permute-done.28 = f32[4,96,256]{2,1,0:T(8,128)S(1)} collective-permute-done((f32[4,96,256]{2,1,0:T(8,128)S(1)}, f32[4,96,256]{2,1,0:T(8,128)S(1)}, u32[]{:S(2)}, u32[]{:S(2)}) %collective-permute-start.28) | collective-permute-done | bytes 393248 | tf_op jit(solution)/shard_map/ppermute | solution.py:126
  151.2 3.5 %collective-permute-done.26 = f32[4,96,256]{2,1,0:T(8,128)S(1)} collective-permute-done((f32[4,96,256]{2,1,0:T(8,128)S(1)}, f32[4,96,256]{2,1,0:T(8,128)S(1)}, u32[]{:S(2)}, u32[]{:S(2)}) %collective-permute-start.26) | collective-permute-done | bytes 393248 | tf_op jit(solution)/shard_map/ppermute | solution.py:126
  154.8 1.4 collective-permute-start.29
  156.2 1.9 %collective-permute-start.31 = (f32[48,256]{1,0:T(8,128)S(1)}, f32[48,256]{1,0:T(8,128)S(1)}, u32[]{:S(2)}, u32[]{:S(2)}) collective-permute-start(f32[48,256]{1,0:T(8,128)S(1)} %get-tuple-element.134), channel_id=1, source_target_pairs={{0,6},{2,0},{4,2},{6,4},{1,7},{3,1},{5,3},{7,5},{8,14},{10,8},{12,... | collective-permute-start | bytes 147464 | tf_op jit(solution)/shard_map/ppermute | solution.py:126
  158.3 3.2 %collective-permute-start.23 = (f32[48,256]{1,0:T(8,128)S(1)}, f32[48,256]{1,0:T(8,128)S(1)}, u32[]{:S(2)}, u32[]{:S(2)}) collective-permute-start(f32[48,256]{1,0:T(8,128)S(1)} %get-tuple-element.128), channel_id=1, source_target_pairs={{0,24},{8,0},{16,8},{24,16},{1,25},{9,1},{17,9},{25,17},{2,26},{10... | collective-permute-start | bytes 147464 | tf_op jit(solution)/shard_map/ppermute | solution.py:126
  161.6 1.9 %collective-permute-start.32 = (f32[96,256]{1,0:T(8,128)S(1)}, f32[96,256]{1,0:T(8,128)S(1)}, u32[]{:S(2)}, u32[]{:S(2)}) collective-permute-start(f32[96,256]{1,0:T(8,128)S(1)} %pad_maximum_fusion.7), channel_id=1, source_target_pairs={{0,6},{2,0},{4,2},{6,4},{1,7},{3,1},{5,3},{7,5},{8,14},{10,8},{12,... | collective-permute-start | bytes 294920 | tf_op jit(solution)/shard_map/ppermute | solution.py:126
  163.8 3.2 %collective-permute-start.24 = (f32[96,256]{1,0:T(8,128)S(1)}, f32[96,256]{1,0:T(8,128)S(1)}, u32[]{:S(2)}, u32[]{:S(2)}) collective-permute-start(f32[96,256]{1,0:T(8,128)S(1)} %pad_maximum_fusion.5), channel_id=1, source_target_pairs={{0,24},{8,0},{16,8},{24,16},{1,25},{9,1},{17,9},{25,17},{2,26},{10... | collective-permute-start | bytes 294920 | tf_op jit(solution)/shard_map/ppermute | solution.py:126
  167.0 2.4 %collective-permute-done.30 = f32[96,256]{1,0:T(8,128)S(1)} collective-permute-done((f32[96,256]{1,0:T(8,128)S(1)}, f32[96,256]{1,0:T(8,128)S(1)}, u32[]{:S(2)}, u32[]{:S(2)}) %collective-permute-start.30) | collective-permute-done | bytes 98336 | tf_op jit(solution)/shard_map/ppermute | solution.py:126
  169.4 3.4 %collective-permute-done.22 = f32[96,256]{1,0:T(8,128)S(1)} collective-permute-done((f32[96,256]{1,0:T(8,128)S(1)}, f32[96,256]{1,0:T(8,128)S(1)}, u32[]{:S(2)}, u32[]{:S(2)}) %collective-permute-start.22) | collective-permute-done | bytes 98336 | tf_op jit(solution)/shard_map/ppermute | solution.py:126
  (84 shorter events, 26.4 us)
Async XLA Ops:
  0.8 2.8 %copy-start = (f32[1,2,12,256,256]{4,3,2,1,0:T(8,128)S(1)}, f32[1,2,12,256,256]{4,3,2,1,0:T(8,128)}, u32[]{:S(2)}) copy-start(f32[1,2,12,256,256]{4,3,2,1,0:T(8,128)} %param.9) | copy-start | bytes 18874372
  3.6 2.8 %copy-start.1 = (f32[1,2,12,256,256]{4,3,2,1,0:T(8,128)S(1)}, f32[1,2,12,256,256]{4,3,2,1,0:T(8,128)}, u32[]{:S(2)}) copy-start(f32[1,2,12,256,256]{4,3,2,1,0:T(8,128)} %param.10) | copy-start | bytes 18874372
  6.3 1.9 %copy-start.2 = (f32[1,12,256,256]{3,2,1,0:T(8,128)S(1)}, f32[1,12,256,256]{3,2,1,0:T(8,128)}, u32[]{:S(2)}) copy-start(f32[1,12,256,256]{3,2,1,0:T(8,128)} %param.7) | copy-start | bytes 9437188
  8.2 1.9 %copy-start.3 = (f32[1,1,12,256,256]{4,3,2,1,0:T(8,128)S(1)}, f32[1,1,12,256,256]{4,3,2,1,0:T(8,128)}, u32[]{:S(2)}) copy-start(f32[1,1,12,256,256]{4,3,2,1,0:T(8,128)} %param.8) | copy-start | bytes 9437188
  10.1 0.7 copy-start.5
  11.4 11.1 %collective-permute-start.1 = (f32[256,256]{1,0:T(8,128)S(1)}, f32[256,256]{1,0:T(8,128)S(1)}, u32[]{:S(2)}, u32[]{:S(2)}) collective-permute-start(f32[256,256]{1,0:T(8,128)S(1)} %get-tuple-element.60), channel_id=1, source_target_pairs={{0,32},{32,64},{64,96},{1,33},{33,65},{65,97},{2,34},{34,66},{66,9... | collective-permute-start | bytes 786440 | tf_op jit(solution)/shard_map/ppermute | solution.py:164
  13.2 14.8 %collective-permute-start = (f32[256,256]{1,0:T(8,128)S(1)}, f32[256,256]{1,0:T(8,128)S(1)}, u32[]{:S(2)}, u32[]{:S(2)}) collective-permute-start(f32[256,256]{1,0:T(8,128)S(1)} %get-tuple-element.59), channel_id=1, source_target_pairs={{0,32},{32,64},{64,96},{1,33},{33,65},{65,97},{2,34},{34,66},{66,9... | collective-permute-start | bytes 786440 | tf_op jit(solution)/shard_map/ppermute | solution.py:164
  22.4 5.6 %slice-start = ((s8[6291456]{0:T(1024)(128)(4,1)}), s8[4194304]{0:T(1024)(128)(4,1)S(1)}, s32[]{:S(2)}) async-start(s8[6291456]{0:T(1024)(128)(4,1)} %bitcast.103), calls=%async_computation | async-start | bytes 8388608
  22.4 5.6 %slice-start.2 = ((s8[6291456]{0:T(1024)(128)(4,1)}), s8[4194304]{0:T(1024)(128)(4,1)S(1)}, s32[]{:S(2)}) async-start(s8[6291456]{0:T(1024)(128)(4,1)} %bitcast.123), calls=%async_computation.2 | async-start | bytes 8388608
  22.4 5.6 %slice-start.1 = ((s8[6291456]{0:T(1024)(128)(4,1)}), s8[2097152]{0:T(1024)(128)(4,1)S(1)}, s32[]{:S(2)}) async-start(s8[6291456]{0:T(1024)(128)(4,1)} %bitcast.103), calls=%async_computation.1 | async-start | bytes 4194304
  22.4 5.6 %slice-start.3 = ((s8[6291456]{0:T(1024)(128)(4,1)}), s8[2097152]{0:T(1024)(128)(4,1)S(1)}, s32[]{:S(2)}) async-start(s8[6291456]{0:T(1024)(128)(4,1)} %bitcast.123), calls=%async_computation.3 | async-start | bytes 4194304
  22.4 5.6 %copy-start.4 = (f32[1,1,12,256,256]{4,3,2,1,0:T(8,128)S(1)}, f32[1,1,12,256,256]{4,3,2,1,0:T(8,128)}, u32[]{:S(2)}) copy-start(f32[1,1,12,256,256]{4,3,2,1,0:T(8,128)} %param.8) | copy-start | bytes 9437188
  23.0 11.0 %collective-permute-start.3 = (f32[256,256]{1,0:T(8,128)S(1)}, f32[256,256]{1,0:T(8,128)S(1)}, u32[]{:S(2)}, u32[]{:S(2)}) collective-permute-start(f32[256,256]{1,0:T(8,128)S(1)} %get-tuple-element.66), channel_id=1, source_target_pairs={{0,32},{32,64},{64,96},{1,33},{33,65},{65,97},{2,34},{34,66},{66,9... | collective-permute-start | bytes 786440 | tf_op jit(solution)/shard_map/ppermute | solution.py:164
  28.7 9.5 %collective-permute-start.2 = (f32[256,256]{1,0:T(8,128)S(1)}, f32[256,256]{1,0:T(8,128)S(1)}, u32[]{:S(2)}, u32[]{:S(2)}) collective-permute-start(f32[256,256]{1,0:T(8,128)S(1)} %get-tuple-element.65), channel_id=1, source_target_pairs={{0,32},{32,64},{64,96},{1,33},{33,65},{65,97},{2,34},{34,66},{66,9... | collective-permute-start | bytes 786440 | tf_op jit(solution)/shard_map/ppermute | solution.py:164
  34.6 10.1 %collective-permute-start.5 = (f32[256,256]{1,0:T(8,128)S(1)}, f32[256,256]{1,0:T(8,128)S(1)}, u32[]{:S(2)}, u32[]{:S(2)}) collective-permute-start(f32[256,256]{1,0:T(8,128)S(1)} %get-tuple-element.72), channel_id=1, source_target_pairs={{0,32},{32,64},{64,96},{1,33},{33,65},{65,97},{2,34},{34,66},{66,9... | collective-permute-start | bytes 786440 | tf_op jit(solution)/shard_map/ppermute | solution.py:164
  38.7 12.1 %collective-permute-start.4 = (f32[256,256]{1,0:T(8,128)S(1)}, f32[256,256]{1,0:T(8,128)S(1)}, u32[]{:S(2)}, u32[]{:S(2)}) collective-permute-start(f32[256,256]{1,0:T(8,128)S(1)} %get-tuple-element.71), channel_id=1, source_target_pairs={{0,32},{32,64},{64,96},{1,33},{33,65},{65,97},{2,34},{34,66},{66,9... | collective-permute-start | bytes 786440 | tf_op jit(solution)/shard_map/ppermute | solution.py:164
  48.9 8.3 %collective-permute-start.7 = (f32[256,256]{1,0:T(8,128)S(1)}, f32[256,256]{1,0:T(8,128)S(1)}, u32[]{:S(2)}, u32[]{:S(2)}) collective-permute-start(f32[256,256]{1,0:T(8,128)S(1)} %get-tuple-element.78), channel_id=1, source_target_pairs={{0,32},{32,64},{64,96},{1,33},{33,65},{65,97},{2,34},{34,66},{66,9... | collective-permute-start | bytes 786440 | tf_op jit(solution)/shard_map/ppermute | solution.py:164
  54.9 8.3 %collective-permute-start.6 = (f32[256,256]{1,0:T(8,128)S(1)}, f32[256,256]{1,0:T(8,128)S(1)}, u32[]{:S(2)}, u32[]{:S(2)}) collective-permute-start(f32[256,256]{1,0:T(8,128)S(1)} %get-tuple-element.77), channel_id=1, source_target_pairs={{0,32},{32,64},{64,96},{1,33},{33,65},{65,97},{2,34},{34,66},{66,9... | collective-permute-start | bytes 786440 | tf_op jit(solution)/shard_map/ppermute | solution.py:164
  61.2 8.5 %collective-permute-start.9 = (f32[256,256]{1,0:T(8,128)S(1)}, f32[256,256]{1,0:T(8,128)S(1)}, u32[]{:S(2)}, u32[]{:S(2)}) collective-permute-start(f32[256,256]{1,0:T(8,128)S(1)} %get-tuple-element.84), channel_id=1, source_target_pairs={{0,32},{32,64},{64,96},{1,33},{33,65},{65,97},{2,34},{34,66},{66,9... | collective-permute-start | bytes 786440 | tf_op jit(solution)/shard_map/ppermute | solution.py:164
  67.5 9.1 %collective-permute-start.8 = (f32[256,256]{1,0:T(8,128)S(1)}, f32[256,256]{1,0:T(8,128)S(1)}, u32[]{:S(2)}, u32[]{:S(2)}) collective-permute-start(f32[256,256]{1,0:T(8,128)S(1)} %get-tuple-element.83), channel_id=1, source_target_pairs={{0,32},{32,64},{64,96},{1,33},{33,65},{65,97},{2,34},{34,66},{66,9... | collective-permute-start | bytes 786440 | tf_op jit(solution)/shard_map/ppermute | solution.py:164
  73.8 9.2 %collective-permute-start.11 = (f32[256,256]{1,0:T(8,128)S(1)}, f32[256,256]{1,0:T(8,128)S(1)}, u32[]{:S(2)}, u32[]{:S(2)}) collective-permute-start(f32[256,256]{1,0:T(8,128)S(1)} %get-tuple-element.90), channel_id=1, source_target_pairs={{0,32},{32,64},{64,96},{1,33},{33,65},{65,97},{2,34},{34,66},{66,9... | collective-permute-start | bytes 786440 | tf_op jit(solution)/shard_map/ppermute | solution.py:164
  80.6 10.9 %collective-permute-start.10 = (f32[256,256]{1,0:T(8,128)S(1)}, f32[256,256]{1,0:T(8,128)S(1)}, u32[]{:S(2)}, u32[]{:S(2)}) collective-permute-start(f32[256,256]{1,0:T(8,128)S(1)} %get-tuple-element.89), channel_id=1, source_target_pairs={{0,32},{32,64},{64,96},{1,33},{33,65},{65,97},{2,34},{34,66},{66,9... | collective-permute-start | bytes 786440 | tf_op jit(solution)/shard_map/ppermute | solution.py:164
  87.1 10.5 %collective-permute-start.13 = (f32[256,256]{1,0:T(8,128)S(1)}, f32[256,256]{1,0:T(8,128)S(1)}, u32[]{:S(2)}, u32[]{:S(2)}) collective-permute-start(f32[256,256]{1,0:T(8,128)S(1)} %get-tuple-element.96), channel_id=1, source_target_pairs={{0,32},{32,64},{64,96},{1,33},{33,65},{65,97},{2,34},{34,66},{66,9... | collective-permute-start | bytes 786440 | tf_op jit(solution)/shard_map/ppermute | solution.py:164
  95.6 11.4 %collective-permute-start.12 = (f32[256,256]{1,0:T(8,128)S(1)}, f32[256,256]{1,0:T(8,128)S(1)}, u32[]{:S(2)}, u32[]{:S(2)}) collective-permute-start(f32[256,256]{1,0:T(8,128)S(1)} %get-tuple-element.95), channel_id=1, source_target_pairs={{0,32},{32,64},{64,96},{1,33},{33,65},{65,97},{2,34},{34,66},{66,9... | collective-permute-start | bytes 786440 | tf_op jit(solution)/shard_map/ppermute | solution.py:164
  101.6 11.4 %collective-permute-start.15 = (f32[256,256]{1,0:T(8,128)S(1)}, f32[256,256]{1,0:T(8,128)S(1)}, u32[]{:S(2)}, u32[]{:S(2)}) collective-permute-start(f32[256,256]{1,0:T(8,128)S(1)} %get-tuple-element.102), channel_id=1, source_target_pairs={{0,32},{32,64},{64,96},{1,33},{33,65},{65,97},{2,34},{34,66},{66,9... | collective-permute-start | bytes 786440 | tf_op jit(solution)/shard_map/ppermute | solution.py:164
  111.1 8.3 %collective-permute-start.14 = (f32[256,256]{1,0:T(8,128)S(1)}, f32[256,256]{1,0:T(8,128)S(1)}, u32[]{:S(2)}, u32[]{:S(2)}) collective-permute-start(f32[256,256]{1,0:T(8,128)S(1)} %get-tuple-element.101), channel_id=1, source_target_pairs={{0,32},{32,64},{64,96},{1,33},{33,65},{65,97},{2,34},{34,66},{66,9... | collective-permute-start | bytes 786440 | tf_op jit(solution)/shard_map/ppermute | solution.py:164
  124.2 5.7 %collective-permute-start.16 = (f32[2,4,4,3,32,256]{5,4,3,2,1,0:T(8,128)S(1)}, f32[2,4,4,3,32,256]{5,4,3,2,1,0:T(8,128)S(1)}, u32[]{:S(2)}, u32[]{:S(2)}) collective-permute-start(f32[2,4,4,3,32,256]{5,4,3,2,1,0:T(8,128)S(1)} %get-tuple-element.108), channel_id=1, source_target_pairs={{0,1},{1,0},{2,3},{3,2},{4,5},{5,4},{6,7},{7,6},{8,9},{9,8},{10,11... | collective-permute-start | bytes 9437192 | tf_op jit(solution)/shard_map/ppermute | solution.py:143
  131.1 9.1 %collective-permute-start.25 = (f32[2,96,256]{2,1,0:T(8,128)S(1)}, f32[2,96,256]{2,1,0:T(8,128)S(1)}, u32[]{:S(2)}, u32[]{:S(2)}) collective-permute-start(f32[2,96,256]{2,1,0:T(8,128)S(1)} %get-tuple-element.121), channel_id=1, source_target_pairs={{0,8},{8,16},{16,24},{24,0},{1,9},{9,17},{17,25},{25,1},{2,10},{10... | collective-permute-start | bytes 589832 | tf_op jit(solution)/shard_map/ppermute | solution.py:126
  132.9 7.2 %collective-permute-start.27 = (f32[2,96,256]{2,1,0:T(8,128)S(1)}, f32[2,96,256]{2,1,0:T(8,128)S(1)}, u32[]{:S(2)}, u32[]{:S(2)}) collective-permute-start(f32[2,96,256]{2,1,0:T(8,128)S(1)} %get-tuple-element.122), channel_id=1, source_target_pairs={{0,24},{8,0},{16,8},{24,16},{1,25},{9,1},{17,9},{25,17},{2,26},{10... | collective-permute-start | bytes 589832 | tf_op jit(solution)/shard_map/ppermute | solution.py:126
  135.1 8.4 %collective-permute-start.17 = (f32[2,96,256]{2,1,0:T(8,128)S(1)}, f32[2,96,256]{2,1,0:T(8,128)S(1)}, u32[]{:S(2)}, u32[]{:S(2)}) collective-permute-start(f32[2,96,256]{2,1,0:T(8,128)S(1)} %get-tuple-element.115), channel_id=1, source_target_pairs={{0,2},{2,4},{4,6},{6,0},{1,3},{3,5},{5,7},{7,1},{8,10},{10,12},{12... | collective-permute-start | bytes 589832 | tf_op jit(solution)/shard_map/ppermute | solution.py:126
  136.5 6.9 %collective-permute-start.19 = (f32[2,96,256]{2,1,0:T(8,128)S(1)}, f32[2,96,256]{2,1,0:T(8,128)S(1)}, u32[]{:S(2)}, u32[]{:S(2)}) collective-permute-start(f32[2,96,256]{2,1,0:T(8,128)S(1)} %get-tuple-element.116), channel_id=1, source_target_pairs={{0,6},{2,0},{4,2},{6,4},{1,7},{3,1},{5,3},{7,5},{8,14},{10,8},{12,... | collective-permute-start | bytes 589832 | tf_op jit(solution)/shard_map/ppermute | solution.py:126
  140.3 10.9 %collective-permute-start.28 = (f32[4,96,256]{2,1,0:T(8,128)S(1)}, f32[4,96,256]{2,1,0:T(8,128)S(1)}, u32[]{:S(2)}, u32[]{:S(2)}) collective-permute-start(f32[4,96,256]{2,1,0:T(8,128)S(1)} %pad_maximum_fusion.3), channel_id=1, source_target_pairs={{0,24},{8,0},{16,8},{24,16},{1,25},{9,1},{17,9},{25,17},{2,26},{10... | collective-permute-start | bytes 1179656 | tf_op jit(solution)/shard_map/ppermute | solution.py:126
  143.4 11.3 %collective-permute-start.26 = (f32[4,96,256]{2,1,0:T(8,128)S(1)}, f32[4,96,256]{2,1,0:T(8,128)S(1)}, u32[]{:S(2)}, u32[]{:S(2)}) collective-permute-start(f32[4,96,256]{2,1,0:T(8,128)S(1)} %pad_maximum_fusion.2), channel_id=1, source_target_pairs={{0,8},{8,16},{16,24},{24,0},{1,9},{9,17},{17,25},{25,1},{2,10},{10... | collective-permute-start | bytes 1179656 | tf_op jit(solution)/shard_map/ppermute | solution.py:126
  143.6 14.5 %collective-permute-start.20 = (f32[4,96,256]{2,1,0:T(8,128)S(1)}, f32[4,96,256]{2,1,0:T(8,128)S(1)}, u32[]{:S(2)}, u32[]{:S(2)}) collective-permute-start(f32[4,96,256]{2,1,0:T(8,128)S(1)} %pad_maximum_fusion.1), channel_id=1, source_target_pairs={{0,6},{2,0},{4,2},{6,4},{1,7},{3,1},{5,3},{7,5},{8,14},{10,8},{12,... | collective-permute-start | bytes 1179656 | tf_op jit(solution)/shard_map/ppermute | solution.py:126
  146.2 11.9 %collective-permute-start.18 = (f32[4,96,256]{2,1,0:T(8,128)S(1)}, f32[4,96,256]{2,1,0:T(8,128)S(1)}, u32[]{:S(2)}, u32[]{:S(2)}) collective-permute-start(f32[4,96,256]{2,1,0:T(8,128)S(1)} %pad_maximum_fusion), channel_id=1, source_target_pairs={{0,2},{2,4},{4,6},{6,0},{1,3},{3,5},{5,7},{7,1},{8,10},{10,12},{12... | collective-permute-start | bytes 1179656 | tf_op jit(solution)/shard_map/ppermute | solution.py:126
  154.8 6.7 %collective-permute-start.29 = (f32[48,256]{1,0:T(8,128)S(1)}, f32[48,256]{1,0:T(8,128)S(1)}, u32[]{:S(2)}, u32[]{:S(2)}) collective-permute-start(f32[48,256]{1,0:T(8,128)S(1)} %get-tuple-element.133), channel_id=1, source_target_pairs={{0,2},{2,4},{4,6},{6,0},{1,3},{3,5},{5,7},{7,1},{8,10},{10,12},{12... | collective-permute-start | bytes 147464 | tf_op jit(solution)/shard_map/ppermute | solution.py:126
  156.2 5.3 %collective-permute-start.31 = (f32[48,256]{1,0:T(8,128)S(1)}, f32[48,256]{1,0:T(8,128)S(1)}, u32[]{:S(2)}, u32[]{:S(2)}) collective-permute-start(f32[48,256]{1,0:T(8,128)S(1)} %get-tuple-element.134), channel_id=1, source_target_pairs={{0,6},{2,0},{4,2},{6,4},{1,7},{3,1},{5,3},{7,5},{8,14},{10,8},{12,... | collective-permute-start | bytes 147464 | tf_op jit(solution)/shard_map/ppermute | solution.py:126
  158.2 5.5 %collective-permute-start.21 = (f32[48,256]{1,0:T(8,128)S(1)}, f32[48,256]{1,0:T(8,128)S(1)}, u32[]{:S(2)}, u32[]{:S(2)}) collective-permute-start(f32[48,256]{1,0:T(8,128)S(1)} %get-tuple-element.127), channel_id=1, source_target_pairs={{0,8},{8,16},{16,24},{24,0},{1,9},{9,17},{17,25},{25,1},{2,10},{10... | collective-permute-start | bytes 147464 | tf_op jit(solution)/shard_map/ppermute | solution.py:126
  158.3 5.4 %collective-permute-start.23 = (f32[48,256]{1,0:T(8,128)S(1)}, f32[48,256]{1,0:T(8,128)S(1)}, u32[]{:S(2)}, u32[]{:S(2)}) collective-permute-start(f32[48,256]{1,0:T(8,128)S(1)} %get-tuple-element.128), channel_id=1, source_target_pairs={{0,24},{8,0},{16,8},{24,16},{1,25},{9,1},{17,9},{25,17},{2,26},{10... | collective-permute-start | bytes 147464 | tf_op jit(solution)/shard_map/ppermute | solution.py:126
  161.6 5.5 %collective-permute-start.32 = (f32[96,256]{1,0:T(8,128)S(1)}, f32[96,256]{1,0:T(8,128)S(1)}, u32[]{:S(2)}, u32[]{:S(2)}) collective-permute-start(f32[96,256]{1,0:T(8,128)S(1)} %pad_maximum_fusion.7), channel_id=1, source_target_pairs={{0,6},{2,0},{4,2},{6,4},{1,7},{3,1},{5,3},{7,5},{8,14},{10,8},{12,... | collective-permute-start | bytes 294920 | tf_op jit(solution)/shard_map/ppermute | solution.py:126
  163.5 5.9 %collective-permute-start.30 = (f32[96,256]{1,0:T(8,128)S(1)}, f32[96,256]{1,0:T(8,128)S(1)}, u32[]{:S(2)}, u32[]{:S(2)}) collective-permute-start(f32[96,256]{1,0:T(8,128)S(1)} %pad_maximum_fusion.6), channel_id=1, source_target_pairs={{0,2},{2,4},{4,6},{6,0},{1,3},{3,5},{5,7},{7,1},{8,10},{10,12},{12... | collective-permute-start | bytes 294920 | tf_op jit(solution)/shard_map/ppermute | solution.py:126
  163.8 5.7 %collective-permute-start.24 = (f32[96,256]{1,0:T(8,128)S(1)}, f32[96,256]{1,0:T(8,128)S(1)}, u32[]{:S(2)}, u32[]{:S(2)}) collective-permute-start(f32[96,256]{1,0:T(8,128)S(1)} %pad_maximum_fusion.5), channel_id=1, source_target_pairs={{0,24},{8,0},{16,8},{24,16},{1,25},{9,1},{17,9},{25,17},{2,26},{10... | collective-permute-start | bytes 294920 | tf_op jit(solution)/shard_map/ppermute | solution.py:126
  166.9 5.9 %collective-permute-start.22 = (f32[96,256]{1,0:T(8,128)S(1)}, f32[96,256]{1,0:T(8,128)S(1)}, u32[]{:S(2)}, u32[]{:S(2)}) collective-permute-start(f32[96,256]{1,0:T(8,128)S(1)} %pad_maximum_fusion.4), channel_id=1, source_target_pairs={{0,8},{8,16},{16,24},{24,0},{1,9},{9,17},{17,25},{25,1},{2,10},{10... | collective-permute-start | bytes 294920 | tf_op jit(solution)/shard_map/ppermute | solution.py:126

commit v2 on v1

--- a/solution.py
+++ b/solution.py
@@ -34,7 +34,7 @@
 
 
 def sector_kernel(step, ints, floats, arrived, previous, left, mps, psi, rights, *rest):
-    environ, keep, send, results, total, stores = rest[-6:]
+    environ, keep, send_far, send_rest, results, total, stores = rest[-7:]
     site, my_z, my_x, core = ints[0], ints[1], ints[2], ints[3]
     q = step - LAG * site
     below = jnp.maximum(q - 1, 0)
@@ -51,16 +51,15 @@
         before = jnp.where(q > 0, before, 0.0)
         s = framed(mps[0, q], size, size)
         u = framed(mps[1, below], under, size)
-        first = c0 * product(halves(now), halves(s), ((1,), (0,)))
-        second = c1 * product(halves(before), halves(u), ((1,), (0,)))
-        moved = product(halves(s.T), halves(first), ((1,), (0,))) + product(
-            halves(u.T), halves(second), ((1,), (0,)))
+        s, u = halves(s.T), halves(u.T)
+        first = c0 * product(halves(now), s, ((1,), (1,)))
+        second = c1 * product(halves(before), u, ((1,), (1,)))
+        moved = product(s, halves(first), ((1,), (0,))) + product(u, halves(second), ((1,), (0,)))
         environ[...] = moved
         total[...] = moved
 
-        def move(state, i, target, near, far, third):
-            return pltpu.make_async_copy(
-                results.at[state, pl.ds(ROWS * i, ROWS)], target.at[state, near, far, third], stores)
+        def move(state, i, target):
+            return pltpu.make_async_copy(results.at[state, pl.ds(ROWS * i, ROWS)], target, stores)
 
         def apply(state, _):
             c = jnp.where(state == 0, floats[2] * present, floats[3] * present_above)
@@ -79,11 +78,15 @@
 
                 @pl.when(mine)
                 def _():
-                    move(state, i, keep, near, far, third).start()
+                    move(state, i, keep.at[state, near, far, third]).start()
 
-                @pl.when(jnp.logical_not(mine))
+                @pl.when(jnp.logical_not(mine) & (near == 2))
                 def _():
-                    move(state, i, send, near, far, third).start()
+                    move(state, i, send_far.at[state, far, third]).start()
+
+                @pl.when(jnp.logical_not(mine) & (near != 2))
+                def _():
+                    move(state, i, send_rest.at[state, jnp.minimum(near, 2), far, third]).start()
 
                 return 0
 
@@ -101,7 +104,7 @@
 
 
 def sector_step(step, ints, floats, arrived, previous, left, mps, psi, rights, held):
-    shape = jax.ShapeDtypeStruct((2, 4, 4, 3, ROWS, W), f32)
+    shapes = [jax.ShapeDtypeStruct(s + (3, ROWS, W), f32) for s in ((2, 4, 4), (2, 4), (2, 3, 4))]
 
     def kernel(*refs):
         sector_kernel(step, *refs)
@@ -109,14 +112,14 @@
     return pl.pallas_call(
         kernel,
         in_specs=[SCALAR] * 2 + [LOCAL] * 6 + [FAR] * len(held),
-        out_specs=[LOCAL, FAR, FAR],
-        out_shape=[jax.ShapeDtypeStruct((W, W), f32), shape, shape],
+        out_specs=[LOCAL] + [FAR] * 3,
+        out_shape=[jax.ShapeDtypeStruct((W, W), f32)] + shapes,
         scratch_shapes=[
             pltpu.VMEM((2, W, W), f32),
             pltpu.VMEM((W, W), f32),
             pltpu.SemaphoreType.DMA,
         ],
-        input_output_aliases={8: 1, 9: 2} if held else {},
+        input_output_aliases={8: 1, 9: 2, 10: 3} if held else {},
         compiler_params=GRANT,
         name=f"sector{step}",
     )(ints, floats, arrived, previous, left, mps, psi, rights, *held)
@@ -126,26 +129,30 @@
     return lax.ppermute(x, axis, [(i, (i + by) % 4) for i in range(4)])
 
 
-def round_far(blocks, axis):
-    half = blocks.shape[1] // 2
-    up = turned(blocks[2, :half], axis, 1)
-    down = turned(blocks[2, half:], axis, -1)
-    return blocks[0], jnp.concatenate([blocks[1, :half] + up, blocks[1, half:]]), jnp.concatenate(
-        [blocks[3, :half], blocks[3, half:] + down])
+def swapped(x):
+    return lax.ppermute(x, "core", [(0, 1), (1, 0)])
 
 
-def round_near(parts, axis):
-    own, ahead, behind = parts
+def first_phase(far, own, ahead, behind, axis):
+    up = turned(far[:2], axis, 1)
+    down = turned(far[2:], axis, -1)
+    ahead = jnp.concatenate([ahead[:2] + up, ahead[2:]])
+    behind = jnp.concatenate([behind[:2], behind[2:] + down])
     return own + turned(ahead, axis, 1) + turned(behind, axis, -1)
 
 
-def reduced(keep, send):
-    both = keep + lax.ppermute(send, "core", [(0, 1), (1, 0)])
-    both = both.reshape(2, 4, 4, 96, W)
-    first, second = round_far(both[0], "x"), round_far(both[1], "z")
-    first, second = round_near(first, "x"), round_near(second, "z")
-    first, second = round_far(first, "z"), round_far(second, "x")
-    return jnp.stack([round_near(first, "z"), round_near(second, "x")])[None]
+def second_phase(blocks, axis):
+    return (blocks[0] + turned(blocks[1], axis, 1)) + (turned(blocks[3], axis, -1) + turned(blocks[2], axis, 2))
+
+
+def reduced(keep, send_far, send_rest):
+    far = (keep[:, 2] + swapped(send_far)).reshape(2, 4, 96, W)
+    rest = swapped(send_rest)
+    own, ahead, behind = [
+        (keep[:, i] + rest[:, j]).reshape(2, 4, 96, W) for i, j in ((0, 0), (1, 1), (3, 2))]
+    first = first_phase(far[0], own[0], ahead[0], behind[0], "x")
+    second = first_phase(far[1], own[1], ahead[1], behind[1], "z")
+    return jnp.stack([second_phase(first, "z"), second_phase(second, "x")])[None]
 
 
 def shards(left_env, right_env, mps, psi, coef, sector_sizes, pattern):
@@ -153,13 +160,14 @@
     ints = jnp.concatenate([place, sector_sizes, pattern[0]])
     floats = coef[0, 0]
     sources = (left_env[0], mps[0], psi[0], right_env[0, 0])
+    starts = (left_env[0, :LAG], mps[0, :, :LAG], psi[0, :, :LAG], right_env[0, 0, : LAG + 1])
     nothing = jnp.zeros((W, W), f32)
     arrivals = {}
     held = ()
     for step in range(LAST):
         arrived = arrivals.get(step, nothing)
         environ, *held = sector_step(
-            step, ints, floats, arrived, arrivals.get(step - 1, nothing), *sources, tuple(held))
+            step, ints, floats, arrived, arrivals.get(step - 1, nothing), *(starts if step < LAG else sources), tuple(held))
         if step + LAG < LAST:
             arrivals[step + LAG] = lax.ppermute(environ, "site", [(0, 1), (1, 2), (2, 3)])
     return reduced(*held)

time: 174 us -> 169 us (0.971)
  waiting for transfers between devices: 59.8 us -> 50.8 us
  Pallas kernels: 53.9 us -> 56.5 us
    ppermute x16, waiting for transfers between devices: 38.2 us -> 30.9 us  [shards(): lax.ppermute(environ, 'site', [(0, 1), (1, 2), (2, 3)])]
    squeeze x4 -> x5, local copies, waits for them, and re-layouts: 0.14 us -> 6.93 us  [the longest x1 2.91 us: shards(): psi[0, :, :LAG]]
    unnamed x20 -> x26, local copies, waits for them, and re-layouts: 10 us -> 5.32 us
    pallas_call x18, Pallas kernels: 53.9 us -> 56.5 us  [sector_step(): pl.pallas_call(kernel, in_specs=[SCALAR] * 2 + [LOCAL] * 6 + [FAR] * len(...]
    ppermute x16 -> x14, waiting for transfers between devices: 15.9 us -> 14.7 us  [turned(): return lax.ppermute(x, axis, [(i, (i + by) % 4) for i in range(4)])]
    ppermute x16 -> x14, starting transfers between devices: 25.1 us -> 24.5 us  [turned(): return lax.ppermute(x, axis, [(i, (i + by) % 4) for i in range(4)])]
    ppermute x1 -> x2, waiting for transfers between devices: 5.65 us -> 5.15 us  [swapped(): return lax.ppermute(x, 'core', [(0, 1), (1, 0)])]
  transfers between devices with their start and end apart: 33 -> 32, of which waited for: 22 -> 24; matrix products, arithmetic and copies ran while one was open for 0% -> 1% of each run, Pallas kernels for 28% -> 30%
where the time goes in v2:
time: 169 us
  Pallas kernels  56.5 us (33%)
  waiting for transfers between devices  50.8 us (30%)
  starting transfers between devices  46.3 us (27%)
  local copies, waits for them, and re-layouts  12.6 us (7%)
  other arithmetic  1.88 us (1%)
    pallas_call x18, Pallas kernels, sector_step(): pl.pallas_call(kernel, in_specs=[SCALAR] * 2 + [LOCAL] * 6 + [FAR] * len(...  56.5 us
    ppermute x16, waiting for transfers between devices, shards(): lax.ppermute(environ, 'site', [(0, 1), (1, 2), (2, 3)])  30.9 us
    ppermute x14, starting transfers between devices, turned(): return lax.ppermute(x, axis, [(i, (i + by) % 4) for i in range(4)])  24.5 us
    ppermute x16, starting transfers between devices, shards(): lax.ppermute(environ, 'site', [(0, 1), (1, 2), (2, 3)])  21.2 us
    ppermute x14, waiting for transfers between devices, turned(): return lax.ppermute(x, axis, [(i, (i + by) % 4) for i in range(4)])  14.7 us
    unnamed x26, local copies, waits for them, and re-layouts  5.32 us
    ppermute x2, waiting for transfers between devices, swapped(): return lax.ppermute(x, 'core', [(0, 1), (1, 0)])  5.15 us
  transfers between devices with their start and end apart: 32, of which 24 were waited for; matrix products, arithmetic and copies ran while one was open for 1% of the time, Pallas kernels for 30%

profile of v2, /device:TPU:24, one launch (start us, length us, event | category | flops | bytes accessed | tf_op | source)
XLA Modules:
  0.0 168.6 jit_solution(10799136477221960722)
XLA Ops:
  0.0 1.9 %slice_bitcast_fusion.4.refs_4_ = f32[2,256,256]{2,1,0:T(8,128)} fusion(f32[1,12,256,256]{3,2,1,0:T(8,128)} %param.7), kind=kLoop, calls=%fused_computation.10 | loop fusion | bytes 1048576 | tf_op jit(solution)/shard_map/squeeze | solution.py:163
  1.9 2.1 %slice_bitcast_fusion.3.refs_7_ = f32[3,256,256]{2,1,0:T(8,128)} fusion(f32[1,1,12,256,256]{4,3,2,1,0:T(8,128)} %param.8), kind=kLoop, calls=%fused_computation.9 | loop fusion | bytes 1572864 | tf_op jit(solution)/shard_map/squeeze | solution.py:163
  4.0 2.9 %slice_bitcast_fusion = (f32[2,2,256,256]{3,2,1,0:T(8,128)S(1)}, f32[2,2,256,256]{3,2,1,0:T(8,128)}) fusion(f32[1,2,12,256,256]{4,3,2,1,0:T(8,128)} %param.10, f32[1,2,12,256,256]{4,3,2,1,0:T(8,128)} %param.9), kind=kLoop, calls=%fused_computation | loop fusion | bytes 4194304 | tf_op jit(solution)/shard_map/squeeze | solution.py:163
  11.0 1.4 collective-permute-start.1
  13.0 1.6 collective-permute-start
  14.6 7.6 %collective-permute-done.1.refs_2_.refs_3_ = f32[256,256]{1,0:T(8,128)S(1)} collective-permute-done((f32[256,256]{1,0:T(8,128)S(1)}, f32[256,256]{1,0:T(8,128)S(1)}, u32[]{:S(2)}, u32[]{:S(2)}) %collective-permute-start.1) | collective-permute-done | bytes 262176 | tf_op jit(solution)/shard_map/ppermute | solution.py:172
  22.2 1.9 %copy-done.1 = f32[1,12,256,256]{3,2,1,0:T(8,128)S(1)} copy-done((f32[1,12,256,256]{3,2,1,0:T(8,128)S(1)}, f32[1,12,256,256]{3,2,1,0:T(8,128)}, u32[]{:S(2)}) %copy-start.1) | copy-done | bytes 3145752
  24.7 1.4 collective-permute-start.3
  27.3 1.3 collective-permute-start.2
  28.6 6.9 %collective-permute-done.3.refs_2_.refs_3_ = f32[256,256]{1,0:T(8,128)S(1)} collective-permute-done((f32[256,256]{1,0:T(8,128)S(1)}, f32[256,256]{1,0:T(8,128)S(1)}, u32[]{:S(2)}, u32[]{:S(2)}) %collective-permute-start.3) | collective-permute-done | bytes 262176 | tf_op jit(solution)/shard_map/ppermute | solution.py:172
  36.0 1.3 collective-permute-start.5
  37.3 1.4 collective-permute-done.2.refs_2_.refs_3_
  39.3 1.3 collective-permute-start.4
  40.6 6.4 %collective-permute-done.5.refs_2_.refs_3_ = f32[256,256]{1,0:T(8,128)S(1)} collective-permute-done((f32[256,256]{1,0:T(8,128)S(1)}, f32[256,256]{1,0:T(8,128)S(1)}, u32[]{:S(2)}, u32[]{:S(2)}) %collective-permute-start.5) | collective-permute-done | bytes 262176 | tf_op jit(solution)/shard_map/ppermute | solution.py:172
  46.9 4.3 %sector6.1 = (f32[256,256]{1,0:T(8,128)S(1)}, f32[2,4,4,3,32,256]{5,4,3,2,1,0:T(8,128)S(1)}, f32[2,4,3,32,256]{4,3,2,1,0:T(8,128)S(1)}, f32[2,3,4,3,32,256]{5,4,3,2,1,0:T(8,128)S(1)}) custom-call(s32[28]{0:T(128)S(1)} %concatenate.15.refs_0_, f32[4]{0:T(128)S(1)} %bitcast.148, ...), custom_call_target="tpu_custom_call", output_to_operand_aliasing={{1}: (8, {}), {2}: (9, {}), {3}: (10, {})} | custom-call | tf_op jit(solution)/shard_map/sector6/pallas_call | solution.py:112
  51.3 1.3 collective-permute-start.7
  53.2 4.3 %sector7.1 = (f32[256,256]{1,0:T(8,128)S(1)}, f32[2,4,4,3,32,256]{5,4,3,2,1,0:T(8,128)S(1)}, f32[2,4,3,32,256]{4,3,2,1,0:T(8,128)S(1)}, f32[2,3,4,3,32,256]{5,4,3,2,1,0:T(8,128)S(1)}) custom-call(s32[28]{0:T(128)S(1)} %concatenate.15.refs_0_, f32[4]{0:T(128)S(1)} %bitcast.149, ...), custom_call_target="tpu_custom_call", output_to_operand_aliasing={{1}: (8, {}), {2}: (9, {}), {3}: (10, {})} | custom-call | tf_op jit(solution)/shard_map/sector7/pallas_call | solution.py:112
  57.5 1.3 collective-permute-start.6
  59.5 4.3 %sector8.1 = (f32[256,256]{1,0:T(8,128)S(1)}, f32[2,4,4,3,32,256]{5,4,3,2,1,0:T(8,128)S(1)}, f32[2,4,3,32,256]{4,3,2,1,0:T(8,128)S(1)}, f32[2,3,4,3,32,256]{5,4,3,2,1,0:T(8,128)S(1)}) custom-call(s32[28]{0:T(128)S(1)} %concatenate.15.refs_0_, f32[4]{0:T(128)S(1)} %bitcast.150, ...), custom_call_target="tpu_custom_call", output_to_operand_aliasing={{1}: (8, {}), {2}: (9, {}), {3}: (10, {})} | custom-call | tf_op jit(solution)/shard_map/sector8/pallas_call | solution.py:112
  63.8 1.3 collective-permute-start.9
  65.8 4.5 %sector9.1 = (f32[256,256]{1,0:T(8,128)S(1)}, f32[2,4,4,3,32,256]{5,4,3,2,1,0:T(8,128)S(1)}, f32[2,4,3,32,256]{4,3,2,1,0:T(8,128)S(1)}, f32[2,3,4,3,32,256]{5,4,3,2,1,0:T(8,128)S(1)}) custom-call(s32[28]{0:T(128)S(1)} %concatenate.15.refs_0_, f32[4]{0:T(128)S(1)} %bitcast.151, ...), custom_call_target="tpu_custom_call", output_to_operand_aliasing={{1}: (8, {}), {2}: (9, {}), {3}: (10, {})} | custom-call | tf_op jit(solution)/shard_map/sector9/pallas_call | solution.py:112
  70.3 1.3 collective-permute-start.8
  72.1 4.3 %sector10.1 = (f32[256,256]{1,0:T(8,128)S(1)}, f32[2,4,4,3,32,256]{5,4,3,2,1,0:T(8,128)S(1)}, f32[2,4,3,32,256]{4,3,2,1,0:T(8,128)S(1)}, f32[2,3,4,3,32,256]{5,4,3,2,1,0:T(8,128)S(1)}) custom-call(s32[28]{0:T(128)S(1)} %concatenate.15.refs_0_, f32[4]{0:T(128)S(1)} %bitcast.152, ...), custom_call_target="tpu_custom_call", output_to_operand_aliasing={{1}: (8, {}), {2}: (9, {}), {3}: (10, {})} | custom-call | tf_op jit(solution)/shard_map/sector10/pallas_call | solution.py:112
  76.4 1.3 collective-permute-start.11
  78.5 4.3 %sector11.1 = (f32[256,256]{1,0:T(8,128)S(1)}, f32[2,4,4,3,32,256]{5,4,3,2,1,0:T(8,128)S(1)}, f32[2,4,3,32,256]{4,3,2,1,0:T(8,128)S(1)}, f32[2,3,4,3,32,256]{5,4,3,2,1,0:T(8,128)S(1)}) custom-call(s32[28]{0:T(128)S(1)} %concatenate.15.refs_0_, f32[4]{0:T(128)S(1)} %bitcast.153, ...), custom_call_target="tpu_custom_call", output_to_operand_aliasing={{1}: (8, {}), {2}: (9, {}), {3}: (10, {})} | custom-call | tf_op jit(solution)/shard_map/sector11/pallas_call | solution.py:112
  82.8 1.3 collective-permute-start.10
  84.8 4.3 %sector12.1 = (f32[256,256]{1,0:T(8,128)S(1)}, f32[2,4,4,3,32,256]{5,4,3,2,1,0:T(8,128)S(1)}, f32[2,4,3,32,256]{4,3,2,1,0:T(8,128)S(1)}, f32[2,3,4,3,32,256]{5,4,3,2,1,0:T(8,128)S(1)}) custom-call(s32[28]{0:T(128)S(1)} %concatenate.15.refs_0_, f32[4]{0:T(128)S(1)} %bitcast.154, ...), custom_call_target="tpu_custom_call", output_to_operand_aliasing={{1}: (8, {}), {2}: (9, {}), {3}: (10, {})} | custom-call | tf_op jit(solution)/shard_map/sector12/pallas_call | solution.py:112
  91.1 4.3 %sector13.1 = (f32[256,256]{1,0:T(8,128)S(1)}, f32[2,4,4,3,32,256]{5,4,3,2,1,0:T(8,128)S(1)}, f32[2,4,3,32,256]{4,3,2,1,0:T(8,128)S(1)}, f32[2,3,4,3,32,256]{5,4,3,2,1,0:T(8,128)S(1)}) custom-call(s32[28]{0:T(128)S(1)} %concatenate.15.refs_0_, f32[4]{0:T(128)S(1)} %bitcast.155, ...), custom_call_target="tpu_custom_call", output_to_operand_aliasing={{1}: (8, {}), {2}: (9, {}), {3}: (10, {})} | custom-call | tf_op jit(solution)/shard_map/sector13/pallas_call | solution.py:112
  97.4 4.3 %sector14.1 = (f32[256,256]{1,0:T(8,128)S(1)}, f32[2,4,4,3,32,256]{5,4,3,2,1,0:T(8,128)S(1)}, f32[2,4,3,32,256]{4,3,2,1,0:T(8,128)S(1)}, f32[2,3,4,3,32,256]{5,4,3,2,1,0:T(8,128)S(1)}) custom-call(s32[28]{0:T(128)S(1)} %concatenate.15.refs_0_, f32[4]{0:T(128)S(1)} %bitcast.156, ...), custom_call_target="tpu_custom_call", output_to_operand_aliasing={{1}: (8, {}), {2}: (9, {}), {3}: (10, {})} | custom-call | tf_op jit(solution)/shard_map/sector14/pallas_call | solution.py:112
  103.7 4.3 %sector15.1 = (f32[256,256]{1,0:T(8,128)S(1)}, f32[2,4,4,3,32,256]{5,4,3,2,1,0:T(8,128)S(1)}, f32[2,4,3,32,256]{4,3,2,1,0:T(8,128)S(1)}, f32[2,3,4,3,32,256]{5,4,3,2,1,0:T(8,128)S(1)}) custom-call(s32[28]{0:T(128)S(1)} %concatenate.15.refs_0_, f32[4]{0:T(128)S(1)} %bitcast.157, ...), custom_call_target="tpu_custom_call", output_to_operand_aliasing={{1}: (8, {}), {2}: (9, {}), {3}: (10, {})} | custom-call | tf_op jit(solution)/shard_map/sector15/pallas_call | solution.py:112
  108.0 1.3 collective-permute-start.14
  109.9 5.0 %sector16.1 = (f32[256,256]{1,0:T(8,128)}, f32[2,4,4,3,32,256]{5,4,3,2,1,0:T(8,128)S(1)}, f32[2,4,3,32,256]{4,3,2,1,0:T(8,128)S(1)}, f32[2,3,4,3,32,256]{5,4,3,2,1,0:T(8,128)S(1)}) custom-call(s32[28]{0:T(128)S(1)} %concatenate.15.refs_0_, f32[4]{0:T(128)S(1)} %bitcast.158, ...), custom_call_target="tpu_custom_call", output_to_operand_aliasing={{1}: (8, {}), {2}: (9, {}), {3}: (10, {})} | custom-call | tf_op jit(solution)/shard_map/sector16/pallas_call | solution.py:112
  114.9 1.3 collective-permute-done.14.refs_2_
  116.2 5.0 %sector17.1 = (f32[256,256]{1,0:T(8,128)}, f32[2,4,4,3,32,256]{5,4,3,2,1,0:T(8,128)S(1)}, f32[2,4,3,32,256]{4,3,2,1,0:T(8,128)S(1)}, f32[2,3,4,3,32,256]{5,4,3,2,1,0:T(8,128)S(1)}) custom-call(s32[28]{0:T(128)S(1)} %concatenate.15.refs_0_, f32[4]{0:T(128)S(1)} %bitcast.159, ...), custom_call_target="tpu_custom_call", output_to_operand_aliasing={{1}: (8, {}), {2}: (9, {}), {3}: (10, {})} | custom-call | tf_op jit(solution)/shard_map/sector17/pallas_call | solution.py:112
  121.8 5.1 %collective-permute-done.17 = f32[2,4,3,32,256]{4,3,2,1,0:T(8,128)S(1)} collective-permute-done((f32[2,4,3,32,256]{4,3,2,1,0:T(8,128)S(1)}, f32[2,4,3,32,256]{4,3,2,1,0:T(8,128)S(1)}, u32[]{:S(2)}, u32[]{:S(2)}) %collective-permute-start.17) | collective-permute-done | bytes 786464 | tf_op jit(solution)/shard_map/ppermute | solution.py:133
  127.2 6.3 %collective-permute-start.27 = (f32[2,96,256]{2,1,0:T(8,128)S(1)}, f32[2,96,256]{2,1,0:T(8,128)S(1)}, u32[]{:S(2)}, u32[]{:S(2)}) collective-permute-start(f32[2,96,256]{2,1,0:T(8,128)S(1)} %bitcast.172), channel_id=1, source_target_pairs={{0,24},{8,0},{16,8},{24,16},{1,25},{9,1},{17,9},{25,17},{2,26},{10... | collective-permute-start | bytes 589832 | tf_op jit(solution)/shard_map/ppermute | solution.py:129
  133.5 1.5 collective-permute-start.18
  135.0 1.7 %collective-permute-start.20 = (f32[2,96,256]{2,1,0:T(8,128)S(1)}, f32[2,96,256]{2,1,0:T(8,128)S(1)}, u32[]{:S(2)}, u32[]{:S(2)}) collective-permute-start(f32[2,96,256]{2,1,0:T(8,128)S(1)} %bitcast.170), channel_id=1, source_target_pairs={{0,6},{2,0},{4,2},{6,4},{1,7},{3,1},{5,3},{7,5},{8,14},{10,8},{12,... | collective-permute-start | bytes 589832 | tf_op jit(solution)/shard_map/ppermute | solution.py:129
  137.5 5.1 %collective-permute-done.25 = f32[2,96,256]{2,1,0:T(8,128)S(1)} collective-permute-done((f32[2,96,256]{2,1,0:T(8,128)S(1)}, f32[2,96,256]{2,1,0:T(8,128)S(1)}, u32[]{:S(2)}, u32[]{:S(2)}) %collective-permute-start.25) | collective-permute-done | bytes 196640 | tf_op jit(solution)/shard_map/ppermute | solution.py:129
  142.9 3.3 %collective-permute-start.28 = (f32[4,96,256]{2,1,0:T(8,128)S(1)}, f32[4,96,256]{2,1,0:T(8,128)S(1)}, u32[]{:S(2)}, u32[]{:S(2)}) collective-permute-start(f32[4,96,256]{2,1,0:T(8,128)S(1)} %pad_maximum_fusion.3), channel_id=1, source_target_pairs={{0,24},{8,0},{16,8},{24,16},{1,25},{9,1},{17,9},{25,17},{2,26},{10... | collective-permute-start | bytes 1179656 | tf_op jit(solution)/shard_map/ppermute | solution.py:129
  146.3 1.5 collective-permute-start.19
  147.9 1.8 %collective-permute-start.21 = (f32[4,96,256]{2,1,0:T(8,128)S(1)}, f32[4,96,256]{2,1,0:T(8,128)S(1)}, u32[]{:S(2)}, u32[]{:S(2)}) collective-permute-start(f32[4,96,256]{2,1,0:T(8,128)S(1)} %pad_maximum_fusion.1), channel_id=1, source_target_pairs={{0,6},{2,0},{4,2},{6,4},{1,7},{3,1},{5,3},{7,5},{8,14},{10,8},{12,... | collective-permute-start | bytes 1179656 | tf_op jit(solution)/shard_map/ppermute | solution.py:129
  149.8 3.9 %collective-permute-done.26 = f32[4,96,256]{2,1,0:T(8,128)S(1)} collective-permute-done((f32[4,96,256]{2,1,0:T(8,128)S(1)}, f32[4,96,256]{2,1,0:T(8,128)S(1)}, u32[]{:S(2)}, u32[]{:S(2)}) %collective-permute-start.26) | collective-permute-done | bytes 393248 | tf_op jit(solution)/shard_map/ppermute | solution.py:129
  153.8 2.8 %collective-permute-start.31 = (f32[96,256]{1,0:T(8,128)S(1)}, f32[96,256]{1,0:T(8,128)S(1)}, u32[]{:S(2)}, u32[]{:S(2)}) collective-permute-start(f32[96,256]{1,0:T(8,128)S(1)} %get-tuple-element.165), channel_id=1, source_target_pairs={{0,4},{2,6},{4,0},{6,2},{1,5},{3,7},{5,1},{7,3},{8,12},{10,14},{12... | collective-permute-start | bytes 294920 | tf_op jit(solution)/shard_map/ppermute | solution.py:129
  156.6 1.4 collective-permute-start.30
  160.5 1.6 collective-permute-start.23
  163.9 1.8 %collective-permute-done.24 = f32[96,256]{1,0:T(8,128)S(1)} collective-permute-done((f32[96,256]{1,0:T(8,128)S(1)}, f32[96,256]{1,0:T(8,128)S(1)}, u32[]{:S(2)}, u32[]{:S(2)}) %collective-permute-start.24) | collective-permute-done | bytes 98336 | tf_op jit(solution)/shard_map/ppermute | solution.py:129
  166.5 1.4 collective-permute-done.22
  (88 shorter events, 26.0 us)
Async XLA Ops:
  1.9 5.0 %copy-start.7 = (s32[12]{0:T(128)S(1)}, s32[12]{0:T(128)}, u32[]{:S(2)}) copy-start(s32[12]{0:T(128)} %param.12) | copy-start | bytes 148
  1.9 5.0 %copy-start.8 = (s32[1,12]{1,0:T(1,128)S(1)}, s32[1,12]{1,0:T(1,128)}, u32[]{:S(2)}) copy-start(s32[1,12]{1,0:T(1,128)} %param.13) | copy-start | bytes 148
  1.9 5.1 %copy-start.6 = (f32[1,1,4]{2,1,0:T(1,128)S(1)}, f32[1,1,4]{2,1,0:T(1,128)}, u32[]{:S(2)}) copy-start(f32[1,1,4]{2,1,0:T(1,128)} %param.11) | copy-start | bytes 52
  4.0 18.2 %slice-start.2 = ((s8[6291456]{0:T(1024)(128)(4,1)}), s8[2097152]{0:T(1024)(128)(4,1)S(1)}, s32[]{:S(2)}) async-start(s8[6291456]{0:T(1024)(128)(4,1)} %bitcast.92), calls=%async_computation.2 | async-start | bytes 4194304
  7.0 1.2 copy-start.3
  8.2 1.1 copy-start.4
  9.4 1.0 copy-start.5
  10.4 11.8 %slice-start = ((s8[6291456]{0:T(1024)(128)(4,1)}), s8[4194304]{0:T(1024)(128)(4,1)S(1)}, s32[]{:S(2)}) async-start(s8[6291456]{0:T(1024)(128)(4,1)} %bitcast.74), calls=%async_computation | async-start | bytes 8388608
  11.0 11.2 %collective-permute-start.1 = (f32[256,256]{1,0:T(8,128)S(1)}, f32[256,256]{1,0:T(8,128)S(1)}, u32[]{:S(2)}, u32[]{:S(2)}) collective-permute-start(f32[256,256]{1,0:T(8,128)S(1)} %get-tuple-element.79), channel_id=1, source_target_pairs={{0,32},{32,64},{64,96},{1,33},{33,65},{65,97},{2,34},{34,66},{66,9... | collective-permute-start | bytes 786440 | tf_op jit(solution)/shard_map/ppermute | solution.py:172
  12.4 9.8 %slice-start.1 = ((s8[6291456]{0:T(1024)(128)(4,1)}), s8[2097152]{0:T(1024)(128)(4,1)S(1)}, s32[]{:S(2)}) async-start(s8[6291456]{0:T(1024)(128)(4,1)} %bitcast.74), calls=%async_computation.1 | async-start | bytes 4194304
  12.4 9.8 %slice-start.3 = ((s8[6291456]{0:T(1024)(128)(4,1)}), s8[4194304]{0:T(1024)(128)(4,1)S(1)}, s32[]{:S(2)}) async-start(s8[6291456]{0:T(1024)(128)(4,1)} %bitcast.92), calls=%async_computation.3 | async-start | bytes 8388608
  12.5 9.8 %copy-start = (f32[1,1,12,256,256]{4,3,2,1,0:T(8,128)S(1)}, f32[1,1,12,256,256]{4,3,2,1,0:T(8,128)}, u32[]{:S(2)}) copy-start(f32[1,1,12,256,256]{4,3,2,1,0:T(8,128)} %param.8) | copy-start | bytes 9437188
  13.0 13.6 %collective-permute-start = (f32[256,256]{1,0:T(8,128)S(1)}, f32[256,256]{1,0:T(8,128)S(1)}, u32[]{:S(2)}, u32[]{:S(2)}) collective-permute-start(f32[256,256]{1,0:T(8,128)S(1)} %get-tuple-element.78), channel_id=1, source_target_pairs={{0,32},{32,64},{64,96},{1,33},{33,65},{65,97},{2,34},{34,66},{66,9... | collective-permute-start | bytes 786440 | tf_op jit(solution)/shard_map/ppermute | solution.py:172
  22.2 1.9 %copy-start.1 = (f32[1,12,256,256]{3,2,1,0:T(8,128)S(1)}, f32[1,12,256,256]{3,2,1,0:T(8,128)}, u32[]{:S(2)}) copy-start(f32[1,12,256,256]{3,2,1,0:T(8,128)} %param.7) | copy-start | bytes 9437188
  24.1 2.6 %copy-start.2 = (f32[1,12,256,256]{3,2,1,0:T(8,128)S(1)}, f32[1,12,256,256]{3,2,1,0:T(8,128)}, u32[]{:S(2)}) copy-start(f32[1,12,256,256]{3,2,1,0:T(8,128)} %param.7) | copy-start | bytes 9437188
  24.7 10.8 %collective-permute-start.3 = (f32[256,256]{1,0:T(8,128)S(1)}, f32[256,256]{1,0:T(8,128)S(1)}, u32[]{:S(2)}, u32[]{:S(2)}) collective-permute-start(f32[256,256]{1,0:T(8,128)S(1)} %get-tuple-element.87), channel_id=1, source_target_pairs={{0,32},{32,64},{64,96},{1,33},{33,65},{65,97},{2,34},{34,66},{66,9... | collective-permute-start | bytes 786440 | tf_op jit(solution)/shard_map/ppermute | solution.py:172
  27.3 11.5 %collective-permute-start.2 = (f32[256,256]{1,0:T(8,128)S(1)}, f32[256,256]{1,0:T(8,128)S(1)}, u32[]{:S(2)}, u32[]{:S(2)}) collective-permute-start(f32[256,256]{1,0:T(8,128)S(1)} %get-tuple-element.86), channel_id=1, source_target_pairs={{0,32},{32,64},{64,96},{1,33},{33,65},{65,97},{2,34},{34,66},{66,9... | collective-permute-start | bytes 786440 | tf_op jit(solution)/shard_map/ppermute | solution.py:172
  36.0 10.9 %collective-permute-start.5 = (f32[256,256]{1,0:T(8,128)S(1)}, f32[256,256]{1,0:T(8,128)S(1)}, u32[]{:S(2)}, u32[]{:S(2)}) collective-permute-start(f32[256,256]{1,0:T(8,128)S(1)} %get-tuple-element.95), channel_id=1, source_target_pairs={{0,32},{32,64},{64,96},{1,33},{33,65},{65,97},{2,34},{34,66},{66,9... | collective-permute-start | bytes 786440 | tf_op jit(solution)/shard_map/ppermute | solution.py:172
  39.3 13.9 %collective-permute-start.4 = (f32[256,256]{1,0:T(8,128)S(1)}, f32[256,256]{1,0:T(8,128)S(1)}, u32[]{:S(2)}, u32[]{:S(2)}) collective-permute-start(f32[256,256]{1,0:T(8,128)S(1)} %get-tuple-element.94), channel_id=1, source_target_pairs={{0,32},{32,64},{64,96},{1,33},{33,65},{65,97},{2,34},{34,66},{66,9... | collective-permute-start | bytes 786440 | tf_op jit(solution)/shard_map/ppermute | solution.py:172
  51.3 8.3 %collective-permute-start.7 = (f32[256,256]{1,0:T(8,128)S(1)}, f32[256,256]{1,0:T(8,128)S(1)}, u32[]{:S(2)}, u32[]{:S(2)}) collective-permute-start(f32[256,256]{1,0:T(8,128)S(1)} %get-tuple-element.103), channel_id=1, source_target_pairs={{0,32},{32,64},{64,96},{1,33},{33,65},{65,97},{2,34},{34,66},{66,9... | collective-permute-start | bytes 786440 | tf_op jit(solution)/shard_map/ppermute | solution.py:172
  57.5 8.3 %collective-permute-start.6 = (f32[256,256]{1,0:T(8,128)S(1)}, f32[256,256]{1,0:T(8,128)S(1)}, u32[]{:S(2)}, u32[]{:S(2)}) collective-permute-start(f32[256,256]{1,0:T(8,128)S(1)} %get-tuple-element.102), channel_id=1, source_target_pairs={{0,32},{32,64},{64,96},{1,33},{33,65},{65,97},{2,34},{34,66},{66,9... | collective-permute-start | bytes 786440 | tf_op jit(solution)/shard_map/ppermute | solution.py:172
  63.8 8.3 %collective-permute-start.9 = (f32[256,256]{1,0:T(8,128)S(1)}, f32[256,256]{1,0:T(8,128)S(1)}, u32[]{:S(2)}, u32[]{:S(2)}) collective-permute-start(f32[256,256]{1,0:T(8,128)S(1)} %get-tuple-element.111), channel_id=1, source_target_pairs={{0,32},{32,64},{64,96},{1,33},{33,65},{65,97},{2,34},{34,66},{66,9... | collective-permute-start | bytes 786440 | tf_op jit(solution)/shard_map/ppermute | solution.py:172
  70.3 8.3 %collective-permute-start.8 = (f32[256,256]{1,0:T(8,128)S(1)}, f32[256,256]{1,0:T(8,128)S(1)}, u32[]{:S(2)}, u32[]{:S(2)}) collective-permute-start(f32[256,256]{1,0:T(8,128)S(1)} %get-tuple-element.110), channel_id=1, source_target_pairs={{0,32},{32,64},{64,96},{1,33},{33,65},{65,97},{2,34},{34,66},{66,9... | collective-permute-start | bytes 786440 | tf_op jit(solution)/shard_map/ppermute | solution.py:172
  76.4 8.4 %collective-permute-start.11 = (f32[256,256]{1,0:T(8,128)S(1)}, f32[256,256]{1,0:T(8,128)S(1)}, u32[]{:S(2)}, u32[]{:S(2)}) collective-permute-start(f32[256,256]{1,0:T(8,128)S(1)} %get-tuple-element.119), channel_id=1, source_target_pairs={{0,32},{32,64},{64,96},{1,33},{33,65},{65,97},{2,34},{34,66},{66,9... | collective-permute-start | bytes 786440 | tf_op jit(solution)/shard_map/ppermute | solution.py:172
  82.8 8.3 %collective-permute-start.10 = (f32[256,256]{1,0:T(8,128)S(1)}, f32[256,256]{1,0:T(8,128)S(1)}, u32[]{:S(2)}, u32[]{:S(2)}) collective-permute-start(f32[256,256]{1,0:T(8,128)S(1)} %get-tuple-element.118), channel_id=1, source_target_pairs={{0,32},{32,64},{64,96},{1,33},{33,65},{65,97},{2,34},{34,66},{66,9... | collective-permute-start | bytes 786440 | tf_op jit(solution)/shard_map/ppermute | solution.py:172
  89.1 8.3 %collective-permute-start.13 = (f32[256,256]{1,0:T(8,128)S(1)}, f32[256,256]{1,0:T(8,128)S(1)}, u32[]{:S(2)}, u32[]{:S(2)}) collective-permute-start(f32[256,256]{1,0:T(8,128)S(1)} %get-tuple-element.127), channel_id=1, source_target_pairs={{0,32},{32,64},{64,96},{1,33},{33,65},{65,97},{2,34},{34,66},{66,9... | collective-permute-start | bytes 786440 | tf_op jit(solution)/shard_map/ppermute | solution.py:172
  95.4 8.3 %collective-permute-start.12 = (f32[256,256]{1,0:T(8,128)S(1)}, f32[256,256]{1,0:T(8,128)S(1)}, u32[]{:S(2)}, u32[]{:S(2)}) collective-permute-start(f32[256,256]{1,0:T(8,128)S(1)} %get-tuple-element.126), channel_id=1, source_target_pairs={{0,32},{32,64},{64,96},{1,33},{33,65},{65,97},{2,34},{34,66},{66,9... | collective-permute-start | bytes 786440 | tf_op jit(solution)/shard_map/ppermute | solution.py:172
  101.6 8.3 %collective-permute-start.15 = (f32[256,256]{1,0:T(8,128)S(1)}, f32[256,256]{1,0:T(8,128)S(1)}, u32[]{:S(2)}, u32[]{:S(2)}) collective-permute-start(f32[256,256]{1,0:T(8,128)S(1)} %get-tuple-element.135), channel_id=1, source_target_pairs={{0,32},{32,64},{64,96},{1,33},{33,65},{65,97},{2,34},{34,66},{66,9... | collective-permute-start | bytes 786440 | tf_op jit(solution)/shard_map/ppermute | solution.py:172
  108.0 8.3 %collective-permute-start.14 = (f32[256,256]{1,0:T(8,128)S(1)}, f32[256,256]{1,0:T(8,128)S(1)}, u32[]{:S(2)}, u32[]{:S(2)}) collective-permute-start(f32[256,256]{1,0:T(8,128)S(1)} %get-tuple-element.134), channel_id=1, source_target_pairs={{0,32},{32,64},{64,96},{1,33},{33,65},{65,97},{2,34},{34,66},{66,9... | collective-permute-start | bytes 786440 | tf_op jit(solution)/shard_map/ppermute | solution.py:172
  121.3 15.5 %collective-permute-start.16 = (f32[2,3,4,3,32,256]{5,4,3,2,1,0:T(8,128)S(1)}, f32[2,3,4,3,32,256]{5,4,3,2,1,0:T(8,128)S(1)}, u32[]{:S(2)}, u32[]{:S(2)}) collective-permute-start(f32[2,3,4,3,32,256]{5,4,3,2,1,0:T(8,128)S(1)} %get-tuple-element.143), channel_id=1, source_target_pairs={{0,1},{1,0},{2,3},{3,2},{4,5},{5,4},{6,7},{7,6},{8,9},{9,8},{10,11... | collective-permute-start | bytes 7077896 | tf_op jit(solution)/shard_map/ppermute | solution.py:133
  121.4 5.6 %collective-permute-start.17 = (f32[2,4,3,32,256]{4,3,2,1,0:T(8,128)S(1)}, f32[2,4,3,32,256]{4,3,2,1,0:T(8,128)S(1)}, u32[]{:S(2)}, u32[]{:S(2)}) collective-permute-start(f32[2,4,3,32,256]{4,3,2,1,0:T(8,128)S(1)} %get-tuple-element.144), channel_id=1, source_target_pairs={{0,1},{1,0},{2,3},{3,2},{4,5},{5,4},{6,7},{7,6},{8,9},{9,8},{10,11... | collective-permute-start | bytes 2359304 | tf_op jit(solution)/shard_map/ppermute | solution.py:133
  127.2 15.7 %collective-permute-start.27 = (f32[2,96,256]{2,1,0:T(8,128)S(1)}, f32[2,96,256]{2,1,0:T(8,128)S(1)}, u32[]{:S(2)}, u32[]{:S(2)}) collective-permute-start(f32[2,96,256]{2,1,0:T(8,128)S(1)} %bitcast.172), channel_id=1, source_target_pairs={{0,24},{8,0},{16,8},{24,16},{1,25},{9,1},{17,9},{25,17},{2,26},{10... | collective-permute-start | bytes 589832 | tf_op jit(solution)/shard_map/ppermute | solution.py:129
  133.5 12.7 %collective-permute-start.18 = (f32[2,96,256]{2,1,0:T(8,128)S(1)}, f32[2,96,256]{2,1,0:T(8,128)S(1)}, u32[]{:S(2)}, u32[]{:S(2)}) collective-permute-start(f32[2,96,256]{2,1,0:T(8,128)S(1)} %bitcast.171), channel_id=1, source_target_pairs={{0,2},{2,4},{4,6},{6,0},{1,3},{3,5},{5,7},{7,1},{8,10},{10,12},{12... | collective-permute-start | bytes 589832 | tf_op jit(solution)/shard_map/ppermute | solution.py:129
  135.0 7.6 %collective-permute-start.25 = (f32[2,96,256]{2,1,0:T(8,128)S(1)}, f32[2,96,256]{2,1,0:T(8,128)S(1)}, u32[]{:S(2)}, u32[]{:S(2)}) collective-permute-start(f32[2,96,256]{2,1,0:T(8,128)S(1)} %bitcast.173), channel_id=1, source_target_pairs={{0,8},{8,16},{16,24},{24,0},{1,9},{9,17},{17,25},{25,1},{2,10},{10... | collective-permute-start | bytes 589832 | tf_op jit(solution)/shard_map/ppermute | solution.py:129
  135.0 12.8 %collective-permute-start.20 = (f32[2,96,256]{2,1,0:T(8,128)S(1)}, f32[2,96,256]{2,1,0:T(8,128)S(1)}, u32[]{:S(2)}, u32[]{:S(2)}) collective-permute-start(f32[2,96,256]{2,1,0:T(8,128)S(1)} %bitcast.170), channel_id=1, source_target_pairs={{0,6},{2,0},{4,2},{6,4},{1,7},{3,1},{5,3},{7,5},{8,14},{10,8},{12,... | collective-permute-start | bytes 589832 | tf_op jit(solution)/shard_map/ppermute | solution.py:129
  142.7 11.0 %collective-permute-start.26 = (f32[4,96,256]{2,1,0:T(8,128)S(1)}, f32[4,96,256]{2,1,0:T(8,128)S(1)}, u32[]{:S(2)}, u32[]{:S(2)}) collective-permute-start(f32[4,96,256]{2,1,0:T(8,128)S(1)} %pad_maximum_fusion.2), channel_id=1, source_target_pairs={{0,8},{8,16},{16,24},{24,0},{1,9},{9,17},{17,25},{25,1},{2,10},{10... | collective-permute-start | bytes 1179656 | tf_op jit(solution)/shard_map/ppermute | solution.py:129
  142.9 10.8 %collective-permute-start.28 = (f32[4,96,256]{2,1,0:T(8,128)S(1)}, f32[4,96,256]{2,1,0:T(8,128)S(1)}, u32[]{:S(2)}, u32[]{:S(2)}) collective-permute-start(f32[4,96,256]{2,1,0:T(8,128)S(1)} %pad_maximum_fusion.3), channel_id=1, source_target_pairs={{0,24},{8,0},{16,8},{24,16},{1,25},{9,1},{17,9},{25,17},{2,26},{10... | collective-permute-start | bytes 1179656 | tf_op jit(solution)/shard_map/ppermute | solution.py:129
  146.3 12.3 %collective-permute-start.19 = (f32[4,96,256]{2,1,0:T(8,128)S(1)}, f32[4,96,256]{2,1,0:T(8,128)S(1)}, u32[]{:S(2)}, u32[]{:S(2)}) collective-permute-start(f32[4,96,256]{2,1,0:T(8,128)S(1)} %pad_maximum_fusion), channel_id=1, source_target_pairs={{0,2},{2,4},{4,6},{6,0},{1,3},{3,5},{5,7},{7,1},{8,10},{10,12},{12... | collective-permute-start | bytes 1179656 | tf_op jit(solution)/shard_map/ppermute | solution.py:129
  147.9 11.5 %collective-permute-start.21 = (f32[4,96,256]{2,1,0:T(8,128)S(1)}, f32[4,96,256]{2,1,0:T(8,128)S(1)}, u32[]{:S(2)}, u32[]{:S(2)}) collective-permute-start(f32[4,96,256]{2,1,0:T(8,128)S(1)} %pad_maximum_fusion.1), channel_id=1, source_target_pairs={{0,6},{2,0},{4,2},{6,4},{1,7},{3,1},{5,3},{7,5},{8,14},{10,8},{12,... | collective-permute-start | bytes 1179656 | tf_op jit(solution)/shard_map/ppermute | solution.py:129
  153.8 8.3 %collective-permute-start.31 = (f32[96,256]{1,0:T(8,128)S(1)}, f32[96,256]{1,0:T(8,128)S(1)}, u32[]{:S(2)}, u32[]{:S(2)}) collective-permute-start(f32[96,256]{1,0:T(8,128)S(1)} %get-tuple-element.165), channel_id=1, source_target_pairs={{0,4},{2,6},{4,0},{6,2},{1,5},{3,7},{5,1},{7,3},{8,12},{10,14},{12... | collective-permute-start | bytes 294920 | tf_op jit(solution)/shard_map/ppermute | solution.py:129
  156.6 6.3 %collective-permute-start.30 = (f32[96,256]{1,0:T(8,128)S(1)}, f32[96,256]{1,0:T(8,128)S(1)}, u32[]{:S(2)}, u32[]{:S(2)}) collective-permute-start(f32[96,256]{1,0:T(8,128)S(1)} %get-tuple-element.166), channel_id=1, source_target_pairs={{0,6},{2,0},{4,2},{6,4},{1,7},{3,1},{5,3},{7,5},{8,14},{10,8},{12,... | collective-permute-start | bytes 294920 | tf_op jit(solution)/shard_map/ppermute | solution.py:129
  158.0 5.8 %collective-permute-start.29 = (f32[96,256]{1,0:T(8,128)S(1)}, f32[96,256]{1,0:T(8,128)S(1)}, u32[]{:S(2)}, u32[]{:S(2)}) collective-permute-start(f32[96,256]{1,0:T(8,128)S(1)} %get-tuple-element.167), channel_id=1, source_target_pairs={{0,2},{2,4},{4,6},{6,0},{1,3},{3,5},{5,7},{7,1},{8,10},{10,12},{12... | collective-permute-start | bytes 294920 | tf_op jit(solution)/shard_map/ppermute | solution.py:129
  159.4 6.2 %collective-permute-start.24 = (f32[96,256]{1,0:T(8,128)S(1)}, f32[96,256]{1,0:T(8,128)S(1)}, u32[]{:S(2)}, u32[]{:S(2)}) collective-permute-start(f32[96,256]{1,0:T(8,128)S(1)} %get-tuple-element.162), channel_id=1, source_target_pairs={{0,16},{8,24},{16,0},{24,8},{1,17},{9,25},{17,1},{25,9},{2,18},{10... | collective-permute-start | bytes 294920 | tf_op jit(solution)/shard_map/ppermute | solution.py:129
  160.5 6.0 %collective-permute-start.23 = (f32[96,256]{1,0:T(8,128)S(1)}, f32[96,256]{1,0:T(8,128)S(1)}, u32[]{:S(2)}, u32[]{:S(2)}) collective-permute-start(f32[96,256]{1,0:T(8,128)S(1)} %get-tuple-element.163), channel_id=1, source_target_pairs={{0,24},{8,0},{16,8},{24,16},{1,25},{9,1},{17,9},{25,17},{2,26},{10... | collective-permute-start | bytes 294920 | tf_op jit(solution)/shard_map/ppermute | solution.py:129
  162.1 5.8 %collective-permute-start.22 = (f32[96,256]{1,0:T(8,128)S(1)}, f32[96,256]{1,0:T(8,128)S(1)}, u32[]{:S(2)}, u32[]{:S(2)}) collective-permute-start(f32[96,256]{1,0:T(8,128)S(1)} %get-tuple-element.164), channel_id=1, source_target_pairs={{0,8},{8,16},{16,24},{24,0},{1,9},{9,17},{17,25},{25,1},{2,10},{10... | collective-permute-start | bytes 294920 | tf_op jit(solution)/shard_map/ppermute | solution.py:129

commit v3 on v1

v3 whole, which is shorter than its diff:
```python
import jax
import jax.numpy as jnp
from jax import lax
from jax.experimental import pallas as pl
from jax.experimental.pallas import tpu as pltpu
from jax.sharding import Mesh, PartitionSpec as P

f32, bf16 = jnp.float32, jnp.bfloat16
W = 256
NQ = 12
ROWS = 32
SITES = 4
LAG = 2


def halves(x):
    high = x.astype(bf16)
    return high, (x - high.astype(f32)).astype(bf16)


def product(a, b, dims):
    (ah, al), (bh, bl) = a, b

    def dot(u, v):
        return lax.dot_general(u, v, (dims, ((), ())), preferred_element_type=f32)

    return dot(ah, bh) + (dot(ah, bl) + dot(al, bh))


def framed(x, rows, columns):
    i = lax.broadcasted_iota(jnp.int32, x.shape, 0)
    j = lax.broadcasted_iota(jnp.int32, x.shape, 1)
    return jnp.where((i < rows) & (j < columns), x, 0.0)


LAST = NQ + LAG * (SITES - 1)
SCALAR = pl.BlockSpec(memory_space=pltpu.SMEM)
LOCAL = pl.BlockSpec(memory_space=pltpu.VMEM)
FAR = pl.BlockSpec(memory_space=pltpu.HBM)
GRANT = pltpu.CompilerParams(vmem_limit_bytes=8 * 2**20)
BUFFER = jax.ShapeDtypeStruct((4, 4, 2, 3, ROWS, W), f32)


def update_part(q, ints, floats, arrived, previous, left, mps):
    site = ints[0]
    below = jnp.maximum(q - 1, 0)
    size, under = ints[4 + q], ints[4 + below]
    c0 = jnp.where(site == 0, ints[16 + q].astype(f32), 1.0) * floats[0]
    c1 = jnp.where(site == 0, ints[16 + below].astype(f32), 1.0) * floats[1]
    now = jnp.where(site == 0, left[q], arrived[...])
    before = jnp.where(site == 0, left[below], previous[...])
    before = jnp.where(q > 0, before, 0.0)
    s = framed(mps[0, q], size, size)
    u = framed(mps[1, below], under, size)
    first = c0 * product(halves(now), halves(s), ((1,), (0,)))
    second = c1 * product(halves(before), halves(u), ((1,), (0,)))
    return product(halves(s.T), halves(first), ((1,), (0,))) + product(
        halves(u.T), halves(second), ((1,), (0,)))


def apply_part(q, ints, floats, psi, rights, keep, send, results, total, stores):
    my_z, my_x, core = ints[1], ints[2], ints[3]
    above = jnp.minimum(q + 1, NQ - 1)
    present_above = jnp.where(q < NQ - 1, ints[16 + above], 0)

    def one_state(state, _):
        other = jnp.where(state == 0, q, above)
        present = jnp.where(state == 0, ints[16 + q], present_above)
        c = floats[2 + state] * present.astype(f32)
        n = ints[4 + other]
        part = c * product(halves(total[...]), halves(psi[state, q]), ((1,), (0,)))
        results[state] = product(halves(part), halves(framed(rights[other], n, n)), ((1,), (1,)))

        def place(target):
            for i in range(W // ROWS):
                piece = (W // ROWS) * q + i
                owner, third = piece // 3, piece % 3
                z = (owner // 8 - my_z + 4) % 4
                x = ((owner // 2) % 4 - my_x + 4) % 4
                near, far = jnp.where(state == 0, x, z), jnp.where(state == 0, z, x)
                pltpu.make_async_copy(
                    results.at[state, pl.ds(ROWS * i, ROWS)], target.at[near, far, owner % 2, third], stores).start()

        @pl.when(state == core)
        def _():
            place(keep)

        @pl.when(state != core)
        def _():
            place(send)

        return 0

    lax.fori_loop(0, 2, one_state, 0)
    pltpu.make_async_copy(results, psi.at[:, 0], stores).wait()


def sector_step(step, ints, floats, arrived, previous, left, mps, psi, rights, saved, held):
    sending, applying = step + LAG < LAST, step >= LAG
    late = NQ <= step < NQ + LAG
    n_in = 6 + (2 if applying else 0) + (1 if late else 0)

    def kernel(*refs):
        ints, floats, arrived, previous, left, mps = refs[:6]
        outs = refs[n_in + len(held):]
        environ = outs[0] if sending else None
        q = step - LAG * ints[0]
        active = (q >= 0) & (q < NQ)
        total = outs[-2] if applying else None

        @pl.when(active)
        def _():
            moved = update_part(q, ints, floats, arrived, previous, left, mps)
            if sending:
                environ[...] = moved
            if applying:
                total[...] = moved

        if applying:
            psi, rights = refs[6:8]
            keep, send = outs[1:3] if sending else outs[:2]
            if late:
                @pl.when(ints[0] == 0)
                def _():
                    total[...] = refs[8][...]

                active = active | (ints[0] == 0)
                q = jnp.where(ints[0] == 0, step - NQ, q)

            @pl.when(active)
            def _():
                apply_part(q, ints, floats, psi, rights, keep, send, *outs[-3:])

    operands = (arrived, previous, left, mps) + ((psi, rights) if applying else ()) + ((saved,) if late else ())
    first_out = 1 if sending else 0
    return pl.pallas_call(
        kernel,
        in_specs=[SCALAR] * 2 + [LOCAL] * len(operands) + [FAR] * len(held),
        out_specs=[LOCAL] * first_out + ([FAR] * 2 if applying else []),
        out_shape=[jax.ShapeDtypeStruct((W, W), f32)] * first_out + ([BUFFER] * 2 if applying else []),
        scratch_shapes=[
            pltpu.VMEM((2, W, W), f32),
            pltpu.VMEM((W, W), f32),
            pltpu.SemaphoreType.DMA,
        ] if applying else [],
        input_output_aliases={n_in + i: first_out + i for i in range(len(held))},
        compiler_params=GRANT,
        name=f"sector{step}",
    )(ints, floats, *operands, *held)


TERM = ("z", "x", "core")


def swapped(x):
    return lax.ppermute(x, "core", [(0, 1), (1, 0)])


def turned(x, first, by):
    pairs = []
    for z in range(4):
        for x_ in range(4):
            for c in range(2):
                along_x = (c == 0) == first
                to = (z, (x_ + by) % 4) if along_x else ((z + by) % 4, x_)
                pairs.append((8 * z + 2 * x_ + c, 8 * to[0] + 2 * to[1] + c))
    return lax.ppermute(x, TERM, pairs)


def reduced(keep, send, core):
    both = (keep + swapped(send)).reshape(4, 4, 192, W)
    up = turned(both[2, :2], True, 1)
    down = turned(both[2, 2:], True, -1)
    ahead = jnp.concatenate([both[1, :2] + up, both[1, 2:]])
    behind = jnp.concatenate([both[3, :2], both[3, 2:] + down])
    line = both[0] + turned(ahead, True, 1) + turned(behind, True, -1)
    rows = (line[0] + turned(line[1], False, 1)) + (turned(line[3], False, -1) + turned(line[2], False, 2))
    rows = rows.reshape(2, 96, W)
    mine = jnp.where(core == 0, rows[0], rows[1])
    got = swapped(jnp.where(core == 0, rows[1], rows[0]))
    return jnp.stack([jnp.where(core == 0, mine, got), jnp.where(core == 0, got, mine)])[None]


def shards(left_env, right_env, mps, psi, coef, sector_sizes, pattern):
    place = jnp.stack([lax.axis_index(a) for a in ("site",) + TERM]).astype(jnp.int32)
    ints = jnp.concatenate([place, sector_sizes, pattern[0]])
    floats = coef[0, 0]
    sources = (left_env[0], mps[0], psi[0], right_env[0, 0])
    nothing = jnp.zeros((W, W), f32)
    arrivals, environs, held = {}, {}, ()
    for step in range(LAST):
        out = sector_step(
            step, ints, floats, arrivals.get(step, nothing), arrivals.get(step - 1, nothing), *sources,
            environs.get(step - NQ), held)
        if step + LAG < LAST:
            environs[step], *out = out
            arrivals[step + LAG] = lax.ppermute(environs[step], "site", [(0, 1), (1, 2), (2, 3)])
        held = tuple(out)
    return reduced(*held, place[3])


def solution(mesh):
    fine = Mesh(mesh.devices.reshape(4, 4, 4, 2), ("site", "z", "x", "core"))
    term = ("z", "x", "core")
    return jax.shard_map(
        shards,
        mesh=fine,
        in_specs=(
            P(term, None, None, None),
            P("site", term, None, None, None),
            P("site", None, None, None, None),
            P("site", None, None, None, None),
            P("site", term, None),
            P(),
            P(term, None),
        ),
        out_specs=P("site", None, term, None),
        check_vma=False,
    )
```

time: 174 us -> 168 us (0.966)
  waiting for transfers between devices: 59.8 us -> 72.5 us
  starting transfers between devices: 46.1 us -> 36.2 us
  local copies, waits for them, and re-layouts: 11.4 us -> 6.38 us
  Pallas kernels: 53.9 us -> 50.2 us
    ppermute x33 -> x25, waiting for transfers between devices: 59.8 us -> 72.5 us  [the longest x16 41.5 us: shards(): lax.ppermute(environs[step], 'site', [(0, 1), (1, 2), (2, 3)])]
    ppermute x33 -> x25, starting transfers between devices: 46.1 us -> 36.2 us  [the longest x16 21.3 us: shards(): lax.ppermute(environs[step], 'site', [(0, 1), (1, 2), (2, 3)])]
    unnamed x20 -> x18, local copies, waits for them, and re-layouts: 10 us -> 5.35 us
    pallas_call x18, Pallas kernels: 53.9 us -> 50.2 us  [sector_step(): pl.pallas_call(kernel, in_specs=[SCALAR] * 2 + [LOCAL] * len(operands) +...]
  transfers between devices with their start and end apart: 33 -> 25, of which waited for: 22 -> 25; matrix products, arithmetic and copies ran while one was open for 0% -> 0% of each run, Pallas kernels for 28% -> 27%
where the time goes in v3:
time: 168 us
  waiting for transfers between devices  72.5 us (43%)
  Pallas kernels  50.2 us (30%)
  starting transfers between devices  36.2 us (22%)
  local copies, waits for them, and re-layouts  6.38 us (4%)
  other arithmetic  1.84 us (1%)
    pallas_call x18, Pallas kernels, sector_step(): pl.pallas_call(kernel, in_specs=[SCALAR] * 2 + [LOCAL] * len(operands) +...  50.2 us
    ppermute x16, waiting for transfers between devices, shards(): lax.ppermute(environs[step], 'site', [(0, 1), (1, 2), (2, 3)])  41.5 us
    ppermute x7, waiting for transfers between devices, turned(): return lax.ppermute(x, TERM, pairs)  24.1 us
    ppermute x16, starting transfers between devices, shards(): lax.ppermute(environs[step], 'site', [(0, 1), (1, 2), (2, 3)])  21.3 us
    ppermute x7, starting transfers between devices, turned(): return lax.ppermute(x, TERM, pairs)  14.7 us
    ppermute x2, waiting for transfers between devices, swapped(): return lax.ppermute(x, 'core', [(0, 1), (1, 0)])  6.93 us
    unnamed x18, local copies, waits for them, and re-layouts  5.35 us
  transfers between devices with their start and end apart: 25, of which 25 were waited for; matrix products, arithmetic and copies ran while one was open for 0% of the time, Pallas kernels for 27%

profile of v3, /device:TPU:24, one launch (start us, length us, event | category | flops | bytes accessed | tf_op | source)
XLA Modules:
  0.0 167.6 jit_solution(4269438667068253696)
XLA Ops:
  0.8 2.8 %copy-done = f32[1,2,12,256,256]{4,3,2,1,0:T(8,128)S(1)} copy-done((f32[1,2,12,256,256]{4,3,2,1,0:T(8,128)S(1)}, f32[1,2,12,256,256]{4,3,2,1,0:T(8,128)}, u32[]{:S(2)}) %copy-start) | copy-done | bytes 6291480
  3.6 1.9 %copy-done.1 = f32[1,12,256,256]{3,2,1,0:T(8,128)S(1)} copy-done((f32[1,12,256,256]{3,2,1,0:T(8,128)S(1)}, f32[1,12,256,256]{3,2,1,0:T(8,128)}, u32[]{:S(2)}) %copy-start.1) | copy-done | bytes 3145752
  6.7 1.6 collective-permute-start.1
  8.8 1.4 collective-permute-start
  10.3 7.8 %collective-permute-done.1.refs_2_.refs_3_ = f32[256,256]{1,0:T(8,128)S(1)} collective-permute-done((f32[256,256]{1,0:T(8,128)S(1)}, f32[256,256]{1,0:T(8,128)S(1)}, u32[]{:S(2)}, u32[]{:S(2)}) %collective-permute-start.1) | collective-permute-done | bytes 262176 | tf_op jit(solution)/shard_map/ppermute | solution.py:197
  18.6 1.6 collective-permute-start.3
  20.2 3.4 %collective-permute-done.refs_2_.refs_3_ = f32[256,256]{1,0:T(8,128)S(1)} collective-permute-done((f32[256,256]{1,0:T(8,128)S(1)}, f32[256,256]{1,0:T(8,128)S(1)}, u32[]{:S(2)}, u32[]{:S(2)}) %collective-permute-start) | collective-permute-done | bytes 262176 | tf_op jit(solution)/shard_map/ppermute | solution.py:197
  24.2 1.3 collective-permute-start.2
  25.5 4.2 %collective-permute-done.3.refs_2_.refs_3_ = f32[256,256]{1,0:T(8,128)S(1)} collective-permute-done((f32[256,256]{1,0:T(8,128)S(1)}, f32[256,256]{1,0:T(8,128)S(1)}, u32[]{:S(2)}, u32[]{:S(2)}) %collective-permute-start.3) | collective-permute-done | bytes 262176 | tf_op jit(solution)/shard_map/ppermute | solution.py:197
  30.3 1.3 collective-permute-start.5
  31.6 2.9 %collective-permute-done.2.refs_2_.refs_3_ = f32[256,256]{1,0:T(8,128)S(1)} collective-permute-done((f32[256,256]{1,0:T(8,128)S(1)}, f32[256,256]{1,0:T(8,128)S(1)}, u32[]{:S(2)}, u32[]{:S(2)}) %collective-permute-start.2) | collective-permute-done | bytes 262176 | tf_op jit(solution)/shard_map/ppermute | solution.py:197
  35.1 1.3 collective-permute-start.4
  36.4 3.8 %collective-permute-done.5.refs_2_.refs_3_ = f32[256,256]{1,0:T(8,128)S(1)} collective-permute-done((f32[256,256]{1,0:T(8,128)S(1)}, f32[256,256]{1,0:T(8,128)S(1)}, u32[]{:S(2)}, u32[]{:S(2)}) %collective-permute-start.5) | collective-permute-done | bytes 262176 | tf_op jit(solution)/shard_map/ppermute | solution.py:197
  40.2 3.9 %sector6.1 = (f32[256,256]{1,0:T(8,128)S(1)}, f32[4,4,2,3,32,256]{5,4,3,2,1,0:T(8,128)S(1)}, f32[4,4,2,3,32,256]{5,4,3,2,1,0:T(8,128)S(1)}) custom-call(s32[28]{0:T(128)S(1)} %concatenate.9.refs_0_, f32[4]{0:T(128)S(1)} %bitcast.124, f32[256,256]{1,0:T(8,128)S(1)} %collective-permute-done.5.refs_2_.refs_3_, ...), custom_call_target="tpu_custom_call", output_to_operand_aliasing={{1}: (8, {}), {2}: (9, {})} | custom-call | tf_op jit(solution)/shard_map/sector6/pallas_call | solution.py:136
  44.0 1.3 collective-permute-start.7
  46.0 4.0 %sector7.1 = (f32[256,256]{1,0:T(8,128)S(1)}, f32[4,4,2,3,32,256]{5,4,3,2,1,0:T(8,128)S(1)}, f32[4,4,2,3,32,256]{5,4,3,2,1,0:T(8,128)S(1)}) custom-call(s32[28]{0:T(128)S(1)} %concatenate.9.refs_0_, f32[4]{0:T(128)S(1)} %bitcast.125, f32[256,256]{1,0:T(8,128)S(1)} %collective-permute-done.4.refs_2_.refs_3_, ...), custom_call_target="tpu_custom_call", output_to_operand_aliasing={{1}: (8, {}), {2}: (9, {})} | custom-call | tf_op jit(solution)/shard_map/sector7/pallas_call | solution.py:136
  51.3 2.2 %collective-permute-done.7.refs_2_.refs_3_ = f32[256,256]{1,0:T(8,128)S(1)} collective-permute-done((f32[256,256]{1,0:T(8,128)S(1)}, f32[256,256]{1,0:T(8,128)S(1)}, u32[]{:S(2)}, u32[]{:S(2)}) %collective-permute-start.7) | collective-permute-done | bytes 262176 | tf_op jit(solution)/shard_map/ppermute | solution.py:197
  53.6 3.9 %sector8.1 = (f32[256,256]{1,0:T(8,128)S(1)}, f32[4,4,2,3,32,256]{5,4,3,2,1,0:T(8,128)S(1)}, f32[4,4,2,3,32,256]{5,4,3,2,1,0:T(8,128)S(1)}) custom-call(s32[28]{0:T(128)S(1)} %concatenate.9.refs_0_, f32[4]{0:T(128)S(1)} %bitcast.126, f32[256,256]{1,0:T(8,128)S(1)} %collective-permute-done.7.refs_2_.refs_3_, ...), custom_call_target="tpu_custom_call", output_to_operand_aliasing={{1}: (8, {}), {2}: (9, {})} | custom-call | tf_op jit(solution)/shard_map/sector8/pallas_call | solution.py:136
  59.8 3.9 %sector9.1 = (f32[256,256]{1,0:T(8,128)S(1)}, f32[4,4,2,3,32,256]{5,4,3,2,1,0:T(8,128)S(1)}, f32[4,4,2,3,32,256]{5,4,3,2,1,0:T(8,128)S(1)}) custom-call(s32[28]{0:T(128)S(1)} %concatenate.9.refs_0_, f32[4]{0:T(128)S(1)} %bitcast.127, f32[256,256]{1,0:T(8,128)S(1)} %collective-permute-done.6.refs_2_.refs_3_, ...), custom_call_target="tpu_custom_call", output_to_operand_aliasing={{1}: (8, {}), {2}: (9, {})} | custom-call | tf_op jit(solution)/shard_map/sector9/pallas_call | solution.py:136
  63.6 1.3 collective-permute-start.8
  64.9 3.1 %collective-permute-done.9.refs_2_.refs_3_ = f32[256,256]{1,0:T(8,128)S(1)} collective-permute-done((f32[256,256]{1,0:T(8,128)S(1)}, f32[256,256]{1,0:T(8,128)S(1)}, u32[]{:S(2)}, u32[]{:S(2)}) %collective-permute-start.9) | collective-permute-done | bytes 262176 | tf_op jit(solution)/shard_map/ppermute | solution.py:197
  68.1 3.9 %sector10.1 = (f32[256,256]{1,0:T(8,128)S(1)}, f32[4,4,2,3,32,256]{5,4,3,2,1,0:T(8,128)S(1)}, f32[4,4,2,3,32,256]{5,4,3,2,1,0:T(8,128)S(1)}) custom-call(s32[28]{0:T(128)S(1)} %concatenate.9.refs_0_, f32[4]{0:T(128)S(1)} %bitcast.128, f32[256,256]{1,0:T(8,128)S(1)} %collective-permute-done.9.refs_2_.refs_3_, ...), custom_call_target="tpu_custom_call", output_to_operand_aliasing={{1}: (8, {}), {2}: (9, {})} | custom-call | tf_op jit(solution)/shard_map/sector10/pallas_call | solution.py:136
  73.3 1.6 collective-permute-done.8.refs_2_.refs_3_
  74.8 3.9 %sector11.1 = (f32[256,256]{1,0:T(8,128)S(1)}, f32[4,4,2,3,32,256]{5,4,3,2,1,0:T(8,128)S(1)}, f32[4,4,2,3,32,256]{5,4,3,2,1,0:T(8,128)S(1)}) custom-call(s32[28]{0:T(128)S(1)} %concatenate.9.refs_0_, f32[4]{0:T(128)S(1)} %bitcast.129, f32[256,256]{1,0:T(8,128)S(1)} %collective-permute-done.8.refs_2_.refs_3_, ...), custom_call_target="tpu_custom_call", output_to_operand_aliasing={{1}: (8, {}), {2}: (9, {})} | custom-call | tf_op jit(solution)/shard_map/sector11/pallas_call | solution.py:136
  80.0 3.1 %collective-permute-done.11.refs_2_.refs_3_ = f32[256,256]{1,0:T(8,128)S(1)} collective-permute-done((f32[256,256]{1,0:T(8,128)S(1)}, f32[256,256]{1,0:T(8,128)S(1)}, u32[]{:S(2)}, u32[]{:S(2)}) %collective-permute-start.11) | collective-permute-done | bytes 262176 | tf_op jit(solution)/shard_map/ppermute | solution.py:197
  83.0 3.9 %sector12.1 = (f32[256,256]{1,0:T(8,128)S(1)}, f32[4,4,2,3,32,256]{5,4,3,2,1,0:T(8,128)S(1)}, f32[4,4,2,3,32,256]{5,4,3,2,1,0:T(8,128)S(1)}) custom-call(s32[28]{0:T(128)S(1)} %concatenate.9.refs_0_, f32[4]{0:T(128)S(1)} %bitcast.130, f32[256,256]{1,0:T(8,128)S(1)} %collective-permute-done.11.refs_2_.refs_3_, ...), custom_call_target="tpu_custom_call", output_to_operand_aliasing={{1}: (9, {}), {2}: (10, {})} | custom-call | tf_op jit(solution)/shard_map/sector12/pallas_call | solution.py:136
  86.9 1.3 collective-permute-start.13
  88.2 1.5 collective-permute-done.10.refs_2_.refs_3_
  89.8 3.9 %sector13.1 = (f32[256,256]{1,0:T(8,128)S(1)}, f32[4,4,2,3,32,256]{5,4,3,2,1,0:T(8,128)S(1)}, f32[4,4,2,3,32,256]{5,4,3,2,1,0:T(8,128)S(1)}) custom-call(s32[28]{0:T(128)S(1)} %concatenate.9.refs_0_, f32[4]{0:T(128)S(1)} %bitcast.131, f32[256,256]{1,0:T(8,128)S(1)} %collective-permute-done.10.refs_2_.refs_3_, ...), custom_call_target="tpu_custom_call", output_to_operand_aliasing={{1}: (9, {}), {2}: (10, {})} | custom-call | tf_op jit(solution)/shard_map/sector13/pallas_call | solution.py:136
  93.7 1.3 collective-permute-start.12
  95.0 2.1 %collective-permute-done.13.refs_2_.refs_3_ = f32[256,256]{1,0:T(8,128)S(1)} collective-permute-done((f32[256,256]{1,0:T(8,128)S(1)}, f32[256,256]{1,0:T(8,128)S(1)}, u32[]{:S(2)}, u32[]{:S(2)}) %collective-permute-start.13) | collective-permute-done | bytes 262176 | tf_op jit(solution)/shard_map/ppermute | solution.py:197
  97.1 4.1 %sector14.1 = (f32[256,256]{1,0:T(8,128)S(1)}, f32[4,4,2,3,32,256]{5,4,3,2,1,0:T(8,128)S(1)}, f32[4,4,2,3,32,256]{5,4,3,2,1,0:T(8,128)S(1)}) custom-call(s32[28]{0:T(128)S(1)} %concatenate.9.refs_0_, f32[4]{0:T(128)S(1)} %bitcast.132, f32[256,256]{1,0:T(8,128)S(1)} %collective-permute-done.13.refs_2_.refs_3_, ...), custom_call_target="tpu_custom_call", output_to_operand_aliasing={{1}: (8, {}), {2}: (9, {})} | custom-call | tf_op jit(solution)/shard_map/sector14/pallas_call | solution.py:136
  103.5 3.9 %sector15.1 = (f32[256,256]{1,0:T(8,128)S(1)}, f32[4,4,2,3,32,256]{5,4,3,2,1,0:T(8,128)S(1)}, f32[4,4,2,3,32,256]{5,4,3,2,1,0:T(8,128)S(1)}) custom-call(s32[28]{0:T(128)S(1)} %concatenate.9.refs_0_, f32[4]{0:T(128)S(1)} %bitcast.133, f32[256,256]{1,0:T(8,128)S(1)} %collective-permute-done.12.refs_2_.refs_3_, ...), custom_call_target="tpu_custom_call", output_to_operand_aliasing={{1}: (8, {}), {2}: (9, {})} | custom-call | tf_op jit(solution)/shard_map/sector15/pallas_call | solution.py:136
  108.7 1.4 collective-permute-done.15.refs_2_.refs_3_
  110.1 3.9 %sector16.1 = (f32[4,4,2,3,32,256]{5,4,3,2,1,0:T(8,128)S(1)}, f32[4,4,2,3,32,256]{5,4,3,2,1,0:T(8,128)S(1)}) custom-call(s32[28]{0:T(128)S(1)} %concatenate.9.refs_0_, f32[4]{0:T(128)S(1)} %bitcast.134, f32[256,256]{1,0:T(8,128)S(1)} %collective-permute-done.15.refs_2_.refs_3_, ...), custom_call_target="tpu_custom_call", output_to_operand_aliasing={{0}: (8, {}), {1}: (9, {})} | custom-call | tf_op jit(solution)/shard_map/sector16/pallas_call | solution.py:136
  113.9 1.7 %collective-permute-done.14.refs_2_ = f32[256,256]{1,0:T(8,128)S(1)} collective-permute-done((f32[256,256]{1,0:T(8,128)S(1)}, f32[256,256]{1,0:T(8,128)S(1)}, u32[]{:S(2)}, u32[]{:S(2)}) %collective-permute-start.14) | collective-permute-done | bytes 262176 | tf_op jit(solution)/shard_map/ppermute | solution.py:197
  115.7 3.9 %sector17.1 = (f32[4,4,2,3,32,256]{5,4,3,2,1,0:T(8,128)S(1)}, f32[4,4,2,3,32,256]{5,4,3,2,1,0:T(8,128)S(1)}) custom-call(s32[28]{0:T(128)S(1)} %concatenate.9.refs_0_, f32[4]{0:T(128)S(1)} %bitcast.135, f32[256,256]{1,0:T(8,128)S(1)} %collective-permute-done.14.refs_2_, ...), custom_call_target="tpu_custom_call", output_to_operand_aliasing={{0}: (8, {}), {1}: (9, {})} | custom-call | tf_op jit(solution)/shard_map/sector17/pallas_call | solution.py:136
  119.6 5.6 %collective-permute-done.16 = f32[4,4,2,3,32,256]{5,4,3,2,1,0:T(8,128)S(1)} collective-permute-done((f32[4,4,2,3,32,256]{5,4,3,2,1,0:T(8,128)S(1)}, f32[4,4,2,3,32,256]{5,4,3,2,1,0:T(8,128)S(1)}, u32[]{:S(2)}, u32[]{:S(2)}) %collective-permute-start.16) | collective-permute-done | bytes 3145760 | tf_op jit(solution)/shard_map/ppermute | solution.py:156
  126.1 1.6 collective-permute-start.17
  127.7 1.7 %collective-permute-start.19 = (f32[2,192,256]{2,1,0:T(8,128)S(1)}, f32[2,192,256]{2,1,0:T(8,128)S(1)}, u32[]{:S(2)}, u32[]{:S(2)}) collective-permute-start(f32[2,192,256]{2,1,0:T(8,128)S(1)} %get-tuple-element.100), channel_id=1, source_target_pairs={{0,6},{1,25},{2,0},{3,27},{4,2},{5,29},{6,4},{7,31},{8,14},{9,1},{... | collective-permute-start | bytes 1179656 | tf_op jit(solution)/shard_map/ppermute | solution.py:167
  129.5 5.8 %collective-permute-done.17 = f32[2,192,256]{2,1,0:T(8,128)S(1)} collective-permute-done((f32[2,192,256]{2,1,0:T(8,128)S(1)}, f32[2,192,256]{2,1,0:T(8,128)S(1)}, u32[]{:S(2)}, u32[]{:S(2)}) %collective-permute-start.17) | collective-permute-done | bytes 393248 | tf_op jit(solution)/shard_map/ppermute | solution.py:167
  135.7 3.0 %collective-permute-start.20 = (f32[4,192,256]{2,1,0:T(8,128)S(1)}, f32[4,192,256]{2,1,0:T(8,128)S(1)}, u32[]{:S(2)}, u32[]{:S(2)}) collective-permute-start(f32[4,192,256]{2,1,0:T(8,128)S(1)} %pad_maximum_fusion.1), channel_id=1, source_target_pairs={{0,6},{1,25},{2,0},{3,27},{4,2},{5,29},{6,4},{7,31},{8,14},{9,1},{... | collective-permute-start | bytes 2359304 | tf_op jit(solution)/shard_map/ppermute | solution.py:167
  138.9 9.3 %collective-permute-done.20 = f32[4,192,256]{2,1,0:T(8,128)S(1)} collective-permute-done((f32[4,192,256]{2,1,0:T(8,128)S(1)}, f32[4,192,256]{2,1,0:T(8,128)S(1)}, u32[]{:S(2)}, u32[]{:S(2)}) %collective-permute-start.20) | collective-permute-done | bytes 786464 | tf_op jit(solution)/shard_map/ppermute | solution.py:167
  148.2 3.8 %collective-permute-done.18 = f32[4,192,256]{2,1,0:T(8,128)S(1)} collective-permute-done((f32[4,192,256]{2,1,0:T(8,128)S(1)}, f32[4,192,256]{2,1,0:T(8,128)S(1)}, u32[]{:S(2)}, u32[]{:S(2)}) %collective-permute-start.18) | collective-permute-done | bytes 786464 | tf_op jit(solution)/shard_map/ppermute | solution.py:167
  152.2 6.2 %collective-permute-start.23 = (f32[192,256]{1,0:T(8,128)S(1)}, f32[192,256]{1,0:T(8,128)S(1)}, u32[]{:S(2)}, u32[]{:S(2)}) collective-permute-start(f32[192,256]{1,0:T(8,128)S(1)} %get-tuple-element.103), channel_id=1, source_target_pairs={{0,16},{1,5},{2,18},{3,7},{4,20},{5,1},{6,22},{7,3},{8,24},{9,13},... | collective-permute-start | bytes 589832 | tf_op jit(solution)/shard_map/ppermute | solution.py:167
  158.5 2.0 %collective-permute-start.21 = (f32[192,256]{1,0:T(8,128)S(1)}, f32[192,256]{1,0:T(8,128)S(1)}, u32[]{:S(2)}, u32[]{:S(2)}) collective-permute-start(f32[192,256]{1,0:T(8,128)S(1)} %get-tuple-element.105), channel_id=1, source_target_pairs={{0,8},{1,3},{2,10},{3,5},{4,12},{5,7},{6,14},{7,1},{8,16},{9,11},{... | collective-permute-start | bytes 589832 | tf_op jit(solution)/shard_map/ppermute | solution.py:167
  160.5 1.6 collective-permute-done.23
  162.1 3.0 %collective-permute-done.22 = f32[192,256]{1,0:T(8,128)S(1)} collective-permute-done((f32[192,256]{1,0:T(8,128)S(1)}, f32[192,256]{1,0:T(8,128)S(1)}, u32[]{:S(2)}, u32[]{:S(2)}) %collective-permute-start.22) | collective-permute-done | bytes 196640 | tf_op jit(solution)/shard_map/ppermute | solution.py:167
  (54 shorter events, 19.5 us)
Async XLA Ops:
  0.8 2.8 %copy-start = (f32[1,2,12,256,256]{4,3,2,1,0:T(8,128)S(1)}, f32[1,2,12,256,256]{4,3,2,1,0:T(8,128)}, u32[]{:S(2)}) copy-start(f32[1,2,12,256,256]{4,3,2,1,0:T(8,128)} %param.9) | copy-start | bytes 18874372
  3.6 1.9 %copy-start.1 = (f32[1,12,256,256]{3,2,1,0:T(8,128)S(1)}, f32[1,12,256,256]{3,2,1,0:T(8,128)}, u32[]{:S(2)}) copy-start(f32[1,12,256,256]{3,2,1,0:T(8,128)} %param.7) | copy-start | bytes 9437188
  5.5 0.7 copy-start.3
  6.1 2.2 %copy-start.4 = (f32[1,1,4]{2,1,0:T(1,128)S(1)}, f32[1,1,4]{2,1,0:T(1,128)}, u32[]{:S(2)}) copy-start(f32[1,1,4]{2,1,0:T(1,128)} %param.11) | copy-start | bytes 52
  6.1 11.9 %slice-start.2 = ((s8[6291456]{0:T(1024)(128)(4,1)}), s8[4194304]{0:T(1024)(128)(4,1)S(1)}, s32[]{:S(2)}) async-start(s8[6291456]{0:T(1024)(128)(4,1)} %bitcast.66), calls=%async_computation.2 | async-start | bytes 8388608
  6.7 11.4 %slice-start.3 = ((s8[6291456]{0:T(1024)(128)(4,1)}), s8[2097152]{0:T(1024)(128)(4,1)S(1)}, s32[]{:S(2)}) async-start(s8[6291456]{0:T(1024)(128)(4,1)} %bitcast.66), calls=%async_computation.3 | async-start | bytes 4194304
  6.7 11.4 %copy-start.2 = (f32[1,1,12,256,256]{4,3,2,1,0:T(8,128)S(1)}, f32[1,1,12,256,256]{4,3,2,1,0:T(8,128)}, u32[]{:S(2)}) copy-start(f32[1,1,12,256,256]{4,3,2,1,0:T(8,128)} %param.8) | copy-start | bytes 9437188
  6.7 11.3 %collective-permute-start.1 = (f32[256,256]{1,0:T(8,128)S(1)}, f32[256,256]{1,0:T(8,128)S(1)}, u32[]{:S(2)}, u32[]{:S(2)}) collective-permute-start(f32[256,256]{1,0:T(8,128)S(1)} %sector0.1.refs_8_), channel_id=1, source_target_pairs={{0,32},{32,64},{64,96},{1,33},{33,65},{65,97},{2,34},{34,66},{66,9... | collective-permute-start | bytes 786440 | tf_op jit(solution)/shard_map/ppermute | solution.py:197
  8.8 14.8 %collective-permute-start = (f32[256,256]{1,0:T(8,128)S(1)}, f32[256,256]{1,0:T(8,128)S(1)}, u32[]{:S(2)}, u32[]{:S(2)}) collective-permute-start(f32[256,256]{1,0:T(8,128)S(1)} %sector1.1.refs_8_), channel_id=1, source_target_pairs={{0,32},{32,64},{64,96},{1,33},{33,65},{65,97},{2,34},{34,66},{66,9... | collective-permute-start | bytes 786440 | tf_op jit(solution)/shard_map/ppermute | solution.py:197
  18.0 5.6 %slice-start = ((s8[6291456]{0:T(1024)(128)(4,1)}), s8[4194304]{0:T(1024)(128)(4,1)S(1)}, s32[]{:S(2)}) async-start(s8[6291456]{0:T(1024)(128)(4,1)} %bitcast.49), calls=%async_computation | async-start | bytes 8388608
  18.1 5.6 %slice-start.1 = ((s8[6291456]{0:T(1024)(128)(4,1)}), s8[2097152]{0:T(1024)(128)(4,1)S(1)}, s32[]{:S(2)}) async-start(s8[6291456]{0:T(1024)(128)(4,1)} %bitcast.49), calls=%async_computation.1 | async-start | bytes 4194304
  18.6 11.1 %collective-permute-start.3 = (f32[256,256]{1,0:T(8,128)S(1)}, f32[256,256]{1,0:T(8,128)S(1)}, u32[]{:S(2)}, u32[]{:S(2)}) collective-permute-start(f32[256,256]{1,0:T(8,128)S(1)} %get-tuple-element.54), channel_id=1, source_target_pairs={{0,32},{32,64},{64,96},{1,33},{33,65},{65,97},{2,34},{34,66},{66,9... | collective-permute-start | bytes 786440 | tf_op jit(solution)/shard_map/ppermute | solution.py:197
  24.2 10.3 %collective-permute-start.2 = (f32[256,256]{1,0:T(8,128)S(1)}, f32[256,256]{1,0:T(8,128)S(1)}, u32[]{:S(2)}, u32[]{:S(2)}) collective-permute-start(f32[256,256]{1,0:T(8,128)S(1)} %get-tuple-element.53), channel_id=1, source_target_pairs={{0,32},{32,64},{64,96},{1,33},{33,65},{65,97},{2,34},{34,66},{66,9... | collective-permute-start | bytes 786440 | tf_op jit(solution)/shard_map/ppermute | solution.py:197
  30.3 9.9 %collective-permute-start.5 = (f32[256,256]{1,0:T(8,128)S(1)}, f32[256,256]{1,0:T(8,128)S(1)}, u32[]{:S(2)}, u32[]{:S(2)}) collective-permute-start(f32[256,256]{1,0:T(8,128)S(1)} %get-tuple-element.60), channel_id=1, source_target_pairs={{0,32},{32,64},{64,96},{1,33},{33,65},{65,97},{2,34},{34,66},{66,9... | collective-permute-start | bytes 786440 | tf_op jit(solution)/shard_map/ppermute | solution.py:197
  35.1 10.9 %collective-permute-start.4 = (f32[256,256]{1,0:T(8,128)S(1)}, f32[256,256]{1,0:T(8,128)S(1)}, u32[]{:S(2)}, u32[]{:S(2)}) collective-permute-start(f32[256,256]{1,0:T(8,128)S(1)} %get-tuple-element.59), channel_id=1, source_target_pairs={{0,32},{32,64},{64,96},{1,33},{33,65},{65,97},{2,34},{34,66},{66,9... | collective-permute-start | bytes 786440 | tf_op jit(solution)/shard_map/ppermute | solution.py:197
  44.0 9.5 %collective-permute-start.7 = (f32[256,256]{1,0:T(8,128)S(1)}, f32[256,256]{1,0:T(8,128)S(1)}, u32[]{:S(2)}, u32[]{:S(2)}) collective-permute-start(f32[256,256]{1,0:T(8,128)S(1)} %get-tuple-element.66), channel_id=1, source_target_pairs={{0,32},{32,64},{64,96},{1,33},{33,65},{65,97},{2,34},{34,66},{66,9... | collective-permute-start | bytes 786440 | tf_op jit(solution)/shard_map/ppermute | solution.py:197
  50.0 9.7 %collective-permute-start.6 = (f32[256,256]{1,0:T(8,128)S(1)}, f32[256,256]{1,0:T(8,128)S(1)}, u32[]{:S(2)}, u32[]{:S(2)}) collective-permute-start(f32[256,256]{1,0:T(8,128)S(1)} %get-tuple-element.65), channel_id=1, source_target_pairs={{0,32},{32,64},{64,96},{1,33},{33,65},{65,97},{2,34},{34,66},{66,9... | collective-permute-start | bytes 786440 | tf_op jit(solution)/shard_map/ppermute | solution.py:197
  57.5 10.6 %collective-permute-start.9 = (f32[256,256]{1,0:T(8,128)S(1)}, f32[256,256]{1,0:T(8,128)S(1)}, u32[]{:S(2)}, u32[]{:S(2)}) collective-permute-start(f32[256,256]{1,0:T(8,128)S(1)} %get-tuple-element.72), channel_id=1, source_target_pairs={{0,32},{32,64},{64,96},{1,33},{33,65},{65,97},{2,34},{34,66},{66,9... | collective-permute-start | bytes 786440 | tf_op jit(solution)/shard_map/ppermute | solution.py:197
  63.6 11.2 %collective-permute-start.8 = (f32[256,256]{1,0:T(8,128)S(1)}, f32[256,256]{1,0:T(8,128)S(1)}, u32[]{:S(2)}, u32[]{:S(2)}) collective-permute-start(f32[256,256]{1,0:T(8,128)S(1)} %get-tuple-element.71), channel_id=1, source_target_pairs={{0,32},{32,64},{64,96},{1,33},{33,65},{65,97},{2,34},{34,66},{66,9... | collective-permute-start | bytes 786440 | tf_op jit(solution)/shard_map/ppermute | solution.py:197
  72.0 11.1 %collective-permute-start.11 = (f32[256,256]{1,0:T(8,128)S(1)}, f32[256,256]{1,0:T(8,128)S(1)}, u32[]{:S(2)}, u32[]{:S(2)}) collective-permute-start(f32[256,256]{1,0:T(8,128)S(1)} %get-tuple-element.78), channel_id=1, source_target_pairs={{0,32},{32,64},{64,96},{1,33},{33,65},{65,97},{2,34},{34,66},{66,9... | collective-permute-start | bytes 786440 | tf_op jit(solution)/shard_map/ppermute | solution.py:197
  78.7 11.1 %collective-permute-start.10 = (f32[256,256]{1,0:T(8,128)S(1)}, f32[256,256]{1,0:T(8,128)S(1)}, u32[]{:S(2)}, u32[]{:S(2)}) collective-permute-start(f32[256,256]{1,0:T(8,128)S(1)} %get-tuple-element.77), channel_id=1, source_target_pairs={{0,32},{32,64},{64,96},{1,33},{33,65},{65,97},{2,34},{34,66},{66,9... | collective-permute-start | bytes 786440 | tf_op jit(solution)/shard_map/ppermute | solution.py:197
  86.9 10.2 %collective-permute-start.13 = (f32[256,256]{1,0:T(8,128)S(1)}, f32[256,256]{1,0:T(8,128)S(1)}, u32[]{:S(2)}, u32[]{:S(2)}) collective-permute-start(f32[256,256]{1,0:T(8,128)S(1)} %get-tuple-element.84), channel_id=1, source_target_pairs={{0,32},{32,64},{64,96},{1,33},{33,65},{65,97},{2,34},{34,66},{66,9... | collective-permute-start | bytes 786440 | tf_op jit(solution)/shard_map/ppermute | solution.py:197
  93.7 9.9 %collective-permute-start.12 = (f32[256,256]{1,0:T(8,128)S(1)}, f32[256,256]{1,0:T(8,128)S(1)}, u32[]{:S(2)}, u32[]{:S(2)}) collective-permute-start(f32[256,256]{1,0:T(8,128)S(1)} %get-tuple-element.83), channel_id=1, source_target_pairs={{0,32},{32,64},{64,96},{1,33},{33,65},{65,97},{2,34},{34,66},{66,9... | collective-permute-start | bytes 786440 | tf_op jit(solution)/shard_map/ppermute | solution.py:197
  101.2 8.8 %collective-permute-start.15 = (f32[256,256]{1,0:T(8,128)S(1)}, f32[256,256]{1,0:T(8,128)S(1)}, u32[]{:S(2)}, u32[]{:S(2)}) collective-permute-start(f32[256,256]{1,0:T(8,128)S(1)} %get-tuple-element.90), channel_id=1, source_target_pairs={{0,32},{32,64},{64,96},{1,33},{33,65},{65,97},{2,34},{34,66},{66,9... | collective-permute-start | bytes 786440 | tf_op jit(solution)/shard_map/ppermute | solution.py:197
  107.4 8.3 %collective-permute-start.14 = (f32[256,256]{1,0:T(8,128)S(1)}, f32[256,256]{1,0:T(8,128)S(1)}, u32[]{:S(2)}, u32[]{:S(2)}) collective-permute-start(f32[256,256]{1,0:T(8,128)S(1)} %get-tuple-element.89), channel_id=1, source_target_pairs={{0,32},{32,64},{64,96},{1,33},{33,65},{65,97},{2,34},{34,66},{66,9... | collective-permute-start | bytes 786440 | tf_op jit(solution)/shard_map/ppermute | solution.py:197
  119.5 5.7 %collective-permute-start.16 = (f32[4,4,2,3,32,256]{5,4,3,2,1,0:T(8,128)S(1)}, f32[4,4,2,3,32,256]{5,4,3,2,1,0:T(8,128)S(1)}, u32[]{:S(2)}, u32[]{:S(2)}) collective-permute-start(f32[4,4,2,3,32,256]{5,4,3,2,1,0:T(8,128)S(1)} %get-tuple-element.96), channel_id=1, source_target_pairs={{0,1},{1,0},{2,3},{3,2},{4,5},{5,4},{6,7},{7,6},{8,9},{9,8},{10,11... | collective-permute-start | bytes 9437192 | tf_op jit(solution)/shard_map/ppermute | solution.py:156
  126.1 9.1 %collective-permute-start.17 = (f32[2,192,256]{2,1,0:T(8,128)S(1)}, f32[2,192,256]{2,1,0:T(8,128)S(1)}, u32[]{:S(2)}, u32[]{:S(2)}) collective-permute-start(f32[2,192,256]{2,1,0:T(8,128)S(1)} %get-tuple-element.99), channel_id=1, source_target_pairs={{0,2},{1,9},{2,4},{3,11},{4,6},{5,13},{6,0},{7,15},{8,10},{9,17},{... | collective-permute-start | bytes 1179656 | tf_op jit(solution)/shard_map/ppermute | solution.py:167
  127.7 7.8 %collective-permute-start.19 = (f32[2,192,256]{2,1,0:T(8,128)S(1)}, f32[2,192,256]{2,1,0:T(8,128)S(1)}, u32[]{:S(2)}, u32[]{:S(2)}) collective-permute-start(f32[2,192,256]{2,1,0:T(8,128)S(1)} %get-tuple-element.100), channel_id=1, source_target_pairs={{0,6},{1,25},{2,0},{3,27},{4,2},{5,29},{6,4},{7,31},{8,14},{9,1},{... | collective-permute-start | bytes 1179656 | tf_op jit(solution)/shard_map/ppermute | solution.py:167
  135.7 12.5 %collective-permute-start.20 = (f32[4,192,256]{2,1,0:T(8,128)S(1)}, f32[4,192,256]{2,1,0:T(8,128)S(1)}, u32[]{:S(2)}, u32[]{:S(2)}) collective-permute-start(f32[4,192,256]{2,1,0:T(8,128)S(1)} %pad_maximum_fusion.1), channel_id=1, source_target_pairs={{0,6},{1,25},{2,0},{3,27},{4,2},{5,29},{6,4},{7,31},{8,14},{9,1},{... | collective-permute-start | bytes 2359304 | tf_op jit(solution)/shard_map/ppermute | solution.py:167
  138.8 13.3 %collective-permute-start.18 = (f32[4,192,256]{2,1,0:T(8,128)S(1)}, f32[4,192,256]{2,1,0:T(8,128)S(1)}, u32[]{:S(2)}, u32[]{:S(2)}) collective-permute-start(f32[4,192,256]{2,1,0:T(8,128)S(1)} %pad_maximum_fusion), channel_id=1, source_target_pairs={{0,2},{1,9},{2,4},{3,11},{4,6},{5,13},{6,0},{7,15},{8,10},{9,17},{... | collective-permute-start | bytes 2359304 | tf_op jit(solution)/shard_map/ppermute | solution.py:167
  152.2 9.9 %collective-permute-start.23 = (f32[192,256]{1,0:T(8,128)S(1)}, f32[192,256]{1,0:T(8,128)S(1)}, u32[]{:S(2)}, u32[]{:S(2)}) collective-permute-start(f32[192,256]{1,0:T(8,128)S(1)} %get-tuple-element.103), channel_id=1, source_target_pairs={{0,16},{1,5},{2,18},{3,7},{4,20},{5,1},{6,22},{7,3},{8,24},{9,13},... | collective-permute-start | bytes 589832 | tf_op jit(solution)/shard_map/ppermute | solution.py:167
  158.5 6.6 %collective-permute-start.22 = (f32[192,256]{1,0:T(8,128)S(1)}, f32[192,256]{1,0:T(8,128)S(1)}, u32[]{:S(2)}, u32[]{:S(2)}) collective-permute-start(f32[192,256]{1,0:T(8,128)S(1)} %get-tuple-element.104), channel_id=1, source_target_pairs={{0,24},{1,7},{2,26},{3,1},{4,28},{5,3},{6,30},{7,5},{8,0},{9,15},{... | collective-permute-start | bytes 589832 | tf_op jit(solution)/shard_map/ppermute | solution.py:167
  158.5 6.9 %collective-permute-start.21 = (f32[192,256]{1,0:T(8,128)S(1)}, f32[192,256]{1,0:T(8,128)S(1)}, u32[]{:S(2)}, u32[]{:S(2)}) collective-permute-start(f32[192,256]{1,0:T(8,128)S(1)} %get-tuple-element.105), channel_id=1, source_target_pairs={{0,8},{1,3},{2,10},{3,5},{4,12},{5,7},{6,14},{7,1},{8,16},{9,11},{... | collective-permute-start | bytes 589832 | tf_op jit(solution)/shard_map/ppermute | solution.py:167
  165.5 1.4 collective-permute-start.24

commit v4 on v3

v4 whole, which is shorter than its diff:
```python
import jax
import jax.numpy as jnp
from jax import lax
from jax.experimental import pallas as pl
from jax.experimental.pallas import tpu as pltpu
from jax.sharding import Mesh, PartitionSpec as P

f32, bf16 = jnp.float32, jnp.bfloat16
W = 256
NQ = 12
ROWS = 32
SITES = 4
LAG = 2


def halves(x):
    high = x.astype(bf16)
    return high, (x - high.astype(f32)).astype(bf16)


def product(a, b, dims):
    (ah, al), (bh, bl) = a, b

    def dot(u, v):
        return lax.dot_general(u, v, (dims, ((), ())), preferred_element_type=f32)

    return dot(ah, bh) + (dot(ah, bl) + dot(al, bh))


def framed(x, rows, columns):
    i = lax.broadcasted_iota(jnp.int32, x.shape, 0)
    j = lax.broadcasted_iota(jnp.int32, x.shape, 1)
    return jnp.where((i < rows) & (j < columns), x, 0.0)


LAST = NQ + LAG * (SITES - 1)
SCALAR = pl.BlockSpec(memory_space=pltpu.SMEM)
LOCAL = pl.BlockSpec(memory_space=pltpu.VMEM)
FAR = pl.BlockSpec(memory_space=pltpu.HBM)
GRANT = pltpu.CompilerParams(vmem_limit_bytes=8 * 2**20)
BUFFER = jax.ShapeDtypeStruct((2, 2, 4, 4, 3, ROWS, W), f32)


def update_part(q, ints, floats, arrived, previous, left, mps):
    site = ints[0]
    below = jnp.maximum(q - 1, 0)
    size, under = ints[4 + q], ints[4 + below]
    c0 = jnp.where(site == 0, ints[16 + q].astype(f32), 1.0) * floats[0]
    c1 = jnp.where(site == 0, ints[16 + below].astype(f32), 1.0) * floats[1]
    now = jnp.where(site == 0, left[q], arrived[...])
    before = jnp.where(site == 0, left[below], previous[...])
    before = jnp.where(q > 0, before, 0.0)
    s = framed(mps[0, q], size, size)
    u = framed(mps[1, below], under, size)
    first = c0 * product(halves(now), halves(s), ((1,), (0,)))
    second = c1 * product(halves(before), halves(u), ((1,), (0,)))
    return product(halves(s.T), halves(first), ((1,), (0,))) + product(
        halves(u.T), halves(second), ((1,), (0,)))


def apply_part(q, e, ints, floats, psi, rights, pieces, results, stores):
    my_z, my_x, core = ints[1], ints[2], ints[3]
    above = jnp.minimum(q + 1, NQ - 1)
    e = halves(e)
    present = ints[16 + q].astype(f32)
    present_above = jnp.where(q < NQ - 1, ints[16 + above], 0).astype(f32)

    def one_state(state, _):
        other = jnp.where(state == 0, q, above)
        c = jnp.where(state == 0, floats[2] * present, floats[3] * present_above)
        n = ints[4 + other]
        part = c * product(e, halves(psi[state, q]), ((1,), (0,)))
        results[state] = product(halves(part), halves(framed(rights[other], n, n)), ((1,), (1,)))
        for i in range(W // ROWS):
            piece = (W // ROWS) * q + i
            owner, third = piece // 3, piece % 3
            z = (owner // 8 - my_z + 4) % 4
            x = ((owner // 2) % 4 - my_x + 4) % 4
            sent = (owner + core) % 2
            near, far = jnp.where(state == 0, x, z), jnp.where(state == 0, z, x)
            pltpu.make_async_copy(
                results.at[state, pl.ds(ROWS * i, ROWS)], pieces.at[sent, state, near, far, third], stores).start()
        return 0

    lax.fori_loop(0, 2, one_state, 0)
    pltpu.make_async_copy(results, psi.at[:, 0], stores).wait()


def update_step(step, ints, floats, arrived, previous, left, mps, held):
    def kernel(ints, floats, arrived, previous, left, mps, *rest):
        environ = rest[-1]
        q = step - LAG * ints[0]

        @pl.when((q >= 0) & (q < NQ))
        def _():
            environ[...] = update_part(q, ints, floats, arrived, previous, left, mps)

    return pl.pallas_call(
        kernel, in_specs=[SCALAR] * 2 + [LOCAL] * 4 + [FAR] * len(held), out_specs=LOCAL, out_shape=jax.ShapeDtypeStruct((W, W), f32),
        compiler_params=GRANT, name=f"update{step}",
    )(ints, floats, arrived, previous, left, mps, *held)


def apply_step(step, ints, floats, environ, psi, rights, saved, held):
    late = NQ <= step < NQ + LAG
    operands = (environ, psi, rights) + ((saved,) if late else ())

    def kernel(*refs):
        ints, floats, environ, psi, rights = refs[:5]
        q = step - LAG * ints[0]
        active = (q >= 0) & (q < NQ)
        first = ints[0] == 0
        if late:
            active = active | first
            q = jnp.where(first, step - NQ, q)

        @pl.when(active)
        def _():
            e = environ[...]
            if late:
                e = jnp.where(first, refs[5][...], e)
            apply_part(q, e, ints, floats, psi, rights, *refs[-3:])

    return pl.pallas_call(
        kernel,
        in_specs=[SCALAR] * 2 + [LOCAL] * len(operands) + [FAR] * len(held),
        out_specs=[FAR],
        out_shape=[BUFFER],
        scratch_shapes=[pltpu.VMEM((2, W, W), f32), pltpu.SemaphoreType.DMA],
        input_output_aliases={2 + len(operands): 0} if held else {},
        compiler_params=GRANT,
        name=f"apply{step}",
    )(ints, floats, *operands, *held)


def turned(x, axis, by):
    return lax.ppermute(x, axis, [(i, (i + by) % 4) for i in range(4)])


def first_phase(both, axis):
    up = turned(both[2, :2], axis, 1)
    down = turned(both[2, 2:], axis, -1)
    ahead = jnp.concatenate([both[1, :2] + up, both[1, 2:]])
    behind = jnp.concatenate([both[3, :2], both[3, 2:] + down])
    return both[0] + turned(ahead, axis, 1) + turned(behind, axis, -1)


def second_phase(line, axis):
    return (line[0] + turned(line[1], axis, 1)) + (turned(line[3], axis, -1) + turned(line[2], axis, 2))


def reduced(pieces):
    both = pieces[0] + lax.ppermute(pieces[1], "core", [(0, 1), (1, 0)])
    both = both.reshape(2, 4, 4, 96, W)
    first = first_phase(both[0], "x")
    second = first_phase(both[1], "z")
    return jnp.stack([second_phase(first, "z"), second_phase(second, "x")])[None]


TERM = ("z", "x", "core")


def shards(left_env, right_env, mps, psi, coef, sector_sizes, pattern):
    place = jnp.stack([lax.axis_index(a) for a in ("site",) + TERM]).astype(jnp.int32)
    ints = jnp.concatenate([place, sector_sizes, pattern[0]])
    floats = coef[0, 0]
    nothing = jnp.zeros((W, W), f32)
    arrivals, environs, held = {}, {}, ()
    for step in range(LAST):
        environ = update_step(
            step, ints, floats, arrivals.get(step, nothing), arrivals.get(step - 1, nothing), left_env[0], mps[0], held)
        environs[step] = environ
        if step + LAG < LAST:
            arrivals[step + LAG] = lax.ppermute(environ, "site", [(0, 1), (1, 2), (2, 3)])
        if step >= LAG:
            held = apply_step(step, ints, floats, environ, psi[0], right_env[0, 0], environs.get(step - NQ), held)
    return reduced(*held)


def solution(mesh):
    fine = Mesh(mesh.devices.reshape(4, 4, 4, 2), ("site", "z", "x", "core"))
    term = ("z", "x", "core")
    return jax.shard_map(
        shards,
        mesh=fine,
        in_specs=(
            P(term, None, None, None),
            P("site", term, None, None, None),
            P("site", None, None, None, None),
            P("site", None, None, None, None),
            P("site", term, None),
            P(),
            P(term, None),
        ),
        out_specs=P("site", None, term, None),
        check_vma=False,
    )
```

time: 168 us -> 163 us (0.970)
  waiting for transfers between devices: 72.5 us -> 50.2 us
  Pallas kernels: 50.2 us -> 59 us
  starting transfers between devices: 36.2 us -> 43.9 us
    ppermute x25 -> x31, waiting for transfers between devices: 72.5 us -> 50.2 us  [the longest x16 29.7 us: shards(): lax.ppermute(environ, 'site', [(0, 1), (1, 2), (2, 3)])]
    pallas_call x18 -> x34, Pallas kernels: 50.2 us -> 59 us  [the longest x16 38.3 us: apply_step(): pl.pallas_call(kernel, in_specs=[SCALAR] * 2 + [LOCAL] * len(operands) +...]
    ppermute x25 -> x31, starting transfers between devices: 36.2 us -> 43.9 us  [the longest x14 22.7 us: turned(): return lax.ppermute(x, axis, [(i, (i + by) % 4) for i in range(4)])]
    unnamed x18 -> x16, local copies, waits for them, and re-layouts: 5.35 us -> 5.36 us
  transfers between devices with their start and end apart: 25 -> 31, of which waited for: 25 -> 20; matrix products, arithmetic and copies ran while one was open for 0% -> 0% of each run, Pallas kernels for 27% -> 33%
where the time goes in v4:
time: 163 us
  Pallas kernels  59 us (36%)
  waiting for transfers between devices  50.2 us (31%)
  starting transfers between devices  43.9 us (27%)
  local copies, waits for them, and re-layouts  7.09 us (4%)
  other arithmetic  2.08 us (1%)
    pallas_call x16, Pallas kernels, apply_step(): pl.pallas_call(kernel, in_specs=[SCALAR] * 2 + [LOCAL] * len(operands) +...  38.3 us
    ppermute x16, waiting for transfers between devices, shards(): lax.ppermute(environ, 'site', [(0, 1), (1, 2), (2, 3)])  29.7 us
    ppermute x14, starting transfers between devices, turned(): return lax.ppermute(x, axis, [(i, (i + by) % 4) for i in range(4)])  22.7 us
    ppermute x16, starting transfers between devices, shards(): lax.ppermute(environ, 'site', [(0, 1), (1, 2), (2, 3)])  21.1 us
    pallas_call x18, Pallas kernels, update_step(): pl.pallas_call(kernel, in_specs=[SCALAR] * 2 + [LOCAL] * 4 + [FAR] * len(...  20.7 us
    ppermute x14, waiting for transfers between devices, turned(): return lax.ppermute(x, axis, [(i, (i + by) % 4) for i in range(4)])  14.9 us
    ppermute x1, waiting for transfers between devices, reduced(): both = pieces[0] + lax.ppermute(pieces[1], 'core', [(0, 1), (1, 0)])  5.65 us
    unnamed x16, local copies, waits for them, and re-layouts  5.36 us
  transfers between devices with their start and end apart: 31, of which 20 were waited for; matrix products, arithmetic and copies ran while one was open for 0% of the time, Pallas kernels for 33%

profile of v4, /device:TPU:24, one launch (start us, length us, event | category | flops | bytes accessed | tf_op | source)
XLA Modules:
  0.0 162.9 jit_solution(331686794862867149)
XLA Ops:
  0.8 2.8 %copy-done = f32[1,2,12,256,256]{4,3,2,1,0:T(8,128)S(1)} copy-done((f32[1,2,12,256,256]{4,3,2,1,0:T(8,128)S(1)}, f32[1,2,12,256,256]{4,3,2,1,0:T(8,128)}, u32[]{:S(2)}) %copy-start) | copy-done | bytes 6291480
  3.6 1.9 %copy-done.1 = f32[1,12,256,256]{3,2,1,0:T(8,128)S(1)} copy-done((f32[1,12,256,256]{3,2,1,0:T(8,128)S(1)}, f32[1,12,256,256]{3,2,1,0:T(8,128)}, u32[]{:S(2)}) %copy-start.1) | copy-done | bytes 3145752
  8.6 1.6 collective-permute-start
  10.1 7.6 %collective-permute-done.1.arrived.previous = f32[256,256]{1,0:T(8,128)S(1)} collective-permute-done((f32[256,256]{1,0:T(8,128)S(1)}, f32[256,256]{1,0:T(8,128)S(1)}, u32[]{:S(2)}, u32[]{:S(2)}) %collective-permute-start.1) | collective-permute-done | bytes 262176 | tf_op jit(solution)/shard_map/ppermute | solution.py:174
  18.3 1.4 collective-permute-start.3
  20.4 3.0 %collective-permute-done.arrived.previous = f32[256,256]{1,0:T(8,128)S(1)} collective-permute-done((f32[256,256]{1,0:T(8,128)S(1)}, f32[256,256]{1,0:T(8,128)S(1)}, u32[]{:S(2)}, u32[]{:S(2)}) %collective-permute-start) | collective-permute-done | bytes 262176 | tf_op jit(solution)/shard_map/ppermute | solution.py:174
  25.8 3.6 %collective-permute-done.3.arrived.previous = f32[256,256]{1,0:T(8,128)S(1)} collective-permute-done((f32[256,256]{1,0:T(8,128)S(1)}, f32[256,256]{1,0:T(8,128)S(1)}, u32[]{:S(2)}, u32[]{:S(2)}) %collective-permute-start.3) | collective-permute-done | bytes 262176 | tf_op jit(solution)/shard_map/ppermute | solution.py:174
  31.9 3.2 %collective-permute-done.2.arrived.previous = f32[256,256]{1,0:T(8,128)S(1)} collective-permute-done((f32[256,256]{1,0:T(8,128)S(1)}, f32[256,256]{1,0:T(8,128)S(1)}, u32[]{:S(2)}, u32[]{:S(2)}) %collective-permute-start.2) | collective-permute-done | bytes 262176 | tf_op jit(solution)/shard_map/ppermute | solution.py:174
  37.5 3.0 %collective-permute-done.5.arrived.previous = f32[256,256]{1,0:T(8,128)S(1)} collective-permute-done((f32[256,256]{1,0:T(8,128)S(1)}, f32[256,256]{1,0:T(8,128)S(1)}, u32[]{:S(2)}, u32[]{:S(2)}) %collective-permute-start.5) | collective-permute-done | bytes 262176 | tf_op jit(solution)/shard_map/ppermute | solution.py:174
  40.4 1.4 update6.1.refs_2_
  43.2 3.0 %apply6.1.rest_0_.refs_5_ = f32[2,2,4,4,3,32,256]{6,5,4,3,2,1,0:T(8,128)S(1)} custom-call(s32[28]{0:T(128)S(1)} %concatenate.15.ints.refs_0_, f32[4]{0:T(128)S(1)} %bitcast.169, f32[256,256]{1,0:T(8,128)S(1)} %update6.1.refs_2_, f32[2,12,256,256]{3,2,1,0:T(8,128)S(1)} %bitcast.112, f32[12,256,256]{2,1,0:T(8,128)S(1)} %bitcast.146, ...), custom_call_target="tpu_custom_call", output_to_operand_aliasing={{}: (5, {})} | custom-call | tf_op jit(solution)/shard_map/apply6/pallas_call | solution.py:124
  46.2 1.4 update7.1.refs_2_
  48.9 3.0 %apply7.1.rest_0_.refs_5_ = f32[2,2,4,4,3,32,256]{6,5,4,3,2,1,0:T(8,128)S(1)} custom-call(s32[28]{0:T(128)S(1)} %concatenate.15.ints.refs_0_, f32[4]{0:T(128)S(1)} %bitcast.171, f32[256,256]{1,0:T(8,128)S(1)} %update7.1.refs_2_, f32[2,12,256,256]{3,2,1,0:T(8,128)S(1)} %bitcast.113, f32[12,256,256]{2,1,0:T(8,128)S(1)} %bitcast.147, ...), custom_call_target="tpu_custom_call", output_to_operand_aliasing={{}: (5, {})} | custom-call | tf_op jit(solution)/shard_map/apply7/pallas_call | solution.py:124
  51.9 1.5 update8.1.refs_2_
  54.7 3.1 %apply8.1.rest_0_.refs_5_ = f32[2,2,4,4,3,32,256]{6,5,4,3,2,1,0:T(8,128)S(1)} custom-call(s32[28]{0:T(128)S(1)} %concatenate.15.ints.refs_0_, f32[4]{0:T(128)S(1)} %bitcast.173, f32[256,256]{1,0:T(8,128)S(1)} %update8.1.refs_2_, f32[2,12,256,256]{3,2,1,0:T(8,128)S(1)} %bitcast.114, f32[12,256,256]{2,1,0:T(8,128)S(1)} %bitcast.148, ...), custom_call_target="tpu_custom_call", output_to_operand_aliasing={{}: (5, {})} | custom-call | tf_op jit(solution)/shard_map/apply8/pallas_call | solution.py:124
  57.9 1.4 update9.1.refs_2_
  60.6 3.0 %apply9.1.rest_0_.refs_5_ = f32[2,2,4,4,3,32,256]{6,5,4,3,2,1,0:T(8,128)S(1)} custom-call(s32[28]{0:T(128)S(1)} %concatenate.15.ints.refs_0_, f32[4]{0:T(128)S(1)} %bitcast.175, f32[256,256]{1,0:T(8,128)S(1)} %update9.1.refs_2_, f32[2,12,256,256]{3,2,1,0:T(8,128)S(1)} %bitcast.115, f32[12,256,256]{2,1,0:T(8,128)S(1)} %bitcast.149, ...), custom_call_target="tpu_custom_call", output_to_operand_aliasing={{}: (5, {})} | custom-call | tf_op jit(solution)/shard_map/apply9/pallas_call | solution.py:124
  64.1 1.5 update10.1.refs_2_
  66.8 3.0 %apply10.1.rest_0_.refs_5_ = f32[2,2,4,4,3,32,256]{6,5,4,3,2,1,0:T(8,128)S(1)} custom-call(s32[28]{0:T(128)S(1)} %concatenate.15.ints.refs_0_, f32[4]{0:T(128)S(1)} %bitcast.177, f32[256,256]{1,0:T(8,128)S(1)} %update10.1.refs_2_, f32[2,12,256,256]{3,2,1,0:T(8,128)S(1)} %bitcast.116, f32[12,256,256]{2,1,0:T(8,128)S(1)} %bitcast.150, ...), custom_call_target="tpu_custom_call", output_to_operand_aliasing={{}: (5, {})} | custom-call | tf_op jit(solution)/shard_map/apply10/pallas_call | solution.py:124
  70.8 1.4 update11.1.refs_2_
  73.6 3.0 %apply11.1.rest_0_.refs_6_ = f32[2,2,4,4,3,32,256]{6,5,4,3,2,1,0:T(8,128)S(1)} custom-call(s32[28]{0:T(128)S(1)} %concatenate.15.ints.refs_0_, f32[4]{0:T(128)S(1)} %bitcast.179, f32[256,256]{1,0:T(8,128)S(1)} %update11.1.refs_2_, f32[2,12,256,256]{3,2,1,0:T(8,128)S(1)} %bitcast.117, f32[12,256,256]{2,1,0:T(8,128)S(1)} %bitcast.151, ...), custom_call_target="tpu_custom_call", output_to_operand_aliasing={{}: (5, {})} | custom-call | tf_op jit(solution)/shard_map/apply11/pallas_call | solution.py:124
  77.2 1.5 update12.1.refs_2_
  79.9 3.0 %apply12.1.rest_0_.refs_6_ = f32[2,2,4,4,3,32,256]{6,5,4,3,2,1,0:T(8,128)S(1)} custom-call(s32[28]{0:T(128)S(1)} %concatenate.15.ints.refs_0_, f32[4]{0:T(128)S(1)} %bitcast.181, f32[256,256]{1,0:T(8,128)S(1)} %update12.1.refs_2_, f32[2,12,256,256]{3,2,1,0:T(8,128)S(1)} %bitcast.118, f32[12,256,256]{2,1,0:T(8,128)S(1)} %bitcast.152, ...), custom_call_target="tpu_custom_call", output_to_operand_aliasing={{}: (6, {})} | custom-call | tf_op jit(solution)/shard_map/apply12/pallas_call | solution.py:124
  83.6 1.5 update13.1.refs_2_
  86.3 3.0 %apply13.1.rest_0_.refs_5_ = f32[2,2,4,4,3,32,256]{6,5,4,3,2,1,0:T(8,128)S(1)} custom-call(s32[28]{0:T(128)S(1)} %concatenate.15.ints.refs_0_, f32[4]{0:T(128)S(1)} %bitcast.183, f32[256,256]{1,0:T(8,128)S(1)} %update13.1.refs_2_, f32[2,12,256,256]{3,2,1,0:T(8,128)S(1)} %bitcast.119, f32[12,256,256]{2,1,0:T(8,128)S(1)} %bitcast.153, ...), custom_call_target="tpu_custom_call", output_to_operand_aliasing={{}: (6, {})} | custom-call | tf_op jit(solution)/shard_map/apply13/pallas_call | solution.py:124
  89.9 1.4 update14.1.refs_2_
  91.4 3.0 %apply14.1.rest_0_.refs_5_ = f32[2,2,4,4,3,32,256]{6,5,4,3,2,1,0:T(8,128)S(1)} custom-call(s32[28]{0:T(128)S(1)} %concatenate.15.ints.refs_0_, f32[4]{0:T(128)S(1)} %bitcast.185, f32[256,256]{1,0:T(8,128)S(1)} %update14.1.refs_2_, f32[2,12,256,256]{3,2,1,0:T(8,128)S(1)} %bitcast.120, f32[12,256,256]{2,1,0:T(8,128)S(1)} %bitcast.154, ...), custom_call_target="tpu_custom_call", output_to_operand_aliasing={{}: (5, {})} | custom-call | tf_op jit(solution)/shard_map/apply14/pallas_call | solution.py:124
  95.8 1.4 update15.1.refs_2_
  98.6 3.0 %apply15.1.rest_0_.refs_5_ = f32[2,2,4,4,3,32,256]{6,5,4,3,2,1,0:T(8,128)S(1)} custom-call(s32[28]{0:T(128)S(1)} %concatenate.15.ints.refs_0_, f32[4]{0:T(128)S(1)} %bitcast.187, f32[256,256]{1,0:T(8,128)S(1)} %update15.1.refs_2_, f32[2,12,256,256]{3,2,1,0:T(8,128)S(1)} %bitcast.121, f32[12,256,256]{2,1,0:T(8,128)S(1)} %bitcast.155, ...), custom_call_target="tpu_custom_call", output_to_operand_aliasing={{}: (5, {})} | custom-call | tf_op jit(solution)/shard_map/apply15/pallas_call | solution.py:124
  101.5 5.8 %collective-permute-done.15.arrived.previous = f32[256,256]{1,0:T(8,128)S(1)} collective-permute-done((f32[256,256]{1,0:T(8,128)S(1)}, f32[256,256]{1,0:T(8,128)S(1)}, u32[]{:S(2)}, u32[]{:S(2)}) %collective-permute-start.15) | collective-permute-done | bytes 262176 | tf_op jit(solution)/shard_map/ppermute | solution.py:174
  107.3 1.4 update16.1.refs_2_
  108.7 3.2 %apply16.1.rest_0_.refs_5_ = f32[2,2,4,4,3,32,256]{6,5,4,3,2,1,0:T(8,128)S(1)} custom-call(s32[28]{0:T(128)S(1)} %concatenate.15.ints.refs_0_, f32[4]{0:T(128)S(1)} %bitcast.189, f32[256,256]{1,0:T(8,128)S(1)} %update16.1.refs_2_, f32[2,12,256,256]{3,2,1,0:T(8,128)S(1)} %bitcast.122, f32[12,256,256]{2,1,0:T(8,128)S(1)} %bitcast.156, ...), custom_call_target="tpu_custom_call", output_to_operand_aliasing={{}: (5, {})} | custom-call | tf_op jit(solution)/shard_map/apply16/pallas_call | solution.py:124
  112.0 1.4 update17.1.refs_2_
  113.4 3.0 %apply17.1 = f32[2,2,4,4,3,32,256]{6,5,4,3,2,1,0:T(8,128)S(1)} custom-call(s32[28]{0:T(128)S(1)} %concatenate.15.ints.refs_0_, f32[4]{0:T(128)S(1)} %bitcast.191, f32[256,256]{1,0:T(8,128)S(1)} %update17.1.refs_2_, f32[2,12,256,256]{3,2,1,0:T(8,128)S(1)} %bitcast.123, f32[12,256,256]{2,1,0:T(8,128)S(1)} %bitcast.157, ...), custom_call_target="tpu_custom_call", output_to_operand_aliasing={{}: (5, {})} | custom-call | tf_op jit(solution)/shard_map/apply17/pallas_call | solution.py:124
  116.9 5.6 %collective-permute-done.16 = f32[2,4,4,3,32,256]{5,4,3,2,1,0:T(8,128)S(1)} collective-permute-done((f32[2,4,4,3,32,256]{5,4,3,2,1,0:T(8,128)S(1)}, f32[2,4,4,3,32,256]{5,4,3,2,1,0:T(8,128)S(1)}, u32[]{:S(2)}, u32[]{:S(2)}) %collective-permute-start.16) | collective-permute-done | bytes 3145760 | tf_op jit(solution)/shard_map/ppermute | solution.py:153
  123.9 2.0 %collective-permute-start.24 = (f32[2,96,256]{2,1,0:T(8,128)S(1)}, f32[2,96,256]{2,1,0:T(8,128)S(1)}, u32[]{:S(2)}, u32[]{:S(2)}) collective-permute-start(f32[2,96,256]{2,1,0:T(8,128)S(1)} %get-tuple-element.17), channel_id=1, source_target_pairs={{0,8},{8,16},{16,24},{24,0},{1,9},{9,17},{17,25},{25,1},{2,10},{10... | collective-permute-start | bytes 589832 | tf_op jit(solution)/shard_map/ppermute | solution.py:137
  125.9 2.2 %collective-permute-start.26 = (f32[2,96,256]{2,1,0:T(8,128)S(1)}, f32[2,96,256]{2,1,0:T(8,128)S(1)}, u32[]{:S(2)}, u32[]{:S(2)}) collective-permute-start(f32[2,96,256]{2,1,0:T(8,128)S(1)} %get-tuple-element.18), channel_id=1, source_target_pairs={{0,24},{8,0},{16,8},{24,16},{1,25},{9,1},{17,9},{25,17},{2,26},{10... | collective-permute-start | bytes 589832 | tf_op jit(solution)/shard_map/ppermute | solution.py:137
  128.2 1.5 collective-permute-start.17
  129.7 1.8 %collective-permute-start.19 = (f32[2,96,256]{2,1,0:T(8,128)S(1)}, f32[2,96,256]{2,1,0:T(8,128)S(1)}, u32[]{:S(2)}, u32[]{:S(2)}) collective-permute-start(f32[2,96,256]{2,1,0:T(8,128)S(1)} %get-tuple-element.12), channel_id=1, source_target_pairs={{0,6},{2,0},{4,2},{6,4},{1,7},{3,1},{5,3},{7,5},{8,14},{10,8},{12,... | collective-permute-start | bytes 589832 | tf_op jit(solution)/shard_map/ppermute | solution.py:137
  131.5 1.7 %collective-permute-done.24 = f32[2,96,256]{2,1,0:T(8,128)S(1)} collective-permute-done((f32[2,96,256]{2,1,0:T(8,128)S(1)}, f32[2,96,256]{2,1,0:T(8,128)S(1)}, u32[]{:S(2)}, u32[]{:S(2)}) %collective-permute-start.24) | collective-permute-done | bytes 196640 | tf_op jit(solution)/shard_map/ppermute | solution.py:137
  133.3 3.1 %collective-permute-start.27 = (f32[4,96,256]{2,1,0:T(8,128)S(1)}, f32[4,96,256]{2,1,0:T(8,128)S(1)}, u32[]{:S(2)}, u32[]{:S(2)}) collective-permute-start(f32[4,96,256]{2,1,0:T(8,128)S(1)} %pad_maximum_fusion.3), channel_id=1, source_target_pairs={{0,24},{8,0},{16,8},{24,16},{1,25},{9,1},{17,9},{25,17},{2,26},{10... | collective-permute-start | bytes 1179656 | tf_op jit(solution)/shard_map/ppermute | solution.py:137
  136.7 2.8 %collective-permute-start.20 = (f32[4,96,256]{2,1,0:T(8,128)S(1)}, f32[4,96,256]{2,1,0:T(8,128)S(1)}, u32[]{:S(2)}, u32[]{:S(2)}) collective-permute-start(f32[4,96,256]{2,1,0:T(8,128)S(1)} %pad_maximum_fusion.1), channel_id=1, source_target_pairs={{0,6},{2,0},{4,2},{6,4},{1,7},{3,1},{5,3},{7,5},{8,14},{10,8},{12,... | collective-permute-start | bytes 1179656 | tf_op jit(solution)/shard_map/ppermute | solution.py:137
  139.6 4.7 %collective-permute-done.27 = f32[4,96,256]{2,1,0:T(8,128)S(1)} collective-permute-done((f32[4,96,256]{2,1,0:T(8,128)S(1)}, f32[4,96,256]{2,1,0:T(8,128)S(1)}, u32[]{:S(2)}, u32[]{:S(2)}) %collective-permute-start.27) | collective-permute-done | bytes 393248 | tf_op jit(solution)/shard_map/ppermute | solution.py:137
  144.2 3.5 %collective-permute-done.25 = f32[4,96,256]{2,1,0:T(8,128)S(1)} collective-permute-done((f32[4,96,256]{2,1,0:T(8,128)S(1)}, f32[4,96,256]{2,1,0:T(8,128)S(1)}, u32[]{:S(2)}, u32[]{:S(2)}) %collective-permute-start.25) | collective-permute-done | bytes 393248 | tf_op jit(solution)/shard_map/ppermute | solution.py:137
  147.9 3.1 %collective-permute-start.30 = (f32[96,256]{1,0:T(8,128)S(1)}, f32[96,256]{1,0:T(8,128)S(1)}, u32[]{:S(2)}, u32[]{:S(2)}) collective-permute-start(f32[96,256]{1,0:T(8,128)S(1)} %get-tuple-element.24), channel_id=1, source_target_pairs={{0,4},{2,6},{4,0},{6,2},{1,5},{3,7},{5,1},{7,3},{8,12},{10,14},{12... | collective-permute-start | bytes 294920 | tf_op jit(solution)/shard_map/ppermute | solution.py:137
  153.1 1.9 %collective-permute-start.23 = (f32[96,256]{1,0:T(8,128)S(1)}, f32[96,256]{1,0:T(8,128)S(1)}, u32[]{:S(2)}, u32[]{:S(2)}) collective-permute-start(f32[96,256]{1,0:T(8,128)S(1)} %get-tuple-element.21), channel_id=1, source_target_pairs={{0,16},{8,24},{16,0},{24,8},{1,17},{9,25},{17,1},{25,9},{2,18},{10... | collective-permute-start | bytes 294920 | tf_op jit(solution)/shard_map/ppermute | solution.py:137
  155.0 1.4 collective-permute-start.22
  159.3 1.5 collective-permute-done.22
  (87 shorter events, 38.2 us)
Async XLA Ops:
  0.8 2.8 %copy-start = (f32[1,2,12,256,256]{4,3,2,1,0:T(8,128)S(1)}, f32[1,2,12,256,256]{4,3,2,1,0:T(8,128)}, u32[]{:S(2)}) copy-start(f32[1,2,12,256,256]{4,3,2,1,0:T(8,128)} %param.9) | copy-start | bytes 18874372
  3.6 1.9 %copy-start.1 = (f32[1,12,256,256]{3,2,1,0:T(8,128)S(1)}, f32[1,12,256,256]{3,2,1,0:T(8,128)}, u32[]{:S(2)}) copy-start(f32[1,12,256,256]{3,2,1,0:T(8,128)} %param.7) | copy-start | bytes 9437188
  5.5 0.7 copy-start.3
  6.7 11.1 %collective-permute-start.1 = (f32[256,256]{1,0:T(8,128)S(1)}, f32[256,256]{1,0:T(8,128)S(1)}, u32[]{:S(2)}, u32[]{:S(2)}) collective-permute-start(f32[256,256]{1,0:T(8,128)S(1)} %update0.1.refs_5_), channel_id=1, source_target_pairs={{0,32},{32,64},{64,96},{1,33},{33,65},{65,97},{2,34},{34,66},{66,9... | collective-permute-start | bytes 786440 | tf_op jit(solution)/shard_map/ppermute | solution.py:174
  8.0 11.8 %slice-start.2 = ((s8[6291456]{0:T(1024)(128)(4,1)}), s8[4194304]{0:T(1024)(128)(4,1)S(1)}, s32[]{:S(2)}) async-start(s8[6291456]{0:T(1024)(128)(4,1)} %bitcast.106), calls=%async_computation.2 | async-start | bytes 8388608
  8.5 11.2 %slice-start.3 = ((s8[6291456]{0:T(1024)(128)(4,1)}), s8[2097152]{0:T(1024)(128)(4,1)S(1)}, s32[]{:S(2)}) async-start(s8[6291456]{0:T(1024)(128)(4,1)} %bitcast.106), calls=%async_computation.3 | async-start | bytes 4194304
  8.6 11.2 %copy-start.2 = (f32[1,1,12,256,256]{4,3,2,1,0:T(8,128)S(1)}, f32[1,1,12,256,256]{4,3,2,1,0:T(8,128)}, u32[]{:S(2)}) copy-start(f32[1,1,12,256,256]{4,3,2,1,0:T(8,128)} %param.8) | copy-start | bytes 9437188
  8.6 14.8 %collective-permute-start = (f32[256,256]{1,0:T(8,128)S(1)}, f32[256,256]{1,0:T(8,128)S(1)}, u32[]{:S(2)}, u32[]{:S(2)}) collective-permute-start(f32[256,256]{1,0:T(8,128)S(1)} %update1.1.refs_5_), channel_id=1, source_target_pairs={{0,32},{32,64},{64,96},{1,33},{33,65},{65,97},{2,34},{34,66},{66,9... | collective-permute-start | bytes 786440 | tf_op jit(solution)/shard_map/ppermute | solution.py:174
  17.7 5.6 %slice-start = ((s8[6291456]{0:T(1024)(128)(4,1)}), s8[4194304]{0:T(1024)(128)(4,1)S(1)}, s32[]{:S(2)}) async-start(s8[6291456]{0:T(1024)(128)(4,1)} %bitcast.89), calls=%async_computation | async-start | bytes 8388608
  18.3 11.1 %collective-permute-start.3 = (f32[256,256]{1,0:T(8,128)S(1)}, f32[256,256]{1,0:T(8,128)S(1)}, u32[]{:S(2)}, u32[]{:S(2)}) collective-permute-start(f32[256,256]{1,0:T(8,128)S(1)} %update2.1.refs_2_), channel_id=1, source_target_pairs={{0,32},{32,64},{64,96},{1,33},{33,65},{65,97},{2,34},{34,66},{66,9... | collective-permute-start | bytes 786440 | tf_op jit(solution)/shard_map/ppermute | solution.py:174
  19.8 3.6 %slice-start.1 = ((s8[6291456]{0:T(1024)(128)(4,1)}), s8[2097152]{0:T(1024)(128)(4,1)S(1)}, s32[]{:S(2)}) async-start(s8[6291456]{0:T(1024)(128)(4,1)} %bitcast.89), calls=%async_computation.1 | async-start | bytes 4194304
  23.9 11.1 %collective-permute-start.2 = (f32[256,256]{1,0:T(8,128)S(1)}, f32[256,256]{1,0:T(8,128)S(1)}, u32[]{:S(2)}, u32[]{:S(2)}) collective-permute-start(f32[256,256]{1,0:T(8,128)S(1)} %update3.1.refs_2_), channel_id=1, source_target_pairs={{0,32},{32,64},{64,96},{1,33},{33,65},{65,97},{2,34},{34,66},{66,9... | collective-permute-start | bytes 786440 | tf_op jit(solution)/shard_map/ppermute | solution.py:174
  30.0 10.5 %collective-permute-start.5 = (f32[256,256]{1,0:T(8,128)S(1)}, f32[256,256]{1,0:T(8,128)S(1)}, u32[]{:S(2)}, u32[]{:S(2)}) collective-permute-start(f32[256,256]{1,0:T(8,128)S(1)} %update4.1.refs_2_), channel_id=1, source_target_pairs={{0,32},{32,64},{64,96},{1,33},{33,65},{65,97},{2,34},{34,66},{66,9... | collective-permute-start | bytes 786440 | tf_op jit(solution)/shard_map/ppermute | solution.py:174
  35.6 10.6 %collective-permute-start.4 = (f32[256,256]{1,0:T(8,128)S(1)}, f32[256,256]{1,0:T(8,128)S(1)}, u32[]{:S(2)}, u32[]{:S(2)}) collective-permute-start(f32[256,256]{1,0:T(8,128)S(1)} %update5.1.refs_2_), channel_id=1, source_target_pairs={{0,32},{32,64},{64,96},{1,33},{33,65},{65,97},{2,34},{34,66},{66,9... | collective-permute-start | bytes 786440 | tf_op jit(solution)/shard_map/ppermute | solution.py:174
  41.9 10.0 %collective-permute-start.7 = (f32[256,256]{1,0:T(8,128)S(1)}, f32[256,256]{1,0:T(8,128)S(1)}, u32[]{:S(2)}, u32[]{:S(2)}) collective-permute-start(f32[256,256]{1,0:T(8,128)S(1)} %update6.1.refs_2_), channel_id=1, source_target_pairs={{0,32},{32,64},{64,96},{1,33},{33,65},{65,97},{2,34},{34,66},{66,9... | collective-permute-start | bytes 786440 | tf_op jit(solution)/shard_map/ppermute | solution.py:174
  47.6 10.3 %collective-permute-start.6 = (f32[256,256]{1,0:T(8,128)S(1)}, f32[256,256]{1,0:T(8,128)S(1)}, u32[]{:S(2)}, u32[]{:S(2)}) collective-permute-start(f32[256,256]{1,0:T(8,128)S(1)} %update7.1.refs_2_), channel_id=1, source_target_pairs={{0,32},{32,64},{64,96},{1,33},{33,65},{65,97},{2,34},{34,66},{66,9... | collective-permute-start | bytes 786440 | tf_op jit(solution)/shard_map/ppermute | solution.py:174
  53.4 10.7 %collective-permute-start.9 = (f32[256,256]{1,0:T(8,128)S(1)}, f32[256,256]{1,0:T(8,128)S(1)}, u32[]{:S(2)}, u32[]{:S(2)}) collective-permute-start(f32[256,256]{1,0:T(8,128)S(1)} %update8.1.refs_2_), channel_id=1, source_target_pairs={{0,32},{32,64},{64,96},{1,33},{33,65},{65,97},{2,34},{34,66},{66,9... | collective-permute-start | bytes 786440 | tf_op jit(solution)/shard_map/ppermute | solution.py:174
  59.3 11.5 %collective-permute-start.8 = (f32[256,256]{1,0:T(8,128)S(1)}, f32[256,256]{1,0:T(8,128)S(1)}, u32[]{:S(2)}, u32[]{:S(2)}) collective-permute-start(f32[256,256]{1,0:T(8,128)S(1)} %update9.1.refs_2_), channel_id=1, source_target_pairs={{0,32},{32,64},{64,96},{1,33},{33,65},{65,97},{2,34},{34,66},{66,9... | collective-permute-start | bytes 786440 | tf_op jit(solution)/shard_map/ppermute | solution.py:174
  65.5 11.6 %collective-permute-start.11 = (f32[256,256]{1,0:T(8,128)S(1)}, f32[256,256]{1,0:T(8,128)S(1)}, u32[]{:S(2)}, u32[]{:S(2)}) collective-permute-start(f32[256,256]{1,0:T(8,128)S(1)} %update10.1.refs_2_), channel_id=1, source_target_pairs={{0,32},{32,64},{64,96},{1,33},{33,65},{65,97},{2,34},{34,66},{66,9... | collective-permute-start | bytes 786440 | tf_op jit(solution)/shard_map/ppermute | solution.py:174
  72.3 11.3 %collective-permute-start.10 = (f32[256,256]{1,0:T(8,128)S(1)}, f32[256,256]{1,0:T(8,128)S(1)}, u32[]{:S(2)}, u32[]{:S(2)}) collective-permute-start(f32[256,256]{1,0:T(8,128)S(1)} %update11.1.refs_2_), channel_id=1, source_target_pairs={{0,32},{32,64},{64,96},{1,33},{33,65},{65,97},{2,34},{34,66},{66,9... | collective-permute-start | bytes 786440 | tf_op jit(solution)/shard_map/ppermute | solution.py:174
  78.6 11.3 %collective-permute-start.13 = (f32[256,256]{1,0:T(8,128)S(1)}, f32[256,256]{1,0:T(8,128)S(1)}, u32[]{:S(2)}, u32[]{:S(2)}) collective-permute-start(f32[256,256]{1,0:T(8,128)S(1)} %update12.1.refs_2_), channel_id=1, source_target_pairs={{0,32},{32,64},{64,96},{1,33},{33,65},{65,97},{2,34},{34,66},{66,9... | collective-permute-start | bytes 786440 | tf_op jit(solution)/shard_map/ppermute | solution.py:174
  85.0 10.8 %collective-permute-start.12 = (f32[256,256]{1,0:T(8,128)S(1)}, f32[256,256]{1,0:T(8,128)S(1)}, u32[]{:S(2)}, u32[]{:S(2)}) collective-permute-start(f32[256,256]{1,0:T(8,128)S(1)} %update13.1.refs_2_), channel_id=1, source_target_pairs={{0,32},{32,64},{64,96},{1,33},{33,65},{65,97},{2,34},{34,66},{66,9... | collective-permute-start | bytes 786440 | tf_op jit(solution)/shard_map/ppermute | solution.py:174
  94.4 12.9 %collective-permute-start.15 = (f32[256,256]{1,0:T(8,128)S(1)}, f32[256,256]{1,0:T(8,128)S(1)}, u32[]{:S(2)}, u32[]{:S(2)}) collective-permute-start(f32[256,256]{1,0:T(8,128)S(1)} %update14.1.refs_2_), channel_id=1, source_target_pairs={{0,32},{32,64},{64,96},{1,33},{33,65},{65,97},{2,34},{34,66},{66,9... | collective-permute-start | bytes 786440 | tf_op jit(solution)/shard_map/ppermute | solution.py:174
  97.3 14.7 %collective-permute-start.14 = (f32[256,256]{1,0:T(8,128)S(1)}, f32[256,256]{1,0:T(8,128)S(1)}, u32[]{:S(2)}, u32[]{:S(2)}) collective-permute-start(f32[256,256]{1,0:T(8,128)S(1)} %update15.1.refs_2_), channel_id=1, source_target_pairs={{0,32},{32,64},{64,96},{1,33},{33,65},{65,97},{2,34},{34,66},{66,9... | collective-permute-start | bytes 786440 | tf_op jit(solution)/shard_map/ppermute | solution.py:174
  116.8 5.7 %collective-permute-start.16 = (f32[2,4,4,3,32,256]{5,4,3,2,1,0:T(8,128)S(1)}, f32[2,4,4,3,32,256]{5,4,3,2,1,0:T(8,128)S(1)}, u32[]{:S(2)}, u32[]{:S(2)}) collective-permute-start(f32[2,4,4,3,32,256]{5,4,3,2,1,0:T(8,128)S(1)} %slice_bitcast_fusion), channel_id=1, source_target_pairs={{0,1},{1,0},{2,3},{3,2},{4,5},{5,4},{6,7},{7,6},{8,9},{9,8},{10,11... | collective-permute-start | bytes 9437192 | tf_op jit(solution)/shard_map/ppermute | solution.py:153
  123.9 9.3 %collective-permute-start.24 = (f32[2,96,256]{2,1,0:T(8,128)S(1)}, f32[2,96,256]{2,1,0:T(8,128)S(1)}, u32[]{:S(2)}, u32[]{:S(2)}) collective-permute-start(f32[2,96,256]{2,1,0:T(8,128)S(1)} %get-tuple-element.17), channel_id=1, source_target_pairs={{0,8},{8,16},{16,24},{24,0},{1,9},{9,17},{17,25},{25,1},{2,10},{10... | collective-permute-start | bytes 589832 | tf_op jit(solution)/shard_map/ppermute | solution.py:137
  125.9 7.3 %collective-permute-start.26 = (f32[2,96,256]{2,1,0:T(8,128)S(1)}, f32[2,96,256]{2,1,0:T(8,128)S(1)}, u32[]{:S(2)}, u32[]{:S(2)}) collective-permute-start(f32[2,96,256]{2,1,0:T(8,128)S(1)} %get-tuple-element.18), channel_id=1, source_target_pairs={{0,24},{8,0},{16,8},{24,16},{1,25},{9,1},{17,9},{25,17},{2,26},{10... | collective-permute-start | bytes 589832 | tf_op jit(solution)/shard_map/ppermute | solution.py:137
  128.2 8.4 %collective-permute-start.17 = (f32[2,96,256]{2,1,0:T(8,128)S(1)}, f32[2,96,256]{2,1,0:T(8,128)S(1)}, u32[]{:S(2)}, u32[]{:S(2)}) collective-permute-start(f32[2,96,256]{2,1,0:T(8,128)S(1)} %get-tuple-element.11), channel_id=1, source_target_pairs={{0,2},{2,4},{4,6},{6,0},{1,3},{3,5},{5,7},{7,1},{8,10},{10,12},{12... | collective-permute-start | bytes 589832 | tf_op jit(solution)/shard_map/ppermute | solution.py:137
  129.7 6.8 %collective-permute-start.19 = (f32[2,96,256]{2,1,0:T(8,128)S(1)}, f32[2,96,256]{2,1,0:T(8,128)S(1)}, u32[]{:S(2)}, u32[]{:S(2)}) collective-permute-start(f32[2,96,256]{2,1,0:T(8,128)S(1)} %get-tuple-element.12), channel_id=1, source_target_pairs={{0,6},{2,0},{4,2},{6,4},{1,7},{3,1},{5,3},{7,5},{8,14},{10,8},{12,... | collective-permute-start | bytes 589832 | tf_op jit(solution)/shard_map/ppermute | solution.py:137
  133.3 10.9 %collective-permute-start.27 = (f32[4,96,256]{2,1,0:T(8,128)S(1)}, f32[4,96,256]{2,1,0:T(8,128)S(1)}, u32[]{:S(2)}, u32[]{:S(2)}) collective-permute-start(f32[4,96,256]{2,1,0:T(8,128)S(1)} %pad_maximum_fusion.3), channel_id=1, source_target_pairs={{0,24},{8,0},{16,8},{24,16},{1,25},{9,1},{17,9},{25,17},{2,26},{10... | collective-permute-start | bytes 1179656 | tf_op jit(solution)/shard_map/ppermute | solution.py:137
  136.5 11.3 %collective-permute-start.25 = (f32[4,96,256]{2,1,0:T(8,128)S(1)}, f32[4,96,256]{2,1,0:T(8,128)S(1)}, u32[]{:S(2)}, u32[]{:S(2)}) collective-permute-start(f32[4,96,256]{2,1,0:T(8,128)S(1)} %pad_maximum_fusion.2), channel_id=1, source_target_pairs={{0,8},{8,16},{16,24},{24,0},{1,9},{9,17},{17,25},{25,1},{2,10},{10... | collective-permute-start | bytes 1179656 | tf_op jit(solution)/shard_map/ppermute | solution.py:137
  136.7 16.3 %collective-permute-start.20 = (f32[4,96,256]{2,1,0:T(8,128)S(1)}, f32[4,96,256]{2,1,0:T(8,128)S(1)}, u32[]{:S(2)}, u32[]{:S(2)}) collective-permute-start(f32[4,96,256]{2,1,0:T(8,128)S(1)} %pad_maximum_fusion.1), channel_id=1, source_target_pairs={{0,6},{2,0},{4,2},{6,4},{1,7},{3,1},{5,3},{7,5},{8,14},{10,8},{12,... | collective-permute-start | bytes 1179656 | tf_op jit(solution)/shard_map/ppermute | solution.py:137
  139.5 13.5 %collective-permute-start.18 = (f32[4,96,256]{2,1,0:T(8,128)S(1)}, f32[4,96,256]{2,1,0:T(8,128)S(1)}, u32[]{:S(2)}, u32[]{:S(2)}) collective-permute-start(f32[4,96,256]{2,1,0:T(8,128)S(1)} %pad_maximum_fusion), channel_id=1, source_target_pairs={{0,2},{2,4},{4,6},{6,0},{1,3},{3,5},{5,7},{7,1},{8,10},{10,12},{12... | collective-permute-start | bytes 1179656 | tf_op jit(solution)/shard_map/ppermute | solution.py:137
  147.9 8.5 %collective-permute-start.30 = (f32[96,256]{1,0:T(8,128)S(1)}, f32[96,256]{1,0:T(8,128)S(1)}, u32[]{:S(2)}, u32[]{:S(2)}) collective-permute-start(f32[96,256]{1,0:T(8,128)S(1)} %get-tuple-element.24), channel_id=1, source_target_pairs={{0,4},{2,6},{4,0},{6,2},{1,5},{3,7},{5,1},{7,3},{8,12},{10,14},{12... | collective-permute-start | bytes 294920 | tf_op jit(solution)/shard_map/ppermute | solution.py:137
  151.0 6.2 %collective-permute-start.29 = (f32[96,256]{1,0:T(8,128)S(1)}, f32[96,256]{1,0:T(8,128)S(1)}, u32[]{:S(2)}, u32[]{:S(2)}) collective-permute-start(f32[96,256]{1,0:T(8,128)S(1)} %get-tuple-element.25), channel_id=1, source_target_pairs={{0,6},{2,0},{4,2},{6,4},{1,7},{3,1},{5,3},{7,5},{8,14},{10,8},{12,... | collective-permute-start | bytes 294920 | tf_op jit(solution)/shard_map/ppermute | solution.py:137
  152.1 5.8 %collective-permute-start.28 = (f32[96,256]{1,0:T(8,128)S(1)}, f32[96,256]{1,0:T(8,128)S(1)}, u32[]{:S(2)}, u32[]{:S(2)}) collective-permute-start(f32[96,256]{1,0:T(8,128)S(1)} %get-tuple-element.26), channel_id=1, source_target_pairs={{0,2},{2,4},{4,6},{6,0},{1,3},{3,5},{5,7},{7,1},{8,10},{10,12},{12... | collective-permute-start | bytes 294920 | tf_op jit(solution)/shard_map/ppermute | solution.py:137
  153.1 6.2 %collective-permute-start.23 = (f32[96,256]{1,0:T(8,128)S(1)}, f32[96,256]{1,0:T(8,128)S(1)}, u32[]{:S(2)}, u32[]{:S(2)}) collective-permute-start(f32[96,256]{1,0:T(8,128)S(1)} %get-tuple-element.21), channel_id=1, source_target_pairs={{0,16},{8,24},{16,0},{24,8},{1,17},{9,25},{17,1},{25,9},{2,18},{10... | collective-permute-start | bytes 294920 | tf_op jit(solution)/shard_map/ppermute | solution.py:137
  155.0 5.8 %collective-permute-start.22 = (f32[96,256]{1,0:T(8,128)S(1)}, f32[96,256]{1,0:T(8,128)S(1)}, u32[]{:S(2)}, u32[]{:S(2)}) collective-permute-start(f32[96,256]{1,0:T(8,128)S(1)} %get-tuple-element.22), channel_id=1, source_target_pairs={{0,24},{8,0},{16,8},{24,16},{1,25},{9,1},{17,9},{25,17},{2,26},{10... | collective-permute-start | bytes 294920 | tf_op jit(solution)/shard_map/ppermute | solution.py:137
  156.4 5.8 %collective-permute-start.21 = (f32[96,256]{1,0:T(8,128)S(1)}, f32[96,256]{1,0:T(8,128)S(1)}, u32[]{:S(2)}, u32[]{:S(2)}) collective-permute-start(f32[96,256]{1,0:T(8,128)S(1)} %get-tuple-element.23), channel_id=1, source_target_pairs={{0,8},{8,16},{16,24},{24,0},{1,9},{9,17},{17,25},{25,1},{2,10},{10... | collective-permute-start | bytes 294920 | tf_op jit(solution)/shard_map/ppermute | solution.py:137

commit v5 on v4

--- a/solution.py
+++ b/solution.py
@@ -4,6 +4,7 @@
 from jax.experimental import pallas as pl
 from jax.experimental.pallas import tpu as pltpu
 from jax.sharding import Mesh, PartitionSpec as P
+
 
 f32, bf16 = jnp.float32, jnp.bfloat16
 W = 256
@@ -58,31 +59,30 @@
         halves(u.T), halves(second), ((1,), (0,)))
 
 
-def apply_part(q, e, ints, floats, psi, rights, pieces, results, stores):
-    my_z, my_x, core = ints[1], ints[2], ints[3]
-    above = jnp.minimum(q + 1, NQ - 1)
+def apply_part(q, ints, floats, environs, psi, rights, pieces, results, stores):
+    site, my_z, my_x, core = ints[0], ints[1], ints[2], ints[3]
+    e = environs[0][...]
+    for k in range(1, SITES):
+        e = jnp.where(site == k, environs[k][...], e)
     e = halves(e)
-    present = ints[16 + q].astype(f32)
-    present_above = jnp.where(q < NQ - 1, ints[16 + above], 0).astype(f32)
-
-    def one_state(state, _):
-        other = jnp.where(state == 0, q, above)
-        c = jnp.where(state == 0, floats[2] * present, floats[3] * present_above)
-        n = ints[4 + other]
-        part = c * product(e, halves(psi[state, q]), ((1,), (0,)))
-        results[state] = product(halves(part), halves(framed(rights[other], n, n)), ((1,), (1,)))
+    scales = [floats[2] * ints[16 + q].astype(f32)]
+    if q < NQ - 1:
+        scales.append(floats[3] * ints[17 + q].astype(f32))
+    for state in range(2):
+        if q + state < NQ:
+            n = ints[4 + q + state]
+            part = scales[state] * product(e, halves(psi[state, q]), ((1,), (0,)))
+            results[state] = product(halves(part), halves(framed(rights[q + state], n, n)), ((1,), (1,)))
+        else:
+            results[state] = jnp.zeros((W, W), f32)
         for i in range(W // ROWS):
-            piece = (W // ROWS) * q + i
-            owner, third = piece // 3, piece % 3
+            owner, third = divmod((W // ROWS) * q + i, 3)
             z = (owner // 8 - my_z + 4) % 4
             x = ((owner // 2) % 4 - my_x + 4) % 4
-            sent = (owner + core) % 2
-            near, far = jnp.where(state == 0, x, z), jnp.where(state == 0, z, x)
+            sent = core if owner % 2 == 0 else 1 - core
+            near, far = ((x, z), (z, x))[state]
             pltpu.make_async_copy(
                 results.at[state, pl.ds(ROWS * i, ROWS)], pieces.at[sent, state, near, far, third], stores).start()
-        return 0
-
-    lax.fori_loop(0, 2, one_state, 0)
     pltpu.make_async_copy(results, psi.at[:, 0], stores).wait()
 
 
@@ -97,30 +97,16 @@
 
     return pl.pallas_call(
         kernel, in_specs=[SCALAR] * 2 + [LOCAL] * 4 + [FAR] * len(held), out_specs=LOCAL, out_shape=jax.ShapeDtypeStruct((W, W), f32),
-        compiler_params=GRANT, name=f"update{step}",
+        compiler_params=GRANT,
     )(ints, floats, arrived, previous, left, mps, *held)
 
 
-def apply_step(step, ints, floats, environ, psi, rights, saved, held):
-    late = NQ <= step < NQ + LAG
-    operands = (environ, psi, rights) + ((saved,) if late else ())
+def apply_step(q, ints, floats, environs, psi, rights, held):
+    def kernel(ints, floats, *refs):
+        psi, rights = refs[SITES:SITES + 2]
+        apply_part(q, ints, floats, refs[:SITES], psi, rights, *refs[-3:])
 
-    def kernel(*refs):
-        ints, floats, environ, psi, rights = refs[:5]
-        q = step - LAG * ints[0]
-        active = (q >= 0) & (q < NQ)
-        first = ints[0] == 0
-        if late:
-            active = active | first
-            q = jnp.where(first, step - NQ, q)
-
-        @pl.when(active)
-        def _():
-            e = environ[...]
-            if late:
-                e = jnp.where(first, refs[5][...], e)
-            apply_part(q, e, ints, floats, psi, rights, *refs[-3:])
-
+    operands = (*environs, psi, rights)
     return pl.pallas_call(
         kernel,
         in_specs=[SCALAR] * 2 + [LOCAL] * len(operands) + [FAR] * len(held),
@@ -129,7 +115,6 @@
         scratch_shapes=[pltpu.VMEM((2, W, W), f32), pltpu.SemaphoreType.DMA],
         input_output_aliases={2 + len(operands): 0} if held else {},
         compiler_params=GRANT,
-        name=f"apply{step}",
     )(ints, floats, *operands, *held)
 
 
@@ -172,8 +157,10 @@
         environs[step] = environ
         if step + LAG < LAST:
             arrivals[step + LAG] = lax.ppermute(environ, "site", [(0, 1), (1, 2), (2, 3)])
-        if step >= LAG:
-            held = apply_step(step, ints, floats, environ, psi[0], right_env[0, 0], environs.get(step - NQ), held)
+        q = step - LAG * (SITES - 1)
+        if q >= 0:
+            held = apply_step(
+                q, ints, floats, [environs[q + LAG * k] for k in range(SITES)], psi[0], right_env[0, 0], held)
     return reduced(*held)
 
 

time: 163 us -> 154 us (0.945)
  Pallas kernels: 59 us -> 49.6 us
  waiting for transfers between devices: 50.2 us -> 46.6 us
  starting transfers between devices: 43.9 us -> 47.1 us
    pallas_call x16 -> x12, Pallas kernels: 38.3 us -> 28.9 us  [apply_step(): pl.pallas_call(kernel, in_specs=[SCALAR] * 2 + [LOCAL] * len(operands) +...]
    ppermute x14, waiting for transfers between devices: 14.9 us -> 9.42 us  [turned(): return lax.ppermute(x, axis, [(i, (i + by) % 4) for i in range(4)])]
    ppermute x14, starting transfers between devices: 22.7 us -> 25.5 us  [turned(): return lax.ppermute(x, axis, [(i, (i + by) % 4) for i in range(4)])]
    ppermute x16, waiting for transfers between devices: 29.7 us -> 31.5 us  [shards(): lax.ppermute(environ, 'site', [(0, 1), (1, 2), (2, 3)])]
    unnamed x16 -> x18, local copies, waits for them, and re-layouts: 5.36 us -> 5.36 us
  transfers between devices with their start and end apart: 31 -> 31, of which waited for: 20 -> 20; matrix products, arithmetic and copies ran while one was open for 0% -> 0% of each run, Pallas kernels for 33% -> 30%
where the time goes in v5:
time: 154 us; the launch traced here: 153 us
  Pallas kernels  49.6 us (32%)
  starting transfers between devices  47.1 us (31%)
  waiting for transfers between devices  46.6 us (30%)
  local copies, waits for them, and re-layouts  7.09 us (5%)
  other arithmetic  2.08 us (1%)
    ppermute x16, waiting for transfers between devices, shards(): lax.ppermute(environ, 'site', [(0, 1), (1, 2), (2, 3)])  31.5 us
    pallas_call x12, Pallas kernels, apply_step(): pl.pallas_call(kernel, in_specs=[SCALAR] * 2 + [LOCAL] * len(operands) +...  28.9 us
    ppermute x14, starting transfers between devices, turned(): return lax.ppermute(x, axis, [(i, (i + by) % 4) for i in range(4)])  25.5 us
    ppermute x16, starting transfers between devices, shards(): lax.ppermute(environ, 'site', [(0, 1), (1, 2), (2, 3)])  21.4 us
    pallas_call x18, Pallas kernels, update_step(): pl.pallas_call(kernel, in_specs=[SCALAR] * 2 + [LOCAL] * 4 + [FAR] * len(...  20.7 us
    ppermute x14, waiting for transfers between devices, turned(): return lax.ppermute(x, axis, [(i, (i + by) % 4) for i in range(4)])  9.42 us
    ppermute x1, waiting for transfers between devices, reduced(): both = pieces[0] + lax.ppermute(pieces[1], 'core', [(0, 1), (1, 0)])  5.65 us
    unnamed x18, local copies, waits for them, and re-layouts  5.36 us
  transfers between devices with their start and end apart: 31, of which 20 were waited for; matrix products, arithmetic and copies ran while one was open for 0% of the time, Pallas kernels for 30%

profile of v5, /device:TPU:24, one launch (start us, length us, event | category | flops | bytes accessed | tf_op | source)
XLA Modules:
  0.0 153.1 jit_solution(13660633052703537691)
XLA Ops:
  0.8 2.8 %copy-done = f32[1,2,12,256,256]{4,3,2,1,0:T(8,128)S(1)} copy-done((f32[1,2,12,256,256]{4,3,2,1,0:T(8,128)S(1)}, f32[1,2,12,256,256]{4,3,2,1,0:T(8,128)}, u32[]{:S(2)}) %copy-start) | copy-done | bytes 6291480
  3.6 1.9 %copy-done.1 = f32[1,12,256,256]{3,2,1,0:T(8,128)S(1)} copy-done((f32[1,12,256,256]{3,2,1,0:T(8,128)S(1)}, f32[1,12,256,256]{3,2,1,0:T(8,128)}, u32[]{:S(2)}) %copy-start.1) | copy-done | bytes 3145752
  8.6 1.6 %collective-permute-start = (f32[256,256]{1,0:T(8,128)S(1)}, f32[256,256]{1,0:T(8,128)S(1)}, u32[]{:S(2)}, u32[]{:S(2)}) collective-permute-start(f32[256,256]{1,0:T(8,128)S(1)} %shard_map.73.refs_0_), channel_id=1, source_target_pairs={{0,32},{32,64},{64,96},{1,33},{33,65},{65,97},{2,34},{34,66},{66,9... | collective-permute-start | bytes 786440 | tf_op jit(solution)/shard_map/ppermute | solution.py:159
  10.1 7.6 %collective-permute-done.1.previous.arrived = f32[256,256]{1,0:T(8,128)S(1)} collective-permute-done((f32[256,256]{1,0:T(8,128)S(1)}, f32[256,256]{1,0:T(8,128)S(1)}, u32[]{:S(2)}, u32[]{:S(2)}) %collective-permute-start.1) | collective-permute-done | bytes 262176 | tf_op jit(solution)/shard_map/ppermute | solution.py:159
  19.6 3.8 %collective-permute-done.arrived.previous = f32[256,256]{1,0:T(8,128)S(1)} collective-permute-done((f32[256,256]{1,0:T(8,128)S(1)}, f32[256,256]{1,0:T(8,128)S(1)}, u32[]{:S(2)}, u32[]{:S(2)}) %collective-permute-start) | collective-permute-done | bytes 262176 | tf_op jit(solution)/shard_map/ppermute | solution.py:159
  25.2 4.1 %collective-permute-done.3.previous.arrived = f32[256,256]{1,0:T(8,128)S(1)} collective-permute-done((f32[256,256]{1,0:T(8,128)S(1)}, f32[256,256]{1,0:T(8,128)S(1)}, u32[]{:S(2)}, u32[]{:S(2)}) %collective-permute-start.3) | collective-permute-done | bytes 262176 | tf_op jit(solution)/shard_map/ppermute | solution.py:159
  31.2 3.8 %collective-permute-done.2.arrived.previous = f32[256,256]{1,0:T(8,128)S(1)} collective-permute-done((f32[256,256]{1,0:T(8,128)S(1)}, f32[256,256]{1,0:T(8,128)S(1)}, u32[]{:S(2)}, u32[]{:S(2)}) %collective-permute-start.2) | collective-permute-done | bytes 262176 | tf_op jit(solution)/shard_map/ppermute | solution.py:159
  35.6 1.6 %collective-permute-start.4 = (f32[256,256]{1,0:T(8,128)S(1)}, f32[256,256]{1,0:T(8,128)S(1)}, u32[]{:S(2)}, u32[]{:S(2)}) collective-permute-start(f32[256,256]{1,0:T(8,128)S(1)} %shard_map.77.refs_2_.refs_1_.refs_0_), channel_id=1, source_target_pairs={{0,32},{32,64},{64,96},{1,33},{33,65},{65,97},{2,34},{34,66},{66,9... | collective-permute-start | bytes 786440 | tf_op jit(solution)/shard_map/ppermute | solution.py:159
  37.1 3.6 %collective-permute-done.5.arrived.previous = f32[256,256]{1,0:T(8,128)S(1)} collective-permute-done((f32[256,256]{1,0:T(8,128)S(1)}, f32[256,256]{1,0:T(8,128)S(1)}, u32[]{:S(2)}, u32[]{:S(2)}) %collective-permute-start.5) | collective-permute-done | bytes 262176 | tf_op jit(solution)/shard_map/ppermute | solution.py:159
  43.6 2.5 %shard_map.80.rest_0_.refs_6_ = f32[2,2,4,4,3,32,256]{6,5,4,3,2,1,0:T(8,128)S(1)} custom-call(s32[28]{0:T(128)S(1)} %concatenate.15.ints, f32[4]{0:T(128)S(1)} %bitcast.157, f32[256,256]{1,0:T(8,128)S(1)} %shard_map.74.refs_0_, f32[256,256]{1,0:T(8,128)S(1)} %shard_map.76.refs_1_.refs_0_, f32[256,256]{1,0:T(8,128)S(1)} %shard_map.78.refs_2_.refs_1_.refs_0_, ...), custom_call_target="tpu_custom_call" | custom-call | tf_op jit(solution)/shard_map/pallas_call | solution.py:110
  46.2 1.5 shard_map.81.refs_3_.refs_2_.refs_1_.refs_0_
  48.9 2.5 %shard_map.82.rest_0_.refs_6_ = f32[2,2,4,4,3,32,256]{6,5,4,3,2,1,0:T(8,128)S(1)} custom-call(s32[28]{0:T(128)S(1)} %concatenate.15.ints, f32[4]{0:T(128)S(1)} %bitcast.159, f32[256,256]{1,0:T(8,128)S(1)} %shard_map.73.refs_0_, f32[256,256]{1,0:T(8,128)S(1)} %shard_map.75.refs_1_.refs_0_, ...), custom_call_target="tpu_custom_call", output_to_operand_aliasing={{}: (8, {})} | custom-call | tf_op jit(solution)/shard_map/pallas_call | solution.py:110
  51.9 1.4 shard_map.83.refs_3_.refs_2_.refs_1_.refs_0_
  54.6 2.5 %shard_map.84.rest_0_.refs_6_ = f32[2,2,4,4,3,32,256]{6,5,4,3,2,1,0:T(8,128)S(1)} custom-call(s32[28]{0:T(128)S(1)} %concatenate.15.ints, f32[4]{0:T(128)S(1)} %bitcast.161, f32[256,256]{1,0:T(8,128)S(1)} %shard_map.76.refs_1_.refs_0_, f32[256,256]{1,0:T(8,128)S(1)} %shard_map.78.refs_2_.refs_1_.refs_0_, ...), custom_call_target="tpu_custom_call", output_to_operand_aliasing={{}: (8, {})} | custom-call | tf_op jit(solution)/shard_map/pallas_call | solution.py:110
  57.8 1.4 shard_map.85.refs_3_.refs_2_.refs_1_.refs_0_
  60.6 2.5 %shard_map.86.rest_0_.refs_6_ = f32[2,2,4,4,3,32,256]{6,5,4,3,2,1,0:T(8,128)S(1)} custom-call(s32[28]{0:T(128)S(1)} %concatenate.15.ints, f32[4]{0:T(128)S(1)} %bitcast.163, f32[256,256]{1,0:T(8,128)S(1)} %shard_map.75.refs_1_.refs_0_, f32[256,256]{1,0:T(8,128)S(1)} %shard_map.77.refs_2_.refs_1_.refs_0_, ...), custom_call_target="tpu_custom_call", output_to_operand_aliasing={{}: (8, {})} | custom-call | tf_op jit(solution)/shard_map/pallas_call | solution.py:110
  65.2 1.5 collective-permute-start.11
  66.6 2.5 %shard_map.88.rest_0_.refs_6_ = f32[2,2,4,4,3,32,256]{6,5,4,3,2,1,0:T(8,128)S(1)} custom-call(s32[28]{0:T(128)S(1)} %concatenate.15.ints, f32[4]{0:T(128)S(1)} %bitcast.165, f32[256,256]{1,0:T(8,128)S(1)} %shard_map.78.refs_2_.refs_1_.refs_0_, f32[256,256]{1,0:T(8,128)S(1)} %shard_map.79.refs_3_.refs_2_.refs_1_.refs_0_, ...), custom_call_target="tpu_custom_call", output_to_operand_aliasing={{}: (8, {})} | custom-call | tf_op jit(solution)/shard_map/pallas_call | solution.py:110
  69.4 1.5 shard_map.89.refs_3_.refs_2_.refs_1_.refs_0_
  72.1 2.5 %shard_map.90.rest_0_.refs_6_ = f32[2,2,4,4,3,32,256]{6,5,4,3,2,1,0:T(8,128)S(1)} custom-call(s32[28]{0:T(128)S(1)} %concatenate.15.ints, f32[4]{0:T(128)S(1)} %bitcast.167, f32[256,256]{1,0:T(8,128)S(1)} %shard_map.77.refs_2_.refs_1_.refs_0_, f32[256,256]{1,0:T(8,128)S(1)} %shard_map.81.refs_3_.refs_2_.refs_1_.refs_0_, ...), custom_call_target="tpu_custom_call", output_to_operand_aliasing={{}: (8, {})} | custom-call | tf_op jit(solution)/shard_map/pallas_call | solution.py:110
  78.4 2.5 %shard_map.92.rest_0_.refs_6_ = f32[2,2,4,4,3,32,256]{6,5,4,3,2,1,0:T(8,128)S(1)} custom-call(s32[28]{0:T(128)S(1)} %concatenate.15.ints, f32[4]{0:T(128)S(1)} %bitcast.169, f32[256,256]{1,0:T(8,128)S(1)} %shard_map.79.refs_3_.refs_2_.refs_1_.refs_0_, f32[256,256]{1,0:T(8,128)S(1)} %shard_map.83.refs_3_.refs_2_.refs_1_.refs_0_, ...), custom_call_target="tpu_custom_call", output_to_operand_aliasing={{}: (8, {})} | custom-call | tf_op jit(solution)/shard_map/pallas_call | solution.py:110
  84.2 2.5 %shard_map.94.rest_0_.refs_6_ = f32[2,2,4,4,3,32,256]{6,5,4,3,2,1,0:T(8,128)S(1)} custom-call(s32[28]{0:T(128)S(1)} %concatenate.15.ints, f32[4]{0:T(128)S(1)} %bitcast.171, f32[256,256]{1,0:T(8,128)S(1)} %shard_map.81.refs_3_.refs_2_.refs_1_.refs_0_, f32[256,256]{1,0:T(8,128)S(1)} %shard_map.85.refs_3_.refs_2_.refs_1_.refs_0_, ...), custom_call_target="tpu_custom_call", output_to_operand_aliasing={{}: (8, {})} | custom-call | tf_op jit(solution)/shard_map/pallas_call | solution.py:110
  87.3 1.4 shard_map.95.refs_3_.refs_2_
  88.8 2.5 %shard_map.96.rest_0_.refs_6_ = f32[2,2,4,4,3,32,256]{6,5,4,3,2,1,0:T(8,128)S(1)} custom-call(s32[28]{0:T(128)S(1)} %concatenate.15.ints, f32[4]{0:T(128)S(1)} %bitcast.173, f32[256,256]{1,0:T(8,128)S(1)} %shard_map.83.refs_3_.refs_2_.refs_1_.refs_0_, f32[256,256]{1,0:T(8,128)S(1)} %shard_map.87.refs_3_.refs_2_.refs_1_.refs_0_, ...), custom_call_target="tpu_custom_call", output_to_operand_aliasing={{}: (8, {})} | custom-call | tf_op jit(solution)/shard_map/pallas_call | solution.py:110
  92.6 1.5 shard_map.97.refs_3_.refs_2_
  95.3 2.5 %shard_map.98.rest_0_.refs_6_ = f32[2,2,4,4,3,32,256]{6,5,4,3,2,1,0:T(8,128)S(1)} custom-call(s32[28]{0:T(128)S(1)} %concatenate.15.ints, f32[4]{0:T(128)S(1)} %bitcast.175, f32[256,256]{1,0:T(8,128)S(1)} %shard_map.85.refs_3_.refs_2_.refs_1_.refs_0_, f32[256,256]{1,0:T(8,128)S(1)} %shard_map.89.refs_3_.refs_2_.refs_1_.refs_0_, ...), custom_call_target="tpu_custom_call", output_to_operand_aliasing={{}: (8, {})} | custom-call | tf_op jit(solution)/shard_map/pallas_call | solution.py:110
  97.8 4.0 %collective-permute-done.15.arrived.previous = f32[256,256]{1,0:T(8,128)S(1)} collective-permute-done((f32[256,256]{1,0:T(8,128)S(1)}, f32[256,256]{1,0:T(8,128)S(1)}, u32[]{:S(2)}, u32[]{:S(2)}) %collective-permute-start.15) | collective-permute-done | bytes 262176 | tf_op jit(solution)/shard_map/ppermute | solution.py:159
  101.8 1.5 shard_map.99.refs_3_
  103.3 2.5 %shard_map.100.rest_0_.refs_6_ = f32[2,2,4,4,3,32,256]{6,5,4,3,2,1,0:T(8,128)S(1)} custom-call(s32[28]{0:T(128)S(1)} %concatenate.15.ints, f32[4]{0:T(128)S(1)} %bitcast.177, f32[256,256]{1,0:T(8,128)S(1)} %shard_map.87.refs_3_.refs_2_.refs_1_.refs_0_, f32[256,256]{1,0:T(8,128)S(1)} %shard_map.91.refs_3_.refs_2_.refs_1_, ...), custom_call_target="tpu_custom_call", output_to_operand_aliasing={{}: (8, {})} | custom-call | tf_op jit(solution)/shard_map/pallas_call | solution.py:110
  105.8 1.5 shard_map.101.refs_3_
  107.2 1.9 %shard_map.102 = f32[2,2,4,4,3,32,256]{6,5,4,3,2,1,0:T(8,128)S(1)} custom-call(s32[28]{0:T(128)S(1)} %concatenate.15.ints, f32[4]{0:T(128)S(1)} %bitcast.179, f32[256,256]{1,0:T(8,128)S(1)} %shard_map.89.refs_3_.refs_2_.refs_1_.refs_0_, f32[256,256]{1,0:T(8,128)S(1)} %shard_map.93.refs_3_.refs_2_.refs_1_, ...), custom_call_target="tpu_custom_call", output_to_operand_aliasing={{}: (8, {})} | custom-call | tf_op jit(solution)/shard_map/pallas_call | solution.py:110
  109.8 5.6 %collective-permute-done.16 = f32[2,4,4,3,32,256]{5,4,3,2,1,0:T(8,128)S(1)} collective-permute-done((f32[2,4,4,3,32,256]{5,4,3,2,1,0:T(8,128)S(1)}, f32[2,4,4,3,32,256]{5,4,3,2,1,0:T(8,128)S(1)}, u32[]{:S(2)}, u32[]{:S(2)}) %collective-permute-start.16) | collective-permute-done | bytes 3145760 | tf_op jit(solution)/shard_map/ppermute | solution.py:138
  116.9 1.5 %collective-permute-start.17 = (f32[2,96,256]{2,1,0:T(8,128)S(1)}, f32[2,96,256]{2,1,0:T(8,128)S(1)}, u32[]{:S(2)}, u32[]{:S(2)}) collective-permute-start(f32[2,96,256]{2,1,0:T(8,128)S(1)} %get-tuple-element.11), channel_id=1, source_target_pairs={{0,2},{2,4},{4,6},{6,0},{1,3},{3,5},{5,7},{7,1},{8,10},{10,12},{12... | collective-permute-start | bytes 589832 | tf_op jit(solution)/shard_map/ppermute | solution.py:122
  118.4 1.8 %collective-permute-start.19 = (f32[2,96,256]{2,1,0:T(8,128)S(1)}, f32[2,96,256]{2,1,0:T(8,128)S(1)}, u32[]{:S(2)}, u32[]{:S(2)}) collective-permute-start(f32[2,96,256]{2,1,0:T(8,128)S(1)} %get-tuple-element.12), channel_id=1, source_target_pairs={{0,6},{2,0},{4,2},{6,4},{1,7},{3,1},{5,3},{7,5},{8,14},{10,8},{12,... | collective-permute-start | bytes 589832 | tf_op jit(solution)/shard_map/ppermute | solution.py:122
  120.2 2.0 %collective-permute-start.24 = (f32[2,96,256]{2,1,0:T(8,128)S(1)}, f32[2,96,256]{2,1,0:T(8,128)S(1)}, u32[]{:S(2)}, u32[]{:S(2)}) collective-permute-start(f32[2,96,256]{2,1,0:T(8,128)S(1)} %get-tuple-element.17), channel_id=1, source_target_pairs={{0,8},{8,16},{16,24},{24,0},{1,9},{9,17},{17,25},{25,1},{2,10},{10... | collective-permute-start | bytes 589832 | tf_op jit(solution)/shard_map/ppermute | solution.py:122
  122.2 2.2 %collective-permute-start.26 = (f32[2,96,256]{2,1,0:T(8,128)S(1)}, f32[2,96,256]{2,1,0:T(8,128)S(1)}, u32[]{:S(2)}, u32[]{:S(2)}) collective-permute-start(f32[2,96,256]{2,1,0:T(8,128)S(1)} %get-tuple-element.18), channel_id=1, source_target_pairs={{0,24},{8,0},{16,8},{24,16},{1,25},{9,1},{17,9},{25,17},{2,26},{10... | collective-permute-start | bytes 589832 | tf_op jit(solution)/shard_map/ppermute | solution.py:122
  125.2 1.6 %collective-permute-start.18 = (f32[4,96,256]{2,1,0:T(8,128)S(1)}, f32[4,96,256]{2,1,0:T(8,128)S(1)}, u32[]{:S(2)}, u32[]{:S(2)}) collective-permute-start(f32[4,96,256]{2,1,0:T(8,128)S(1)} %pad_maximum_fusion), channel_id=1, source_target_pairs={{0,2},{2,4},{4,6},{6,0},{1,3},{3,5},{5,7},{7,1},{8,10},{10,12},{12... | collective-permute-start | bytes 1179656 | tf_op jit(solution)/shard_map/ppermute | solution.py:122
  126.8 1.8 %collective-permute-start.20 = (f32[4,96,256]{2,1,0:T(8,128)S(1)}, f32[4,96,256]{2,1,0:T(8,128)S(1)}, u32[]{:S(2)}, u32[]{:S(2)}) collective-permute-start(f32[4,96,256]{2,1,0:T(8,128)S(1)} %pad_maximum_fusion.1), channel_id=1, source_target_pairs={{0,6},{2,0},{4,2},{6,4},{1,7},{3,1},{5,3},{7,5},{8,14},{10,8},{12,... | collective-permute-start | bytes 1179656 | tf_op jit(solution)/shard_map/ppermute | solution.py:122
  129.1 1.6 %collective-permute-start.25 = (f32[4,96,256]{2,1,0:T(8,128)S(1)}, f32[4,96,256]{2,1,0:T(8,128)S(1)}, u32[]{:S(2)}, u32[]{:S(2)}) collective-permute-start(f32[4,96,256]{2,1,0:T(8,128)S(1)} %pad_maximum_fusion.2), channel_id=1, source_target_pairs={{0,8},{8,16},{16,24},{24,0},{1,9},{9,17},{17,25},{25,1},{2,10},{10... | collective-permute-start | bytes 1179656 | tf_op jit(solution)/shard_map/ppermute | solution.py:122
  130.7 2.2 %collective-permute-start.27 = (f32[4,96,256]{2,1,0:T(8,128)S(1)}, f32[4,96,256]{2,1,0:T(8,128)S(1)}, u32[]{:S(2)}, u32[]{:S(2)}) collective-permute-start(f32[4,96,256]{2,1,0:T(8,128)S(1)} %pad_maximum_fusion.3), channel_id=1, source_target_pairs={{0,24},{8,0},{16,8},{24,16},{1,25},{9,1},{17,9},{25,17},{2,26},{10... | collective-permute-start | bytes 1179656 | tf_op jit(solution)/shard_map/ppermute | solution.py:122
  132.9 3.9 %collective-permute-done.18 = f32[4,96,256]{2,1,0:T(8,128)S(1)} collective-permute-done((f32[4,96,256]{2,1,0:T(8,128)S(1)}, f32[4,96,256]{2,1,0:T(8,128)S(1)}, u32[]{:S(2)}, u32[]{:S(2)}) %collective-permute-start.18) | collective-permute-done | bytes 393248 | tf_op jit(solution)/shard_map/ppermute | solution.py:122
  136.9 2.0 %collective-permute-start.21 = (f32[96,256]{1,0:T(8,128)S(1)}, f32[96,256]{1,0:T(8,128)S(1)}, u32[]{:S(2)}, u32[]{:S(2)}) collective-permute-start(f32[96,256]{1,0:T(8,128)S(1)} %get-tuple-element.23), channel_id=1, source_target_pairs={{0,8},{8,16},{16,24},{24,0},{1,9},{9,17},{17,25},{25,1},{2,10},{10... | collective-permute-start | bytes 294920 | tf_op jit(solution)/shard_map/ppermute | solution.py:122
  138.9 2.2 %collective-permute-start.22 = (f32[96,256]{1,0:T(8,128)S(1)}, f32[96,256]{1,0:T(8,128)S(1)}, u32[]{:S(2)}, u32[]{:S(2)}) collective-permute-start(f32[96,256]{1,0:T(8,128)S(1)} %get-tuple-element.22), channel_id=1, source_target_pairs={{0,24},{8,0},{16,8},{24,16},{1,25},{9,1},{17,9},{25,17},{2,26},{10... | collective-permute-start | bytes 294920 | tf_op jit(solution)/shard_map/ppermute | solution.py:122
  141.1 1.8 %collective-permute-start.23 = (f32[96,256]{1,0:T(8,128)S(1)}, f32[96,256]{1,0:T(8,128)S(1)}, u32[]{:S(2)}, u32[]{:S(2)}) collective-permute-start(f32[96,256]{1,0:T(8,128)S(1)} %get-tuple-element.21), channel_id=1, source_target_pairs={{0,16},{8,24},{16,0},{24,8},{1,17},{9,25},{17,1},{25,9},{2,18},{10... | collective-permute-start | bytes 294920 | tf_op jit(solution)/shard_map/ppermute | solution.py:122
  144.1 2.2 %collective-permute-start.29 = (f32[96,256]{1,0:T(8,128)S(1)}, f32[96,256]{1,0:T(8,128)S(1)}, u32[]{:S(2)}, u32[]{:S(2)}) collective-permute-start(f32[96,256]{1,0:T(8,128)S(1)} %get-tuple-element.25), channel_id=1, source_target_pairs={{0,6},{2,0},{4,2},{6,4},{1,7},{3,1},{5,3},{7,5},{8,14},{10,8},{12,... | collective-permute-start | bytes 294920 | tf_op jit(solution)/shard_map/ppermute | solution.py:122
  146.3 1.5 collective-permute-start.30
  147.8 1.7 %collective-permute-done.28 = f32[96,256]{1,0:T(8,128)S(1)} collective-permute-done((f32[96,256]{1,0:T(8,128)S(1)}, f32[96,256]{1,0:T(8,128)S(1)}, u32[]{:S(2)}, u32[]{:S(2)}) %collective-permute-start.28) | collective-permute-done | bytes 98336 | tf_op jit(solution)/shard_map/ppermute | solution.py:122
  149.5 2.9 %collective-permute-done.30 = f32[96,256]{1,0:T(8,128)S(1)} collective-permute-done((f32[96,256]{1,0:T(8,128)S(1)}, f32[96,256]{1,0:T(8,128)S(1)}, u32[]{:S(2)}, u32[]{:S(2)}) %collective-permute-start.30) | collective-permute-done | bytes 98336 | tf_op jit(solution)/shard_map/ppermute | solution.py:122
  (85 shorter events, 37.3 us)
Async XLA Ops:
  0.8 2.8 %copy-start = (f32[1,2,12,256,256]{4,3,2,1,0:T(8,128)S(1)}, f32[1,2,12,256,256]{4,3,2,1,0:T(8,128)}, u32[]{:S(2)}) copy-start(f32[1,2,12,256,256]{4,3,2,1,0:T(8,128)} %param.9) | copy-start | bytes 18874372
  3.6 1.9 %copy-start.1 = (f32[1,12,256,256]{3,2,1,0:T(8,128)S(1)}, f32[1,12,256,256]{3,2,1,0:T(8,128)}, u32[]{:S(2)}) copy-start(f32[1,12,256,256]{3,2,1,0:T(8,128)} %param.7) | copy-start | bytes 9437188
  5.5 0.7 copy-start.4
  6.7 11.1 %collective-permute-start.1 = (f32[256,256]{1,0:T(8,128)S(1)}, f32[256,256]{1,0:T(8,128)S(1)}, u32[]{:S(2)}, u32[]{:S(2)}) collective-permute-start(f32[256,256]{1,0:T(8,128)S(1)} %shard_map.74.refs_0_), channel_id=1, source_target_pairs={{0,32},{32,64},{64,96},{1,33},{33,65},{65,97},{2,34},{34,66},{66,9... | collective-permute-start | bytes 786440 | tf_op jit(solution)/shard_map/ppermute | solution.py:159
  8.0 15.4 %slice-start = ((s8[6291456]{0:T(1024)(128)(4,1)}), s8[4194304]{0:T(1024)(128)(4,1)S(1)}, s32[]{:S(2)}) async-start(s8[6291456]{0:T(1024)(128)(4,1)} %bitcast.89), calls=%async_computation | async-start | bytes 8388608
  8.5 14.8 %slice-start.1 = ((s8[6291456]{0:T(1024)(128)(4,1)}), s8[2097152]{0:T(1024)(128)(4,1)S(1)}, s32[]{:S(2)}) async-start(s8[6291456]{0:T(1024)(128)(4,1)} %bitcast.89), calls=%async_computation.1 | async-start | bytes 4194304
  8.6 14.8 %collective-permute-start = (f32[256,256]{1,0:T(8,128)S(1)}, f32[256,256]{1,0:T(8,128)S(1)}, u32[]{:S(2)}, u32[]{:S(2)}) collective-permute-start(f32[256,256]{1,0:T(8,128)S(1)} %shard_map.73.refs_0_), channel_id=1, source_target_pairs={{0,32},{32,64},{64,96},{1,33},{33,65},{65,97},{2,34},{34,66},{66,9... | collective-permute-start | bytes 786440 | tf_op jit(solution)/shard_map/ppermute | solution.py:159
  18.3 11.1 %collective-permute-start.3 = (f32[256,256]{1,0:T(8,128)S(1)}, f32[256,256]{1,0:T(8,128)S(1)}, u32[]{:S(2)}, u32[]{:S(2)}) collective-permute-start(f32[256,256]{1,0:T(8,128)S(1)} %shard_map.76.refs_1_.refs_0_), channel_id=1, source_target_pairs={{0,32},{32,64},{64,96},{1,33},{33,65},{65,97},{2,34},{34,66},{66,9... | collective-permute-start | bytes 786440 | tf_op jit(solution)/shard_map/ppermute | solution.py:159
  23.9 11.1 %collective-permute-start.2 = (f32[256,256]{1,0:T(8,128)S(1)}, f32[256,256]{1,0:T(8,128)S(1)}, u32[]{:S(2)}, u32[]{:S(2)}) collective-permute-start(f32[256,256]{1,0:T(8,128)S(1)} %shard_map.75.refs_1_.refs_0_), channel_id=1, source_target_pairs={{0,32},{32,64},{64,96},{1,33},{33,65},{65,97},{2,34},{34,66},{66,9... | collective-permute-start | bytes 786440 | tf_op jit(solution)/shard_map/ppermute | solution.py:159
  29.9 10.9 %collective-permute-start.5 = (f32[256,256]{1,0:T(8,128)S(1)}, f32[256,256]{1,0:T(8,128)S(1)}, u32[]{:S(2)}, u32[]{:S(2)}) collective-permute-start(f32[256,256]{1,0:T(8,128)S(1)} %shard_map.78.refs_2_.refs_1_.refs_0_), channel_id=1, source_target_pairs={{0,32},{32,64},{64,96},{1,33},{33,65},{65,97},{2,34},{34,66},{66,9... | collective-permute-start | bytes 786440 | tf_op jit(solution)/shard_map/ppermute | solution.py:159
  35.0 8.5 %slice-start.2 = ((s8[6291456]{0:T(1024)(128)(4,1)}), s8[4194304]{0:T(1024)(128)(4,1)S(1)}, s32[]{:S(2)}) async-start(s8[6291456]{0:T(1024)(128)(4,1)} %bitcast.124), calls=%async_computation.2 | async-start | bytes 8388608
  35.6 8.0 %slice-start.3 = ((s8[6291456]{0:T(1024)(128)(4,1)}), s8[2097152]{0:T(1024)(128)(4,1)S(1)}, s32[]{:S(2)}) async-start(s8[6291456]{0:T(1024)(128)(4,1)} %bitcast.124), calls=%async_computation.3 | async-start | bytes 4194304
  35.6 8.0 %copy-start.3 = (f32[1,1,12,256,256]{4,3,2,1,0:T(8,128)S(1)}, f32[1,1,12,256,256]{4,3,2,1,0:T(8,128)}, u32[]{:S(2)}) copy-start(f32[1,1,12,256,256]{4,3,2,1,0:T(8,128)} %param.8) | copy-start | bytes 9437188
  35.6 10.6 %collective-permute-start.4 = (f32[256,256]{1,0:T(8,128)S(1)}, f32[256,256]{1,0:T(8,128)S(1)}, u32[]{:S(2)}, u32[]{:S(2)}) collective-permute-start(f32[256,256]{1,0:T(8,128)S(1)} %shard_map.77.refs_2_.refs_1_.refs_0_), channel_id=1, source_target_pairs={{0,32},{32,64},{64,96},{1,33},{33,65},{65,97},{2,34},{34,66},{66,9... | collective-permute-start | bytes 786440 | tf_op jit(solution)/shard_map/ppermute | solution.py:159
  42.2 9.6 %collective-permute-start.7 = (f32[256,256]{1,0:T(8,128)S(1)}, f32[256,256]{1,0:T(8,128)S(1)}, u32[]{:S(2)}, u32[]{:S(2)}) collective-permute-start(f32[256,256]{1,0:T(8,128)S(1)} %shard_map.79.refs_3_.refs_2_.refs_1_.refs_0_), channel_id=1, source_target_pairs={{0,32},{32,64},{64,96},{1,33},{33,65},{65,97},{2,34},{34,66},{66,9... | collective-permute-start | bytes 786440 | tf_op jit(solution)/shard_map/ppermute | solution.py:159
  43.6 2.6 %copy-start.2 = (f32[1,12,256,256]{3,2,1,0:T(8,128)S(1)}, f32[1,12,256,256]{3,2,1,0:T(8,128)}, u32[]{:S(2)}) copy-start(f32[1,12,256,256]{3,2,1,0:T(8,128)} %param.7) | copy-start | bytes 9437188
  47.6 10.2 %collective-permute-start.6 = (f32[256,256]{1,0:T(8,128)S(1)}, f32[256,256]{1,0:T(8,128)S(1)}, u32[]{:S(2)}, u32[]{:S(2)}) collective-permute-start(f32[256,256]{1,0:T(8,128)S(1)} %shard_map.81.refs_3_.refs_2_.refs_1_.refs_0_), channel_id=1, source_target_pairs={{0,32},{32,64},{64,96},{1,33},{33,65},{65,97},{2,34},{34,66},{66,9... | collective-permute-start | bytes 786440 | tf_op jit(solution)/shard_map/ppermute | solution.py:159
  53.3 10.4 %collective-permute-start.9 = (f32[256,256]{1,0:T(8,128)S(1)}, f32[256,256]{1,0:T(8,128)S(1)}, u32[]{:S(2)}, u32[]{:S(2)}) collective-permute-start(f32[256,256]{1,0:T(8,128)S(1)} %shard_map.83.refs_3_.refs_2_.refs_1_.refs_0_), channel_id=1, source_target_pairs={{0,32},{32,64},{64,96},{1,33},{33,65},{65,97},{2,34},{34,66},{66,9... | collective-permute-start | bytes 786440 | tf_op jit(solution)/shard_map/ppermute | solution.py:159
  59.3 10.1 %collective-permute-start.8 = (f32[256,256]{1,0:T(8,128)S(1)}, f32[256,256]{1,0:T(8,128)S(1)}, u32[]{:S(2)}, u32[]{:S(2)}) collective-permute-start(f32[256,256]{1,0:T(8,128)S(1)} %shard_map.85.refs_3_.refs_2_.refs_1_.refs_0_), channel_id=1, source_target_pairs={{0,32},{32,64},{64,96},{1,33},{33,65},{65,97},{2,34},{34,66},{66,9... | collective-permute-start | bytes 786440 | tf_op jit(solution)/shard_map/ppermute | solution.py:159
  65.2 10.4 %collective-permute-start.11 = (f32[256,256]{1,0:T(8,128)S(1)}, f32[256,256]{1,0:T(8,128)S(1)}, u32[]{:S(2)}, u32[]{:S(2)}) collective-permute-start(f32[256,256]{1,0:T(8,128)S(1)} %shard_map.87.refs_3_.refs_2_.refs_1_.refs_0_), channel_id=1, source_target_pairs={{0,32},{32,64},{64,96},{1,33},{33,65},{65,97},{2,34},{34,66},{66,9... | collective-permute-start | bytes 786440 | tf_op jit(solution)/shard_map/ppermute | solution.py:159
  70.8 10.6 %collective-permute-start.10 = (f32[256,256]{1,0:T(8,128)S(1)}, f32[256,256]{1,0:T(8,128)S(1)}, u32[]{:S(2)}, u32[]{:S(2)}) collective-permute-start(f32[256,256]{1,0:T(8,128)S(1)} %shard_map.89.refs_3_.refs_2_.refs_1_.refs_0_), channel_id=1, source_target_pairs={{0,32},{32,64},{64,96},{1,33},{33,65},{65,97},{2,34},{34,66},{66,9... | collective-permute-start | bytes 786440 | tf_op jit(solution)/shard_map/ppermute | solution.py:159
  77.1 10.3 %collective-permute-start.13 = (f32[256,256]{1,0:T(8,128)S(1)}, f32[256,256]{1,0:T(8,128)S(1)}, u32[]{:S(2)}, u32[]{:S(2)}) collective-permute-start(f32[256,256]{1,0:T(8,128)S(1)} %shard_map.91.refs_3_.refs_2_.refs_1_), channel_id=1, source_target_pairs={{0,32},{32,64},{64,96},{1,33},{33,65},{65,97},{2,34},{34,66},{66,9... | collective-permute-start | bytes 786440 | tf_op jit(solution)/shard_map/ppermute | solution.py:159
  82.9 9.6 %collective-permute-start.12 = (f32[256,256]{1,0:T(8,128)S(1)}, f32[256,256]{1,0:T(8,128)S(1)}, u32[]{:S(2)}, u32[]{:S(2)}) collective-permute-start(f32[256,256]{1,0:T(8,128)S(1)} %shard_map.93.refs_3_.refs_2_.refs_1_), channel_id=1, source_target_pairs={{0,32},{32,64},{64,96},{1,33},{33,65},{65,97},{2,34},{34,66},{66,9... | collective-permute-start | bytes 786440 | tf_op jit(solution)/shard_map/ppermute | solution.py:159
  91.3 10.6 %collective-permute-start.15 = (f32[256,256]{1,0:T(8,128)S(1)}, f32[256,256]{1,0:T(8,128)S(1)}, u32[]{:S(2)}, u32[]{:S(2)}) collective-permute-start(f32[256,256]{1,0:T(8,128)S(1)} %shard_map.95.refs_3_.refs_2_), channel_id=1, source_target_pairs={{0,32},{32,64},{64,96},{1,33},{33,65},{65,97},{2,34},{34,66},{66,9... | collective-permute-start | bytes 786440 | tf_op jit(solution)/shard_map/ppermute | solution.py:159
  94.0 11.7 %collective-permute-start.14 = (f32[256,256]{1,0:T(8,128)S(1)}, f32[256,256]{1,0:T(8,128)S(1)}, u32[]{:S(2)}, u32[]{:S(2)}) collective-permute-start(f32[256,256]{1,0:T(8,128)S(1)} %shard_map.97.refs_3_.refs_2_), channel_id=1, source_target_pairs={{0,32},{32,64},{64,96},{1,33},{33,65},{65,97},{2,34},{34,66},{66,9... | collective-permute-start | bytes 786440 | tf_op jit(solution)/shard_map/ppermute | solution.py:159
  109.5 6.0 %collective-permute-start.16 = (f32[2,4,4,3,32,256]{5,4,3,2,1,0:T(8,128)S(1)}, f32[2,4,4,3,32,256]{5,4,3,2,1,0:T(8,128)S(1)}, u32[]{:S(2)}, u32[]{:S(2)}) collective-permute-start(f32[2,4,4,3,32,256]{5,4,3,2,1,0:T(8,128)S(1)} %slice_bitcast_fusion), channel_id=1, source_target_pairs={{0,1},{1,0},{2,3},{3,2},{4,5},{5,4},{6,7},{7,6},{8,9},{9,8},{10,11... | collective-permute-start | bytes 9437192 | tf_op jit(solution)/shard_map/ppermute | solution.py:138
  116.9 8.2 %collective-permute-start.17 = (f32[2,96,256]{2,1,0:T(8,128)S(1)}, f32[2,96,256]{2,1,0:T(8,128)S(1)}, u32[]{:S(2)}, u32[]{:S(2)}) collective-permute-start(f32[2,96,256]{2,1,0:T(8,128)S(1)} %get-tuple-element.11), channel_id=1, source_target_pairs={{0,2},{2,4},{4,6},{6,0},{1,3},{3,5},{5,7},{7,1},{8,10},{10,12},{12... | collective-permute-start | bytes 589832 | tf_op jit(solution)/shard_map/ppermute | solution.py:122
  118.4 6.7 %collective-permute-start.19 = (f32[2,96,256]{2,1,0:T(8,128)S(1)}, f32[2,96,256]{2,1,0:T(8,128)S(1)}, u32[]{:S(2)}, u32[]{:S(2)}) collective-permute-start(f32[2,96,256]{2,1,0:T(8,128)S(1)} %get-tuple-element.12), channel_id=1, source_target_pairs={{0,6},{2,0},{4,2},{6,4},{1,7},{3,1},{5,3},{7,5},{8,14},{10,8},{12,... | collective-permute-start | bytes 589832 | tf_op jit(solution)/shard_map/ppermute | solution.py:122
  120.2 8.7 %collective-permute-start.24 = (f32[2,96,256]{2,1,0:T(8,128)S(1)}, f32[2,96,256]{2,1,0:T(8,128)S(1)}, u32[]{:S(2)}, u32[]{:S(2)}) collective-permute-start(f32[2,96,256]{2,1,0:T(8,128)S(1)} %get-tuple-element.17), channel_id=1, source_target_pairs={{0,8},{8,16},{16,24},{24,0},{1,9},{9,17},{17,25},{25,1},{2,10},{10... | collective-permute-start | bytes 589832 | tf_op jit(solution)/shard_map/ppermute | solution.py:122
  122.2 6.8 %collective-permute-start.26 = (f32[2,96,256]{2,1,0:T(8,128)S(1)}, f32[2,96,256]{2,1,0:T(8,128)S(1)}, u32[]{:S(2)}, u32[]{:S(2)}) collective-permute-start(f32[2,96,256]{2,1,0:T(8,128)S(1)} %get-tuple-element.18), channel_id=1, source_target_pairs={{0,24},{8,0},{16,8},{24,16},{1,25},{9,1},{17,9},{25,17},{2,26},{10... | collective-permute-start | bytes 589832 | tf_op jit(solution)/shard_map/ppermute | solution.py:122
  125.2 11.6 %collective-permute-start.18 = (f32[4,96,256]{2,1,0:T(8,128)S(1)}, f32[4,96,256]{2,1,0:T(8,128)S(1)}, u32[]{:S(2)}, u32[]{:S(2)}) collective-permute-start(f32[4,96,256]{2,1,0:T(8,128)S(1)} %pad_maximum_fusion), channel_id=1, source_target_pairs={{0,2},{2,4},{4,6},{6,0},{1,3},{3,5},{5,7},{7,1},{8,10},{10,12},{12... | collective-permute-start | bytes 1179656 | tf_op jit(solution)/shard_map/ppermute | solution.py:122
  126.8 10.0 %collective-permute-start.20 = (f32[4,96,256]{2,1,0:T(8,128)S(1)}, f32[4,96,256]{2,1,0:T(8,128)S(1)}, u32[]{:S(2)}, u32[]{:S(2)}) collective-permute-start(f32[4,96,256]{2,1,0:T(8,128)S(1)} %pad_maximum_fusion.1), channel_id=1, source_target_pairs={{0,6},{2,0},{4,2},{6,4},{1,7},{3,1},{5,3},{7,5},{8,14},{10,8},{12,... | collective-permute-start | bytes 1179656 | tf_op jit(solution)/shard_map/ppermute | solution.py:122
  129.1 13.8 %collective-permute-start.25 = (f32[4,96,256]{2,1,0:T(8,128)S(1)}, f32[4,96,256]{2,1,0:T(8,128)S(1)}, u32[]{:S(2)}, u32[]{:S(2)}) collective-permute-start(f32[4,96,256]{2,1,0:T(8,128)S(1)} %pad_maximum_fusion.2), channel_id=1, source_target_pairs={{0,8},{8,16},{16,24},{24,0},{1,9},{9,17},{17,25},{25,1},{2,10},{10... | collective-permute-start | bytes 1179656 | tf_op jit(solution)/shard_map/ppermute | solution.py:122
  130.7 12.2 %collective-permute-start.27 = (f32[4,96,256]{2,1,0:T(8,128)S(1)}, f32[4,96,256]{2,1,0:T(8,128)S(1)}, u32[]{:S(2)}, u32[]{:S(2)}) collective-permute-start(f32[4,96,256]{2,1,0:T(8,128)S(1)} %pad_maximum_fusion.3), channel_id=1, source_target_pairs={{0,24},{8,0},{16,8},{24,16},{1,25},{9,1},{17,9},{25,17},{2,26},{10... | collective-permute-start | bytes 1179656 | tf_op jit(solution)/shard_map/ppermute | solution.py:122
  136.9 9.4 %collective-permute-start.21 = (f32[96,256]{1,0:T(8,128)S(1)}, f32[96,256]{1,0:T(8,128)S(1)}, u32[]{:S(2)}, u32[]{:S(2)}) collective-permute-start(f32[96,256]{1,0:T(8,128)S(1)} %get-tuple-element.23), channel_id=1, source_target_pairs={{0,8},{8,16},{16,24},{24,0},{1,9},{9,17},{17,25},{25,1},{2,10},{10... | collective-permute-start | bytes 294920 | tf_op jit(solution)/shard_map/ppermute | solution.py:122
  138.9 8.9 %collective-permute-start.22 = (f32[96,256]{1,0:T(8,128)S(1)}, f32[96,256]{1,0:T(8,128)S(1)}, u32[]{:S(2)}, u32[]{:S(2)}) collective-permute-start(f32[96,256]{1,0:T(8,128)S(1)} %get-tuple-element.22), channel_id=1, source_target_pairs={{0,24},{8,0},{16,8},{24,16},{1,25},{9,1},{17,9},{25,17},{2,26},{10... | collective-permute-start | bytes 294920 | tf_op jit(solution)/shard_map/ppermute | solution.py:122
  141.1 6.8 %collective-permute-start.23 = (f32[96,256]{1,0:T(8,128)S(1)}, f32[96,256]{1,0:T(8,128)S(1)}, u32[]{:S(2)}, u32[]{:S(2)}) collective-permute-start(f32[96,256]{1,0:T(8,128)S(1)} %get-tuple-element.21), channel_id=1, source_target_pairs={{0,16},{8,24},{16,0},{24,8},{1,17},{9,25},{17,1},{25,9},{2,18},{10... | collective-permute-start | bytes 294920 | tf_op jit(solution)/shard_map/ppermute | solution.py:122
  143.0 6.5 %collective-permute-start.28 = (f32[96,256]{1,0:T(8,128)S(1)}, f32[96,256]{1,0:T(8,128)S(1)}, u32[]{:S(2)}, u32[]{:S(2)}) collective-permute-start(f32[96,256]{1,0:T(8,128)S(1)} %get-tuple-element.26), channel_id=1, source_target_pairs={{0,2},{2,4},{4,6},{6,0},{1,3},{3,5},{5,7},{7,1},{8,10},{10,12},{12... | collective-permute-start | bytes 294920 | tf_op jit(solution)/shard_map/ppermute | solution.py:122
  144.1 5.5 %collective-permute-start.29 = (f32[96,256]{1,0:T(8,128)S(1)}, f32[96,256]{1,0:T(8,128)S(1)}, u32[]{:S(2)}, u32[]{:S(2)}) collective-permute-start(f32[96,256]{1,0:T(8,128)S(1)} %get-tuple-element.25), channel_id=1, source_target_pairs={{0,6},{2,0},{4,2},{6,4},{1,7},{3,1},{5,3},{7,5},{8,14},{10,8},{12,... | collective-permute-start | bytes 294920 | tf_op jit(solution)/shard_map/ppermute | solution.py:122
  146.3 6.1 %collective-permute-start.30 = (f32[96,256]{1,0:T(8,128)S(1)}, f32[96,256]{1,0:T(8,128)S(1)}, u32[]{:S(2)}, u32[]{:S(2)}) collective-permute-start(f32[96,256]{1,0:T(8,128)S(1)} %get-tuple-element.24), channel_id=1, source_target_pairs={{0,4},{2,6},{4,0},{6,2},{1,5},{3,7},{5,1},{7,3},{8,12},{10,14},{12... | collective-permute-start | bytes 294920 | tf_op jit(solution)/shard_map/ppermute | solution.py:122

commit v6 on v5

--- a/solution.py
+++ b/solution.py
@@ -39,7 +39,7 @@
 LOCAL = pl.BlockSpec(memory_space=pltpu.VMEM)
 FAR = pl.BlockSpec(memory_space=pltpu.HBM)
 GRANT = pltpu.CompilerParams(vmem_limit_bytes=8 * 2**20)
-BUFFER = jax.ShapeDtypeStruct((2, 2, 4, 4, 3, ROWS, W), f32)
+EARLY = 9
 
 
 def update_part(q, ints, floats, arrived, previous, left, mps):
@@ -60,7 +60,7 @@
 
 
 def apply_part(q, ints, floats, environs, psi, rights, pieces, results, stores):
-    site, my_z, my_x, core = ints[0], ints[1], ints[2], ints[3]
+    site, my_x, core = ints[0], ints[2], ints[3]
     e = environs[0][...]
     for k in range(1, SITES):
         e = jnp.where(site == k, environs[k][...], e)
@@ -77,12 +77,11 @@
             results[state] = jnp.zeros((W, W), f32)
         for i in range(W // ROWS):
             owner, third = divmod((W // ROWS) * q + i, 3)
-            z = (owner // 8 - my_z + 4) % 4
+            group = owner // 8 if q < EARLY else 0
             x = ((owner // 2) % 4 - my_x + 4) % 4
             sent = core if owner % 2 == 0 else 1 - core
-            near, far = ((x, z), (z, x))[state]
             pltpu.make_async_copy(
-                results.at[state, pl.ds(ROWS * i, ROWS)], pieces.at[sent, state, near, far, third], stores).start()
+                results.at[state, pl.ds(ROWS * i, ROWS)], pieces.at[sent, state, group, x, third], stores).start()
     pltpu.make_async_copy(results, psi.at[:, 0], stores).wait()
 
 
@@ -111,9 +110,9 @@
         kernel,
         in_specs=[SCALAR] * 2 + [LOCAL] * len(operands) + [FAR] * len(held),
         out_specs=[FAR],
-        out_shape=[BUFFER],
+        out_shape=[jax.ShapeDtypeStruct((2, 2, 3 if q < EARLY else 1, 4, 3, ROWS, W), f32)],
         scratch_shapes=[pltpu.VMEM((2, W, W), f32), pltpu.SemaphoreType.DMA],
-        input_output_aliases={2 + len(operands): 0} if held else {},
+        input_output_aliases={2 + len(operands): 0} if q not in (0, EARLY) else {},
         compiler_params=GRANT,
     )(ints, floats, *operands, *held)
 
@@ -131,12 +130,34 @@
 
 
 def second_phase(line, axis):
-    return (line[0] + turned(line[1], axis, 1)) + (turned(line[3], axis, -1) + turned(line[2], axis, 2))
-
-
-def reduced(pieces):
-    both = pieces[0] + lax.ppermute(pieces[1], "core", [(0, 1), (1, 0)])
-    both = both.reshape(2, 4, 4, 96, W)
+    even = lax.axis_index(axis) % 2 == 0
+    given = jnp.stack([jnp.where(even, line[1], line[3]), line[2]])
+    taken = lax.ppermute(given, axis, [(i, i ^ 1) for i in range(4)])
+    rest = jnp.where(even, line[3], line[1]) + taken[1]
+    return (line[0] + taken[0]) + lax.ppermute(rest, axis, [(i, i ^ 3) for i in range(4)])
+
+
+def combine_kernel(ints, early, early_got, late, late_got, out):
+    for group in range(4):
+        z = (group - ints[1] + 4) % 4
+        own, got, g = (early, early_got, group) if group < 3 else (late, late_got, 0)
+        for x in range(4):
+            out[0, x, z] = own[0, 0, g, x] + got[0, g, x]
+            out[1, z, x] = own[0, 1, g, x] + got[1, g, x]
+
+
+def swapped(pieces):
+    return lax.ppermute(pieces[1], "core", [(0, 1), (1, 0)])
+
+
+def reduced(ints, early, early_got, late, late_got):
+    shape = (4, 96, W)
+    parts = (early.reshape(2, 2, 3, *shape), early_got.reshape(2, 3, *shape),
+             late.reshape(2, 2, 1, *shape), late_got.reshape(2, 1, *shape))
+    both = pl.pallas_call(
+        combine_kernel, in_specs=[SCALAR] + [LOCAL] * 4, out_specs=LOCAL,
+        out_shape=jax.ShapeDtypeStruct((2, 4) + shape, f32), compiler_params=GRANT, name="combine",
+    )(ints, *parts)
     first = first_phase(both[0], "x")
     second = first_phase(both[1], "z")
     return jnp.stack([second_phase(first, "z"), second_phase(second, "x")])[None]
@@ -159,9 +180,12 @@
             arrivals[step + LAG] = lax.ppermute(environ, "site", [(0, 1), (1, 2), (2, 3)])
         q = step - LAG * (SITES - 1)
         if q >= 0:
+            if q == EARLY:
+                early = held
+                early_got = swapped(early[0])
             held = apply_step(
                 q, ints, floats, [environs[q + LAG * k] for k in range(SITES)], psi[0], right_env[0, 0], held)
-    return reduced(*held)
+    return reduced(ints, early[0], early_got, held[0], swapped(held[0]))
 
 
 def solution(mesh):

time: 154 us -> 169 us (1.097)
  waiting for transfers between devices: 46.6 us -> 64.6 us
  starting transfers between devices: 47.1 us -> 39.8 us
  other arithmetic: 2.08 us -> 5.51 us
    ppermute x14 -> x8, starting transfers between devices: 25.5 us -> 14.5 us  [turned(): return lax.ppermute(x, axis, [(i, (i + by) % 4) for i in range(4)])]
    ppermute x16, waiting for transfers between devices: 31.5 us -> 39.7 us  [shards(): lax.ppermute(environ, 'site', [(0, 1), (1, 2), (2, 3)])]
    ppermute x1 -> x6, waiting for transfers between devices: 5.65 us -> 13.3 us  [the longest x2 5.79 us: second_phase(): lax.ppermute(rest, axis, [(i, i ^ 3) for i in range(4)])]
    ppermute x1 -> x6, starting transfers between devices: 0.31 us -> 3.95 us  [the longest x2 3.11 us: second_phase(): lax.ppermute(rest, axis, [(i, i ^ 3) for i in range(4)])]
    ppermute x14 -> x8, waiting for transfers between devices: 9.42 us -> 11.7 us  [turned(): return lax.ppermute(x, axis, [(i, (i + by) % 4) for i in range(4)])]
    unnamed x18 -> x20, local copies, waits for them, and re-layouts: 5.36 us -> 5.37 us
  transfers between devices with their start and end apart: 31 -> 30, of which waited for: 20 -> 22; matrix products, arithmetic and copies ran while one was open for 0% -> 2% of each run, Pallas kernels for 30% -> 27%
where the time goes in v6:
time: 169 us; the launch traced here: 168 us
  waiting for transfers between devices  64.6 us (38%)
  Pallas kernels  50.5 us (30%)
  starting transfers between devices  39.8 us (24%)
  local copies, waits for them, and re-layouts  6.91 us (4%)
  other arithmetic  5.51 us (3%)
    ppermute x16, waiting for transfers between devices, shards(): lax.ppermute(environ, 'site', [(0, 1), (1, 2), (2, 3)])  39.7 us
    pallas_call x12, Pallas kernels, apply_step(): pl.pallas_call(kernel, in_specs=[SCALAR] * 2 + [LOCAL] * len(operands) +...  28.9 us
    ppermute x16, starting transfers between devices, shards(): lax.ppermute(environ, 'site', [(0, 1), (1, 2), (2, 3)])  21.4 us
    pallas_call x18, Pallas kernels, update_step(): pl.pallas_call(kernel, in_specs=[SCALAR] * 2 + [LOCAL] * 4 + [FAR] * len(...  20.7 us
    ppermute x8, starting transfers between devices, turned(): return lax.ppermute(x, axis, [(i, (i + by) % 4) for i in range(4)])  14.5 us
    ppermute x8, waiting for transfers between devices, turned(): return lax.ppermute(x, axis, [(i, (i + by) % 4) for i in range(4)])  11.7 us
    ppermute x2, waiting for transfers between devices, second_phase(): lax.ppermute(rest, axis, [(i, i ^ 3) for i in range(4)])  5.79 us
    unnamed x20, local copies, waits for them, and re-layouts  5.37 us
  transfers between devices with their start and end apart: 30, of which 22 were waited for; matrix products, arithmetic and copies ran while one was open for 2% of the time, Pallas kernels for 27%

profile of v6, /device:TPU:24, one launch (start us, length us, event | category | flops | bytes accessed | tf_op | source)
XLA Modules:
  0.0 168.0 jit_solution(1143267691726405216)
XLA Ops:
  0.8 2.8 %copy-done = f32[1,2,12,256,256]{4,3,2,1,0:T(8,128)S(1)} copy-done((f32[1,2,12,256,256]{4,3,2,1,0:T(8,128)S(1)}, f32[1,2,12,256,256]{4,3,2,1,0:T(8,128)}, u32[]{:S(2)}) %copy-start) | copy-done | bytes 6291480
  3.6 1.9 %copy-done.1 = f32[1,12,256,256]{3,2,1,0:T(8,128)S(1)} copy-done((f32[1,12,256,256]{3,2,1,0:T(8,128)S(1)}, f32[1,12,256,256]{3,2,1,0:T(8,128)}, u32[]{:S(2)}) %copy-start.1) | copy-done | bytes 3145752
  8.6 1.6 collective-permute-start.2
  10.1 7.6 %collective-permute-done.arrived.previous = f32[256,256]{1,0:T(8,128)S(1)} collective-permute-done((f32[256,256]{1,0:T(8,128)S(1)}, f32[256,256]{1,0:T(8,128)S(1)}, u32[]{:S(2)}, u32[]{:S(2)}) %collective-permute-start) | collective-permute-done | bytes 262176 | tf_op jit(solution)/shard_map/ppermute | solution.py:180
  19.6 3.8 %collective-permute-done.2.previous.arrived = f32[256,256]{1,0:T(8,128)S(1)} collective-permute-done((f32[256,256]{1,0:T(8,128)S(1)}, f32[256,256]{1,0:T(8,128)S(1)}, u32[]{:S(2)}, u32[]{:S(2)}) %collective-permute-start.2) | collective-permute-done | bytes 262176 | tf_op jit(solution)/shard_map/ppermute | solution.py:180
  25.2 4.1 %collective-permute-done.1.arrived.previous = f32[256,256]{1,0:T(8,128)S(1)} collective-permute-done((f32[256,256]{1,0:T(8,128)S(1)}, f32[256,256]{1,0:T(8,128)S(1)}, u32[]{:S(2)}, u32[]{:S(2)}) %collective-permute-start.1) | collective-permute-done | bytes 262176 | tf_op jit(solution)/shard_map/ppermute | solution.py:180
  31.2 3.8 %collective-permute-done.4.previous.arrived = f32[256,256]{1,0:T(8,128)S(1)} collective-permute-done((f32[256,256]{1,0:T(8,128)S(1)}, f32[256,256]{1,0:T(8,128)S(1)}, u32[]{:S(2)}, u32[]{:S(2)}) %collective-permute-start.4) | collective-permute-done | bytes 262176 | tf_op jit(solution)/shard_map/ppermute | solution.py:180
  35.6 1.6 collective-permute-start.6
  37.1 3.6 %collective-permute-done.3.arrived.previous = f32[256,256]{1,0:T(8,128)S(1)} collective-permute-done((f32[256,256]{1,0:T(8,128)S(1)}, f32[256,256]{1,0:T(8,128)S(1)}, u32[]{:S(2)}, u32[]{:S(2)}) %collective-permute-start.3) | collective-permute-done | bytes 262176 | tf_op jit(solution)/shard_map/ppermute | solution.py:180
  40.8 1.4 shard_map.78.refs_3_.refs_2_.refs_1_.refs_0_
  43.6 2.4 %shard_map.80.rest_0_.refs_6_ = f32[2,2,3,4,3,32,256]{6,5,4,3,2,1,0:T(8,128)S(1)} custom-call(s32[28]{0:T(128)S(1)} %concatenate.15.ints, f32[4]{0:T(128)S(1)} %bitcast.163, f32[256,256]{1,0:T(8,128)S(1)} %shard_map.73.refs_0_, f32[256,256]{1,0:T(8,128)S(1)} %shard_map.74.refs_1_.refs_0_, f32[256,256]{1,0:T(8,128)S(1)} %shard_map.76.refs_2_.refs_1_.refs_0_, ...), custom_call_target="tpu_custom_call" | custom-call | tf_op jit(solution)/shard_map/pallas_call | solution.py:109
  46.2 1.4 shard_map.81.refs_3_.refs_2_.refs_1_.refs_0_
  48.9 2.5 %shard_map.82.rest_0_.refs_6_ = f32[2,2,3,4,3,32,256]{6,5,4,3,2,1,0:T(8,128)S(1)} custom-call(s32[28]{0:T(128)S(1)} %concatenate.15.ints, f32[4]{0:T(128)S(1)} %bitcast.165, f32[256,256]{1,0:T(8,128)S(1)} %shard_map.75.refs_0_, f32[256,256]{1,0:T(8,128)S(1)} %shard_map.77.refs_1_.refs_0_, ...), custom_call_target="tpu_custom_call", output_to_operand_aliasing={{}: (8, {})} | custom-call | tf_op jit(solution)/shard_map/pallas_call | solution.py:109
  54.6 2.4 %shard_map.84.rest_0_.refs_6_ = f32[2,2,3,4,3,32,256]{6,5,4,3,2,1,0:T(8,128)S(1)} custom-call(s32[28]{0:T(128)S(1)} %concatenate.15.ints, f32[4]{0:T(128)S(1)} %bitcast.167, f32[256,256]{1,0:T(8,128)S(1)} %shard_map.74.refs_1_.refs_0_, f32[256,256]{1,0:T(8,128)S(1)} %shard_map.76.refs_2_.refs_1_.refs_0_, ...), custom_call_target="tpu_custom_call", output_to_operand_aliasing={{}: (8, {})} | custom-call | tf_op jit(solution)/shard_map/pallas_call | solution.py:109
  57.8 1.4 shard_map.85.refs_3_.refs_2_.refs_1_.refs_0_
  60.6 2.5 %shard_map.86.rest_0_.refs_6_ = f32[2,2,3,4,3,32,256]{6,5,4,3,2,1,0:T(8,128)S(1)} custom-call(s32[28]{0:T(128)S(1)} %concatenate.15.ints, f32[4]{0:T(128)S(1)} %bitcast.169, f32[256,256]{1,0:T(8,128)S(1)} %shard_map.77.refs_1_.refs_0_, f32[256,256]{1,0:T(8,128)S(1)} %shard_map.79.refs_2_.refs_1_.refs_0_, ...), custom_call_target="tpu_custom_call", output_to_operand_aliasing={{}: (8, {})} | custom-call | tf_op jit(solution)/shard_map/pallas_call | solution.py:109
  63.7 1.5 shard_map.87.refs_3_.refs_2_.refs_1_.refs_0_
  65.2 1.5 collective-permute-start.9
  66.7 2.5 %shard_map.88.rest_0_.refs_6_ = f32[2,2,3,4,3,32,256]{6,5,4,3,2,1,0:T(8,128)S(1)} custom-call(s32[28]{0:T(128)S(1)} %concatenate.15.ints, f32[4]{0:T(128)S(1)} %bitcast.171, f32[256,256]{1,0:T(8,128)S(1)} %shard_map.76.refs_2_.refs_1_.refs_0_, f32[256,256]{1,0:T(8,128)S(1)} %shard_map.78.refs_3_.refs_2_.refs_1_.refs_0_, ...), custom_call_target="tpu_custom_call", output_to_operand_aliasing={{}: (8, {})} | custom-call | tf_op jit(solution)/shard_map/pallas_call | solution.py:109
  69.5 1.4 shard_map.89.refs_3_.refs_2_.refs_1_.refs_0_
  71.0 2.5 %shard_map.90.rest_0_.refs_6_ = f32[2,2,3,4,3,32,256]{6,5,4,3,2,1,0:T(8,128)S(1)} custom-call(s32[28]{0:T(128)S(1)} %concatenate.15.ints, f32[4]{0:T(128)S(1)} %bitcast.173, f32[256,256]{1,0:T(8,128)S(1)} %shard_map.79.refs_2_.refs_1_.refs_0_, f32[256,256]{1,0:T(8,128)S(1)} %shard_map.81.refs_3_.refs_2_.refs_1_.refs_0_, ...), custom_call_target="tpu_custom_call", output_to_operand_aliasing={{}: (8, {})} | custom-call | tf_op jit(solution)/shard_map/pallas_call | solution.py:109
  74.8 1.4 shard_map.91.refs_3_.refs_2_.refs_1_
  77.6 2.5 %shard_map.92.rest_0_.refs_6_ = f32[2,2,3,4,3,32,256]{6,5,4,3,2,1,0:T(8,128)S(1)} custom-call(s32[28]{0:T(128)S(1)} %concatenate.15.ints, f32[4]{0:T(128)S(1)} %bitcast.175, f32[256,256]{1,0:T(8,128)S(1)} %shard_map.78.refs_3_.refs_2_.refs_1_.refs_0_, f32[256,256]{1,0:T(8,128)S(1)} %shard_map.83.refs_3_.refs_2_.refs_1_.refs_0_, ...), custom_call_target="tpu_custom_call", output_to_operand_aliasing={{}: (8, {})} | custom-call | tf_op jit(solution)/shard_map/pallas_call | solution.py:109
  80.0 4.2 %collective-permute-done.12.arrived.previous = f32[256,256]{1,0:T(8,128)S(1)} collective-permute-done((f32[256,256]{1,0:T(8,128)S(1)}, f32[256,256]{1,0:T(8,128)S(1)}, u32[]{:S(2)}, u32[]{:S(2)}) %collective-permute-start.12) | collective-permute-done | bytes 262176 | tf_op jit(solution)/shard_map/ppermute | solution.py:180
  84.3 1.4 shard_map.93.refs_3_.refs_2_.refs_1_
  85.7 2.5 %shard_map.94.rest_0_.refs_6_ = f32[2,2,3,4,3,32,256]{6,5,4,3,2,1,0:T(8,128)S(1)} custom-call(s32[28]{0:T(128)S(1)} %concatenate.15.ints, f32[4]{0:T(128)S(1)} %bitcast.177, f32[256,256]{1,0:T(8,128)S(1)} %shard_map.81.refs_3_.refs_2_.refs_1_.refs_0_, f32[256,256]{1,0:T(8,128)S(1)} %shard_map.85.refs_3_.refs_2_.refs_1_.refs_0_, ...), custom_call_target="tpu_custom_call", output_to_operand_aliasing={{}: (8, {})} | custom-call | tf_op jit(solution)/shard_map/pallas_call | solution.py:109
  88.2 1.5 shard_map.95.refs_3_.refs_2_
  89.6 2.5 %shard_map.96.rest_0_.refs_6_ = f32[2,2,3,4,3,32,256]{6,5,4,3,2,1,0:T(8,128)S(1)} custom-call(s32[28]{0:T(128)S(1)} %concatenate.15.ints, f32[4]{0:T(128)S(1)} %bitcast.179, f32[256,256]{1,0:T(8,128)S(1)} %shard_map.83.refs_3_.refs_2_.refs_1_.refs_0_, f32[256,256]{1,0:T(8,128)S(1)} %shard_map.87.refs_3_.refs_2_.refs_1_.refs_0_, ...), custom_call_target="tpu_custom_call", output_to_operand_aliasing={{}: (8, {})} | custom-call | tf_op jit(solution)/shard_map/pallas_call | solution.py:109
  95.1 8.5 %collective-permute-done.14.arrived.previous = f32[256,256]{1,0:T(8,128)S(1)} collective-permute-done((f32[256,256]{1,0:T(8,128)S(1)}, f32[256,256]{1,0:T(8,128)S(1)}, u32[]{:S(2)}, u32[]{:S(2)}) %collective-permute-start.14) | collective-permute-done | bytes 262176 | tf_op jit(solution)/shard_map/ppermute | solution.py:180
  103.6 1.4 shard_map.97.refs_3_.refs_2_
  106.3 2.5 %shard_map.98.rest_0_.refs_6_ = f32[2,2,1,4,3,32,256]{6,5,4,3,2,1,0:T(8,128)S(1)} custom-call(s32[28]{0:T(128)S(1)} %concatenate.15.ints, f32[4]{0:T(128)S(1)} %bitcast.181, f32[256,256]{1,0:T(8,128)S(1)} %shard_map.85.refs_3_.refs_2_.refs_1_.refs_0_, f32[256,256]{1,0:T(8,128)S(1)} %shard_map.89.refs_3_.refs_2_.refs_1_.refs_0_, ...), custom_call_target="tpu_custom_call" | custom-call | tf_op jit(solution)/shard_map/pallas_call | solution.py:109
  108.8 1.4 shard_map.99.refs_3_
  110.3 2.5 %shard_map.100.rest_0_.refs_6_ = f32[2,2,1,4,3,32,256]{6,5,4,3,2,1,0:T(8,128)S(1)} custom-call(s32[28]{0:T(128)S(1)} %concatenate.15.ints, f32[4]{0:T(128)S(1)} %bitcast.183, f32[256,256]{1,0:T(8,128)S(1)} %shard_map.87.refs_3_.refs_2_.refs_1_.refs_0_, f32[256,256]{1,0:T(8,128)S(1)} %shard_map.91.refs_3_.refs_2_.refs_1_, ...), custom_call_target="tpu_custom_call", output_to_operand_aliasing={{}: (8, {})} | custom-call | tf_op jit(solution)/shard_map/pallas_call | solution.py:109
  112.7 1.6 collective-permute-done.15.arrived
  115.8 1.9 %shard_map.102 = f32[2,2,1,4,3,32,256]{6,5,4,3,2,1,0:T(8,128)S(1)} custom-call(s32[28]{0:T(128)S(1)} %concatenate.15.ints, f32[4]{0:T(128)S(1)} %bitcast.185, f32[256,256]{1,0:T(8,128)S(1)} %shard_map.89.refs_3_.refs_2_.refs_1_.refs_0_, f32[256,256]{1,0:T(8,128)S(1)} %shard_map.93.refs_3_.refs_2_.refs_1_, ...), custom_call_target="tpu_custom_call", output_to_operand_aliasing={{}: (8, {})} | custom-call | tf_op jit(solution)/shard_map/pallas_call | solution.py:109
  118.0 2.3 %collective-permute-done.17 = f32[2,1,4,3,32,256]{5,4,3,2,0,1:T(8,128)S(1)} collective-permute-done((f32[2,1,4,3,32,256]{5,4,3,2,0,1:T(8,128)S(1)}, f32[2,1,4,3,32,256]{5,4,3,2,0,1:T(8,128)S(1)}, u32[]{:S(2)}, u32[]{:S(2)}) %collective-permute-start.17) | collective-permute-done | bytes 786464 | tf_op jit(solution)/shard_map/ppermute | solution.py:150
  121.6 1.6 collective-permute-start.18
  123.1 1.7 %collective-permute-start.20 = (f32[2,96,256]{2,1,0:T(8,128)S(1)}, f32[2,96,256]{2,1,0:T(8,128)S(1)}, u32[]{:S(2)}, u32[]{:S(2)}) collective-permute-start(f32[2,96,256]{2,1,0:T(8,128)S(1)} %get-tuple-element.12), channel_id=1, source_target_pairs={{0,6},{2,0},{4,2},{6,4},{1,7},{3,1},{5,3},{7,5},{8,14},{10,8},{12,... | collective-permute-start | bytes 589832 | tf_op jit(solution)/shard_map/ppermute | solution.py:121
  124.9 2.0 %collective-permute-start.24 = (f32[2,96,256]{2,1,0:T(8,128)S(1)}, f32[2,96,256]{2,1,0:T(8,128)S(1)}, u32[]{:S(2)}, u32[]{:S(2)}) collective-permute-start(f32[2,96,256]{2,1,0:T(8,128)S(1)} %get-tuple-element.17), channel_id=1, source_target_pairs={{0,8},{8,16},{16,24},{24,0},{1,9},{9,17},{17,25},{25,1},{2,10},{10... | collective-permute-start | bytes 589832 | tf_op jit(solution)/shard_map/ppermute | solution.py:121
  126.9 2.2 %collective-permute-start.26 = (f32[2,96,256]{2,1,0:T(8,128)S(1)}, f32[2,96,256]{2,1,0:T(8,128)S(1)}, u32[]{:S(2)}, u32[]{:S(2)}) collective-permute-start(f32[2,96,256]{2,1,0:T(8,128)S(1)} %get-tuple-element.18), channel_id=1, source_target_pairs={{0,24},{8,0},{16,8},{24,16},{1,25},{9,1},{17,9},{25,17},{2,26},{10... | collective-permute-start | bytes 589832 | tf_op jit(solution)/shard_map/ppermute | solution.py:121
  130.7 3.0 %collective-permute-start.21 = (f32[4,96,256]{2,1,0:T(8,128)}, f32[4,96,256]{2,1,0:T(8,128)S(1)}, u32[]{:S(2)}, u32[]{:S(2)}) collective-permute-start(f32[4,96,256]{2,1,0:T(8,128)} %pad_maximum_fusion.1), channel_id=1, source_target_pairs={{0,6},{2,0},{4,2},{6,4},{1,7},{3,1},{5,3},{7,5},{8,14},{10,8},{12,... | collective-permute-start | bytes 1179656 | tf_op jit(solution)/shard_map/ppermute | solution.py:121
  135.3 4.0 %collective-permute-start.27 = (f32[4,96,256]{2,1,0:T(8,128)}, f32[4,96,256]{2,1,0:T(8,128)}, u32[]{:S(2)}, u32[]{:S(2)}) collective-permute-start(f32[4,96,256]{2,1,0:T(8,128)} %pad_maximum_fusion.3), channel_id=1, source_target_pairs={{0,24},{8,0},{16,8},{24,16},{1,25},{9,1},{17,9},{25,17},{2,26},{10... | collective-permute-start | bytes 1179656 | tf_op jit(solution)/shard_map/ppermute | solution.py:121
  141.5 4.2 %collective-permute-done.19 = f32[4,96,256]{2,1,0:T(8,128)} collective-permute-done((f32[4,96,256]{2,1,0:T(8,128)}, f32[4,96,256]{2,1,0:T(8,128)}, u32[]{:S(2)}, u32[]{:S(2)}) %collective-permute-start.19) | collective-permute-done | bytes 393248 | tf_op jit(solution)/shard_map/ppermute | solution.py:121
  146.9 4.2 %collective-permute-done.25 = f32[4,96,256]{2,1,0:T(8,128)} collective-permute-done((f32[4,96,256]{2,1,0:T(8,128)}, f32[4,96,256]{2,1,0:T(8,128)}, u32[]{:S(2)}, u32[]{:S(2)}) %collective-permute-start.25) | collective-permute-done | bytes 393248 | tf_op jit(solution)/shard_map/ppermute | solution.py:121
  153.0 5.3 %collective-permute-done.28 = f32[2,96,256]{2,1,0:T(8,128)S(1)} collective-permute-done((f32[2,96,256]{2,1,0:T(8,128)S(1)}, f32[2,96,256]{2,1,0:T(8,128)S(1)}, u32[]{:S(2)}, u32[]{:S(2)}) %collective-permute-start.28) | collective-permute-done | bytes 196640 | tf_op jit(solution)/shard_map/ppermute | solution.py:135
  158.3 3.0 %collective-permute-start.29 = (f32[96,256]{1,0:T(8,128)S(1)}, f32[96,256]{1,0:T(8,128)S(1)}, u32[]{:S(2)}, u32[]{:S(2)}) collective-permute-start(f32[96,256]{1,0:T(8,128)S(1)} %fusion.8), channel_id=1, source_target_pairs={{0,6},{2,4},{4,2},{6,0},{1,7},{3,5},{5,3},{7,1},{8,14},{10,12},{12... | collective-permute-start | bytes 294920 | tf_op jit(solution)/shard_map/ppermute | solution.py:137
  161.5 2.8 %collective-permute-done.29 = f32[96,256]{1,0:T(8,128)S(1)} collective-permute-done((f32[96,256]{1,0:T(8,128)S(1)}, f32[96,256]{1,0:T(8,128)S(1)}, u32[]{:S(2)}, u32[]{:S(2)}) %collective-permute-start.29) | collective-permute-done | bytes 98336 | tf_op jit(solution)/shard_map/ppermute | solution.py:137
  164.2 3.0 %collective-permute-done.23 = f32[96,256]{1,0:T(8,128)S(1)} collective-permute-done((f32[96,256]{1,0:T(8,128)S(1)}, f32[96,256]{1,0:T(8,128)S(1)}, u32[]{:S(2)}, u32[]{:S(2)}) %collective-permute-start.23) | collective-permute-done | bytes 98336 | tf_op jit(solution)/shard_map/ppermute | solution.py:137
  (88 shorter events, 38.2 us)
Async XLA Ops:
  0.8 2.8 %copy-start = (f32[1,2,12,256,256]{4,3,2,1,0:T(8,128)S(1)}, f32[1,2,12,256,256]{4,3,2,1,0:T(8,128)}, u32[]{:S(2)}) copy-start(f32[1,2,12,256,256]{4,3,2,1,0:T(8,128)} %param.9) | copy-start | bytes 18874372
  3.6 1.9 %copy-start.1 = (f32[1,12,256,256]{3,2,1,0:T(8,128)S(1)}, f32[1,12,256,256]{3,2,1,0:T(8,128)}, u32[]{:S(2)}) copy-start(f32[1,12,256,256]{3,2,1,0:T(8,128)} %param.7) | copy-start | bytes 9437188
  5.5 0.7 copy-start.4
  6.7 11.1 %collective-permute-start = (f32[256,256]{1,0:T(8,128)S(1)}, f32[256,256]{1,0:T(8,128)S(1)}, u32[]{:S(2)}, u32[]{:S(2)}) collective-permute-start(f32[256,256]{1,0:T(8,128)S(1)} %shard_map.73.refs_0_), channel_id=1, source_target_pairs={{0,32},{32,64},{64,96},{1,33},{33,65},{65,97},{2,34},{34,66},{66,9... | collective-permute-start | bytes 786440 | tf_op jit(solution)/shard_map/ppermute | solution.py:180
  8.0 15.4 %slice-start = ((s8[6291456]{0:T(1024)(128)(4,1)}), s8[4194304]{0:T(1024)(128)(4,1)S(1)}, s32[]{:S(2)}) async-start(s8[6291456]{0:T(1024)(128)(4,1)} %bitcast.91), calls=%async_computation | async-start | bytes 8388608
  8.5 14.8 %slice-start.1 = ((s8[6291456]{0:T(1024)(128)(4,1)}), s8[2097152]{0:T(1024)(128)(4,1)S(1)}, s32[]{:S(2)}) async-start(s8[6291456]{0:T(1024)(128)(4,1)} %bitcast.91), calls=%async_computation.1 | async-start | bytes 4194304
  8.6 14.8 %collective-permute-start.2 = (f32[256,256]{1,0:T(8,128)S(1)}, f32[256,256]{1,0:T(8,128)S(1)}, u32[]{:S(2)}, u32[]{:S(2)}) collective-permute-start(f32[256,256]{1,0:T(8,128)S(1)} %shard_map.75.refs_0_), channel_id=1, source_target_pairs={{0,32},{32,64},{64,96},{1,33},{33,65},{65,97},{2,34},{34,66},{66,9... | collective-permute-start | bytes 786440 | tf_op jit(solution)/shard_map/ppermute | solution.py:180
  18.3 11.1 %collective-permute-start.1 = (f32[256,256]{1,0:T(8,128)S(1)}, f32[256,256]{1,0:T(8,128)S(1)}, u32[]{:S(2)}, u32[]{:S(2)}) collective-permute-start(f32[256,256]{1,0:T(8,128)S(1)} %shard_map.74.refs_1_.refs_0_), channel_id=1, source_target_pairs={{0,32},{32,64},{64,96},{1,33},{33,65},{65,97},{2,34},{34,66},{66,9... | collective-permute-start | bytes 786440 | tf_op jit(solution)/shard_map/ppermute | solution.py:180
  23.9 11.1 %collective-permute-start.4 = (f32[256,256]{1,0:T(8,128)S(1)}, f32[256,256]{1,0:T(8,128)S(1)}, u32[]{:S(2)}, u32[]{:S(2)}) collective-permute-start(f32[256,256]{1,0:T(8,128)S(1)} %shard_map.77.refs_1_.refs_0_), channel_id=1, source_target_pairs={{0,32},{32,64},{64,96},{1,33},{33,65},{65,97},{2,34},{34,66},{66,9... | collective-permute-start | bytes 786440 | tf_op jit(solution)/shard_map/ppermute | solution.py:180
  29.9 10.9 %collective-permute-start.3 = (f32[256,256]{1,0:T(8,128)S(1)}, f32[256,256]{1,0:T(8,128)S(1)}, u32[]{:S(2)}, u32[]{:S(2)}) collective-permute-start(f32[256,256]{1,0:T(8,128)S(1)} %shard_map.76.refs_2_.refs_1_.refs_0_), channel_id=1, source_target_pairs={{0,32},{32,64},{64,96},{1,33},{33,65},{65,97},{2,34},{34,66},{66,9... | collective-permute-start | bytes 786440 | tf_op jit(solution)/shard_map/ppermute | solution.py:180
  35.0 8.5 %slice-start.2 = ((s8[6291456]{0:T(1024)(128)(4,1)}), s8[4194304]{0:T(1024)(128)(4,1)S(1)}, s32[]{:S(2)}) async-start(s8[6291456]{0:T(1024)(128)(4,1)} %bitcast.127), calls=%async_computation.2 | async-start | bytes 8388608
  35.6 8.0 %slice-start.3 = ((s8[6291456]{0:T(1024)(128)(4,1)}), s8[2097152]{0:T(1024)(128)(4,1)S(1)}, s32[]{:S(2)}) async-start(s8[6291456]{0:T(1024)(128)(4,1)} %bitcast.127), calls=%async_computation.3 | async-start | bytes 4194304
  35.6 8.0 %copy-start.3 = (f32[1,1,12,256,256]{4,3,2,1,0:T(8,128)S(1)}, f32[1,1,12,256,256]{4,3,2,1,0:T(8,128)}, u32[]{:S(2)}) copy-start(f32[1,1,12,256,256]{4,3,2,1,0:T(8,128)} %param.8) | copy-start | bytes 9437188
  35.6 10.6 %collective-permute-start.6 = (f32[256,256]{1,0:T(8,128)S(1)}, f32[256,256]{1,0:T(8,128)S(1)}, u32[]{:S(2)}, u32[]{:S(2)}) collective-permute-start(f32[256,256]{1,0:T(8,128)S(1)} %shard_map.79.refs_2_.refs_1_.refs_0_), channel_id=1, source_target_pairs={{0,32},{32,64},{64,96},{1,33},{33,65},{65,97},{2,34},{34,66},{66,9... | collective-permute-start | bytes 786440 | tf_op jit(solution)/shard_map/ppermute | solution.py:180
  42.2 9.6 %collective-permute-start.5 = (f32[256,256]{1,0:T(8,128)S(1)}, f32[256,256]{1,0:T(8,128)S(1)}, u32[]{:S(2)}, u32[]{:S(2)}) collective-permute-start(f32[256,256]{1,0:T(8,128)S(1)} %shard_map.78.refs_3_.refs_2_.refs_1_.refs_0_), channel_id=1, source_target_pairs={{0,32},{32,64},{64,96},{1,33},{33,65},{65,97},{2,34},{34,66},{66,9... | collective-permute-start | bytes 786440 | tf_op jit(solution)/shard_map/ppermute | solution.py:180
  43.6 2.6 %copy-start.2 = (f32[1,12,256,256]{3,2,1,0:T(8,128)S(1)}, f32[1,12,256,256]{3,2,1,0:T(8,128)}, u32[]{:S(2)}) copy-start(f32[1,12,256,256]{3,2,1,0:T(8,128)} %param.7) | copy-start | bytes 9437188
  47.6 10.2 %collective-permute-start.8 = (f32[256,256]{1,0:T(8,128)S(1)}, f32[256,256]{1,0:T(8,128)S(1)}, u32[]{:S(2)}, u32[]{:S(2)}) collective-permute-start(f32[256,256]{1,0:T(8,128)S(1)} %shard_map.81.refs_3_.refs_2_.refs_1_.refs_0_), channel_id=1, source_target_pairs={{0,32},{32,64},{64,96},{1,33},{33,65},{65,97},{2,34},{34,66},{66,9... | collective-permute-start | bytes 786440 | tf_op jit(solution)/shard_map/ppermute | solution.py:180
  53.3 10.4 %collective-permute-start.7 = (f32[256,256]{1,0:T(8,128)S(1)}, f32[256,256]{1,0:T(8,128)S(1)}, u32[]{:S(2)}, u32[]{:S(2)}) collective-permute-start(f32[256,256]{1,0:T(8,128)S(1)} %shard_map.83.refs_3_.refs_2_.refs_1_.refs_0_), channel_id=1, source_target_pairs={{0,32},{32,64},{64,96},{1,33},{33,65},{65,97},{2,34},{34,66},{66,9... | collective-permute-start | bytes 786440 | tf_op jit(solution)/shard_map/ppermute | solution.py:180
  59.3 10.3 %collective-permute-start.10 = (f32[256,256]{1,0:T(8,128)S(1)}, f32[256,256]{1,0:T(8,128)S(1)}, u32[]{:S(2)}, u32[]{:S(2)}) collective-permute-start(f32[256,256]{1,0:T(8,128)S(1)} %shard_map.85.refs_3_.refs_2_.refs_1_.refs_0_), channel_id=1, source_target_pairs={{0,32},{32,64},{64,96},{1,33},{33,65},{65,97},{2,34},{34,66},{66,9... | collective-permute-start | bytes 786440 | tf_op jit(solution)/shard_map/ppermute | solution.py:180
  65.2 9.6 %collective-permute-start.9 = (f32[256,256]{1,0:T(8,128)S(1)}, f32[256,256]{1,0:T(8,128)S(1)}, u32[]{:S(2)}, u32[]{:S(2)}) collective-permute-start(f32[256,256]{1,0:T(8,128)S(1)} %shard_map.87.refs_3_.refs_2_.refs_1_.refs_0_), channel_id=1, source_target_pairs={{0,32},{32,64},{64,96},{1,33},{33,65},{65,97},{2,34},{34,66},{66,9... | collective-permute-start | bytes 786440 | tf_op jit(solution)/shard_map/ppermute | solution.py:180
  73.5 10.8 %collective-permute-start.12 = (f32[256,256]{1,0:T(8,128)S(1)}, f32[256,256]{1,0:T(8,128)S(1)}, u32[]{:S(2)}, u32[]{:S(2)}) collective-permute-start(f32[256,256]{1,0:T(8,128)S(1)} %shard_map.89.refs_3_.refs_2_.refs_1_.refs_0_), channel_id=1, source_target_pairs={{0,32},{32,64},{64,96},{1,33},{33,65},{65,97},{2,34},{34,66},{66,9... | collective-permute-start | bytes 786440 | tf_op jit(solution)/shard_map/ppermute | solution.py:180
  76.3 11.9 %collective-permute-start.11 = (f32[256,256]{1,0:T(8,128)S(1)}, f32[256,256]{1,0:T(8,128)S(1)}, u32[]{:S(2)}, u32[]{:S(2)}) collective-permute-start(f32[256,256]{1,0:T(8,128)S(1)} %shard_map.91.refs_3_.refs_2_.refs_1_), channel_id=1, source_target_pairs={{0,32},{32,64},{64,96},{1,33},{33,65},{65,97},{2,34},{34,66},{66,9... | collective-permute-start | bytes 786440 | tf_op jit(solution)/shard_map/ppermute | solution.py:180
  92.1 11.5 %copy-start.5 = (f32[1,1,4]{2,1,0:T(1,128)S(1)}, f32[1,1,4]{2,1,0:T(1,128)}, u32[]{:S(2)}) copy-start(f32[1,1,4]{2,1,0:T(1,128)} %param.11) | copy-start | bytes 52
  92.4 27.9 %collective-permute-start.13 = (f32[2,3,4,3,32,256]{5,4,3,2,1,0:T(8,128)S(1)}, f32[2,3,4,3,32,256]{5,4,3,2,1,0:T(8,128)S(1)}, u32[]{:S(2)}, u32[]{:S(2)}) collective-permute-start(f32[2,3,4,3,32,256]{5,4,3,2,1,0:T(8,128)S(1)} %slice_bitcast_fusion), channel_id=1, source_target_pairs={{0,1},{1,0},{2,3},{3,2},{4,5},{5,4},{6,7},{7,6},{8,9},{9,8},{10,11... | collective-permute-start | bytes 7077896 | tf_op jit(solution)/shard_map/ppermute | solution.py:150
  92.5 11.1 %collective-permute-start.14 = (f32[256,256]{1,0:T(8,128)S(1)}, f32[256,256]{1,0:T(8,128)S(1)}, u32[]{:S(2)}, u32[]{:S(2)}) collective-permute-start(f32[256,256]{1,0:T(8,128)S(1)} %shard_map.93.refs_3_.refs_2_.refs_1_), channel_id=1, source_target_pairs={{0,32},{32,64},{64,96},{1,33},{33,65},{65,97},{2,34},{34,66},{66,9... | collective-permute-start | bytes 786440 | tf_op jit(solution)/shard_map/ppermute | solution.py:180
  93.8 15.0 %collective-permute-start.16 = (f32[256,256]{1,0:T(8,128)S(1)}, f32[256,256]{1,0:T(8,128)S(1)}, u32[]{:S(2)}, u32[]{:S(2)}) collective-permute-start(f32[256,256]{1,0:T(8,128)S(1)} %shard_map.95.refs_3_.refs_2_), channel_id=1, source_target_pairs={{0,32},{32,64},{64,96},{1,33},{33,65},{65,97},{2,34},{34,66},{66,9... | collective-permute-start | bytes 786440 | tf_op jit(solution)/shard_map/ppermute | solution.py:180
  105.0 9.3 %collective-permute-start.15 = (f32[256,256]{1,0:T(8,128)S(1)}, f32[256,256]{1,0:T(8,128)S(1)}, u32[]{:S(2)}, u32[]{:S(2)}) collective-permute-start(f32[256,256]{1,0:T(8,128)S(1)} %shard_map.97.refs_3_.refs_2_), channel_id=1, source_target_pairs={{0,32},{32,64},{64,96},{1,33},{33,65},{65,97},{2,34},{34,66},{66,9... | collective-permute-start | bytes 786440 | tf_op jit(solution)/shard_map/ppermute | solution.py:180
  117.7 2.6 %collective-permute-start.17 = (f32[2,1,4,3,32,256]{5,4,3,2,0,1:T(8,128)S(1)}, f32[2,1,4,3,32,256]{5,4,3,2,0,1:T(8,128)S(1)}, u32[]{:S(2)}, u32[]{:S(2)}) collective-permute-start(f32[2,1,4,3,32,256]{5,4,3,2,0,1:T(8,128)S(1)} %slice_bitcast_fusion.3), channel_id=1, source_target_pairs={{0,1},{1,0},{2,3},{3,2},{4,5},{5,4},{6,7},{7,6},{8,9},{9,8},{10,11... | collective-permute-start | bytes 2359304 | tf_op jit(solution)/shard_map/ppermute | solution.py:150
  121.6 8.2 %collective-permute-start.18 = (f32[2,96,256]{2,1,0:T(8,128)S(1)}, f32[2,96,256]{2,1,0:T(8,128)S(1)}, u32[]{:S(2)}, u32[]{:S(2)}) collective-permute-start(f32[2,96,256]{2,1,0:T(8,128)S(1)} %get-tuple-element.11), channel_id=1, source_target_pairs={{0,2},{2,4},{4,6},{6,0},{1,3},{3,5},{5,7},{7,1},{8,10},{10,12},{12... | collective-permute-start | bytes 589832 | tf_op jit(solution)/shard_map/ppermute | solution.py:121
  123.1 6.7 %collective-permute-start.20 = (f32[2,96,256]{2,1,0:T(8,128)S(1)}, f32[2,96,256]{2,1,0:T(8,128)S(1)}, u32[]{:S(2)}, u32[]{:S(2)}) collective-permute-start(f32[2,96,256]{2,1,0:T(8,128)S(1)} %get-tuple-element.12), channel_id=1, source_target_pairs={{0,6},{2,0},{4,2},{6,4},{1,7},{3,1},{5,3},{7,5},{8,14},{10,8},{12,... | collective-permute-start | bytes 589832 | tf_op jit(solution)/shard_map/ppermute | solution.py:121
  124.9 9.5 %collective-permute-start.24 = (f32[2,96,256]{2,1,0:T(8,128)S(1)}, f32[2,96,256]{2,1,0:T(8,128)S(1)}, u32[]{:S(2)}, u32[]{:S(2)}) collective-permute-start(f32[2,96,256]{2,1,0:T(8,128)S(1)} %get-tuple-element.17), channel_id=1, source_target_pairs={{0,8},{8,16},{16,24},{24,0},{1,9},{9,17},{17,25},{25,1},{2,10},{10... | collective-permute-start | bytes 589832 | tf_op jit(solution)/shard_map/ppermute | solution.py:121
  126.9 7.5 %collective-permute-start.26 = (f32[2,96,256]{2,1,0:T(8,128)S(1)}, f32[2,96,256]{2,1,0:T(8,128)S(1)}, u32[]{:S(2)}, u32[]{:S(2)}) collective-permute-start(f32[2,96,256]{2,1,0:T(8,128)S(1)} %get-tuple-element.18), channel_id=1, source_target_pairs={{0,24},{8,0},{16,8},{24,16},{1,25},{9,1},{17,9},{25,17},{2,26},{10... | collective-permute-start | bytes 589832 | tf_op jit(solution)/shard_map/ppermute | solution.py:121
  130.7 10.8 %collective-permute-start.21 = (f32[4,96,256]{2,1,0:T(8,128)}, f32[4,96,256]{2,1,0:T(8,128)S(1)}, u32[]{:S(2)}, u32[]{:S(2)}) collective-permute-start(f32[4,96,256]{2,1,0:T(8,128)} %pad_maximum_fusion.1), channel_id=1, source_target_pairs={{0,6},{2,0},{4,2},{6,4},{1,7},{3,1},{5,3},{7,5},{8,14},{10,8},{12,... | collective-permute-start | bytes 1179656 | tf_op jit(solution)/shard_map/ppermute | solution.py:121
  134.4 11.3 %collective-permute-start.19 = (f32[4,96,256]{2,1,0:T(8,128)}, f32[4,96,256]{2,1,0:T(8,128)}, u32[]{:S(2)}, u32[]{:S(2)}) collective-permute-start(f32[4,96,256]{2,1,0:T(8,128)} %pad_maximum_fusion), channel_id=1, source_target_pairs={{0,2},{2,4},{4,6},{6,0},{1,3},{3,5},{5,7},{7,1},{8,10},{10,12},{12... | collective-permute-start | bytes 1179656 | tf_op jit(solution)/shard_map/ppermute | solution.py:121
  135.3 11.6 %collective-permute-start.27 = (f32[4,96,256]{2,1,0:T(8,128)}, f32[4,96,256]{2,1,0:T(8,128)}, u32[]{:S(2)}, u32[]{:S(2)}) collective-permute-start(f32[4,96,256]{2,1,0:T(8,128)} %pad_maximum_fusion.3), channel_id=1, source_target_pairs={{0,24},{8,0},{16,8},{24,16},{1,25},{9,1},{17,9},{25,17},{2,26},{10... | collective-permute-start | bytes 1179656 | tf_op jit(solution)/shard_map/ppermute | solution.py:121
  140.1 11.0 %collective-permute-start.25 = (f32[4,96,256]{2,1,0:T(8,128)}, f32[4,96,256]{2,1,0:T(8,128)}, u32[]{:S(2)}, u32[]{:S(2)}) collective-permute-start(f32[4,96,256]{2,1,0:T(8,128)} %pad_maximum_fusion.2), channel_id=1, source_target_pairs={{0,8},{8,16},{16,24},{24,0},{1,9},{9,17},{17,25},{25,1},{2,10},{10... | collective-permute-start | bytes 1179656 | tf_op jit(solution)/shard_map/ppermute | solution.py:121
  152.5 5.7 %collective-permute-start.28 = (f32[2,96,256]{2,1,0:T(8,128)S(1)}, f32[2,96,256]{2,1,0:T(8,128)S(1)}, u32[]{:S(2)}, u32[]{:S(2)}) collective-permute-start(f32[2,96,256]{2,1,0:T(8,128)S(1)} %pad_maximum_fusion.5), channel_id=1, source_target_pairs={{0,2},{2,0},{4,6},{6,4},{1,3},{3,1},{5,7},{7,5},{8,10},{10,8},{12,... | collective-permute-start | bytes 589832 | tf_op jit(solution)/shard_map/ppermute | solution.py:135
  152.9 8.4 %collective-permute-start.22 = (f32[2,96,256]{2,1,0:T(8,128)S(1)}, f32[2,96,256]{2,1,0:T(8,128)S(1)}, u32[]{:S(2)}, u32[]{:S(2)}) collective-permute-start(f32[2,96,256]{2,1,0:T(8,128)S(1)} %pad_maximum_fusion.4), channel_id=1, source_target_pairs={{0,8},{8,0},{16,24},{24,16},{1,9},{9,1},{17,25},{25,17},{2,10},{10... | collective-permute-start | bytes 589832 | tf_op jit(solution)/shard_map/ppermute | solution.py:135
  158.3 5.9 %collective-permute-start.29 = (f32[96,256]{1,0:T(8,128)S(1)}, f32[96,256]{1,0:T(8,128)S(1)}, u32[]{:S(2)}, u32[]{:S(2)}) collective-permute-start(f32[96,256]{1,0:T(8,128)S(1)} %fusion.8), channel_id=1, source_target_pairs={{0,6},{2,4},{4,2},{6,0},{1,7},{3,5},{5,3},{7,1},{8,14},{10,12},{12... | collective-permute-start | bytes 294920 | tf_op jit(solution)/shard_map/ppermute | solution.py:137
  161.4 5.9 %collective-permute-start.23 = (f32[96,256]{1,0:T(8,128)S(1)}, f32[96,256]{1,0:T(8,128)S(1)}, u32[]{:S(2)}, u32[]{:S(2)}) collective-permute-start(f32[96,256]{1,0:T(8,128)S(1)} %fusion.12), channel_id=1, source_target_pairs={{0,24},{8,16},{16,8},{24,0},{1,25},{9,17},{17,9},{25,1},{2,26},{10... | collective-permute-start | bytes 294920 | tf_op jit(solution)/shard_map/ppermute | solution.py:137

commit v7 on v5

--- a/solution.py
+++ b/solution.py
@@ -86,6 +86,33 @@
     pltpu.make_async_copy(results, psi.at[:, 0], stores).wait()
 
 
+def early_step(q, ints, floats, left, mps):
+    def kernel(ints, floats, left, mps, environ, blocks, sems):
+        @pl.when(ints[0] == 0)
+        def _():
+            sources = [left.at[q], mps.at[0, q]] + ([left.at[q - 1], mps.at[1, q - 1]] if q else [])
+            copies = [pltpu.make_async_copy(source, blocks.at[i], sems.at[i]) for i, source in enumerate(sources)]
+            for copy in copies:
+                copy.start()
+            for copy in copies:
+                copy.wait()
+            size = ints[4 + q]
+            s = framed(blocks[1], size, size)
+            first = floats[0] * ints[16 + q].astype(f32) * product(halves(blocks[0]), halves(s), ((1,), (0,)))
+            moved = product(halves(s.T), halves(first), ((1,), (0,)))
+            if q:
+                u = framed(blocks[3], ints[3 + q], size)
+                second = floats[1] * ints[15 + q].astype(f32) * product(halves(blocks[2]), halves(u), ((1,), (0,)))
+                moved = moved + product(halves(u.T), halves(second), ((1,), (0,)))
+            environ[...] = moved
+
+    return pl.pallas_call(
+        kernel, in_specs=[SCALAR] * 2 + [FAR] * 2, out_specs=LOCAL, out_shape=jax.ShapeDtypeStruct((W, W), f32),
+        scratch_shapes=[pltpu.VMEM((4, W, W), f32), pltpu.SemaphoreType.DMA((4,))],
+        compiler_params=pltpu.CompilerParams(vmem_limit_bytes=52 * 2**20),
+    )(ints, floats, left, mps)
+
+
 def update_step(step, ints, floats, arrived, previous, left, mps, held):
     def kernel(ints, floats, arrived, previous, left, mps, *rest):
         environ = rest[-1]
@@ -152,8 +179,11 @@
     nothing = jnp.zeros((W, W), f32)
     arrivals, environs, held = {}, {}, ()
     for step in range(LAST):
-        environ = update_step(
-            step, ints, floats, arrivals.get(step, nothing), arrivals.get(step - 1, nothing), left_env[0], mps[0], held)
+        if step < LAG:
+            environ = early_step(step, ints, floats, left_env[0], mps[0])
+        else:
+            environ = update_step(
+                step, ints, floats, arrivals[step], arrivals.get(step - 1, nothing), left_env[0], mps[0], held)
         environs[step] = environ
         if step + LAG < LAST:
             arrivals[step + LAG] = lax.ppermute(environ, "site", [(0, 1), (1, 2), (2, 3)])

time: 154 us -> 149 us (0.968)
  local copies, waits for them, and re-layouts: 7.09 us -> 2.43 us
    unnamed x18 -> x16, local copies, waits for them, and re-layouts: 5.36 us -> 0.7 us
    pallas_call x18 -> x16, Pallas kernels: 20.7 us -> 19.6 us  [update_step(): pl.pallas_call(kernel, in_specs=[SCALAR] * 2 + [LOCAL] * 4 + [FAR] * len(...]
  transfers between devices with their start and end apart: 31 -> 31, of which waited for: 20 -> 20; matrix products, arithmetic and copies ran while one was open for 0% -> 0% of each run, Pallas kernels for 30% -> 31%
where the time goes in v7:
time: 149 us
  Pallas kernels  49.7 us (33%)
  starting transfers between devices  47.2 us (32%)
  waiting for transfers between devices  46.7 us (31%)
  local copies, waits for them, and re-layouts  2.43 us (2%)
  other arithmetic  2.08 us (1%)
    ppermute x16, waiting for transfers between devices, shards(): lax.ppermute(environ, 'site', [(0, 1), (1, 2), (2, 3)])  31.6 us
    pallas_call x12, Pallas kernels, apply_step(): pl.pallas_call(kernel, in_specs=[SCALAR] * 2 + [LOCAL] * len(operands) +...  28.9 us
    ppermute x14, starting transfers between devices, turned(): return lax.ppermute(x, axis, [(i, (i + by) % 4) for i in range(4)])  25.5 us
    ppermute x16, starting transfers between devices, shards(): lax.ppermute(environ, 'site', [(0, 1), (1, 2), (2, 3)])  21.4 us
    pallas_call x16, Pallas kernels, update_step(): pl.pallas_call(kernel, in_specs=[SCALAR] * 2 + [LOCAL] * 4 + [FAR] * len(...  19.6 us
    ppermute x14, waiting for transfers between devices, turned(): return lax.ppermute(x, axis, [(i, (i + by) % 4) for i in range(4)])  9.42 us
    ppermute x1, waiting for transfers between devices, reduced(): both = pieces[0] + lax.ppermute(pieces[1], 'core', [(0, 1), (1, 0)])  5.65 us
  transfers between devices with their start and end apart: 31, of which 20 were waited for; matrix products, arithmetic and copies ran while one was open for 0% of the time, Pallas kernels for 31%

profile of v7, /device:TPU:24, one launch (start us, length us, event | category | flops | bytes accessed | tf_op | source)
XLA Modules:
  0.0 148.7 jit_solution(4691243980545545047)
XLA Ops:
  2.0 1.6 %collective-permute-start.1 = (f32[256,256]{1,0:T(8,128)S(1)}, f32[256,256]{1,0:T(8,128)S(1)}, u32[]{:S(2)}, u32[]{:S(2)}) collective-permute-start(f32[256,256]{1,0:T(8,128)S(1)} %shard_map.74.refs_0_), channel_id=1, source_target_pairs={{0,32},{32,64},{64,96},{1,33},{33,65},{65,97},{2,34},{34,66},{66,9... | collective-permute-start | bytes 786440 | tf_op jit(solution)/shard_map/ppermute | solution.py:189
  5.5 7.9 %collective-permute-done.1.previous.arrived = f32[256,256]{1,0:T(8,128)S(1)} collective-permute-done((f32[256,256]{1,0:T(8,128)S(1)}, f32[256,256]{1,0:T(8,128)S(1)}, u32[]{:S(2)}, u32[]{:S(2)}) %collective-permute-start.1) | collective-permute-done | bytes 262176 | tf_op jit(solution)/shard_map/ppermute | solution.py:189
  15.3 3.7 %collective-permute-done.arrived.previous = f32[256,256]{1,0:T(8,128)S(1)} collective-permute-done((f32[256,256]{1,0:T(8,128)S(1)}, f32[256,256]{1,0:T(8,128)S(1)}, u32[]{:S(2)}, u32[]{:S(2)}) %collective-permute-start) | collective-permute-done | bytes 262176 | tf_op jit(solution)/shard_map/ppermute | solution.py:189
  20.8 4.2 %collective-permute-done.3.previous.arrived = f32[256,256]{1,0:T(8,128)S(1)} collective-permute-done((f32[256,256]{1,0:T(8,128)S(1)}, f32[256,256]{1,0:T(8,128)S(1)}, u32[]{:S(2)}, u32[]{:S(2)}) %collective-permute-start.3) | collective-permute-done | bytes 262176 | tf_op jit(solution)/shard_map/ppermute | solution.py:189
  26.9 3.8 %collective-permute-done.2.arrived.previous = f32[256,256]{1,0:T(8,128)S(1)} collective-permute-done((f32[256,256]{1,0:T(8,128)S(1)}, f32[256,256]{1,0:T(8,128)S(1)}, u32[]{:S(2)}, u32[]{:S(2)}) %collective-permute-start.2) | collective-permute-done | bytes 262176 | tf_op jit(solution)/shard_map/ppermute | solution.py:189
  31.3 1.6 %collective-permute-start.4 = (f32[256,256]{1,0:T(8,128)S(1)}, f32[256,256]{1,0:T(8,128)S(1)}, u32[]{:S(2)}, u32[]{:S(2)}) collective-permute-start(f32[256,256]{1,0:T(8,128)S(1)} %shard_map.77.refs_2_.refs_1_.refs_0_), channel_id=1, source_target_pairs={{0,32},{32,64},{64,96},{1,33},{33,65},{65,97},{2,34},{34,66},{66,9... | collective-permute-start | bytes 786440 | tf_op jit(solution)/shard_map/ppermute | solution.py:189
  32.8 3.6 %collective-permute-done.5.arrived.previous = f32[256,256]{1,0:T(8,128)S(1)} collective-permute-done((f32[256,256]{1,0:T(8,128)S(1)}, f32[256,256]{1,0:T(8,128)S(1)}, u32[]{:S(2)}, u32[]{:S(2)}) %collective-permute-start.5) | collective-permute-done | bytes 262176 | tf_op jit(solution)/shard_map/ppermute | solution.py:189
  36.5 1.4 shard_map.79.refs_3_.refs_2_.refs_1_.refs_0_
  39.2 2.5 %shard_map.80.rest_0_.refs_6_ = f32[2,2,4,4,3,32,256]{6,5,4,3,2,1,0:T(8,128)S(1)} custom-call(s32[28]{0:T(128)S(1)} %concatenate.15.ints, f32[4]{0:T(128)S(1)} %bitcast.157, f32[256,256]{1,0:T(8,128)S(1)} %shard_map.74.refs_0_, f32[256,256]{1,0:T(8,128)S(1)} %shard_map.76.refs_1_.refs_0_, f32[256,256]{1,0:T(8,128)S(1)} %shard_map.78.refs_2_.refs_1_.refs_0_, ...), custom_call_target="tpu_custom_call" | custom-call | tf_op jit(solution)/shard_map/pallas_call | solution.py:137
  44.6 2.5 %shard_map.82.rest_0_.refs_6_ = f32[2,2,4,4,3,32,256]{6,5,4,3,2,1,0:T(8,128)S(1)} custom-call(s32[28]{0:T(128)S(1)} %concatenate.15.ints, f32[4]{0:T(128)S(1)} %bitcast.159, f32[256,256]{1,0:T(8,128)S(1)} %shard_map.73.refs_0_, f32[256,256]{1,0:T(8,128)S(1)} %shard_map.75.refs_1_.refs_0_, ...), custom_call_target="tpu_custom_call", output_to_operand_aliasing={{}: (8, {})} | custom-call | tf_op jit(solution)/shard_map/pallas_call | solution.py:137
  47.7 1.4 shard_map.83.refs_3_.refs_2_.refs_1_.refs_0_
  50.4 2.5 %shard_map.84.rest_0_.refs_6_ = f32[2,2,4,4,3,32,256]{6,5,4,3,2,1,0:T(8,128)S(1)} custom-call(s32[28]{0:T(128)S(1)} %concatenate.15.ints, f32[4]{0:T(128)S(1)} %bitcast.161, f32[256,256]{1,0:T(8,128)S(1)} %shard_map.76.refs_1_.refs_0_, f32[256,256]{1,0:T(8,128)S(1)} %shard_map.78.refs_2_.refs_1_.refs_0_, ...), custom_call_target="tpu_custom_call", output_to_operand_aliasing={{}: (8, {})} | custom-call | tf_op jit(solution)/shard_map/pallas_call | solution.py:137
  53.6 1.4 shard_map.85.refs_3_.refs_2_.refs_1_.refs_0_
  56.4 2.5 %shard_map.86.rest_0_.refs_6_ = f32[2,2,4,4,3,32,256]{6,5,4,3,2,1,0:T(8,128)S(1)} custom-call(s32[28]{0:T(128)S(1)} %concatenate.15.ints, f32[4]{0:T(128)S(1)} %bitcast.163, f32[256,256]{1,0:T(8,128)S(1)} %shard_map.75.refs_1_.refs_0_, f32[256,256]{1,0:T(8,128)S(1)} %shard_map.77.refs_2_.refs_1_.refs_0_, ...), custom_call_target="tpu_custom_call", output_to_operand_aliasing={{}: (8, {})} | custom-call | tf_op jit(solution)/shard_map/pallas_call | solution.py:137
  59.5 1.4 shard_map.87.refs_3_.refs_2_.refs_1_.refs_0_
  60.9 1.5 collective-permute-start.11
  62.4 2.5 %shard_map.88.rest_0_.refs_6_ = f32[2,2,4,4,3,32,256]{6,5,4,3,2,1,0:T(8,128)S(1)} custom-call(s32[28]{0:T(128)S(1)} %concatenate.15.ints, f32[4]{0:T(128)S(1)} %bitcast.165, f32[256,256]{1,0:T(8,128)S(1)} %shard_map.78.refs_2_.refs_1_.refs_0_, f32[256,256]{1,0:T(8,128)S(1)} %shard_map.79.refs_3_.refs_2_.refs_1_.refs_0_, ...), custom_call_target="tpu_custom_call", output_to_operand_aliasing={{}: (8, {})} | custom-call | tf_op jit(solution)/shard_map/pallas_call | solution.py:137
  65.3 1.4 shard_map.89.refs_3_.refs_2_.refs_1_.refs_0_
  68.1 2.5 %shard_map.90.rest_0_.refs_6_ = f32[2,2,4,4,3,32,256]{6,5,4,3,2,1,0:T(8,128)S(1)} custom-call(s32[28]{0:T(128)S(1)} %concatenate.15.ints, f32[4]{0:T(128)S(1)} %bitcast.167, f32[256,256]{1,0:T(8,128)S(1)} %shard_map.77.refs_2_.refs_1_.refs_0_, f32[256,256]{1,0:T(8,128)S(1)} %shard_map.81.refs_3_.refs_2_.refs_1_.refs_0_, ...), custom_call_target="tpu_custom_call", output_to_operand_aliasing={{}: (8, {})} | custom-call | tf_op jit(solution)/shard_map/pallas_call | solution.py:137
  71.0 1.5 shard_map.91.refs_3_.refs_2_.refs_1_
  73.8 2.5 %shard_map.92.rest_0_.refs_6_ = f32[2,2,4,4,3,32,256]{6,5,4,3,2,1,0:T(8,128)S(1)} custom-call(s32[28]{0:T(128)S(1)} %concatenate.15.ints, f32[4]{0:T(128)S(1)} %bitcast.169, f32[256,256]{1,0:T(8,128)S(1)} %shard_map.79.refs_3_.refs_2_.refs_1_.refs_0_, f32[256,256]{1,0:T(8,128)S(1)} %shard_map.83.refs_3_.refs_2_.refs_1_.refs_0_, ...), custom_call_target="tpu_custom_call", output_to_operand_aliasing={{}: (8, {})} | custom-call | tf_op jit(solution)/shard_map/pallas_call | solution.py:137
  77.3 1.4 shard_map.93.refs_3_.refs_2_.refs_1_
  80.0 2.5 %shard_map.94.rest_0_.refs_6_ = f32[2,2,4,4,3,32,256]{6,5,4,3,2,1,0:T(8,128)S(1)} custom-call(s32[28]{0:T(128)S(1)} %concatenate.15.ints, f32[4]{0:T(128)S(1)} %bitcast.171, f32[256,256]{1,0:T(8,128)S(1)} %shard_map.81.refs_3_.refs_2_.refs_1_.refs_0_, f32[256,256]{1,0:T(8,128)S(1)} %shard_map.85.refs_3_.refs_2_.refs_1_.refs_0_, ...), custom_call_target="tpu_custom_call", output_to_operand_aliasing={{}: (8, {})} | custom-call | tf_op jit(solution)/shard_map/pallas_call | solution.py:137
  84.6 2.5 %shard_map.96.rest_0_.refs_6_ = f32[2,2,4,4,3,32,256]{6,5,4,3,2,1,0:T(8,128)S(1)} custom-call(s32[28]{0:T(128)S(1)} %concatenate.15.ints, f32[4]{0:T(128)S(1)} %bitcast.173, f32[256,256]{1,0:T(8,128)S(1)} %shard_map.83.refs_3_.refs_2_.refs_1_.refs_0_, f32[256,256]{1,0:T(8,128)S(1)} %shard_map.87.refs_3_.refs_2_.refs_1_.refs_0_, ...), custom_call_target="tpu_custom_call", output_to_operand_aliasing={{}: (8, {})} | custom-call | tf_op jit(solution)/shard_map/pallas_call | solution.py:137
  88.3 1.5 shard_map.97.refs_3_.refs_2_
  91.1 2.5 %shard_map.98.rest_0_.refs_6_ = f32[2,2,4,4,3,32,256]{6,5,4,3,2,1,0:T(8,128)S(1)} custom-call(s32[28]{0:T(128)S(1)} %concatenate.15.ints, f32[4]{0:T(128)S(1)} %bitcast.175, f32[256,256]{1,0:T(8,128)S(1)} %shard_map.85.refs_3_.refs_2_.refs_1_.refs_0_, f32[256,256]{1,0:T(8,128)S(1)} %shard_map.89.refs_3_.refs_2_.refs_1_.refs_0_, ...), custom_call_target="tpu_custom_call", output_to_operand_aliasing={{}: (8, {})} | custom-call | tf_op jit(solution)/shard_map/pallas_call | solution.py:137
  93.6 3.8 %collective-permute-done.15.arrived.previous = f32[256,256]{1,0:T(8,128)S(1)} collective-permute-done((f32[256,256]{1,0:T(8,128)S(1)}, f32[256,256]{1,0:T(8,128)S(1)}, u32[]{:S(2)}, u32[]{:S(2)}) %collective-permute-start.15) | collective-permute-done | bytes 262176 | tf_op jit(solution)/shard_map/ppermute | solution.py:189
  97.4 1.5 shard_map.99.refs_3_
  98.8 2.5 %shard_map.100.rest_0_.refs_6_ = f32[2,2,4,4,3,32,256]{6,5,4,3,2,1,0:T(8,128)S(1)} custom-call(s32[28]{0:T(128)S(1)} %concatenate.15.ints, f32[4]{0:T(128)S(1)} %bitcast.177, f32[256,256]{1,0:T(8,128)S(1)} %shard_map.87.refs_3_.refs_2_.refs_1_.refs_0_, f32[256,256]{1,0:T(8,128)S(1)} %shard_map.91.refs_3_.refs_2_.refs_1_, ...), custom_call_target="tpu_custom_call", output_to_operand_aliasing={{}: (8, {})} | custom-call | tf_op jit(solution)/shard_map/pallas_call | solution.py:137
  101.3 1.5 shard_map.101.refs_3_
  102.8 1.9 %shard_map.102 = f32[2,2,4,4,3,32,256]{6,5,4,3,2,1,0:T(8,128)S(1)} custom-call(s32[28]{0:T(128)S(1)} %concatenate.15.ints, f32[4]{0:T(128)S(1)} %bitcast.179, f32[256,256]{1,0:T(8,128)S(1)} %shard_map.89.refs_3_.refs_2_.refs_1_.refs_0_, f32[256,256]{1,0:T(8,128)S(1)} %shard_map.93.refs_3_.refs_2_.refs_1_, ...), custom_call_target="tpu_custom_call", output_to_operand_aliasing={{}: (8, {})} | custom-call | tf_op jit(solution)/shard_map/pallas_call | solution.py:137
  105.4 5.6 %collective-permute-done.16 = f32[2,4,4,3,32,256]{5,4,3,2,1,0:T(8,128)S(1)} collective-permute-done((f32[2,4,4,3,32,256]{5,4,3,2,1,0:T(8,128)S(1)}, f32[2,4,4,3,32,256]{5,4,3,2,1,0:T(8,128)S(1)}, u32[]{:S(2)}, u32[]{:S(2)}) %collective-permute-start.16) | collective-permute-done | bytes 3145760 | tf_op jit(solution)/shard_map/ppermute | solution.py:165
  112.4 1.6 %collective-permute-start.17 = (f32[2,96,256]{2,1,0:T(8,128)S(1)}, f32[2,96,256]{2,1,0:T(8,128)S(1)}, u32[]{:S(2)}, u32[]{:S(2)}) collective-permute-start(f32[2,96,256]{2,1,0:T(8,128)S(1)} %get-tuple-element.11), channel_id=1, source_target_pairs={{0,2},{2,4},{4,6},{6,0},{1,3},{3,5},{5,7},{7,1},{8,10},{10,12},{12... | collective-permute-start | bytes 589832 | tf_op jit(solution)/shard_map/ppermute | solution.py:149
  114.0 1.7 %collective-permute-start.19 = (f32[2,96,256]{2,1,0:T(8,128)S(1)}, f32[2,96,256]{2,1,0:T(8,128)S(1)}, u32[]{:S(2)}, u32[]{:S(2)}) collective-permute-start(f32[2,96,256]{2,1,0:T(8,128)S(1)} %get-tuple-element.12), channel_id=1, source_target_pairs={{0,6},{2,0},{4,2},{6,4},{1,7},{3,1},{5,3},{7,5},{8,14},{10,8},{12,... | collective-permute-start | bytes 589832 | tf_op jit(solution)/shard_map/ppermute | solution.py:149
  115.8 2.0 %collective-permute-start.24 = (f32[2,96,256]{2,1,0:T(8,128)S(1)}, f32[2,96,256]{2,1,0:T(8,128)S(1)}, u32[]{:S(2)}, u32[]{:S(2)}) collective-permute-start(f32[2,96,256]{2,1,0:T(8,128)S(1)} %get-tuple-element.17), channel_id=1, source_target_pairs={{0,8},{8,16},{16,24},{24,0},{1,9},{9,17},{17,25},{25,1},{2,10},{10... | collective-permute-start | bytes 589832 | tf_op jit(solution)/shard_map/ppermute | solution.py:149
  117.8 2.2 %collective-permute-start.26 = (f32[2,96,256]{2,1,0:T(8,128)S(1)}, f32[2,96,256]{2,1,0:T(8,128)S(1)}, u32[]{:S(2)}, u32[]{:S(2)}) collective-permute-start(f32[2,96,256]{2,1,0:T(8,128)S(1)} %get-tuple-element.18), channel_id=1, source_target_pairs={{0,24},{8,0},{16,8},{24,16},{1,25},{9,1},{17,9},{25,17},{2,26},{10... | collective-permute-start | bytes 589832 | tf_op jit(solution)/shard_map/ppermute | solution.py:149
  120.7 1.6 %collective-permute-start.18 = (f32[4,96,256]{2,1,0:T(8,128)S(1)}, f32[4,96,256]{2,1,0:T(8,128)S(1)}, u32[]{:S(2)}, u32[]{:S(2)}) collective-permute-start(f32[4,96,256]{2,1,0:T(8,128)S(1)} %pad_maximum_fusion), channel_id=1, source_target_pairs={{0,2},{2,4},{4,6},{6,0},{1,3},{3,5},{5,7},{7,1},{8,10},{10,12},{12... | collective-permute-start | bytes 1179656 | tf_op jit(solution)/shard_map/ppermute | solution.py:149
  122.3 1.8 %collective-permute-start.20 = (f32[4,96,256]{2,1,0:T(8,128)S(1)}, f32[4,96,256]{2,1,0:T(8,128)S(1)}, u32[]{:S(2)}, u32[]{:S(2)}) collective-permute-start(f32[4,96,256]{2,1,0:T(8,128)S(1)} %pad_maximum_fusion.1), channel_id=1, source_target_pairs={{0,6},{2,0},{4,2},{6,4},{1,7},{3,1},{5,3},{7,5},{8,14},{10,8},{12,... | collective-permute-start | bytes 1179656 | tf_op jit(solution)/shard_map/ppermute | solution.py:149
  124.6 1.6 %collective-permute-start.25 = (f32[4,96,256]{2,1,0:T(8,128)S(1)}, f32[4,96,256]{2,1,0:T(8,128)S(1)}, u32[]{:S(2)}, u32[]{:S(2)}) collective-permute-start(f32[4,96,256]{2,1,0:T(8,128)S(1)} %pad_maximum_fusion.2), channel_id=1, source_target_pairs={{0,8},{8,16},{16,24},{24,0},{1,9},{9,17},{17,25},{25,1},{2,10},{10... | collective-permute-start | bytes 1179656 | tf_op jit(solution)/shard_map/ppermute | solution.py:149
  126.3 2.2 %collective-permute-start.27 = (f32[4,96,256]{2,1,0:T(8,128)S(1)}, f32[4,96,256]{2,1,0:T(8,128)S(1)}, u32[]{:S(2)}, u32[]{:S(2)}) collective-permute-start(f32[4,96,256]{2,1,0:T(8,128)S(1)} %pad_maximum_fusion.3), channel_id=1, source_target_pairs={{0,24},{8,0},{16,8},{24,16},{1,25},{9,1},{17,9},{25,17},{2,26},{10... | collective-permute-start | bytes 1179656 | tf_op jit(solution)/shard_map/ppermute | solution.py:149
  128.5 3.9 %collective-permute-done.18 = f32[4,96,256]{2,1,0:T(8,128)S(1)} collective-permute-done((f32[4,96,256]{2,1,0:T(8,128)S(1)}, f32[4,96,256]{2,1,0:T(8,128)S(1)}, u32[]{:S(2)}, u32[]{:S(2)}) %collective-permute-start.18) | collective-permute-done | bytes 393248 | tf_op jit(solution)/shard_map/ppermute | solution.py:149
  132.4 2.0 %collective-permute-start.21 = (f32[96,256]{1,0:T(8,128)S(1)}, f32[96,256]{1,0:T(8,128)S(1)}, u32[]{:S(2)}, u32[]{:S(2)}) collective-permute-start(f32[96,256]{1,0:T(8,128)S(1)} %get-tuple-element.23), channel_id=1, source_target_pairs={{0,8},{8,16},{16,24},{24,0},{1,9},{9,17},{17,25},{25,1},{2,10},{10... | collective-permute-start | bytes 294920 | tf_op jit(solution)/shard_map/ppermute | solution.py:149
  134.4 2.2 %collective-permute-start.22 = (f32[96,256]{1,0:T(8,128)S(1)}, f32[96,256]{1,0:T(8,128)S(1)}, u32[]{:S(2)}, u32[]{:S(2)}) collective-permute-start(f32[96,256]{1,0:T(8,128)S(1)} %get-tuple-element.22), channel_id=1, source_target_pairs={{0,24},{8,0},{16,8},{24,16},{1,25},{9,1},{17,9},{25,17},{2,26},{10... | collective-permute-start | bytes 294920 | tf_op jit(solution)/shard_map/ppermute | solution.py:149
  136.6 1.8 %collective-permute-start.23 = (f32[96,256]{1,0:T(8,128)S(1)}, f32[96,256]{1,0:T(8,128)S(1)}, u32[]{:S(2)}, u32[]{:S(2)}) collective-permute-start(f32[96,256]{1,0:T(8,128)S(1)} %get-tuple-element.21), channel_id=1, source_target_pairs={{0,16},{8,24},{16,0},{24,8},{1,17},{9,25},{17,1},{25,9},{2,18},{10... | collective-permute-start | bytes 294920 | tf_op jit(solution)/shard_map/ppermute | solution.py:149
  139.6 2.2 %collective-permute-start.29 = (f32[96,256]{1,0:T(8,128)S(1)}, f32[96,256]{1,0:T(8,128)S(1)}, u32[]{:S(2)}, u32[]{:S(2)}) collective-permute-start(f32[96,256]{1,0:T(8,128)S(1)} %get-tuple-element.25), channel_id=1, source_target_pairs={{0,6},{2,0},{4,2},{6,4},{1,7},{3,1},{5,3},{7,5},{8,14},{10,8},{12,... | collective-permute-start | bytes 294920 | tf_op jit(solution)/shard_map/ppermute | solution.py:149
  141.8 1.5 %collective-permute-start.30 = (f32[96,256]{1,0:T(8,128)S(1)}, f32[96,256]{1,0:T(8,128)S(1)}, u32[]{:S(2)}, u32[]{:S(2)}) collective-permute-start(f32[96,256]{1,0:T(8,128)S(1)} %get-tuple-element.24), channel_id=1, source_target_pairs={{0,4},{2,6},{4,0},{6,2},{1,5},{3,7},{5,1},{7,3},{8,12},{10,14},{12... | collective-permute-start | bytes 294920 | tf_op jit(solution)/shard_map/ppermute | solution.py:149
  143.4 1.7 %collective-permute-done.28 = f32[96,256]{1,0:T(8,128)S(1)} collective-permute-done((f32[96,256]{1,0:T(8,128)S(1)}, f32[96,256]{1,0:T(8,128)S(1)}, u32[]{:S(2)}, u32[]{:S(2)}) %collective-permute-start.28) | collective-permute-done | bytes 98336 | tf_op jit(solution)/shard_map/ppermute | solution.py:149
  145.1 2.9 %collective-permute-done.30 = f32[96,256]{1,0:T(8,128)S(1)} collective-permute-done((f32[96,256]{1,0:T(8,128)S(1)}, f32[96,256]{1,0:T(8,128)S(1)}, u32[]{:S(2)}, u32[]{:S(2)}) %collective-permute-start.30) | collective-permute-done | bytes 98336 | tf_op jit(solution)/shard_map/ppermute | solution.py:149
  (83 shorter events, 34.6 us)
Async XLA Ops:
  0.7 0.7 copy-start.2
  1.4 2.2 %copy-start.3 = (f32[1,1,4]{2,1,0:T(1,128)S(1)}, f32[1,1,4]{2,1,0:T(1,128)}, u32[]{:S(2)}) copy-start(f32[1,1,4]{2,1,0:T(1,128)} %param.11) | copy-start | bytes 52
  1.4 12.0 %slice-start = ((s8[6291456]{0:T(1024)(128)(4,1)}), s8[4194304]{0:T(1024)(128)(4,1)S(1)}, s32[]{:S(2)}) async-start(s8[6291456]{0:T(1024)(128)(4,1)} %bitcast.88), calls=%async_computation | async-start | bytes 8388608
  2.0 11.4 %slice-start.1 = ((s8[6291456]{0:T(1024)(128)(4,1)}), s8[2097152]{0:T(1024)(128)(4,1)S(1)}, s32[]{:S(2)}) async-start(s8[6291456]{0:T(1024)(128)(4,1)} %bitcast.88), calls=%async_computation.1 | async-start | bytes 4194304
  2.0 11.4 %copy-start = (f32[1,12,256,256]{3,2,1,0:T(8,128)S(1)}, f32[1,12,256,256]{3,2,1,0:T(8,128)}, u32[]{:S(2)}) copy-start(f32[1,12,256,256]{3,2,1,0:T(8,128)} %param.7) | copy-start | bytes 9437188
  2.0 11.3 %collective-permute-start.1 = (f32[256,256]{1,0:T(8,128)S(1)}, f32[256,256]{1,0:T(8,128)S(1)}, u32[]{:S(2)}, u32[]{:S(2)}) collective-permute-start(f32[256,256]{1,0:T(8,128)S(1)} %shard_map.74.refs_0_), channel_id=1, source_target_pairs={{0,32},{32,64},{64,96},{1,33},{33,65},{65,97},{2,34},{34,66},{66,9... | collective-permute-start | bytes 786440 | tf_op jit(solution)/shard_map/ppermute | solution.py:189
  4.2 14.8 %collective-permute-start = (f32[256,256]{1,0:T(8,128)S(1)}, f32[256,256]{1,0:T(8,128)S(1)}, u32[]{:S(2)}, u32[]{:S(2)}) collective-permute-start(f32[256,256]{1,0:T(8,128)S(1)} %shard_map.73.refs_0_), channel_id=1, source_target_pairs={{0,32},{32,64},{64,96},{1,33},{33,65},{65,97},{2,34},{34,66},{66,9... | collective-permute-start | bytes 786440 | tf_op jit(solution)/shard_map/ppermute | solution.py:189
  14.0 11.1 %collective-permute-start.3 = (f32[256,256]{1,0:T(8,128)S(1)}, f32[256,256]{1,0:T(8,128)S(1)}, u32[]{:S(2)}, u32[]{:S(2)}) collective-permute-start(f32[256,256]{1,0:T(8,128)S(1)} %shard_map.76.refs_1_.refs_0_), channel_id=1, source_target_pairs={{0,32},{32,64},{64,96},{1,33},{33,65},{65,97},{2,34},{34,66},{66,9... | collective-permute-start | bytes 786440 | tf_op jit(solution)/shard_map/ppermute | solution.py:189
  19.5 11.1 %collective-permute-start.2 = (f32[256,256]{1,0:T(8,128)S(1)}, f32[256,256]{1,0:T(8,128)S(1)}, u32[]{:S(2)}, u32[]{:S(2)}) collective-permute-start(f32[256,256]{1,0:T(8,128)S(1)} %shard_map.75.refs_1_.refs_0_), channel_id=1, source_target_pairs={{0,32},{32,64},{64,96},{1,33},{33,65},{65,97},{2,34},{34,66},{66,9... | collective-permute-start | bytes 786440 | tf_op jit(solution)/shard_map/ppermute | solution.py:189
  25.6 10.8 %collective-permute-start.5 = (f32[256,256]{1,0:T(8,128)S(1)}, f32[256,256]{1,0:T(8,128)S(1)}, u32[]{:S(2)}, u32[]{:S(2)}) collective-permute-start(f32[256,256]{1,0:T(8,128)S(1)} %shard_map.78.refs_2_.refs_1_.refs_0_), channel_id=1, source_target_pairs={{0,32},{32,64},{64,96},{1,33},{33,65},{65,97},{2,34},{34,66},{66,9... | collective-permute-start | bytes 786440 | tf_op jit(solution)/shard_map/ppermute | solution.py:189
  30.7 8.5 %slice-start.2 = ((s8[6291456]{0:T(1024)(128)(4,1)}), s8[4194304]{0:T(1024)(128)(4,1)S(1)}, s32[]{:S(2)}) async-start(s8[6291456]{0:T(1024)(128)(4,1)} %bitcast.124), calls=%async_computation.2 | async-start | bytes 8388608
  31.2 8.0 %slice-start.3 = ((s8[6291456]{0:T(1024)(128)(4,1)}), s8[2097152]{0:T(1024)(128)(4,1)S(1)}, s32[]{:S(2)}) async-start(s8[6291456]{0:T(1024)(128)(4,1)} %bitcast.124), calls=%async_computation.3 | async-start | bytes 4194304
  31.2 8.0 %copy-start.1 = (f32[1,1,12,256,256]{4,3,2,1,0:T(8,128)S(1)}, f32[1,1,12,256,256]{4,3,2,1,0:T(8,128)}, u32[]{:S(2)}) copy-start(f32[1,1,12,256,256]{4,3,2,1,0:T(8,128)} %param.8) | copy-start | bytes 9437188
  31.3 10.6 %collective-permute-start.4 = (f32[256,256]{1,0:T(8,128)S(1)}, f32[256,256]{1,0:T(8,128)S(1)}, u32[]{:S(2)}, u32[]{:S(2)}) collective-permute-start(f32[256,256]{1,0:T(8,128)S(1)} %shard_map.77.refs_2_.refs_1_.refs_0_), channel_id=1, source_target_pairs={{0,32},{32,64},{64,96},{1,33},{33,65},{65,97},{2,34},{34,66},{66,9... | collective-permute-start | bytes 786440 | tf_op jit(solution)/shard_map/ppermute | solution.py:189
  37.9 9.8 %collective-permute-start.7 = (f32[256,256]{1,0:T(8,128)S(1)}, f32[256,256]{1,0:T(8,128)S(1)}, u32[]{:S(2)}, u32[]{:S(2)}) collective-permute-start(f32[256,256]{1,0:T(8,128)S(1)} %shard_map.79.refs_3_.refs_2_.refs_1_.refs_0_), channel_id=1, source_target_pairs={{0,32},{32,64},{64,96},{1,33},{33,65},{65,97},{2,34},{34,66},{66,9... | collective-permute-start | bytes 786440 | tf_op jit(solution)/shard_map/ppermute | solution.py:189
  43.3 10.3 %collective-permute-start.6 = (f32[256,256]{1,0:T(8,128)S(1)}, f32[256,256]{1,0:T(8,128)S(1)}, u32[]{:S(2)}, u32[]{:S(2)}) collective-permute-start(f32[256,256]{1,0:T(8,128)S(1)} %shard_map.81.refs_3_.refs_2_.refs_1_.refs_0_), channel_id=1, source_target_pairs={{0,32},{32,64},{64,96},{1,33},{33,65},{65,97},{2,34},{34,66},{66,9... | collective-permute-start | bytes 786440 | tf_op jit(solution)/shard_map/ppermute | solution.py:189
  49.1 10.4 %collective-permute-start.9 = (f32[256,256]{1,0:T(8,128)S(1)}, f32[256,256]{1,0:T(8,128)S(1)}, u32[]{:S(2)}, u32[]{:S(2)}) collective-permute-start(f32[256,256]{1,0:T(8,128)S(1)} %shard_map.83.refs_3_.refs_2_.refs_1_.refs_0_), channel_id=1, source_target_pairs={{0,32},{32,64},{64,96},{1,33},{33,65},{65,97},{2,34},{34,66},{66,9... | collective-permute-start | bytes 786440 | tf_op jit(solution)/shard_map/ppermute | solution.py:189
  55.1 10.3 %collective-permute-start.8 = (f32[256,256]{1,0:T(8,128)S(1)}, f32[256,256]{1,0:T(8,128)S(1)}, u32[]{:S(2)}, u32[]{:S(2)}) collective-permute-start(f32[256,256]{1,0:T(8,128)S(1)} %shard_map.85.refs_3_.refs_2_.refs_1_.refs_0_), channel_id=1, source_target_pairs={{0,32},{32,64},{64,96},{1,33},{33,65},{65,97},{2,34},{34,66},{66,9... | collective-permute-start | bytes 786440 | tf_op jit(solution)/shard_map/ppermute | solution.py:189
  60.9 10.1 %collective-permute-start.11 = (f32[256,256]{1,0:T(8,128)S(1)}, f32[256,256]{1,0:T(8,128)S(1)}, u32[]{:S(2)}, u32[]{:S(2)}) collective-permute-start(f32[256,256]{1,0:T(8,128)S(1)} %shard_map.87.refs_3_.refs_2_.refs_1_.refs_0_), channel_id=1, source_target_pairs={{0,32},{32,64},{64,96},{1,33},{33,65},{65,97},{2,34},{34,66},{66,9... | collective-permute-start | bytes 786440 | tf_op jit(solution)/shard_map/ppermute | solution.py:189
  66.8 10.5 %collective-permute-start.10 = (f32[256,256]{1,0:T(8,128)S(1)}, f32[256,256]{1,0:T(8,128)S(1)}, u32[]{:S(2)}, u32[]{:S(2)}) collective-permute-start(f32[256,256]{1,0:T(8,128)S(1)} %shard_map.89.refs_3_.refs_2_.refs_1_.refs_0_), channel_id=1, source_target_pairs={{0,32},{32,64},{64,96},{1,33},{33,65},{65,97},{2,34},{34,66},{66,9... | collective-permute-start | bytes 786440 | tf_op jit(solution)/shard_map/ppermute | solution.py:189
  72.5 10.6 %collective-permute-start.13 = (f32[256,256]{1,0:T(8,128)S(1)}, f32[256,256]{1,0:T(8,128)S(1)}, u32[]{:S(2)}, u32[]{:S(2)}) collective-permute-start(f32[256,256]{1,0:T(8,128)S(1)} %shard_map.91.refs_3_.refs_2_.refs_1_), channel_id=1, source_target_pairs={{0,32},{32,64},{64,96},{1,33},{33,65},{65,97},{2,34},{34,66},{66,9... | collective-permute-start | bytes 786440 | tf_op jit(solution)/shard_map/ppermute | solution.py:189
  78.7 9.6 %collective-permute-start.12 = (f32[256,256]{1,0:T(8,128)S(1)}, f32[256,256]{1,0:T(8,128)S(1)}, u32[]{:S(2)}, u32[]{:S(2)}) collective-permute-start(f32[256,256]{1,0:T(8,128)S(1)} %shard_map.93.refs_3_.refs_2_.refs_1_), channel_id=1, source_target_pairs={{0,32},{32,64},{64,96},{1,33},{33,65},{65,97},{2,34},{34,66},{66,9... | collective-permute-start | bytes 786440 | tf_op jit(solution)/shard_map/ppermute | solution.py:189
  87.0 10.4 %collective-permute-start.15 = (f32[256,256]{1,0:T(8,128)S(1)}, f32[256,256]{1,0:T(8,128)S(1)}, u32[]{:S(2)}, u32[]{:S(2)}) collective-permute-start(f32[256,256]{1,0:T(8,128)S(1)} %shard_map.95.refs_3_.refs_2_), channel_id=1, source_target_pairs={{0,32},{32,64},{64,96},{1,33},{33,65},{65,97},{2,34},{34,66},{66,9... | collective-permute-start | bytes 786440 | tf_op jit(solution)/shard_map/ppermute | solution.py:189
  89.8 11.5 %collective-permute-start.14 = (f32[256,256]{1,0:T(8,128)S(1)}, f32[256,256]{1,0:T(8,128)S(1)}, u32[]{:S(2)}, u32[]{:S(2)}) collective-permute-start(f32[256,256]{1,0:T(8,128)S(1)} %shard_map.97.refs_3_.refs_2_), channel_id=1, source_target_pairs={{0,32},{32,64},{64,96},{1,33},{33,65},{65,97},{2,34},{34,66},{66,9... | collective-permute-start | bytes 786440 | tf_op jit(solution)/shard_map/ppermute | solution.py:189
  105.1 6.0 %collective-permute-start.16 = (f32[2,4,4,3,32,256]{5,4,3,2,1,0:T(8,128)S(1)}, f32[2,4,4,3,32,256]{5,4,3,2,1,0:T(8,128)S(1)}, u32[]{:S(2)}, u32[]{:S(2)}) collective-permute-start(f32[2,4,4,3,32,256]{5,4,3,2,1,0:T(8,128)S(1)} %slice_bitcast_fusion), channel_id=1, source_target_pairs={{0,1},{1,0},{2,3},{3,2},{4,5},{5,4},{6,7},{7,6},{8,9},{9,8},{10,11... | collective-permute-start | bytes 9437192 | tf_op jit(solution)/shard_map/ppermute | solution.py:165
  112.4 8.2 %collective-permute-start.17 = (f32[2,96,256]{2,1,0:T(8,128)S(1)}, f32[2,96,256]{2,1,0:T(8,128)S(1)}, u32[]{:S(2)}, u32[]{:S(2)}) collective-permute-start(f32[2,96,256]{2,1,0:T(8,128)S(1)} %get-tuple-element.11), channel_id=1, source_target_pairs={{0,2},{2,4},{4,6},{6,0},{1,3},{3,5},{5,7},{7,1},{8,10},{10,12},{12... | collective-permute-start | bytes 589832 | tf_op jit(solution)/shard_map/ppermute | solution.py:149
  114.0 6.7 %collective-permute-start.19 = (f32[2,96,256]{2,1,0:T(8,128)S(1)}, f32[2,96,256]{2,1,0:T(8,128)S(1)}, u32[]{:S(2)}, u32[]{:S(2)}) collective-permute-start(f32[2,96,256]{2,1,0:T(8,128)S(1)} %get-tuple-element.12), channel_id=1, source_target_pairs={{0,6},{2,0},{4,2},{6,4},{1,7},{3,1},{5,3},{7,5},{8,14},{10,8},{12,... | collective-permute-start | bytes 589832 | tf_op jit(solution)/shard_map/ppermute | solution.py:149
  115.8 8.7 %collective-permute-start.24 = (f32[2,96,256]{2,1,0:T(8,128)S(1)}, f32[2,96,256]{2,1,0:T(8,128)S(1)}, u32[]{:S(2)}, u32[]{:S(2)}) collective-permute-start(f32[2,96,256]{2,1,0:T(8,128)S(1)} %get-tuple-element.17), channel_id=1, source_target_pairs={{0,8},{8,16},{16,24},{24,0},{1,9},{9,17},{17,25},{25,1},{2,10},{10... | collective-permute-start | bytes 589832 | tf_op jit(solution)/shard_map/ppermute | solution.py:149
  117.8 6.8 %collective-permute-start.26 = (f32[2,96,256]{2,1,0:T(8,128)S(1)}, f32[2,96,256]{2,1,0:T(8,128)S(1)}, u32[]{:S(2)}, u32[]{:S(2)}) collective-permute-start(f32[2,96,256]{2,1,0:T(8,128)S(1)} %get-tuple-element.18), channel_id=1, source_target_pairs={{0,24},{8,0},{16,8},{24,16},{1,25},{9,1},{17,9},{25,17},{2,26},{10... | collective-permute-start | bytes 589832 | tf_op jit(solution)/shard_map/ppermute | solution.py:149
  120.7 11.6 %collective-permute-start.18 = (f32[4,96,256]{2,1,0:T(8,128)S(1)}, f32[4,96,256]{2,1,0:T(8,128)S(1)}, u32[]{:S(2)}, u32[]{:S(2)}) collective-permute-start(f32[4,96,256]{2,1,0:T(8,128)S(1)} %pad_maximum_fusion), channel_id=1, source_target_pairs={{0,2},{2,4},{4,6},{6,0},{1,3},{3,5},{5,7},{7,1},{8,10},{10,12},{12... | collective-permute-start | bytes 1179656 | tf_op jit(solution)/shard_map/ppermute | solution.py:149
  122.3 10.0 %collective-permute-start.20 = (f32[4,96,256]{2,1,0:T(8,128)S(1)}, f32[4,96,256]{2,1,0:T(8,128)S(1)}, u32[]{:S(2)}, u32[]{:S(2)}) collective-permute-start(f32[4,96,256]{2,1,0:T(8,128)S(1)} %pad_maximum_fusion.1), channel_id=1, source_target_pairs={{0,6},{2,0},{4,2},{6,4},{1,7},{3,1},{5,3},{7,5},{8,14},{10,8},{12,... | collective-permute-start | bytes 1179656 | tf_op jit(solution)/shard_map/ppermute | solution.py:149
  124.6 13.8 %collective-permute-start.25 = (f32[4,96,256]{2,1,0:T(8,128)S(1)}, f32[4,96,256]{2,1,0:T(8,128)S(1)}, u32[]{:S(2)}, u32[]{:S(2)}) collective-permute-start(f32[4,96,256]{2,1,0:T(8,128)S(1)} %pad_maximum_fusion.2), channel_id=1, source_target_pairs={{0,8},{8,16},{16,24},{24,0},{1,9},{9,17},{17,25},{25,1},{2,10},{10... | collective-permute-start | bytes 1179656 | tf_op jit(solution)/shard_map/ppermute | solution.py:149
  126.3 12.2 %collective-permute-start.27 = (f32[4,96,256]{2,1,0:T(8,128)S(1)}, f32[4,96,256]{2,1,0:T(8,128)S(1)}, u32[]{:S(2)}, u32[]{:S(2)}) collective-permute-start(f32[4,96,256]{2,1,0:T(8,128)S(1)} %pad_maximum_fusion.3), channel_id=1, source_target_pairs={{0,24},{8,0},{16,8},{24,16},{1,25},{9,1},{17,9},{25,17},{2,26},{10... | collective-permute-start | bytes 1179656 | tf_op jit(solution)/shard_map/ppermute | solution.py:149
  132.4 9.4 %collective-permute-start.21 = (f32[96,256]{1,0:T(8,128)S(1)}, f32[96,256]{1,0:T(8,128)S(1)}, u32[]{:S(2)}, u32[]{:S(2)}) collective-permute-start(f32[96,256]{1,0:T(8,128)S(1)} %get-tuple-element.23), channel_id=1, source_target_pairs={{0,8},{8,16},{16,24},{24,0},{1,9},{9,17},{17,25},{25,1},{2,10},{10... | collective-permute-start | bytes 294920 | tf_op jit(solution)/shard_map/ppermute | solution.py:149
  134.4 8.9 %collective-permute-start.22 = (f32[96,256]{1,0:T(8,128)S(1)}, f32[96,256]{1,0:T(8,128)S(1)}, u32[]{:S(2)}, u32[]{:S(2)}) collective-permute-start(f32[96,256]{1,0:T(8,128)S(1)} %get-tuple-element.22), channel_id=1, source_target_pairs={{0,24},{8,0},{16,8},{24,16},{1,25},{9,1},{17,9},{25,17},{2,26},{10... | collective-permute-start | bytes 294920 | tf_op jit(solution)/shard_map/ppermute | solution.py:149
  136.6 6.8 %collective-permute-start.23 = (f32[96,256]{1,0:T(8,128)S(1)}, f32[96,256]{1,0:T(8,128)S(1)}, u32[]{:S(2)}, u32[]{:S(2)}) collective-permute-start(f32[96,256]{1,0:T(8,128)S(1)} %get-tuple-element.21), channel_id=1, source_target_pairs={{0,16},{8,24},{16,0},{24,8},{1,17},{9,25},{17,1},{25,9},{2,18},{10... | collective-permute-start | bytes 294920 | tf_op jit(solution)/shard_map/ppermute | solution.py:149
  138.5 6.5 %collective-permute-start.28 = (f32[96,256]{1,0:T(8,128)S(1)}, f32[96,256]{1,0:T(8,128)S(1)}, u32[]{:S(2)}, u32[]{:S(2)}) collective-permute-start(f32[96,256]{1,0:T(8,128)S(1)} %get-tuple-element.26), channel_id=1, source_target_pairs={{0,2},{2,4},{4,6},{6,0},{1,3},{3,5},{5,7},{7,1},{8,10},{10,12},{12... | collective-permute-start | bytes 294920 | tf_op jit(solution)/shard_map/ppermute | solution.py:149
  139.6 5.5 %collective-permute-start.29 = (f32[96,256]{1,0:T(8,128)S(1)}, f32[96,256]{1,0:T(8,128)S(1)}, u32[]{:S(2)}, u32[]{:S(2)}) collective-permute-start(f32[96,256]{1,0:T(8,128)S(1)} %get-tuple-element.25), channel_id=1, source_target_pairs={{0,6},{2,0},{4,2},{6,4},{1,7},{3,1},{5,3},{7,5},{8,14},{10,8},{12,... | collective-permute-start | bytes 294920 | tf_op jit(solution)/shard_map/ppermute | solution.py:149
  141.8 6.1 %collective-permute-start.30 = (f32[96,256]{1,0:T(8,128)S(1)}, f32[96,256]{1,0:T(8,128)S(1)}, u32[]{:S(2)}, u32[]{:S(2)}) collective-permute-start(f32[96,256]{1,0:T(8,128)S(1)} %get-tuple-element.24), channel_id=1, source_target_pairs={{0,4},{2,6},{4,0},{6,2},{1,5},{3,7},{5,1},{7,3},{8,12},{10,14},{12... | collective-permute-start | bytes 294920 | tf_op jit(solution)/shard_map/ppermute | solution.py:149

commit v8 on v7

--- a/solution.py
+++ b/solution.py
@@ -39,7 +39,7 @@
 LOCAL = pl.BlockSpec(memory_space=pltpu.VMEM)
 FAR = pl.BlockSpec(memory_space=pltpu.HBM)
 GRANT = pltpu.CompilerParams(vmem_limit_bytes=8 * 2**20)
-BUFFER = jax.ShapeDtypeStruct((2, 2, 4, 4, 3, ROWS, W), f32)
+BUFFER = jax.ShapeDtypeStruct((2, 4, 4, 3, ROWS, W), f32)
 
 
 def update_part(q, ints, floats, arrived, previous, left, mps):
@@ -65,25 +65,25 @@
     for k in range(1, SITES):
         e = jnp.where(site == k, environs[k][...], e)
     e = halves(e)
-    scales = [floats[2] * ints[16 + q].astype(f32)]
-    if q < NQ - 1:
-        scales.append(floats[3] * ints[17 + q].astype(f32))
-    for state in range(2):
-        if q + state < NQ:
+    work = [(0, q)] + [(1, q)] * (q < NQ - 1) + [(1, NQ - 1)] * (q == NQ - 2)
+    for slot, (state, at) in enumerate(work):
+        if at + state < NQ:
             n = ints[4 + q + state]
-            part = scales[state] * product(e, halves(psi[state, q]), ((1,), (0,)))
-            results[state] = product(halves(part), halves(framed(rights[q + state], n, n)), ((1,), (1,)))
+            c = floats[2 + state] * ints[16 + q + state].astype(f32)
+            part = c * product(e, halves(psi[state, q]), ((1,), (0,)))
+            results[slot] = product(halves(part), halves(framed(rights[q + state], n, n)), ((1,), (1,)))
         else:
-            results[state] = jnp.zeros((W, W), f32)
+            results[slot] = jnp.zeros((W, W), f32)
         for i in range(W // ROWS):
-            owner, third = divmod((W // ROWS) * q + i, 3)
+            owner, third = divmod((W // ROWS) * at + i, 3)
             z = (owner // 8 - my_z + 4) % 4
             x = ((owner // 2) % 4 - my_x + 4) % 4
             sent = core if owner % 2 == 0 else 1 - core
             near, far = ((x, z), (z, x))[state]
             pltpu.make_async_copy(
-                results.at[state, pl.ds(ROWS * i, ROWS)], pieces.at[sent, state, near, far, third], stores).start()
-    pltpu.make_async_copy(results, psi.at[:, 0], stores).wait()
+                results.at[slot, pl.ds(ROWS * i, ROWS)], pieces[state].at[sent, near, far, third], stores).start()
+    stored = results.at[pl.ds(0, len(work))]
+    pltpu.make_async_copy(stored, stored, stores).wait()
 
 
 def early_step(q, ints, floats, left, mps):
@@ -129,18 +129,20 @@
 
 
 def apply_step(q, ints, floats, environs, psi, rights, held):
+    operands = (*environs, psi, rights)
+    states = 1 if q == NQ - 1 else 2
+
     def kernel(ints, floats, *refs):
         psi, rights = refs[SITES:SITES + 2]
-        apply_part(q, ints, floats, refs[:SITES], psi, rights, *refs[-3:])
-
-    operands = (*environs, psi, rights)
+        apply_part(q, ints, floats, refs[:SITES], psi, rights, refs[-2 - states:-2], *refs[-2:])
+
     return pl.pallas_call(
         kernel,
         in_specs=[SCALAR] * 2 + [LOCAL] * len(operands) + [FAR] * len(held),
-        out_specs=[FAR],
-        out_shape=[BUFFER],
-        scratch_shapes=[pltpu.VMEM((2, W, W), f32), pltpu.SemaphoreType.DMA],
-        input_output_aliases={2 + len(operands): 0} if held else {},
+        out_specs=[FAR] * states,
+        out_shape=[BUFFER] * states,
+        scratch_shapes=[pltpu.VMEM((3, W, W), f32), pltpu.SemaphoreType.DMA],
+        input_output_aliases={2 + len(operands) + i: i for i in range(len(held))},
         compiler_params=GRANT,
     )(ints, floats, *operands, *held)
 
@@ -161,11 +163,17 @@
     return (line[0] + turned(line[1], axis, 1)) + (turned(line[3], axis, -1) + turned(line[2], axis, 2))
 
 
-def reduced(pieces):
-    both = pieces[0] + lax.ppermute(pieces[1], "core", [(0, 1), (1, 0)])
-    both = both.reshape(2, 4, 4, 96, W)
-    first = first_phase(both[0], "x")
-    second = first_phase(both[1], "z")
+def swapped(pieces):
+    return lax.ppermute(pieces[1], "core", [(0, 1), (1, 0)])
+
+
+def reduced(first, first_got, second, second_got):
+    shape = (4, 4, 96, W)
+    second = (second[0] + second_got).reshape(shape)
+    second, first_got = lax.optimization_barrier((second, first_got))
+    first = (first[0] + first_got).reshape(shape)
+    second = first_phase(second, "z")
+    first = first_phase(first, "x")
     return jnp.stack([second_phase(first, "z"), second_phase(second, "x")])[None]
 
 
@@ -188,10 +196,13 @@
         if step + LAG < LAST:
             arrivals[step + LAG] = lax.ppermute(environ, "site", [(0, 1), (1, 2), (2, 3)])
         q = step - LAG * (SITES - 1)
+        if q == NQ - 1:
+            second, held = held[1], held[:1]
+            second_got = swapped(second)
         if q >= 0:
             held = apply_step(
                 q, ints, floats, [environs[q + LAG * k] for k in range(SITES)], psi[0], right_env[0, 0], held)
-    return reduced(*held)
+    return reduced(held[0], swapped(held[0]), second, second_got)
 
 
 def solution(mesh):

time: 149 us -> 147 us (0.987)
  waiting for transfers between devices: 46.7 us -> 44.2 us
    ppermute x1 -> x2, waiting for transfers between devices: 5.65 us -> 3.12 us  [swapped(): return lax.ppermute(pieces[1], 'core', [(0, 1), (1, 0)])]
  transfers between devices with their start and end apart: 31 -> 32, of which waited for: 20 -> 21; matrix products, arithmetic and copies ran while one was open for 0% -> 1% of each run, Pallas kernels for 31% -> 34%
where the time goes in v8:
time: 147 us; the launch traced here: 145 us
  Pallas kernels  49.6 us (34%)
  starting transfers between devices  47.4 us (32%)
  waiting for transfers between devices  44.2 us (30%)
  local copies, waits for them, and re-layouts  1.95 us (1%)
  other arithmetic  1.67 us (1%)
    ppermute x16, waiting for transfers between devices, shards(): lax.ppermute(environ, 'site', [(0, 1), (1, 2), (2, 3)])  31.7 us
    pallas_call x12, Pallas kernels, apply_step(): pl.pallas_call(kernel, in_specs=[SCALAR] * 2 + [LOCAL] * len(operands) +...  28.9 us
    ppermute x14, starting transfers between devices, turned(): return lax.ppermute(x, axis, [(i, (i + by) % 4) for i in range(4)])  25.6 us
    ppermute x16, starting transfers between devices, shards(): lax.ppermute(environ, 'site', [(0, 1), (1, 2), (2, 3)])  21.4 us
    pallas_call x16, Pallas kernels, update_step(): pl.pallas_call(kernel, in_specs=[SCALAR] * 2 + [LOCAL] * 4 + [FAR] * len(...  19.6 us
    ppermute x14, waiting for transfers between devices, turned(): return lax.ppermute(x, axis, [(i, (i + by) % 4) for i in range(4)])  9.38 us
    ppermute x2, waiting for transfers between devices, swapped(): return lax.ppermute(pieces[1], 'core', [(0, 1), (1, 0)])  3.12 us
  transfers between devices with their start and end apart: 32, of which 21 were waited for; matrix products, arithmetic and copies ran while one was open for 1% of the time, Pallas kernels for 34%

profile of v8, /device:TPU:24, one launch (start us, length us, event | category | flops | bytes accessed | tf_op | source)
XLA Modules:
  0.0 145.5 jit_solution(663291983235878994)
XLA Ops:
  2.0 1.6 %collective-permute-start.1 = (f32[256,256]{1,0:T(8,128)S(1)}, f32[256,256]{1,0:T(8,128)S(1)}, u32[]{:S(2)}, u32[]{:S(2)}) collective-permute-start(f32[256,256]{1,0:T(8,128)S(1)} %shard_map.74.refs_0_), channel_id=1, source_target_pairs={{0,32},{32,64},{64,96},{1,33},{33,65},{65,97},{2,34},{34,66},{66,9... | collective-permute-start | bytes 786440 | tf_op jit(solution)/shard_map/ppermute | solution.py:197
  5.5 7.9 %collective-permute-done.1.previous.arrived = f32[256,256]{1,0:T(8,128)S(1)} collective-permute-done((f32[256,256]{1,0:T(8,128)S(1)}, f32[256,256]{1,0:T(8,128)S(1)}, u32[]{:S(2)}, u32[]{:S(2)}) %collective-permute-start.1) | collective-permute-done | bytes 262176 | tf_op jit(solution)/shard_map/ppermute | solution.py:197
  15.3 3.7 %collective-permute-done.arrived.previous = f32[256,256]{1,0:T(8,128)S(1)} collective-permute-done((f32[256,256]{1,0:T(8,128)S(1)}, f32[256,256]{1,0:T(8,128)S(1)}, u32[]{:S(2)}, u32[]{:S(2)}) %collective-permute-start) | collective-permute-done | bytes 262176 | tf_op jit(solution)/shard_map/ppermute | solution.py:197
  20.8 4.2 %collective-permute-done.3.previous.arrived = f32[256,256]{1,0:T(8,128)S(1)} collective-permute-done((f32[256,256]{1,0:T(8,128)S(1)}, f32[256,256]{1,0:T(8,128)S(1)}, u32[]{:S(2)}, u32[]{:S(2)}) %collective-permute-start.3) | collective-permute-done | bytes 262176 | tf_op jit(solution)/shard_map/ppermute | solution.py:197
  26.9 3.8 %collective-permute-done.2.arrived.previous = f32[256,256]{1,0:T(8,128)S(1)} collective-permute-done((f32[256,256]{1,0:T(8,128)S(1)}, f32[256,256]{1,0:T(8,128)S(1)}, u32[]{:S(2)}, u32[]{:S(2)}) %collective-permute-start.2) | collective-permute-done | bytes 262176 | tf_op jit(solution)/shard_map/ppermute | solution.py:197
  31.3 1.6 %collective-permute-start.4 = (f32[256,256]{1,0:T(8,128)S(1)}, f32[256,256]{1,0:T(8,128)S(1)}, u32[]{:S(2)}, u32[]{:S(2)}) collective-permute-start(f32[256,256]{1,0:T(8,128)S(1)} %shard_map.77.refs_2_.refs_1_.refs_0_), channel_id=1, source_target_pairs={{0,32},{32,64},{64,96},{1,33},{33,65},{65,97},{2,34},{34,66},{66,9... | collective-permute-start | bytes 786440 | tf_op jit(solution)/shard_map/ppermute | solution.py:197
  32.8 3.6 %collective-permute-done.5.arrived.previous = f32[256,256]{1,0:T(8,128)S(1)} collective-permute-done((f32[256,256]{1,0:T(8,128)S(1)}, f32[256,256]{1,0:T(8,128)S(1)}, u32[]{:S(2)}, u32[]{:S(2)}) %collective-permute-start.5) | collective-permute-done | bytes 262176 | tf_op jit(solution)/shard_map/ppermute | solution.py:197
  36.5 1.4 shard_map.79.refs_3_.refs_2_.refs_1_.refs_0_
  39.2 2.5 %shard_map.80 = (f32[2,4,4,3,32,256]{5,4,3,2,1,0:T(8,128)S(1)}, f32[2,4,4,3,32,256]{5,4,3,2,1,0:T(8,128)S(1)}) custom-call(s32[28]{0:T(128)S(1)} %concatenate.15.ints, f32[4]{0:T(128)S(1)} %bitcast.160, f32[256,256]{1,0:T(8,128)S(1)} %shard_map.74.refs_0_, f32[256,256]{1,0:T(8,128)S(1)} %shard_map.76.refs_1_.refs_0_, ...), custom_call_target="tpu_custom_call" | custom-call | tf_op jit(solution)/shard_map/pallas_call | solution.py:139
  44.6 2.5 %shard_map.82 = (f32[2,4,4,3,32,256]{5,4,3,2,1,0:T(8,128)S(1)}, f32[2,4,4,3,32,256]{5,4,3,2,1,0:T(8,128)S(1)}) custom-call(s32[28]{0:T(128)S(1)} %concatenate.15.ints, f32[4]{0:T(128)S(1)} %bitcast.162, f32[256,256]{1,0:T(8,128)S(1)} %shard_map.73.refs_0_, f32[256,256]{1,0:T(8,128)S(1)} %shard_map.75.refs_1_.refs_0_, ...), custom_call_target="tpu_custom_call", output_to_operand_aliasing={{0}: (8, {}), {1}: (9, {})} | custom-call | tf_op jit(solution)/shard_map/pallas_call | solution.py:139
  47.7 1.4 shard_map.83.refs_3_.refs_2_.refs_1_.refs_0_
  50.4 2.5 %shard_map.84 = (f32[2,4,4,3,32,256]{5,4,3,2,1,0:T(8,128)S(1)}, f32[2,4,4,3,32,256]{5,4,3,2,1,0:T(8,128)S(1)}) custom-call(s32[28]{0:T(128)S(1)} %concatenate.15.ints, f32[4]{0:T(128)S(1)} %bitcast.164, f32[256,256]{1,0:T(8,128)S(1)} %shard_map.76.refs_1_.refs_0_, ...), custom_call_target="tpu_custom_call", output_to_operand_aliasing={{0}: (8, {}), {1}: (9, {})} | custom-call | tf_op jit(solution)/shard_map/pallas_call | solution.py:139
  56.4 2.5 %shard_map.86 = (f32[2,4,4,3,32,256]{5,4,3,2,1,0:T(8,128)S(1)}, f32[2,4,4,3,32,256]{5,4,3,2,1,0:T(8,128)S(1)}) custom-call(s32[28]{0:T(128)S(1)} %concatenate.15.ints, f32[4]{0:T(128)S(1)} %bitcast.166, f32[256,256]{1,0:T(8,128)S(1)} %shard_map.75.refs_1_.refs_0_, ...), custom_call_target="tpu_custom_call", output_to_operand_aliasing={{0}: (8, {}), {1}: (9, {})} | custom-call | tf_op jit(solution)/shard_map/pallas_call | solution.py:139
  59.5 1.4 shard_map.87.refs_3_.refs_2_.refs_1_.refs_0_
  60.9 1.5 %collective-permute-start.11 = (f32[256,256]{1,0:T(8,128)S(1)}, f32[256,256]{1,0:T(8,128)S(1)}, u32[]{:S(2)}, u32[]{:S(2)}) collective-permute-start(f32[256,256]{1,0:T(8,128)S(1)} %shard_map.87.refs_3_.refs_2_.refs_1_.refs_0_), channel_id=1, source_target_pairs={{0,32},{32,64},{64,96},{1,33},{33,65},{65,97},{2,34},{34,66},{66,9... | collective-permute-start | bytes 786440 | tf_op jit(solution)/shard_map/ppermute | solution.py:197
  62.4 2.5 %shard_map.88 = (f32[2,4,4,3,32,256]{5,4,3,2,1,0:T(8,128)S(1)}, f32[2,4,4,3,32,256]{5,4,3,2,1,0:T(8,128)S(1)}) custom-call(s32[28]{0:T(128)S(1)} %concatenate.15.ints, f32[4]{0:T(128)S(1)} %bitcast.168, f32[256,256]{1,0:T(8,128)S(1)} %shard_map.78.refs_2_.refs_1_.refs_0_, ...), custom_call_target="tpu_custom_call", output_to_operand_aliasing={{0}: (8, {}), {1}: (9, {})} | custom-call | tf_op jit(solution)/shard_map/pallas_call | solution.py:139
  65.3 1.4 shard_map.89.refs_3_.refs_2_.refs_1_.refs_0_
  68.1 2.5 %shard_map.90 = (f32[2,4,4,3,32,256]{5,4,3,2,1,0:T(8,128)S(1)}, f32[2,4,4,3,32,256]{5,4,3,2,1,0:T(8,128)S(1)}) custom-call(s32[28]{0:T(128)S(1)} %concatenate.15.ints, f32[4]{0:T(128)S(1)} %bitcast.170, f32[256,256]{1,0:T(8,128)S(1)} %shard_map.77.refs_2_.refs_1_.refs_0_, ...), custom_call_target="tpu_custom_call", output_to_operand_aliasing={{0}: (8, {}), {1}: (9, {})} | custom-call | tf_op jit(solution)/shard_map/pallas_call | solution.py:139
  71.0 1.5 shard_map.91.refs_3_.refs_2_.refs_1_
  73.8 2.5 %shard_map.92 = (f32[2,4,4,3,32,256]{5,4,3,2,1,0:T(8,128)S(1)}, f32[2,4,4,3,32,256]{5,4,3,2,1,0:T(8,128)S(1)}) custom-call(s32[28]{0:T(128)S(1)} %concatenate.15.ints, f32[4]{0:T(128)S(1)} %bitcast.172, f32[256,256]{1,0:T(8,128)S(1)} %shard_map.79.refs_3_.refs_2_.refs_1_.refs_0_, ...), custom_call_target="tpu_custom_call", output_to_operand_aliasing={{0}: (8, {}), {1}: (9, {})} | custom-call | tf_op jit(solution)/shard_map/pallas_call | solution.py:139
  77.2 1.4 shard_map.93.refs_3_.refs_2_.refs_1_
  80.0 2.5 %shard_map.94 = (f32[2,4,4,3,32,256]{5,4,3,2,1,0:T(8,128)S(1)}, f32[2,4,4,3,32,256]{5,4,3,2,1,0:T(8,128)S(1)}) custom-call(s32[28]{0:T(128)S(1)} %concatenate.15.ints, f32[4]{0:T(128)S(1)} %bitcast.174, f32[256,256]{1,0:T(8,128)S(1)} %shard_map.81.refs_3_.refs_2_.refs_1_.refs_0_, ...), custom_call_target="tpu_custom_call", output_to_operand_aliasing={{0}: (8, {}), {1}: (9, {})} | custom-call | tf_op jit(solution)/shard_map/pallas_call | solution.py:139
  83.1 1.4 shard_map.95.refs_3_.refs_2_
  85.8 2.5 %shard_map.96 = (f32[2,4,4,3,32,256]{5,4,3,2,1,0:T(8,128)S(1)}, f32[2,4,4,3,32,256]{5,4,3,2,1,0:T(8,128)S(1)}) custom-call(s32[28]{0:T(128)S(1)} %concatenate.15.ints, f32[4]{0:T(128)S(1)} %bitcast.176, f32[256,256]{1,0:T(8,128)S(1)} %shard_map.83.refs_3_.refs_2_.refs_1_.refs_0_, ...), custom_call_target="tpu_custom_call", output_to_operand_aliasing={{0}: (8, {}), {1}: (9, {})} | custom-call | tf_op jit(solution)/shard_map/pallas_call | solution.py:139
  88.9 1.4 shard_map.97.refs_3_.refs_2_
  90.4 2.5 %shard_map.98 = (f32[2,4,4,3,32,256]{5,4,3,2,1,0:T(8,128)S(1)}, f32[2,4,4,3,32,256]{5,4,3,2,1,0:T(8,128)S(1)}) custom-call(s32[28]{0:T(128)S(1)} %concatenate.15.ints, f32[4]{0:T(128)S(1)} %bitcast.178, f32[256,256]{1,0:T(8,128)S(1)} %shard_map.85.refs_3_.refs_2_.refs_1_.refs_0_, ...), custom_call_target="tpu_custom_call", output_to_operand_aliasing={{0}: (8, {}), {1}: (9, {})} | custom-call | tf_op jit(solution)/shard_map/pallas_call | solution.py:139
  94.2 1.4 shard_map.99.refs_3_
  95.6 2.8 %shard_map.100 = (f32[2,4,4,3,32,256]{5,4,3,2,1,0:T(8,128)S(1)}, f32[2,4,4,3,32,256]{5,4,3,2,1,0:T(8,128)S(1)}) custom-call(s32[28]{0:T(128)S(1)} %concatenate.15.ints, f32[4]{0:T(128)S(1)} %bitcast.180, f32[256,256]{1,0:T(8,128)S(1)} %shard_map.87.refs_3_.refs_2_.refs_1_.refs_0_, ...), custom_call_target="tpu_custom_call", output_to_operand_aliasing={{0}: (8, {}), {1}: (9, {})} | custom-call | tf_op jit(solution)/shard_map/pallas_call | solution.py:139
  98.7 3.2 %collective-permute-done.14.arrived = f32[256,256]{1,0:T(8,128)S(1)} collective-permute-done((f32[256,256]{1,0:T(8,128)S(1)}, f32[256,256]{1,0:T(8,128)S(1)}, u32[]{:S(2)}, u32[]{:S(2)}) %collective-permute-start.14) | collective-permute-done | bytes 262176 | tf_op jit(solution)/shard_map/ppermute | solution.py:197
  102.0 1.4 shard_map.101.refs_3_
  103.4 1.5 %shard_map.102 = f32[2,4,4,3,32,256]{5,4,3,2,1,0:T(8,128)S(1)} custom-call(s32[28]{0:T(128)S(1)} %concatenate.15.ints, f32[4]{0:T(128)S(1)} %bitcast.182, f32[256,256]{1,0:T(8,128)S(1)} %shard_map.89.refs_3_.refs_2_.refs_1_.refs_0_, f32[256,256]{1,0:T(8,128)S(1)} %shard_map.93.refs_3_.refs_2_.refs_1_, ...), custom_call_target="tpu_custom_call", output_to_operand_aliasing={{}: (8, {})} | custom-call | tf_op jit(solution)/shard_map/pallas_call | solution.py:139
  105.6 3.1 %collective-permute-done.17 = f32[4,4,3,32,256]{4,3,2,1,0:T(8,128)S(1)} collective-permute-done((f32[4,4,3,32,256]{4,3,2,1,0:T(8,128)S(1)}, f32[4,4,3,32,256]{4,3,2,1,0:T(8,128)S(1)}, u32[]{:S(2)}, u32[]{:S(2)}) %collective-permute-start.17) | collective-permute-done | bytes 1572896 | tf_op jit(solution)/shard_map/ppermute | solution.py:167
  109.1 1.6 %collective-permute-start.18 = (f32[2,96,256]{2,1,0:T(8,128)S(1)}, f32[2,96,256]{2,1,0:T(8,128)S(1)}, u32[]{:S(2)}, u32[]{:S(2)}) collective-permute-start(f32[2,96,256]{2,1,0:T(8,128)S(1)} %get-tuple-element.55), channel_id=1, source_target_pairs={{0,2},{2,4},{4,6},{6,0},{1,3},{3,5},{5,7},{7,1},{8,10},{10,12},{12... | collective-permute-start | bytes 589832 | tf_op jit(solution)/shard_map/ppermute | solution.py:151
  110.7 1.7 %collective-permute-start.20 = (f32[2,96,256]{2,1,0:T(8,128)S(1)}, f32[2,96,256]{2,1,0:T(8,128)S(1)}, u32[]{:S(2)}, u32[]{:S(2)}) collective-permute-start(f32[2,96,256]{2,1,0:T(8,128)S(1)} %get-tuple-element.56), channel_id=1, source_target_pairs={{0,6},{2,0},{4,2},{6,4},{1,7},{3,1},{5,3},{7,5},{8,14},{10,8},{12,... | collective-permute-start | bytes 589832 | tf_op jit(solution)/shard_map/ppermute | solution.py:151
  112.5 2.1 %collective-permute-start.25 = (f32[2,96,256]{2,1,0:T(8,128)S(1)}, f32[2,96,256]{2,1,0:T(8,128)S(1)}, u32[]{:S(2)}, u32[]{:S(2)}) collective-permute-start(f32[2,96,256]{2,1,0:T(8,128)S(1)} %get-tuple-element.61), channel_id=1, source_target_pairs={{0,8},{8,16},{16,24},{24,0},{1,9},{9,17},{17,25},{25,1},{2,10},{10... | collective-permute-start | bytes 589832 | tf_op jit(solution)/shard_map/ppermute | solution.py:151
  114.6 2.1 %collective-permute-start.27 = (f32[2,96,256]{2,1,0:T(8,128)S(1)}, f32[2,96,256]{2,1,0:T(8,128)S(1)}, u32[]{:S(2)}, u32[]{:S(2)}) collective-permute-start(f32[2,96,256]{2,1,0:T(8,128)S(1)} %get-tuple-element.62), channel_id=1, source_target_pairs={{0,24},{8,0},{16,8},{24,16},{1,25},{9,1},{17,9},{25,17},{2,26},{10... | collective-permute-start | bytes 589832 | tf_op jit(solution)/shard_map/ppermute | solution.py:151
  117.5 1.6 %collective-permute-start.19 = (f32[4,96,256]{2,1,0:T(8,128)S(1)}, f32[4,96,256]{2,1,0:T(8,128)S(1)}, u32[]{:S(2)}, u32[]{:S(2)}) collective-permute-start(f32[4,96,256]{2,1,0:T(8,128)S(1)} %pad_maximum_fusion), channel_id=1, source_target_pairs={{0,2},{2,4},{4,6},{6,0},{1,3},{3,5},{5,7},{7,1},{8,10},{10,12},{12... | collective-permute-start | bytes 1179656 | tf_op jit(solution)/shard_map/ppermute | solution.py:151
  119.1 1.7 %collective-permute-start.21 = (f32[4,96,256]{2,1,0:T(8,128)S(1)}, f32[4,96,256]{2,1,0:T(8,128)S(1)}, u32[]{:S(2)}, u32[]{:S(2)}) collective-permute-start(f32[4,96,256]{2,1,0:T(8,128)S(1)} %pad_maximum_fusion.1), channel_id=1, source_target_pairs={{0,6},{2,0},{4,2},{6,4},{1,7},{3,1},{5,3},{7,5},{8,14},{10,8},{12,... | collective-permute-start | bytes 1179656 | tf_op jit(solution)/shard_map/ppermute | solution.py:151
  121.4 1.7 %collective-permute-start.26 = (f32[4,96,256]{2,1,0:T(8,128)S(1)}, f32[4,96,256]{2,1,0:T(8,128)S(1)}, u32[]{:S(2)}, u32[]{:S(2)}) collective-permute-start(f32[4,96,256]{2,1,0:T(8,128)S(1)} %pad_maximum_fusion.2), channel_id=1, source_target_pairs={{0,8},{8,16},{16,24},{24,0},{1,9},{9,17},{17,25},{25,1},{2,10},{10... | collective-permute-start | bytes 1179656 | tf_op jit(solution)/shard_map/ppermute | solution.py:151
  123.1 2.2 %collective-permute-start.28 = (f32[4,96,256]{2,1,0:T(8,128)S(1)}, f32[4,96,256]{2,1,0:T(8,128)S(1)}, u32[]{:S(2)}, u32[]{:S(2)}) collective-permute-start(f32[4,96,256]{2,1,0:T(8,128)S(1)} %pad_maximum_fusion.3), channel_id=1, source_target_pairs={{0,24},{8,0},{16,8},{24,16},{1,25},{9,1},{17,9},{25,17},{2,26},{10... | collective-permute-start | bytes 1179656 | tf_op jit(solution)/shard_map/ppermute | solution.py:151
  125.3 3.7 %collective-permute-done.19 = f32[4,96,256]{2,1,0:T(8,128)S(1)} collective-permute-done((f32[4,96,256]{2,1,0:T(8,128)S(1)}, f32[4,96,256]{2,1,0:T(8,128)S(1)}, u32[]{:S(2)}, u32[]{:S(2)}) %collective-permute-start.19) | collective-permute-done | bytes 393248 | tf_op jit(solution)/shard_map/ppermute | solution.py:151
  129.2 2.1 %collective-permute-start.22 = (f32[96,256]{1,0:T(8,128)S(1)}, f32[96,256]{1,0:T(8,128)S(1)}, u32[]{:S(2)}, u32[]{:S(2)}) collective-permute-start(f32[96,256]{1,0:T(8,128)S(1)} %get-tuple-element.67), channel_id=1, source_target_pairs={{0,8},{8,16},{16,24},{24,0},{1,9},{9,17},{17,25},{25,1},{2,10},{10... | collective-permute-start | bytes 294920 | tf_op jit(solution)/shard_map/ppermute | solution.py:151
  131.2 2.1 %collective-permute-start.23 = (f32[96,256]{1,0:T(8,128)S(1)}, f32[96,256]{1,0:T(8,128)S(1)}, u32[]{:S(2)}, u32[]{:S(2)}) collective-permute-start(f32[96,256]{1,0:T(8,128)S(1)} %get-tuple-element.66), channel_id=1, source_target_pairs={{0,24},{8,0},{16,8},{24,16},{1,25},{9,1},{17,9},{25,17},{2,26},{10... | collective-permute-start | bytes 294920 | tf_op jit(solution)/shard_map/ppermute | solution.py:151
  133.4 1.9 %collective-permute-start.24 = (f32[96,256]{1,0:T(8,128)S(1)}, f32[96,256]{1,0:T(8,128)S(1)}, u32[]{:S(2)}, u32[]{:S(2)}) collective-permute-start(f32[96,256]{1,0:T(8,128)S(1)} %get-tuple-element.65), channel_id=1, source_target_pairs={{0,16},{8,24},{16,0},{24,8},{1,17},{9,25},{17,1},{25,9},{2,18},{10... | collective-permute-start | bytes 294920 | tf_op jit(solution)/shard_map/ppermute | solution.py:151
  136.4 2.2 %collective-permute-start.30 = (f32[96,256]{1,0:T(8,128)S(1)}, f32[96,256]{1,0:T(8,128)S(1)}, u32[]{:S(2)}, u32[]{:S(2)}) collective-permute-start(f32[96,256]{1,0:T(8,128)S(1)} %get-tuple-element.69), channel_id=1, source_target_pairs={{0,6},{2,0},{4,2},{6,4},{1,7},{3,1},{5,3},{7,5},{8,14},{10,8},{12,... | collective-permute-start | bytes 294920 | tf_op jit(solution)/shard_map/ppermute | solution.py:151
  138.6 1.5 %collective-permute-start.31 = (f32[96,256]{1,0:T(8,128)S(1)}, f32[96,256]{1,0:T(8,128)S(1)}, u32[]{:S(2)}, u32[]{:S(2)}) collective-permute-start(f32[96,256]{1,0:T(8,128)S(1)} %get-tuple-element.68), channel_id=1, source_target_pairs={{0,4},{2,6},{4,0},{6,2},{1,5},{3,7},{5,1},{7,3},{8,12},{10,14},{12... | collective-permute-start | bytes 294920 | tf_op jit(solution)/shard_map/ppermute | solution.py:151
  140.2 1.7 %collective-permute-done.29 = f32[96,256]{1,0:T(8,128)S(1)} collective-permute-done((f32[96,256]{1,0:T(8,128)S(1)}, f32[96,256]{1,0:T(8,128)S(1)}, u32[]{:S(2)}, u32[]{:S(2)}) %collective-permute-start.29) | collective-permute-done | bytes 98336 | tf_op jit(solution)/shard_map/ppermute | solution.py:151
  141.9 2.9 %collective-permute-done.31 = f32[96,256]{1,0:T(8,128)S(1)} collective-permute-done((f32[96,256]{1,0:T(8,128)S(1)}, f32[96,256]{1,0:T(8,128)S(1)}, u32[]{:S(2)}, u32[]{:S(2)}) %collective-permute-start.31) | collective-permute-done | bytes 98336 | tf_op jit(solution)/shard_map/ppermute | solution.py:151
  (86 shorter events, 34.5 us)
Async XLA Ops:
  0.7 0.7 copy-start.2
  1.4 2.2 %copy-start.3 = (f32[1,1,4]{2,1,0:T(1,128)S(1)}, f32[1,1,4]{2,1,0:T(1,128)}, u32[]{:S(2)}) copy-start(f32[1,1,4]{2,1,0:T(1,128)} %param.11) | copy-start | bytes 52
  1.4 12.0 %slice-start = ((s8[6291456]{0:T(1024)(128)(4,1)}), s8[4194304]{0:T(1024)(128)(4,1)S(1)}, s32[]{:S(2)}) async-start(s8[6291456]{0:T(1024)(128)(4,1)} %bitcast.91), calls=%async_computation | async-start | bytes 8388608
  2.0 11.4 %slice-start.1 = ((s8[6291456]{0:T(1024)(128)(4,1)}), s8[2097152]{0:T(1024)(128)(4,1)S(1)}, s32[]{:S(2)}) async-start(s8[6291456]{0:T(1024)(128)(4,1)} %bitcast.91), calls=%async_computation.1 | async-start | bytes 4194304
  2.0 11.4 %copy-start = (f32[1,12,256,256]{3,2,1,0:T(8,128)S(1)}, f32[1,12,256,256]{3,2,1,0:T(8,128)}, u32[]{:S(2)}) copy-start(f32[1,12,256,256]{3,2,1,0:T(8,128)} %param.7) | copy-start | bytes 9437188
  2.0 11.3 %collective-permute-start.1 = (f32[256,256]{1,0:T(8,128)S(1)}, f32[256,256]{1,0:T(8,128)S(1)}, u32[]{:S(2)}, u32[]{:S(2)}) collective-permute-start(f32[256,256]{1,0:T(8,128)S(1)} %shard_map.74.refs_0_), channel_id=1, source_target_pairs={{0,32},{32,64},{64,96},{1,33},{33,65},{65,97},{2,34},{34,66},{66,9... | collective-permute-start | bytes 786440 | tf_op jit(solution)/shard_map/ppermute | solution.py:197
  4.2 14.8 %collective-permute-start = (f32[256,256]{1,0:T(8,128)S(1)}, f32[256,256]{1,0:T(8,128)S(1)}, u32[]{:S(2)}, u32[]{:S(2)}) collective-permute-start(f32[256,256]{1,0:T(8,128)S(1)} %shard_map.73.refs_0_), channel_id=1, source_target_pairs={{0,32},{32,64},{64,96},{1,33},{33,65},{65,97},{2,34},{34,66},{66,9... | collective-permute-start | bytes 786440 | tf_op jit(solution)/shard_map/ppermute | solution.py:197
  14.0 11.1 %collective-permute-start.3 = (f32[256,256]{1,0:T(8,128)S(1)}, f32[256,256]{1,0:T(8,128)S(1)}, u32[]{:S(2)}, u32[]{:S(2)}) collective-permute-start(f32[256,256]{1,0:T(8,128)S(1)} %shard_map.76.refs_1_.refs_0_), channel_id=1, source_target_pairs={{0,32},{32,64},{64,96},{1,33},{33,65},{65,97},{2,34},{34,66},{66,9... | collective-permute-start | bytes 786440 | tf_op jit(solution)/shard_map/ppermute | solution.py:197
  19.5 11.1 %collective-permute-start.2 = (f32[256,256]{1,0:T(8,128)S(1)}, f32[256,256]{1,0:T(8,128)S(1)}, u32[]{:S(2)}, u32[]{:S(2)}) collective-permute-start(f32[256,256]{1,0:T(8,128)S(1)} %shard_map.75.refs_1_.refs_0_), channel_id=1, source_target_pairs={{0,32},{32,64},{64,96},{1,33},{33,65},{65,97},{2,34},{34,66},{66,9... | collective-permute-start | bytes 786440 | tf_op jit(solution)/shard_map/ppermute | solution.py:197
  25.6 10.8 %collective-permute-start.5 = (f32[256,256]{1,0:T(8,128)S(1)}, f32[256,256]{1,0:T(8,128)S(1)}, u32[]{:S(2)}, u32[]{:S(2)}) collective-permute-start(f32[256,256]{1,0:T(8,128)S(1)} %shard_map.78.refs_2_.refs_1_.refs_0_), channel_id=1, source_target_pairs={{0,32},{32,64},{64,96},{1,33},{33,65},{65,97},{2,34},{34,66},{66,9... | collective-permute-start | bytes 786440 | tf_op jit(solution)/shard_map/ppermute | solution.py:197
  30.7 8.5 %slice-start.2 = ((s8[6291456]{0:T(1024)(128)(4,1)}), s8[4194304]{0:T(1024)(128)(4,1)S(1)}, s32[]{:S(2)}) async-start(s8[6291456]{0:T(1024)(128)(4,1)} %bitcast.127), calls=%async_computation.2 | async-start | bytes 8388608
  31.2 8.0 %slice-start.3 = ((s8[6291456]{0:T(1024)(128)(4,1)}), s8[2097152]{0:T(1024)(128)(4,1)S(1)}, s32[]{:S(2)}) async-start(s8[6291456]{0:T(1024)(128)(4,1)} %bitcast.127), calls=%async_computation.3 | async-start | bytes 4194304
  31.2 8.0 %copy-start.1 = (f32[1,1,12,256,256]{4,3,2,1,0:T(8,128)S(1)}, f32[1,1,12,256,256]{4,3,2,1,0:T(8,128)}, u32[]{:S(2)}) copy-start(f32[1,1,12,256,256]{4,3,2,1,0:T(8,128)} %param.8) | copy-start | bytes 9437188
  31.3 10.6 %collective-permute-start.4 = (f32[256,256]{1,0:T(8,128)S(1)}, f32[256,256]{1,0:T(8,128)S(1)}, u32[]{:S(2)}, u32[]{:S(2)}) collective-permute-start(f32[256,256]{1,0:T(8,128)S(1)} %shard_map.77.refs_2_.refs_1_.refs_0_), channel_id=1, source_target_pairs={{0,32},{32,64},{64,96},{1,33},{33,65},{65,97},{2,34},{34,66},{66,9... | collective-permute-start | bytes 786440 | tf_op jit(solution)/shard_map/ppermute | solution.py:197
  37.9 9.8 %collective-permute-start.7 = (f32[256,256]{1,0:T(8,128)S(1)}, f32[256,256]{1,0:T(8,128)S(1)}, u32[]{:S(2)}, u32[]{:S(2)}) collective-permute-start(f32[256,256]{1,0:T(8,128)S(1)} %shard_map.79.refs_3_.refs_2_.refs_1_.refs_0_), channel_id=1, source_target_pairs={{0,32},{32,64},{64,96},{1,33},{33,65},{65,97},{2,34},{34,66},{66,9... | collective-permute-start | bytes 786440 | tf_op jit(solution)/shard_map/ppermute | solution.py:197
  43.3 10.3 %collective-permute-start.6 = (f32[256,256]{1,0:T(8,128)S(1)}, f32[256,256]{1,0:T(8,128)S(1)}, u32[]{:S(2)}, u32[]{:S(2)}) collective-permute-start(f32[256,256]{1,0:T(8,128)S(1)} %shard_map.81.refs_3_.refs_2_.refs_1_.refs_0_), channel_id=1, source_target_pairs={{0,32},{32,64},{64,96},{1,33},{33,65},{65,97},{2,34},{34,66},{66,9... | collective-permute-start | bytes 786440 | tf_op jit(solution)/shard_map/ppermute | solution.py:197
  49.1 10.3 %collective-permute-start.9 = (f32[256,256]{1,0:T(8,128)S(1)}, f32[256,256]{1,0:T(8,128)S(1)}, u32[]{:S(2)}, u32[]{:S(2)}) collective-permute-start(f32[256,256]{1,0:T(8,128)S(1)} %shard_map.83.refs_3_.refs_2_.refs_1_.refs_0_), channel_id=1, source_target_pairs={{0,32},{32,64},{64,96},{1,33},{33,65},{65,97},{2,34},{34,66},{66,9... | collective-permute-start | bytes 786440 | tf_op jit(solution)/shard_map/ppermute | solution.py:197
  55.1 10.3 %collective-permute-start.8 = (f32[256,256]{1,0:T(8,128)S(1)}, f32[256,256]{1,0:T(8,128)S(1)}, u32[]{:S(2)}, u32[]{:S(2)}) collective-permute-start(f32[256,256]{1,0:T(8,128)S(1)} %shard_map.85.refs_3_.refs_2_.refs_1_.refs_0_), channel_id=1, source_target_pairs={{0,32},{32,64},{64,96},{1,33},{33,65},{65,97},{2,34},{34,66},{66,9... | collective-permute-start | bytes 786440 | tf_op jit(solution)/shard_map/ppermute | solution.py:197
  60.9 10.1 %collective-permute-start.11 = (f32[256,256]{1,0:T(8,128)S(1)}, f32[256,256]{1,0:T(8,128)S(1)}, u32[]{:S(2)}, u32[]{:S(2)}) collective-permute-start(f32[256,256]{1,0:T(8,128)S(1)} %shard_map.87.refs_3_.refs_2_.refs_1_.refs_0_), channel_id=1, source_target_pairs={{0,32},{32,64},{64,96},{1,33},{33,65},{65,97},{2,34},{34,66},{66,9... | collective-permute-start | bytes 786440 | tf_op jit(solution)/shard_map/ppermute | solution.py:197
  66.8 10.4 %collective-permute-start.10 = (f32[256,256]{1,0:T(8,128)S(1)}, f32[256,256]{1,0:T(8,128)S(1)}, u32[]{:S(2)}, u32[]{:S(2)}) collective-permute-start(f32[256,256]{1,0:T(8,128)S(1)} %shard_map.89.refs_3_.refs_2_.refs_1_.refs_0_), channel_id=1, source_target_pairs={{0,32},{32,64},{64,96},{1,33},{33,65},{65,97},{2,34},{34,66},{66,9... | collective-permute-start | bytes 786440 | tf_op jit(solution)/shard_map/ppermute | solution.py:197
  72.5 10.6 %collective-permute-start.13 = (f32[256,256]{1,0:T(8,128)S(1)}, f32[256,256]{1,0:T(8,128)S(1)}, u32[]{:S(2)}, u32[]{:S(2)}) collective-permute-start(f32[256,256]{1,0:T(8,128)S(1)} %shard_map.91.refs_3_.refs_2_.refs_1_), channel_id=1, source_target_pairs={{0,32},{32,64},{64,96},{1,33},{33,65},{65,97},{2,34},{34,66},{66,9... | collective-permute-start | bytes 786440 | tf_op jit(solution)/shard_map/ppermute | solution.py:197
  78.7 10.3 %collective-permute-start.12 = (f32[256,256]{1,0:T(8,128)S(1)}, f32[256,256]{1,0:T(8,128)S(1)}, u32[]{:S(2)}, u32[]{:S(2)}) collective-permute-start(f32[256,256]{1,0:T(8,128)S(1)} %shard_map.93.refs_3_.refs_2_.refs_1_), channel_id=1, source_target_pairs={{0,32},{32,64},{64,96},{1,33},{33,65},{65,97},{2,34},{34,66},{66,9... | collective-permute-start | bytes 786440 | tf_op jit(solution)/shard_map/ppermute | solution.py:197
  84.5 9.6 %collective-permute-start.15 = (f32[256,256]{1,0:T(8,128)S(1)}, f32[256,256]{1,0:T(8,128)S(1)}, u32[]{:S(2)}, u32[]{:S(2)}) collective-permute-start(f32[256,256]{1,0:T(8,128)S(1)} %shard_map.95.refs_3_.refs_2_), channel_id=1, source_target_pairs={{0,32},{32,64},{64,96},{1,33},{33,65},{65,97},{2,34},{34,66},{66,9... | collective-permute-start | bytes 786440 | tf_op jit(solution)/shard_map/ppermute | solution.py:197
  92.9 9.1 %collective-permute-start.14 = (f32[256,256]{1,0:T(8,128)S(1)}, f32[256,256]{1,0:T(8,128)S(1)}, u32[]{:S(2)}, u32[]{:S(2)}) collective-permute-start(f32[256,256]{1,0:T(8,128)S(1)} %shard_map.97.refs_3_.refs_2_), channel_id=1, source_target_pairs={{0,32},{32,64},{64,96},{1,33},{33,65},{65,97},{2,34},{34,66},{66,9... | collective-permute-start | bytes 786440 | tf_op jit(solution)/shard_map/ppermute | solution.py:197
  98.6 6.7 %collective-permute-start.16 = (f32[4,4,3,32,256]{4,3,2,1,0:T(8,128)S(1)}, f32[4,4,3,32,256]{4,3,2,1,0:T(8,128)S(1)}, u32[]{:S(2)}, u32[]{:S(2)}) collective-permute-start(f32[4,4,3,32,256]{4,3,2,1,0:T(8,128)S(1)} %slice_bitcast_fusion.2), channel_id=1, source_target_pairs={{0,1},{1,0},{2,3},{3,2},{4,5},{5,4},{6,7},{7,6},{8,9},{9,8},{10,11... | collective-permute-start | bytes 4718600 | tf_op jit(solution)/shard_map/ppermute | solution.py:167
  105.0 3.7 %collective-permute-start.17 = (f32[4,4,3,32,256]{4,3,2,1,0:T(8,128)S(1)}, f32[4,4,3,32,256]{4,3,2,1,0:T(8,128)S(1)}, u32[]{:S(2)}, u32[]{:S(2)}) collective-permute-start(f32[4,4,3,32,256]{4,3,2,1,0:T(8,128)S(1)} %slice_bitcast_fusion), channel_id=1, source_target_pairs={{0,1},{1,0},{2,3},{3,2},{4,5},{5,4},{6,7},{7,6},{8,9},{9,8},{10,11... | collective-permute-start | bytes 4718600 | tf_op jit(solution)/shard_map/ppermute | solution.py:167
  109.1 8.2 %collective-permute-start.18 = (f32[2,96,256]{2,1,0:T(8,128)S(1)}, f32[2,96,256]{2,1,0:T(8,128)S(1)}, u32[]{:S(2)}, u32[]{:S(2)}) collective-permute-start(f32[2,96,256]{2,1,0:T(8,128)S(1)} %get-tuple-element.55), channel_id=1, source_target_pairs={{0,2},{2,4},{4,6},{6,0},{1,3},{3,5},{5,7},{7,1},{8,10},{10,12},{12... | collective-permute-start | bytes 589832 | tf_op jit(solution)/shard_map/ppermute | solution.py:151
  110.7 6.7 %collective-permute-start.20 = (f32[2,96,256]{2,1,0:T(8,128)S(1)}, f32[2,96,256]{2,1,0:T(8,128)S(1)}, u32[]{:S(2)}, u32[]{:S(2)}) collective-permute-start(f32[2,96,256]{2,1,0:T(8,128)S(1)} %get-tuple-element.56), channel_id=1, source_target_pairs={{0,6},{2,0},{4,2},{6,4},{1,7},{3,1},{5,3},{7,5},{8,14},{10,8},{12,... | collective-permute-start | bytes 589832 | tf_op jit(solution)/shard_map/ppermute | solution.py:151
  112.5 8.8 %collective-permute-start.25 = (f32[2,96,256]{2,1,0:T(8,128)S(1)}, f32[2,96,256]{2,1,0:T(8,128)S(1)}, u32[]{:S(2)}, u32[]{:S(2)}) collective-permute-start(f32[2,96,256]{2,1,0:T(8,128)S(1)} %get-tuple-element.61), channel_id=1, source_target_pairs={{0,8},{8,16},{16,24},{24,0},{1,9},{9,17},{17,25},{25,1},{2,10},{10... | collective-permute-start | bytes 589832 | tf_op jit(solution)/shard_map/ppermute | solution.py:151
  114.6 6.7 %collective-permute-start.27 = (f32[2,96,256]{2,1,0:T(8,128)S(1)}, f32[2,96,256]{2,1,0:T(8,128)S(1)}, u32[]{:S(2)}, u32[]{:S(2)}) collective-permute-start(f32[2,96,256]{2,1,0:T(8,128)S(1)} %get-tuple-element.62), channel_id=1, source_target_pairs={{0,24},{8,0},{16,8},{24,16},{1,25},{9,1},{17,9},{25,17},{2,26},{10... | collective-permute-start | bytes 589832 | tf_op jit(solution)/shard_map/ppermute | solution.py:151
  117.5 11.6 %collective-permute-start.19 = (f32[4,96,256]{2,1,0:T(8,128)S(1)}, f32[4,96,256]{2,1,0:T(8,128)S(1)}, u32[]{:S(2)}, u32[]{:S(2)}) collective-permute-start(f32[4,96,256]{2,1,0:T(8,128)S(1)} %pad_maximum_fusion), channel_id=1, source_target_pairs={{0,2},{2,4},{4,6},{6,0},{1,3},{3,5},{5,7},{7,1},{8,10},{10,12},{12... | collective-permute-start | bytes 1179656 | tf_op jit(solution)/shard_map/ppermute | solution.py:151
  119.1 9.9 %collective-permute-start.21 = (f32[4,96,256]{2,1,0:T(8,128)S(1)}, f32[4,96,256]{2,1,0:T(8,128)S(1)}, u32[]{:S(2)}, u32[]{:S(2)}) collective-permute-start(f32[4,96,256]{2,1,0:T(8,128)S(1)} %pad_maximum_fusion.1), channel_id=1, source_target_pairs={{0,6},{2,0},{4,2},{6,4},{1,7},{3,1},{5,3},{7,5},{8,14},{10,8},{12,... | collective-permute-start | bytes 1179656 | tf_op jit(solution)/shard_map/ppermute | solution.py:151
  121.4 13.8 %collective-permute-start.26 = (f32[4,96,256]{2,1,0:T(8,128)S(1)}, f32[4,96,256]{2,1,0:T(8,128)S(1)}, u32[]{:S(2)}, u32[]{:S(2)}) collective-permute-start(f32[4,96,256]{2,1,0:T(8,128)S(1)} %pad_maximum_fusion.2), channel_id=1, source_target_pairs={{0,8},{8,16},{16,24},{24,0},{1,9},{9,17},{17,25},{25,1},{2,10},{10... | collective-permute-start | bytes 1179656 | tf_op jit(solution)/shard_map/ppermute | solution.py:151
  123.1 12.1 %collective-permute-start.28 = (f32[4,96,256]{2,1,0:T(8,128)S(1)}, f32[4,96,256]{2,1,0:T(8,128)S(1)}, u32[]{:S(2)}, u32[]{:S(2)}) collective-permute-start(f32[4,96,256]{2,1,0:T(8,128)S(1)} %pad_maximum_fusion.3), channel_id=1, source_target_pairs={{0,24},{8,0},{16,8},{24,16},{1,25},{9,1},{17,9},{25,17},{2,26},{10... | collective-permute-start | bytes 1179656 | tf_op jit(solution)/shard_map/ppermute | solution.py:151
  129.2 9.5 %collective-permute-start.22 = (f32[96,256]{1,0:T(8,128)S(1)}, f32[96,256]{1,0:T(8,128)S(1)}, u32[]{:S(2)}, u32[]{:S(2)}) collective-permute-start(f32[96,256]{1,0:T(8,128)S(1)} %get-tuple-element.67), channel_id=1, source_target_pairs={{0,8},{8,16},{16,24},{24,0},{1,9},{9,17},{17,25},{25,1},{2,10},{10... | collective-permute-start | bytes 294920 | tf_op jit(solution)/shard_map/ppermute | solution.py:151
  131.2 8.9 %collective-permute-start.23 = (f32[96,256]{1,0:T(8,128)S(1)}, f32[96,256]{1,0:T(8,128)S(1)}, u32[]{:S(2)}, u32[]{:S(2)}) collective-permute-start(f32[96,256]{1,0:T(8,128)S(1)} %get-tuple-element.66), channel_id=1, source_target_pairs={{0,24},{8,0},{16,8},{24,16},{1,25},{9,1},{17,9},{25,17},{2,26},{10... | collective-permute-start | bytes 294920 | tf_op jit(solution)/shard_map/ppermute | solution.py:151
  133.4 6.8 %collective-permute-start.24 = (f32[96,256]{1,0:T(8,128)S(1)}, f32[96,256]{1,0:T(8,128)S(1)}, u32[]{:S(2)}, u32[]{:S(2)}) collective-permute-start(f32[96,256]{1,0:T(8,128)S(1)} %get-tuple-element.65), channel_id=1, source_target_pairs={{0,16},{8,24},{16,0},{24,8},{1,17},{9,25},{17,1},{25,9},{2,18},{10... | collective-permute-start | bytes 294920 | tf_op jit(solution)/shard_map/ppermute | solution.py:151
  135.3 6.5 %collective-permute-start.29 = (f32[96,256]{1,0:T(8,128)S(1)}, f32[96,256]{1,0:T(8,128)S(1)}, u32[]{:S(2)}, u32[]{:S(2)}) collective-permute-start(f32[96,256]{1,0:T(8,128)S(1)} %get-tuple-element.70), channel_id=1, source_target_pairs={{0,2},{2,4},{4,6},{6,0},{1,3},{3,5},{5,7},{7,1},{8,10},{10,12},{12... | collective-permute-start | bytes 294920 | tf_op jit(solution)/shard_map/ppermute | solution.py:151
  136.4 5.5 %collective-permute-start.30 = (f32[96,256]{1,0:T(8,128)S(1)}, f32[96,256]{1,0:T(8,128)S(1)}, u32[]{:S(2)}, u32[]{:S(2)}) collective-permute-start(f32[96,256]{1,0:T(8,128)S(1)} %get-tuple-element.69), channel_id=1, source_target_pairs={{0,6},{2,0},{4,2},{6,4},{1,7},{3,1},{5,3},{7,5},{8,14},{10,8},{12,... | collective-permute-start | bytes 294920 | tf_op jit(solution)/shard_map/ppermute | solution.py:151
  138.6 6.1 %collective-permute-start.31 = (f32[96,256]{1,0:T(8,128)S(1)}, f32[96,256]{1,0:T(8,128)S(1)}, u32[]{:S(2)}, u32[]{:S(2)}) collective-permute-start(f32[96,256]{1,0:T(8,128)S(1)} %get-tuple-element.68), channel_id=1, source_target_pairs={{0,4},{2,6},{4,0},{6,2},{1,5},{3,7},{5,1},{7,3},{8,12},{10,14},{12... | collective-permute-start | bytes 294920 | tf_op jit(solution)/shard_map/ppermute | solution.py:151

commit v9 on v8

--- a/solution.py
+++ b/solution.py
@@ -151,12 +151,12 @@
     return lax.ppermute(x, axis, [(i, (i + by) % 4) for i in range(4)])
 
 
-def first_phase(both, axis):
-    up = turned(both[2, :2], axis, 1)
-    down = turned(both[2, 2:], axis, -1)
-    ahead = jnp.concatenate([both[1, :2] + up, both[1, 2:]])
-    behind = jnp.concatenate([both[3, :2], both[3, 2:] + down])
-    return both[0] + turned(ahead, axis, 1) + turned(behind, axis, -1)
+def first_phase(far, own, ahead, behind, axis):
+    up = turned(far[0], axis, 1)
+    down = turned(far[1], axis, -1)
+    ahead = jnp.concatenate([ahead[:2] + up, ahead[2:]])
+    behind = jnp.concatenate([behind[:2], behind[2:] + down])
+    return own + turned(ahead, axis, 1) + turned(behind, axis, -1)
 
 
 def second_phase(line, axis):
@@ -169,11 +169,13 @@
 
 def reduced(first, first_got, second, second_got):
     shape = (4, 4, 96, W)
-    second = (second[0] + second_got).reshape(shape)
-    second, first_got = lax.optimization_barrier((second, first_got))
+    kept, got = second[0].reshape(shape), second_got.reshape(shape)
+    far = kept[2, :2] + got[2, :2], kept[2, 2:] + got[2, 2:]
+    rest = [kept[i] + got[i] for i in (0, 1, 3)]
+    *rest, first_got = lax.optimization_barrier((*rest, first_got))
+    second = first_phase(far, *rest, "z")
     first = (first[0] + first_got).reshape(shape)
-    second = first_phase(second, "z")
-    first = first_phase(first, "x")
+    first = first_phase((first[2, :2], first[2, 2:]), first[0], first[1], first[3], "x")
     return jnp.stack([second_phase(first, "z"), second_phase(second, "x")])[None]
 
 
@@ -202,7 +204,8 @@
         if q >= 0:
             held = apply_step(
                 q, ints, floats, [environs[q + LAG * k] for k in range(SITES)], psi[0], right_env[0, 0], held)
-    return reduced(held[0], swapped(held[0]), second, second_got)
+    first_got = swapped(held[0])
+    return reduced(held[0], first_got, second, second_got)
 
 
 def solution(mesh):

time: 147 us -> 149 us (1.014)
  waiting for transfers between devices: 44.2 us -> 45.7 us
  transfers between devices with their start and end apart: 32 -> 32, of which waited for: 21 -> 22; matrix products, arithmetic and copies ran while one was open for 1% -> 1% of each run, Pallas kernels for 34% -> 31%
where the time goes in v9:
time: 149 us; the launch traced here: 148 us
  Pallas kernels  49.6 us (33%)
  starting transfers between devices  47.6 us (32%)
  waiting for transfers between devices  45.7 us (31%)
  local copies, waits for them, and re-layouts  2.4 us (2%)
  other arithmetic  1.61 us (1%)
    ppermute x16, waiting for transfers between devices, shards(): lax.ppermute(environ, 'site', [(0, 1), (1, 2), (2, 3)])  31.6 us
    pallas_call x12, Pallas kernels, apply_step(): pl.pallas_call(kernel, in_specs=[SCALAR] * 2 + [LOCAL] * len(operands) +...  28.9 us
    ppermute x14, starting transfers between devices, turned(): return lax.ppermute(x, axis, [(i, (i + by) % 4) for i in range(4)])  25.3 us
    ppermute x16, starting transfers between devices, shards(): lax.ppermute(environ, 'site', [(0, 1), (1, 2), (2, 3)])  21.4 us
    pallas_call x16, Pallas kernels, update_step(): pl.pallas_call(kernel, in_specs=[SCALAR] * 2 + [LOCAL] * 4 + [FAR] * len(...  19.6 us
    ppermute x14, waiting for transfers between devices, turned(): return lax.ppermute(x, axis, [(i, (i + by) % 4) for i in range(4)])  9.62 us
    ppermute x2, waiting for transfers between devices, swapped(): return lax.ppermute(pieces[1], 'core', [(0, 1), (1, 0)])  4.51 us
  transfers between devices with their start and end apart: 32, of which 22 were waited for; matrix products, arithmetic and copies ran while one was open for 1% of the time, Pallas kernels for 31%

profile of v9, /device:TPU:24, one launch (start us, length us, event | category | flops | bytes accessed | tf_op | source)
XLA Modules:
  0.0 147.6 jit_solution(1877209076772831792)
XLA Ops:
  2.0 1.6 %collective-permute-start.1 = (f32[256,256]{1,0:T(8,128)S(1)}, f32[256,256]{1,0:T(8,128)S(1)}, u32[]{:S(2)}, u32[]{:S(2)}) collective-permute-start(f32[256,256]{1,0:T(8,128)S(1)} %shard_map.74.refs_0_), channel_id=1, source_target_pairs={{0,32},{32,64},{64,96},{1,33},{33,65},{65,97},{2,34},{34,66},{66,9... | collective-permute-start | bytes 786440 | tf_op jit(solution)/shard_map/ppermute | solution.py:199
  5.5 7.9 %collective-permute-done.1.previous.arrived = f32[256,256]{1,0:T(8,128)S(1)} collective-permute-done((f32[256,256]{1,0:T(8,128)S(1)}, f32[256,256]{1,0:T(8,128)S(1)}, u32[]{:S(2)}, u32[]{:S(2)}) %collective-permute-start.1) | collective-permute-done | bytes 262176 | tf_op jit(solution)/shard_map/ppermute | solution.py:199
  15.3 3.7 %collective-permute-done.arrived.previous = f32[256,256]{1,0:T(8,128)S(1)} collective-permute-done((f32[256,256]{1,0:T(8,128)S(1)}, f32[256,256]{1,0:T(8,128)S(1)}, u32[]{:S(2)}, u32[]{:S(2)}) %collective-permute-start) | collective-permute-done | bytes 262176 | tf_op jit(solution)/shard_map/ppermute | solution.py:199
  20.8 4.2 %collective-permute-done.3.previous.arrived = f32[256,256]{1,0:T(8,128)S(1)} collective-permute-done((f32[256,256]{1,0:T(8,128)S(1)}, f32[256,256]{1,0:T(8,128)S(1)}, u32[]{:S(2)}, u32[]{:S(2)}) %collective-permute-start.3) | collective-permute-done | bytes 262176 | tf_op jit(solution)/shard_map/ppermute | solution.py:199
  26.9 3.8 %collective-permute-done.2.arrived.previous = f32[256,256]{1,0:T(8,128)S(1)} collective-permute-done((f32[256,256]{1,0:T(8,128)S(1)}, f32[256,256]{1,0:T(8,128)S(1)}, u32[]{:S(2)}, u32[]{:S(2)}) %collective-permute-start.2) | collective-permute-done | bytes 262176 | tf_op jit(solution)/shard_map/ppermute | solution.py:199
  31.3 1.6 %collective-permute-start.4 = (f32[256,256]{1,0:T(8,128)S(1)}, f32[256,256]{1,0:T(8,128)S(1)}, u32[]{:S(2)}, u32[]{:S(2)}) collective-permute-start(f32[256,256]{1,0:T(8,128)S(1)} %shard_map.77.refs_2_.refs_1_.refs_0_), channel_id=1, source_target_pairs={{0,32},{32,64},{64,96},{1,33},{33,65},{65,97},{2,34},{34,66},{66,9... | collective-permute-start | bytes 786440 | tf_op jit(solution)/shard_map/ppermute | solution.py:199
  32.8 3.6 %collective-permute-done.5.arrived.previous = f32[256,256]{1,0:T(8,128)S(1)} collective-permute-done((f32[256,256]{1,0:T(8,128)S(1)}, f32[256,256]{1,0:T(8,128)S(1)}, u32[]{:S(2)}, u32[]{:S(2)}) %collective-permute-start.5) | collective-permute-done | bytes 262176 | tf_op jit(solution)/shard_map/ppermute | solution.py:199
  36.5 1.4 shard_map.79.refs_3_.refs_2_.refs_1_.refs_0_
  39.2 2.5 %shard_map.80 = (f32[2,4,4,3,32,256]{5,4,3,2,1,0:T(8,128)S(1)}, f32[2,4,4,3,32,256]{5,4,3,2,1,0:T(8,128)S(1)}) custom-call(s32[28]{0:T(128)S(1)} %concatenate.15.ints, f32[4]{0:T(128)S(1)} %bitcast.145, f32[256,256]{1,0:T(8,128)S(1)} %shard_map.74.refs_0_, f32[256,256]{1,0:T(8,128)S(1)} %shard_map.76.refs_1_.refs_0_, ...), custom_call_target="tpu_custom_call" | custom-call | tf_op jit(solution)/shard_map/pallas_call | solution.py:139
  41.9 1.4 shard_map.81.refs_3_.refs_2_.refs_1_.refs_0_
  44.6 2.5 %shard_map.82 = (f32[2,4,4,3,32,256]{5,4,3,2,1,0:T(8,128)S(1)}, f32[2,4,4,3,32,256]{5,4,3,2,1,0:T(8,128)S(1)}) custom-call(s32[28]{0:T(128)S(1)} %concatenate.15.ints, f32[4]{0:T(128)S(1)} %bitcast.147, f32[256,256]{1,0:T(8,128)S(1)} %shard_map.73.refs_0_, f32[256,256]{1,0:T(8,128)S(1)} %shard_map.75.refs_1_.refs_0_, ...), custom_call_target="tpu_custom_call", output_to_operand_aliasing={{0}: (8, {}), {1}: (9, {})} | custom-call | tf_op jit(solution)/shard_map/pallas_call | solution.py:139
  47.7 1.4 shard_map.83.refs_3_.refs_2_.refs_1_.refs_0_
  50.4 2.5 %shard_map.84 = (f32[2,4,4,3,32,256]{5,4,3,2,1,0:T(8,128)S(1)}, f32[2,4,4,3,32,256]{5,4,3,2,1,0:T(8,128)S(1)}) custom-call(s32[28]{0:T(128)S(1)} %concatenate.15.ints, f32[4]{0:T(128)S(1)} %bitcast.149, f32[256,256]{1,0:T(8,128)S(1)} %shard_map.76.refs_1_.refs_0_, ...), custom_call_target="tpu_custom_call", output_to_operand_aliasing={{0}: (8, {}), {1}: (9, {})} | custom-call | tf_op jit(solution)/shard_map/pallas_call | solution.py:139
  56.4 2.5 %shard_map.86 = (f32[2,4,4,3,32,256]{5,4,3,2,1,0:T(8,128)S(1)}, f32[2,4,4,3,32,256]{5,4,3,2,1,0:T(8,128)S(1)}) custom-call(s32[28]{0:T(128)S(1)} %concatenate.15.ints, f32[4]{0:T(128)S(1)} %bitcast.151, f32[256,256]{1,0:T(8,128)S(1)} %shard_map.75.refs_1_.refs_0_, ...), custom_call_target="tpu_custom_call", output_to_operand_aliasing={{0}: (8, {}), {1}: (9, {})} | custom-call | tf_op jit(solution)/shard_map/pallas_call | solution.py:139
  59.5 1.4 shard_map.87.refs_3_.refs_2_.refs_1_.refs_0_
  60.9 1.5 collective-permute-start.11
  62.4 2.5 %shard_map.88 = (f32[2,4,4,3,32,256]{5,4,3,2,1,0:T(8,128)S(1)}, f32[2,4,4,3,32,256]{5,4,3,2,1,0:T(8,128)S(1)}) custom-call(s32[28]{0:T(128)S(1)} %concatenate.15.ints, f32[4]{0:T(128)S(1)} %bitcast.153, f32[256,256]{1,0:T(8,128)S(1)} %shard_map.78.refs_2_.refs_1_.refs_0_, ...), custom_call_target="tpu_custom_call", output_to_operand_aliasing={{0}: (8, {}), {1}: (9, {})} | custom-call | tf_op jit(solution)/shard_map/pallas_call | solution.py:139
  65.3 1.4 shard_map.89.refs_3_.refs_2_.refs_1_.refs_0_
  68.1 2.5 %shard_map.90 = (f32[2,4,4,3,32,256]{5,4,3,2,1,0:T(8,128)S(1)}, f32[2,4,4,3,32,256]{5,4,3,2,1,0:T(8,128)S(1)}) custom-call(s32[28]{0:T(128)S(1)} %concatenate.15.ints, f32[4]{0:T(128)S(1)} %bitcast.155, f32[256,256]{1,0:T(8,128)S(1)} %shard_map.77.refs_2_.refs_1_.refs_0_, ...), custom_call_target="tpu_custom_call", output_to_operand_aliasing={{0}: (8, {}), {1}: (9, {})} | custom-call | tf_op jit(solution)/shard_map/pallas_call | solution.py:139
  71.0 1.5 shard_map.91.refs_3_.refs_2_.refs_1_
  73.8 2.5 %shard_map.92 = (f32[2,4,4,3,32,256]{5,4,3,2,1,0:T(8,128)S(1)}, f32[2,4,4,3,32,256]{5,4,3,2,1,0:T(8,128)S(1)}) custom-call(s32[28]{0:T(128)S(1)} %concatenate.15.ints, f32[4]{0:T(128)S(1)} %bitcast.157, f32[256,256]{1,0:T(8,128)S(1)} %shard_map.79.refs_3_.refs_2_.refs_1_.refs_0_, ...), custom_call_target="tpu_custom_call", output_to_operand_aliasing={{0}: (8, {}), {1}: (9, {})} | custom-call | tf_op jit(solution)/shard_map/pallas_call | solution.py:139
  77.2 1.4 shard_map.93.refs_3_.refs_2_.refs_1_
  80.0 2.5 %shard_map.94 = (f32[2,4,4,3,32,256]{5,4,3,2,1,0:T(8,128)S(1)}, f32[2,4,4,3,32,256]{5,4,3,2,1,0:T(8,128)S(1)}) custom-call(s32[28]{0:T(128)S(1)} %concatenate.15.ints, f32[4]{0:T(128)S(1)} %bitcast.159, f32[256,256]{1,0:T(8,128)S(1)} %shard_map.81.refs_3_.refs_2_.refs_1_.refs_0_, ...), custom_call_target="tpu_custom_call", output_to_operand_aliasing={{0}: (8, {}), {1}: (9, {})} | custom-call | tf_op jit(solution)/shard_map/pallas_call | solution.py:139
  83.1 1.4 shard_map.95.refs_3_.refs_2_
  85.8 2.5 %shard_map.96 = (f32[2,4,4,3,32,256]{5,4,3,2,1,0:T(8,128)S(1)}, f32[2,4,4,3,32,256]{5,4,3,2,1,0:T(8,128)S(1)}) custom-call(s32[28]{0:T(128)S(1)} %concatenate.15.ints, f32[4]{0:T(128)S(1)} %bitcast.161, f32[256,256]{1,0:T(8,128)S(1)} %shard_map.83.refs_3_.refs_2_.refs_1_.refs_0_, ...), custom_call_target="tpu_custom_call", output_to_operand_aliasing={{0}: (8, {}), {1}: (9, {})} | custom-call | tf_op jit(solution)/shard_map/pallas_call | solution.py:139
  88.9 1.4 shard_map.97.refs_3_.refs_2_
  90.4 2.5 %shard_map.98 = (f32[2,4,4,3,32,256]{5,4,3,2,1,0:T(8,128)S(1)}, f32[2,4,4,3,32,256]{5,4,3,2,1,0:T(8,128)S(1)}) custom-call(s32[28]{0:T(128)S(1)} %concatenate.15.ints, f32[4]{0:T(128)S(1)} %bitcast.163, f32[256,256]{1,0:T(8,128)S(1)} %shard_map.85.refs_3_.refs_2_.refs_1_.refs_0_, ...), custom_call_target="tpu_custom_call", output_to_operand_aliasing={{0}: (8, {}), {1}: (9, {})} | custom-call | tf_op jit(solution)/shard_map/pallas_call | solution.py:139
  94.2 1.4 shard_map.99.refs_3_
  95.6 2.8 %shard_map.100 = (f32[2,4,4,3,32,256]{5,4,3,2,1,0:T(8,128)S(1)}, f32[2,4,4,3,32,256]{5,4,3,2,1,0:T(8,128)S(1)}) custom-call(s32[28]{0:T(128)S(1)} %concatenate.15.ints, f32[4]{0:T(128)S(1)} %bitcast.165, f32[256,256]{1,0:T(8,128)S(1)} %shard_map.87.refs_3_.refs_2_.refs_1_.refs_0_, ...), custom_call_target="tpu_custom_call", output_to_operand_aliasing={{0}: (8, {}), {1}: (9, {})} | custom-call | tf_op jit(solution)/shard_map/pallas_call | solution.py:139
  98.9 3.1 %collective-permute-done.14.arrived = f32[256,256]{1,0:T(8,128)S(1)} collective-permute-done((f32[256,256]{1,0:T(8,128)S(1)}, f32[256,256]{1,0:T(8,128)S(1)}, u32[]{:S(2)}, u32[]{:S(2)}) %collective-permute-start.14) | collective-permute-done | bytes 262176 | tf_op jit(solution)/shard_map/ppermute | solution.py:199
  102.0 1.5 shard_map.101.refs_3_
  103.4 1.5 %shard_map.102 = f32[2,4,4,3,32,256]{5,4,3,2,1,0:T(8,128)S(1)} custom-call(s32[28]{0:T(128)S(1)} %concatenate.15.ints, f32[4]{0:T(128)S(1)} %bitcast.167, f32[256,256]{1,0:T(8,128)S(1)} %shard_map.89.refs_3_.refs_2_.refs_1_.refs_0_, f32[256,256]{1,0:T(8,128)S(1)} %shard_map.93.refs_3_.refs_2_.refs_1_, ...), custom_call_target="tpu_custom_call", output_to_operand_aliasing={{}: (8, {})} | custom-call | tf_op jit(solution)/shard_map/pallas_call | solution.py:139
  106.1 2.5 %collective-permute-done.16 = f32[4,4,3,32,256]{4,3,2,1,0:T(8,128)S(1)} collective-permute-done((f32[4,4,3,32,256]{4,3,2,1,0:T(8,128)S(1)}, f32[4,4,3,32,256]{4,3,2,1,0:T(8,128)S(1)}, u32[]{:S(2)}, u32[]{:S(2)}) %collective-permute-start.16) | collective-permute-done | bytes 1572896 | tf_op jit(solution)/shard_map/ppermute | solution.py:167
  108.9 2.0 %collective-permute-done.17 = f32[4,4,3,32,256]{4,3,2,1,0:T(8,128)S(1)} collective-permute-done((f32[4,4,3,32,256]{4,3,2,1,0:T(8,128)S(1)}, f32[4,4,3,32,256]{4,3,2,1,0:T(8,128)S(1)}, u32[]{:S(2)}, u32[]{:S(2)}) %collective-permute-start.17) | collective-permute-done | bytes 1572896 | tf_op jit(solution)/shard_map/ppermute | solution.py:167
  111.3 1.6 %collective-permute-start.18 = (f32[2,96,256]{2,1,0:T(8,128)S(1)}, f32[2,96,256]{2,1,0:T(8,128)S(1)}, u32[]{:S(2)}, u32[]{:S(2)}) collective-permute-start(f32[2,96,256]{2,1,0:T(8,128)S(1)} %get-tuple-element.64), channel_id=1, source_target_pairs={{0,2},{2,4},{4,6},{6,0},{1,3},{3,5},{5,7},{7,1},{8,10},{10,12},{12... | collective-permute-start | bytes 589832 | tf_op jit(solution)/shard_map/ppermute | solution.py:151
  112.8 1.7 %collective-permute-start.20 = (f32[2,96,256]{2,1,0:T(8,128)S(1)}, f32[2,96,256]{2,1,0:T(8,128)S(1)}, u32[]{:S(2)}, u32[]{:S(2)}) collective-permute-start(f32[2,96,256]{2,1,0:T(8,128)S(1)} %get-tuple-element.65), channel_id=1, source_target_pairs={{0,6},{2,0},{4,2},{6,4},{1,7},{3,1},{5,3},{7,5},{8,14},{10,8},{12,... | collective-permute-start | bytes 589832 | tf_op jit(solution)/shard_map/ppermute | solution.py:151
  114.7 2.0 %collective-permute-start.25 = (f32[2,96,256]{2,1,0:T(8,128)S(1)}, f32[2,96,256]{2,1,0:T(8,128)S(1)}, u32[]{:S(2)}, u32[]{:S(2)}) collective-permute-start(f32[2,96,256]{2,1,0:T(8,128)S(1)} %get-tuple-element.57), channel_id=1, source_target_pairs={{0,8},{8,16},{16,24},{24,0},{1,9},{9,17},{17,25},{25,1},{2,10},{10... | collective-permute-start | bytes 589832 | tf_op jit(solution)/shard_map/ppermute | solution.py:151
  116.7 2.1 %collective-permute-start.27 = (f32[2,96,256]{2,1,0:T(8,128)S(1)}, f32[2,96,256]{2,1,0:T(8,128)S(1)}, u32[]{:S(2)}, u32[]{:S(2)}) collective-permute-start(f32[2,96,256]{2,1,0:T(8,128)S(1)} %get-tuple-element.58), channel_id=1, source_target_pairs={{0,24},{8,0},{16,8},{24,16},{1,25},{9,1},{17,9},{25,17},{2,26},{10... | collective-permute-start | bytes 589832 | tf_op jit(solution)/shard_map/ppermute | solution.py:151
  120.0 3.0 %collective-permute-start.21 = (f32[4,96,256]{2,1,0:T(8,128)S(1)}, f32[4,96,256]{2,1,0:T(8,128)S(1)}, u32[]{:S(2)}, u32[]{:S(2)}) collective-permute-start(f32[4,96,256]{2,1,0:T(8,128)S(1)} %pad_maximum_fusion.1), channel_id=1, source_target_pairs={{0,6},{2,0},{4,2},{6,4},{1,7},{3,1},{5,3},{7,5},{8,14},{10,8},{12,... | collective-permute-start | bytes 1179656 | tf_op jit(solution)/shard_map/ppermute | solution.py:151
  123.5 1.6 %collective-permute-start.26 = (f32[4,96,256]{2,1,0:T(8,128)S(1)}, f32[4,96,256]{2,1,0:T(8,128)S(1)}, u32[]{:S(2)}, u32[]{:S(2)}) collective-permute-start(f32[4,96,256]{2,1,0:T(8,128)S(1)} %pad_maximum_fusion.2), channel_id=1, source_target_pairs={{0,8},{8,16},{16,24},{24,0},{1,9},{9,17},{17,25},{25,1},{2,10},{10... | collective-permute-start | bytes 1179656 | tf_op jit(solution)/shard_map/ppermute | solution.py:151
  125.2 2.1 %collective-permute-start.28 = (f32[4,96,256]{2,1,0:T(8,128)S(1)}, f32[4,96,256]{2,1,0:T(8,128)S(1)}, u32[]{:S(2)}, u32[]{:S(2)}) collective-permute-start(f32[4,96,256]{2,1,0:T(8,128)S(1)} %pad_maximum_fusion.3), channel_id=1, source_target_pairs={{0,24},{8,0},{16,8},{24,16},{1,25},{9,1},{17,9},{25,17},{2,26},{10... | collective-permute-start | bytes 1179656 | tf_op jit(solution)/shard_map/ppermute | solution.py:151
  127.4 3.8 %collective-permute-done.19 = f32[4,96,256]{2,1,0:T(8,128)S(1)} collective-permute-done((f32[4,96,256]{2,1,0:T(8,128)S(1)}, f32[4,96,256]{2,1,0:T(8,128)S(1)}, u32[]{:S(2)}, u32[]{:S(2)}) %collective-permute-start.19) | collective-permute-done | bytes 393248 | tf_op jit(solution)/shard_map/ppermute | solution.py:151
  131.3 2.0 %collective-permute-start.22 = (f32[96,256]{1,0:T(8,128)S(1)}, f32[96,256]{1,0:T(8,128)S(1)}, u32[]{:S(2)}, u32[]{:S(2)}) collective-permute-start(f32[96,256]{1,0:T(8,128)S(1)} %get-tuple-element.75), channel_id=1, source_target_pairs={{0,8},{8,16},{16,24},{24,0},{1,9},{9,17},{17,25},{25,1},{2,10},{10... | collective-permute-start | bytes 294920 | tf_op jit(solution)/shard_map/ppermute | solution.py:151
  133.3 2.1 %collective-permute-start.23 = (f32[96,256]{1,0:T(8,128)S(1)}, f32[96,256]{1,0:T(8,128)S(1)}, u32[]{:S(2)}, u32[]{:S(2)}) collective-permute-start(f32[96,256]{1,0:T(8,128)S(1)} %get-tuple-element.74), channel_id=1, source_target_pairs={{0,24},{8,0},{16,8},{24,16},{1,25},{9,1},{17,9},{25,17},{2,26},{10... | collective-permute-start | bytes 294920 | tf_op jit(solution)/shard_map/ppermute | solution.py:151
  135.4 1.9 %collective-permute-start.24 = (f32[96,256]{1,0:T(8,128)S(1)}, f32[96,256]{1,0:T(8,128)S(1)}, u32[]{:S(2)}, u32[]{:S(2)}) collective-permute-start(f32[96,256]{1,0:T(8,128)S(1)} %get-tuple-element.73), channel_id=1, source_target_pairs={{0,16},{8,24},{16,0},{24,8},{1,17},{9,25},{17,1},{25,9},{2,18},{10... | collective-permute-start | bytes 294920 | tf_op jit(solution)/shard_map/ppermute | solution.py:151
  137.8 2.9 %collective-permute-start.30 = (f32[96,256]{1,0:T(8,128)S(1)}, f32[96,256]{1,0:T(8,128)S(1)}, u32[]{:S(2)}, u32[]{:S(2)}) collective-permute-start(f32[96,256]{1,0:T(8,128)S(1)} %get-tuple-element.77), channel_id=1, source_target_pairs={{0,6},{2,0},{4,2},{6,4},{1,7},{3,1},{5,3},{7,5},{8,14},{10,8},{12,... | collective-permute-start | bytes 294920 | tf_op jit(solution)/shard_map/ppermute | solution.py:151
  142.1 1.9 %collective-permute-done.29 = f32[96,256]{1,0:T(8,128)S(1)} collective-permute-done((f32[96,256]{1,0:T(8,128)S(1)}, f32[96,256]{1,0:T(8,128)S(1)}, u32[]{:S(2)}, u32[]{:S(2)}) %collective-permute-start.29) | collective-permute-done | bytes 98336 | tf_op jit(solution)/shard_map/ppermute | solution.py:151
  144.0 2.9 %collective-permute-done.31 = f32[96,256]{1,0:T(8,128)S(1)} collective-permute-done((f32[96,256]{1,0:T(8,128)S(1)}, f32[96,256]{1,0:T(8,128)S(1)}, u32[]{:S(2)}, u32[]{:S(2)}) %collective-permute-start.31) | collective-permute-done | bytes 98336 | tf_op jit(solution)/shard_map/ppermute | solution.py:151
  (92 shorter events, 35.0 us)
Async XLA Ops:
  0.7 0.7 copy-start.2
  1.4 2.2 %copy-start.3 = (f32[1,1,4]{2,1,0:T(1,128)S(1)}, f32[1,1,4]{2,1,0:T(1,128)}, u32[]{:S(2)}) copy-start(f32[1,1,4]{2,1,0:T(1,128)} %param.11) | copy-start | bytes 52
  1.4 12.0 %slice-start = ((s8[6291456]{0:T(1024)(128)(4,1)}), s8[4194304]{0:T(1024)(128)(4,1)S(1)}, s32[]{:S(2)}) async-start(s8[6291456]{0:T(1024)(128)(4,1)} %bitcast.76), calls=%async_computation | async-start | bytes 8388608
  2.0 11.4 %slice-start.1 = ((s8[6291456]{0:T(1024)(128)(4,1)}), s8[2097152]{0:T(1024)(128)(4,1)S(1)}, s32[]{:S(2)}) async-start(s8[6291456]{0:T(1024)(128)(4,1)} %bitcast.76), calls=%async_computation.1 | async-start | bytes 4194304
  2.0 11.4 %copy-start = (f32[1,12,256,256]{3,2,1,0:T(8,128)S(1)}, f32[1,12,256,256]{3,2,1,0:T(8,128)}, u32[]{:S(2)}) copy-start(f32[1,12,256,256]{3,2,1,0:T(8,128)} %param.7) | copy-start | bytes 9437188
  2.0 11.3 %collective-permute-start.1 = (f32[256,256]{1,0:T(8,128)S(1)}, f32[256,256]{1,0:T(8,128)S(1)}, u32[]{:S(2)}, u32[]{:S(2)}) collective-permute-start(f32[256,256]{1,0:T(8,128)S(1)} %shard_map.74.refs_0_), channel_id=1, source_target_pairs={{0,32},{32,64},{64,96},{1,33},{33,65},{65,97},{2,34},{34,66},{66,9... | collective-permute-start | bytes 786440 | tf_op jit(solution)/shard_map/ppermute | solution.py:199
  4.2 14.8 %collective-permute-start = (f32[256,256]{1,0:T(8,128)S(1)}, f32[256,256]{1,0:T(8,128)S(1)}, u32[]{:S(2)}, u32[]{:S(2)}) collective-permute-start(f32[256,256]{1,0:T(8,128)S(1)} %shard_map.73.refs_0_), channel_id=1, source_target_pairs={{0,32},{32,64},{64,96},{1,33},{33,65},{65,97},{2,34},{34,66},{66,9... | collective-permute-start | bytes 786440 | tf_op jit(solution)/shard_map/ppermute | solution.py:199
  14.0 11.1 %collective-permute-start.3 = (f32[256,256]{1,0:T(8,128)S(1)}, f32[256,256]{1,0:T(8,128)S(1)}, u32[]{:S(2)}, u32[]{:S(2)}) collective-permute-start(f32[256,256]{1,0:T(8,128)S(1)} %shard_map.76.refs_1_.refs_0_), channel_id=1, source_target_pairs={{0,32},{32,64},{64,96},{1,33},{33,65},{65,97},{2,34},{34,66},{66,9... | collective-permute-start | bytes 786440 | tf_op jit(solution)/shard_map/ppermute | solution.py:199
  19.5 11.1 %collective-permute-start.2 = (f32[256,256]{1,0:T(8,128)S(1)}, f32[256,256]{1,0:T(8,128)S(1)}, u32[]{:S(2)}, u32[]{:S(2)}) collective-permute-start(f32[256,256]{1,0:T(8,128)S(1)} %shard_map.75.refs_1_.refs_0_), channel_id=1, source_target_pairs={{0,32},{32,64},{64,96},{1,33},{33,65},{65,97},{2,34},{34,66},{66,9... | collective-permute-start | bytes 786440 | tf_op jit(solution)/shard_map/ppermute | solution.py:199
  25.6 10.8 %collective-permute-start.5 = (f32[256,256]{1,0:T(8,128)S(1)}, f32[256,256]{1,0:T(8,128)S(1)}, u32[]{:S(2)}, u32[]{:S(2)}) collective-permute-start(f32[256,256]{1,0:T(8,128)S(1)} %shard_map.78.refs_2_.refs_1_.refs_0_), channel_id=1, source_target_pairs={{0,32},{32,64},{64,96},{1,33},{33,65},{65,97},{2,34},{34,66},{66,9... | collective-permute-start | bytes 786440 | tf_op jit(solution)/shard_map/ppermute | solution.py:199
  30.7 8.5 %slice-start.2 = ((s8[6291456]{0:T(1024)(128)(4,1)}), s8[4194304]{0:T(1024)(128)(4,1)S(1)}, s32[]{:S(2)}) async-start(s8[6291456]{0:T(1024)(128)(4,1)} %bitcast.112), calls=%async_computation.2 | async-start | bytes 8388608
  31.2 8.0 %slice-start.3 = ((s8[6291456]{0:T(1024)(128)(4,1)}), s8[2097152]{0:T(1024)(128)(4,1)S(1)}, s32[]{:S(2)}) async-start(s8[6291456]{0:T(1024)(128)(4,1)} %bitcast.112), calls=%async_computation.3 | async-start | bytes 4194304
  31.2 8.0 %copy-start.1 = (f32[1,1,12,256,256]{4,3,2,1,0:T(8,128)S(1)}, f32[1,1,12,256,256]{4,3,2,1,0:T(8,128)}, u32[]{:S(2)}) copy-start(f32[1,1,12,256,256]{4,3,2,1,0:T(8,128)} %param.8) | copy-start | bytes 9437188
  31.3 10.6 %collective-permute-start.4 = (f32[256,256]{1,0:T(8,128)S(1)}, f32[256,256]{1,0:T(8,128)S(1)}, u32[]{:S(2)}, u32[]{:S(2)}) collective-permute-start(f32[256,256]{1,0:T(8,128)S(1)} %shard_map.77.refs_2_.refs_1_.refs_0_), channel_id=1, source_target_pairs={{0,32},{32,64},{64,96},{1,33},{33,65},{65,97},{2,34},{34,66},{66,9... | collective-permute-start | bytes 786440 | tf_op jit(solution)/shard_map/ppermute | solution.py:199
  37.9 9.8 %collective-permute-start.7 = (f32[256,256]{1,0:T(8,128)S(1)}, f32[256,256]{1,0:T(8,128)S(1)}, u32[]{:S(2)}, u32[]{:S(2)}) collective-permute-start(f32[256,256]{1,0:T(8,128)S(1)} %shard_map.79.refs_3_.refs_2_.refs_1_.refs_0_), channel_id=1, source_target_pairs={{0,32},{32,64},{64,96},{1,33},{33,65},{65,97},{2,34},{34,66},{66,9... | collective-permute-start | bytes 786440 | tf_op jit(solution)/shard_map/ppermute | solution.py:199
  43.3 10.3 %collective-permute-start.6 = (f32[256,256]{1,0:T(8,128)S(1)}, f32[256,256]{1,0:T(8,128)S(1)}, u32[]{:S(2)}, u32[]{:S(2)}) collective-permute-start(f32[256,256]{1,0:T(8,128)S(1)} %shard_map.81.refs_3_.refs_2_.refs_1_.refs_0_), channel_id=1, source_target_pairs={{0,32},{32,64},{64,96},{1,33},{33,65},{65,97},{2,34},{34,66},{66,9... | collective-permute-start | bytes 786440 | tf_op jit(solution)/shard_map/ppermute | solution.py:199
  49.1 10.3 %collective-permute-start.9 = (f32[256,256]{1,0:T(8,128)S(1)}, f32[256,256]{1,0:T(8,128)S(1)}, u32[]{:S(2)}, u32[]{:S(2)}) collective-permute-start(f32[256,256]{1,0:T(8,128)S(1)} %shard_map.83.refs_3_.refs_2_.refs_1_.refs_0_), channel_id=1, source_target_pairs={{0,32},{32,64},{64,96},{1,33},{33,65},{65,97},{2,34},{34,66},{66,9... | collective-permute-start | bytes 786440 | tf_op jit(solution)/shard_map/ppermute | solution.py:199
  55.1 10.3 %collective-permute-start.8 = (f32[256,256]{1,0:T(8,128)S(1)}, f32[256,256]{1,0:T(8,128)S(1)}, u32[]{:S(2)}, u32[]{:S(2)}) collective-permute-start(f32[256,256]{1,0:T(8,128)S(1)} %shard_map.85.refs_3_.refs_2_.refs_1_.refs_0_), channel_id=1, source_target_pairs={{0,32},{32,64},{64,96},{1,33},{33,65},{65,97},{2,34},{34,66},{66,9... | collective-permute-start | bytes 786440 | tf_op jit(solution)/shard_map/ppermute | solution.py:199
  60.9 10.1 %collective-permute-start.11 = (f32[256,256]{1,0:T(8,128)S(1)}, f32[256,256]{1,0:T(8,128)S(1)}, u32[]{:S(2)}, u32[]{:S(2)}) collective-permute-start(f32[256,256]{1,0:T(8,128)S(1)} %shard_map.87.refs_3_.refs_2_.refs_1_.refs_0_), channel_id=1, source_target_pairs={{0,32},{32,64},{64,96},{1,33},{33,65},{65,97},{2,34},{34,66},{66,9... | collective-permute-start | bytes 786440 | tf_op jit(solution)/shard_map/ppermute | solution.py:199
  66.8 10.4 %collective-permute-start.10 = (f32[256,256]{1,0:T(8,128)S(1)}, f32[256,256]{1,0:T(8,128)S(1)}, u32[]{:S(2)}, u32[]{:S(2)}) collective-permute-start(f32[256,256]{1,0:T(8,128)S(1)} %shard_map.89.refs_3_.refs_2_.refs_1_.refs_0_), channel_id=1, source_target_pairs={{0,32},{32,64},{64,96},{1,33},{33,65},{65,97},{2,34},{34,66},{66,9... | collective-permute-start | bytes 786440 | tf_op jit(solution)/shard_map/ppermute | solution.py:199
  72.5 10.6 %collective-permute-start.13 = (f32[256,256]{1,0:T(8,128)S(1)}, f32[256,256]{1,0:T(8,128)S(1)}, u32[]{:S(2)}, u32[]{:S(2)}) collective-permute-start(f32[256,256]{1,0:T(8,128)S(1)} %shard_map.91.refs_3_.refs_2_.refs_1_), channel_id=1, source_target_pairs={{0,32},{32,64},{64,96},{1,33},{33,65},{65,97},{2,34},{34,66},{66,9... | collective-permute-start | bytes 786440 | tf_op jit(solution)/shard_map/ppermute | solution.py:199
  78.7 10.3 %collective-permute-start.12 = (f32[256,256]{1,0:T(8,128)S(1)}, f32[256,256]{1,0:T(8,128)S(1)}, u32[]{:S(2)}, u32[]{:S(2)}) collective-permute-start(f32[256,256]{1,0:T(8,128)S(1)} %shard_map.93.refs_3_.refs_2_.refs_1_), channel_id=1, source_target_pairs={{0,32},{32,64},{64,96},{1,33},{33,65},{65,97},{2,34},{34,66},{66,9... | collective-permute-start | bytes 786440 | tf_op jit(solution)/shard_map/ppermute | solution.py:199
  84.5 9.6 %collective-permute-start.15 = (f32[256,256]{1,0:T(8,128)S(1)}, f32[256,256]{1,0:T(8,128)S(1)}, u32[]{:S(2)}, u32[]{:S(2)}) collective-permute-start(f32[256,256]{1,0:T(8,128)S(1)} %shard_map.95.refs_3_.refs_2_), channel_id=1, source_target_pairs={{0,32},{32,64},{64,96},{1,33},{33,65},{65,97},{2,34},{34,66},{66,9... | collective-permute-start | bytes 786440 | tf_op jit(solution)/shard_map/ppermute | solution.py:199
  92.9 9.1 %collective-permute-start.14 = (f32[256,256]{1,0:T(8,128)S(1)}, f32[256,256]{1,0:T(8,128)S(1)}, u32[]{:S(2)}, u32[]{:S(2)}) collective-permute-start(f32[256,256]{1,0:T(8,128)S(1)} %shard_map.97.refs_3_.refs_2_), channel_id=1, source_target_pairs={{0,32},{32,64},{64,96},{1,33},{33,65},{65,97},{2,34},{34,66},{66,9... | collective-permute-start | bytes 786440 | tf_op jit(solution)/shard_map/ppermute | solution.py:199
  104.9 3.7 %collective-permute-start.16 = (f32[4,4,3,32,256]{4,3,2,1,0:T(8,128)S(1)}, f32[4,4,3,32,256]{4,3,2,1,0:T(8,128)S(1)}, u32[]{:S(2)}, u32[]{:S(2)}) collective-permute-start(f32[4,4,3,32,256]{4,3,2,1,0:T(8,128)S(1)} %get-tuple-element.63), channel_id=1, source_target_pairs={{0,1},{1,0},{2,3},{3,2},{4,5},{5,4},{6,7},{7,6},{8,9},{9,8},{10,11... | collective-permute-start | bytes 4718600 | tf_op jit(solution)/shard_map/ppermute | solution.py:167
  105.4 5.5 %collective-permute-start.17 = (f32[4,4,3,32,256]{4,3,2,1,0:T(8,128)S(1)}, f32[4,4,3,32,256]{4,3,2,1,0:T(8,128)S(1)}, u32[]{:S(2)}, u32[]{:S(2)}) collective-permute-start(f32[4,4,3,32,256]{4,3,2,1,0:T(8,128)S(1)} %slice_bitcast_fusion), channel_id=1, source_target_pairs={{0,1},{1,0},{2,3},{3,2},{4,5},{5,4},{6,7},{7,6},{8,9},{9,8},{10,11... | collective-permute-start | bytes 4718600 | tf_op jit(solution)/shard_map/ppermute | solution.py:167
  111.3 8.2 %collective-permute-start.18 = (f32[2,96,256]{2,1,0:T(8,128)S(1)}, f32[2,96,256]{2,1,0:T(8,128)S(1)}, u32[]{:S(2)}, u32[]{:S(2)}) collective-permute-start(f32[2,96,256]{2,1,0:T(8,128)S(1)} %get-tuple-element.64), channel_id=1, source_target_pairs={{0,2},{2,4},{4,6},{6,0},{1,3},{3,5},{5,7},{7,1},{8,10},{10,12},{12... | collective-permute-start | bytes 589832 | tf_op jit(solution)/shard_map/ppermute | solution.py:151
  112.8 7.1 %collective-permute-start.20 = (f32[2,96,256]{2,1,0:T(8,128)S(1)}, f32[2,96,256]{2,1,0:T(8,128)S(1)}, u32[]{:S(2)}, u32[]{:S(2)}) collective-permute-start(f32[2,96,256]{2,1,0:T(8,128)S(1)} %get-tuple-element.65), channel_id=1, source_target_pairs={{0,6},{2,0},{4,2},{6,4},{1,7},{3,1},{5,3},{7,5},{8,14},{10,8},{12,... | collective-permute-start | bytes 589832 | tf_op jit(solution)/shard_map/ppermute | solution.py:151
  114.7 8.7 %collective-permute-start.25 = (f32[2,96,256]{2,1,0:T(8,128)S(1)}, f32[2,96,256]{2,1,0:T(8,128)S(1)}, u32[]{:S(2)}, u32[]{:S(2)}) collective-permute-start(f32[2,96,256]{2,1,0:T(8,128)S(1)} %get-tuple-element.57), channel_id=1, source_target_pairs={{0,8},{8,16},{16,24},{24,0},{1,9},{9,17},{17,25},{25,1},{2,10},{10... | collective-permute-start | bytes 589832 | tf_op jit(solution)/shard_map/ppermute | solution.py:151
  116.7 6.7 %collective-permute-start.27 = (f32[2,96,256]{2,1,0:T(8,128)S(1)}, f32[2,96,256]{2,1,0:T(8,128)S(1)}, u32[]{:S(2)}, u32[]{:S(2)}) collective-permute-start(f32[2,96,256]{2,1,0:T(8,128)S(1)} %get-tuple-element.58), channel_id=1, source_target_pairs={{0,24},{8,0},{16,8},{24,16},{1,25},{9,1},{17,9},{25,17},{2,26},{10... | collective-permute-start | bytes 589832 | tf_op jit(solution)/shard_map/ppermute | solution.py:151
  119.6 11.6 %collective-permute-start.19 = (f32[4,96,256]{2,1,0:T(8,128)S(1)}, f32[4,96,256]{2,1,0:T(8,128)S(1)}, u32[]{:S(2)}, u32[]{:S(2)}) collective-permute-start(f32[4,96,256]{2,1,0:T(8,128)S(1)} %pad_maximum_fusion), channel_id=1, source_target_pairs={{0,2},{2,4},{4,6},{6,0},{1,3},{3,5},{5,7},{7,1},{8,10},{10,12},{12... | collective-permute-start | bytes 1179656 | tf_op jit(solution)/shard_map/ppermute | solution.py:151
  120.0 11.2 %collective-permute-start.21 = (f32[4,96,256]{2,1,0:T(8,128)S(1)}, f32[4,96,256]{2,1,0:T(8,128)S(1)}, u32[]{:S(2)}, u32[]{:S(2)}) collective-permute-start(f32[4,96,256]{2,1,0:T(8,128)S(1)} %pad_maximum_fusion.1), channel_id=1, source_target_pairs={{0,6},{2,0},{4,2},{6,4},{1,7},{3,1},{5,3},{7,5},{8,14},{10,8},{12,... | collective-permute-start | bytes 1179656 | tf_op jit(solution)/shard_map/ppermute | solution.py:151
  123.5 13.8 %collective-permute-start.26 = (f32[4,96,256]{2,1,0:T(8,128)S(1)}, f32[4,96,256]{2,1,0:T(8,128)S(1)}, u32[]{:S(2)}, u32[]{:S(2)}) collective-permute-start(f32[4,96,256]{2,1,0:T(8,128)S(1)} %pad_maximum_fusion.2), channel_id=1, source_target_pairs={{0,8},{8,16},{16,24},{24,0},{1,9},{9,17},{17,25},{25,1},{2,10},{10... | collective-permute-start | bytes 1179656 | tf_op jit(solution)/shard_map/ppermute | solution.py:151
  125.2 12.1 %collective-permute-start.28 = (f32[4,96,256]{2,1,0:T(8,128)S(1)}, f32[4,96,256]{2,1,0:T(8,128)S(1)}, u32[]{:S(2)}, u32[]{:S(2)}) collective-permute-start(f32[4,96,256]{2,1,0:T(8,128)S(1)} %pad_maximum_fusion.3), channel_id=1, source_target_pairs={{0,24},{8,0},{16,8},{24,16},{1,25},{9,1},{17,9},{25,17},{2,26},{10... | collective-permute-start | bytes 1179656 | tf_op jit(solution)/shard_map/ppermute | solution.py:151
  131.3 9.5 %collective-permute-start.22 = (f32[96,256]{1,0:T(8,128)S(1)}, f32[96,256]{1,0:T(8,128)S(1)}, u32[]{:S(2)}, u32[]{:S(2)}) collective-permute-start(f32[96,256]{1,0:T(8,128)S(1)} %get-tuple-element.75), channel_id=1, source_target_pairs={{0,8},{8,16},{16,24},{24,0},{1,9},{9,17},{17,25},{25,1},{2,10},{10... | collective-permute-start | bytes 294920 | tf_op jit(solution)/shard_map/ppermute | solution.py:151
  133.3 8.7 %collective-permute-start.23 = (f32[96,256]{1,0:T(8,128)S(1)}, f32[96,256]{1,0:T(8,128)S(1)}, u32[]{:S(2)}, u32[]{:S(2)}) collective-permute-start(f32[96,256]{1,0:T(8,128)S(1)} %get-tuple-element.74), channel_id=1, source_target_pairs={{0,24},{8,0},{16,8},{24,16},{1,25},{9,1},{17,9},{25,17},{2,26},{10... | collective-permute-start | bytes 294920 | tf_op jit(solution)/shard_map/ppermute | solution.py:151
  135.4 6.6 %collective-permute-start.24 = (f32[96,256]{1,0:T(8,128)S(1)}, f32[96,256]{1,0:T(8,128)S(1)}, u32[]{:S(2)}, u32[]{:S(2)}) collective-permute-start(f32[96,256]{1,0:T(8,128)S(1)} %get-tuple-element.73), channel_id=1, source_target_pairs={{0,16},{8,24},{16,0},{24,8},{1,17},{9,25},{17,1},{25,9},{2,18},{10... | collective-permute-start | bytes 294920 | tf_op jit(solution)/shard_map/ppermute | solution.py:151
  137.4 6.5 %collective-permute-start.29 = (f32[96,256]{1,0:T(8,128)S(1)}, f32[96,256]{1,0:T(8,128)S(1)}, u32[]{:S(2)}, u32[]{:S(2)}) collective-permute-start(f32[96,256]{1,0:T(8,128)S(1)} %get-tuple-element.78), channel_id=1, source_target_pairs={{0,2},{2,4},{4,6},{6,0},{1,3},{3,5},{5,7},{7,1},{8,10},{10,12},{12... | collective-permute-start | bytes 294920 | tf_op jit(solution)/shard_map/ppermute | solution.py:151
  137.8 6.1 %collective-permute-start.30 = (f32[96,256]{1,0:T(8,128)S(1)}, f32[96,256]{1,0:T(8,128)S(1)}, u32[]{:S(2)}, u32[]{:S(2)}) collective-permute-start(f32[96,256]{1,0:T(8,128)S(1)} %get-tuple-element.77), channel_id=1, source_target_pairs={{0,6},{2,0},{4,2},{6,4},{1,7},{3,1},{5,3},{7,5},{8,14},{10,8},{12,... | collective-permute-start | bytes 294920 | tf_op jit(solution)/shard_map/ppermute | solution.py:151
  140.7 6.1 %collective-permute-start.31 = (f32[96,256]{1,0:T(8,128)S(1)}, f32[96,256]{1,0:T(8,128)S(1)}, u32[]{:S(2)}, u32[]{:S(2)}) collective-permute-start(f32[96,256]{1,0:T(8,128)S(1)} %get-tuple-element.76), channel_id=1, source_target_pairs={{0,4},{2,6},{4,0},{6,2},{1,5},{3,7},{5,1},{7,3},{8,12},{10,14},{12... | collective-permute-start | bytes 294920 | tf_op jit(solution)/shard_map/ppermute | solution.py:151

commit v10 on v9

--- a/solution.py
+++ b/solution.py
@@ -66,12 +66,15 @@
         e = jnp.where(site == k, environs[k][...], e)
     e = halves(e)
     work = [(0, q)] + [(1, q)] * (q < NQ - 1) + [(1, NQ - 1)] * (q == NQ - 2)
+    parts = {}
+    for state, at in work:
+        if at + state < NQ:
+            c = floats[2 + state] * ints[16 + q + state].astype(f32)
+            parts[state] = halves(c * product(e, halves(psi[state, q]), ((1,), (0,))))
     for slot, (state, at) in enumerate(work):
         if at + state < NQ:
             n = ints[4 + q + state]
-            c = floats[2 + state] * ints[16 + q + state].astype(f32)
-            part = c * product(e, halves(psi[state, q]), ((1,), (0,)))
-            results[slot] = product(halves(part), halves(framed(rights[q + state], n, n)), ((1,), (1,)))
+            results[slot] = product(parts[state], halves(framed(rights[q + state], n, n)), ((1,), (1,)))
         else:
             results[slot] = jnp.zeros((W, W), f32)
         for i in range(W // ROWS):

time: 149 us -> 149 us (level)
  Pallas kernels: 49.6 us -> 47.4 us
  waiting for transfers between devices: 45.7 us -> 47.7 us
    ppermute x16, waiting for transfers between devices: 31.6 us -> 33.9 us  [shards(): lax.ppermute(environ, 'site', [(0, 1), (1, 2), (2, 3)])]
    pallas_call x12, Pallas kernels: 28.9 us -> 26.7 us  [apply_step(): pl.pallas_call(kernel, in_specs=[SCALAR] * 2 + [LOCAL] * len(operands) +...]
  transfers between devices with their start and end apart: 32 -> 32, of which waited for: 22 -> 23; matrix products, arithmetic and copies ran while one was open for 1% -> 1% of each run, Pallas kernels for 31% -> 30%
where the time goes in v10:
time: 149 us; the launch traced here: 147 us
  starting transfers between devices  47.7 us (32%)
  waiting for transfers between devices  47.7 us (32%)
  Pallas kernels  47.4 us (32%)
  local copies, waits for them, and re-layouts  2.4 us (2%)
  other arithmetic  1.61 us (1%)
    ppermute x16, waiting for transfers between devices, shards(): lax.ppermute(environ, 'site', [(0, 1), (1, 2), (2, 3)])  33.9 us
    pallas_call x12, Pallas kernels, apply_step(): pl.pallas_call(kernel, in_specs=[SCALAR] * 2 + [LOCAL] * len(operands) +...  26.7 us
    ppermute x14, starting transfers between devices, turned(): return lax.ppermute(x, axis, [(i, (i + by) % 4) for i in range(4)])  25.4 us
    ppermute x16, starting transfers between devices, shards(): lax.ppermute(environ, 'site', [(0, 1), (1, 2), (2, 3)])  21.4 us
    pallas_call x16, Pallas kernels, update_step(): pl.pallas_call(kernel, in_specs=[SCALAR] * 2 + [LOCAL] * 4 + [FAR] * len(...  19.6 us
    ppermute x14, waiting for transfers between devices, turned(): return lax.ppermute(x, axis, [(i, (i + by) % 4) for i in range(4)])  9.55 us
    ppermute x2, waiting for transfers between devices, swapped(): return lax.ppermute(pieces[1], 'core', [(0, 1), (1, 0)])  4.28 us
  transfers between devices with their start and end apart: 32, of which 23 were waited for; matrix products, arithmetic and copies ran while one was open for 1% of the time, Pallas kernels for 30%

profile of v10, /device:TPU:24, one launch (start us, length us, event | category | flops | bytes accessed | tf_op | source)
XLA Modules:
  0.0 147.5 jit_solution(2047417067468228351)
XLA Ops:
  2.0 1.6 %collective-permute-start.1 = (f32[256,256]{1,0:T(8,128)S(1)}, f32[256,256]{1,0:T(8,128)S(1)}, u32[]{:S(2)}, u32[]{:S(2)}) collective-permute-start(f32[256,256]{1,0:T(8,128)S(1)} %shard_map.74.refs_0_), channel_id=1, source_target_pairs={{0,32},{32,64},{64,96},{1,33},{33,65},{65,97},{2,34},{34,66},{66,9... | collective-permute-start | bytes 786440 | tf_op jit(solution)/shard_map/ppermute | solution.py:202
  5.5 7.9 %collective-permute-done.1.previous.arrived = f32[256,256]{1,0:T(8,128)S(1)} collective-permute-done((f32[256,256]{1,0:T(8,128)S(1)}, f32[256,256]{1,0:T(8,128)S(1)}, u32[]{:S(2)}, u32[]{:S(2)}) %collective-permute-start.1) | collective-permute-done | bytes 262176 | tf_op jit(solution)/shard_map/ppermute | solution.py:202
  15.3 3.7 %collective-permute-done.arrived.previous = f32[256,256]{1,0:T(8,128)S(1)} collective-permute-done((f32[256,256]{1,0:T(8,128)S(1)}, f32[256,256]{1,0:T(8,128)S(1)}, u32[]{:S(2)}, u32[]{:S(2)}) %collective-permute-start) | collective-permute-done | bytes 262176 | tf_op jit(solution)/shard_map/ppermute | solution.py:202
  20.8 4.2 %collective-permute-done.3.previous.arrived = f32[256,256]{1,0:T(8,128)S(1)} collective-permute-done((f32[256,256]{1,0:T(8,128)S(1)}, f32[256,256]{1,0:T(8,128)S(1)}, u32[]{:S(2)}, u32[]{:S(2)}) %collective-permute-start.3) | collective-permute-done | bytes 262176 | tf_op jit(solution)/shard_map/ppermute | solution.py:202
  26.9 3.8 %collective-permute-done.2.arrived.previous = f32[256,256]{1,0:T(8,128)S(1)} collective-permute-done((f32[256,256]{1,0:T(8,128)S(1)}, f32[256,256]{1,0:T(8,128)S(1)}, u32[]{:S(2)}, u32[]{:S(2)}) %collective-permute-start.2) | collective-permute-done | bytes 262176 | tf_op jit(solution)/shard_map/ppermute | solution.py:202
  31.3 1.6 %collective-permute-start.4 = (f32[256,256]{1,0:T(8,128)S(1)}, f32[256,256]{1,0:T(8,128)S(1)}, u32[]{:S(2)}, u32[]{:S(2)}) collective-permute-start(f32[256,256]{1,0:T(8,128)S(1)} %shard_map.77.refs_2_.refs_1_.refs_0_), channel_id=1, source_target_pairs={{0,32},{32,64},{64,96},{1,33},{33,65},{65,97},{2,34},{34,66},{66,9... | collective-permute-start | bytes 786440 | tf_op jit(solution)/shard_map/ppermute | solution.py:202
  32.8 3.6 %collective-permute-done.5.arrived.previous = f32[256,256]{1,0:T(8,128)S(1)} collective-permute-done((f32[256,256]{1,0:T(8,128)S(1)}, f32[256,256]{1,0:T(8,128)S(1)}, u32[]{:S(2)}, u32[]{:S(2)}) %collective-permute-start.5) | collective-permute-done | bytes 262176 | tf_op jit(solution)/shard_map/ppermute | solution.py:202
  36.5 1.4 shard_map.79.refs_3_.refs_2_.refs_1_.refs_0_
  39.2 2.3 %shard_map.80 = (f32[2,4,4,3,32,256]{5,4,3,2,1,0:T(8,128)S(1)}, f32[2,4,4,3,32,256]{5,4,3,2,1,0:T(8,128)S(1)}) custom-call(s32[28]{0:T(128)S(1)} %concatenate.15.ints, f32[4]{0:T(128)S(1)} %bitcast.145, f32[256,256]{1,0:T(8,128)S(1)} %shard_map.74.refs_0_, f32[256,256]{1,0:T(8,128)S(1)} %shard_map.76.refs_1_.refs_0_, ...), custom_call_target="tpu_custom_call" | custom-call | tf_op jit(solution)/shard_map/pallas_call | solution.py:142
  41.9 1.4 shard_map.81.refs_3_.refs_2_.refs_1_.refs_0_
  44.6 2.3 %shard_map.82 = (f32[2,4,4,3,32,256]{5,4,3,2,1,0:T(8,128)S(1)}, f32[2,4,4,3,32,256]{5,4,3,2,1,0:T(8,128)S(1)}) custom-call(s32[28]{0:T(128)S(1)} %concatenate.15.ints, f32[4]{0:T(128)S(1)} %bitcast.147, f32[256,256]{1,0:T(8,128)S(1)} %shard_map.73.refs_0_, f32[256,256]{1,0:T(8,128)S(1)} %shard_map.75.refs_1_.refs_0_, ...), custom_call_target="tpu_custom_call", output_to_operand_aliasing={{0}: (8, {}), {1}: (9, {})} | custom-call | tf_op jit(solution)/shard_map/pallas_call | solution.py:142
  47.9 1.4 shard_map.83.refs_3_.refs_2_.refs_1_.refs_0_
  50.6 2.3 %shard_map.84 = (f32[2,4,4,3,32,256]{5,4,3,2,1,0:T(8,128)S(1)}, f32[2,4,4,3,32,256]{5,4,3,2,1,0:T(8,128)S(1)}) custom-call(s32[28]{0:T(128)S(1)} %concatenate.15.ints, f32[4]{0:T(128)S(1)} %bitcast.149, f32[256,256]{1,0:T(8,128)S(1)} %shard_map.76.refs_1_.refs_0_, ...), custom_call_target="tpu_custom_call", output_to_operand_aliasing={{0}: (8, {}), {1}: (9, {})} | custom-call | tf_op jit(solution)/shard_map/pallas_call | solution.py:142
  53.6 1.4 shard_map.85.refs_3_.refs_2_.refs_1_.refs_0_
  56.3 2.3 %shard_map.86 = (f32[2,4,4,3,32,256]{5,4,3,2,1,0:T(8,128)S(1)}, f32[2,4,4,3,32,256]{5,4,3,2,1,0:T(8,128)S(1)}) custom-call(s32[28]{0:T(128)S(1)} %concatenate.15.ints, f32[4]{0:T(128)S(1)} %bitcast.151, f32[256,256]{1,0:T(8,128)S(1)} %shard_map.75.refs_1_.refs_0_, ...), custom_call_target="tpu_custom_call", output_to_operand_aliasing={{0}: (8, {}), {1}: (9, {})} | custom-call | tf_op jit(solution)/shard_map/pallas_call | solution.py:142
  59.4 1.5 shard_map.87.refs_3_.refs_2_.refs_1_.refs_0_
  60.8 1.5 collective-permute-start.11
  62.3 2.3 %shard_map.88 = (f32[2,4,4,3,32,256]{5,4,3,2,1,0:T(8,128)S(1)}, f32[2,4,4,3,32,256]{5,4,3,2,1,0:T(8,128)S(1)}) custom-call(s32[28]{0:T(128)S(1)} %concatenate.15.ints, f32[4]{0:T(128)S(1)} %bitcast.153, f32[256,256]{1,0:T(8,128)S(1)} %shard_map.78.refs_2_.refs_1_.refs_0_, ...), custom_call_target="tpu_custom_call", output_to_operand_aliasing={{0}: (8, {}), {1}: (9, {})} | custom-call | tf_op jit(solution)/shard_map/pallas_call | solution.py:142
  65.7 1.4 shard_map.89.refs_3_.refs_2_.refs_1_.refs_0_
  68.5 2.3 %shard_map.90 = (f32[2,4,4,3,32,256]{5,4,3,2,1,0:T(8,128)S(1)}, f32[2,4,4,3,32,256]{5,4,3,2,1,0:T(8,128)S(1)}) custom-call(s32[28]{0:T(128)S(1)} %concatenate.15.ints, f32[4]{0:T(128)S(1)} %bitcast.155, f32[256,256]{1,0:T(8,128)S(1)} %shard_map.77.refs_2_.refs_1_.refs_0_, ...), custom_call_target="tpu_custom_call", output_to_operand_aliasing={{0}: (8, {}), {1}: (9, {})} | custom-call | tf_op jit(solution)/shard_map/pallas_call | solution.py:142
  73.9 2.3 %shard_map.92 = (f32[2,4,4,3,32,256]{5,4,3,2,1,0:T(8,128)S(1)}, f32[2,4,4,3,32,256]{5,4,3,2,1,0:T(8,128)S(1)}) custom-call(s32[28]{0:T(128)S(1)} %concatenate.15.ints, f32[4]{0:T(128)S(1)} %bitcast.157, f32[256,256]{1,0:T(8,128)S(1)} %shard_map.79.refs_3_.refs_2_.refs_1_.refs_0_, ...), custom_call_target="tpu_custom_call", output_to_operand_aliasing={{0}: (8, {}), {1}: (9, {})} | custom-call | tf_op jit(solution)/shard_map/pallas_call | solution.py:142
  76.2 2.2 %collective-permute-done.10.arrived.previous = f32[256,256]{1,0:T(8,128)S(1)} collective-permute-done((f32[256,256]{1,0:T(8,128)S(1)}, f32[256,256]{1,0:T(8,128)S(1)}, u32[]{:S(2)}, u32[]{:S(2)}) %collective-permute-start.10) | collective-permute-done | bytes 262176 | tf_op jit(solution)/shard_map/ppermute | solution.py:202
  78.4 1.4 shard_map.93.refs_3_.refs_2_.refs_1_
  81.2 2.3 %shard_map.94 = (f32[2,4,4,3,32,256]{5,4,3,2,1,0:T(8,128)S(1)}, f32[2,4,4,3,32,256]{5,4,3,2,1,0:T(8,128)S(1)}) custom-call(s32[28]{0:T(128)S(1)} %concatenate.15.ints, f32[4]{0:T(128)S(1)} %bitcast.159, f32[256,256]{1,0:T(8,128)S(1)} %shard_map.81.refs_3_.refs_2_.refs_1_.refs_0_, ...), custom_call_target="tpu_custom_call", output_to_operand_aliasing={{0}: (8, {}), {1}: (9, {})} | custom-call | tf_op jit(solution)/shard_map/pallas_call | solution.py:142
  84.3 1.4 shard_map.95.refs_3_.refs_2_
  87.0 2.3 %shard_map.96 = (f32[2,4,4,3,32,256]{5,4,3,2,1,0:T(8,128)S(1)}, f32[2,4,4,3,32,256]{5,4,3,2,1,0:T(8,128)S(1)}) custom-call(s32[28]{0:T(128)S(1)} %concatenate.15.ints, f32[4]{0:T(128)S(1)} %bitcast.161, f32[256,256]{1,0:T(8,128)S(1)} %shard_map.83.refs_3_.refs_2_.refs_1_.refs_0_, ...), custom_call_target="tpu_custom_call", output_to_operand_aliasing={{0}: (8, {}), {1}: (9, {})} | custom-call | tf_op jit(solution)/shard_map/pallas_call | solution.py:142
  91.5 2.3 %shard_map.98 = (f32[2,4,4,3,32,256]{5,4,3,2,1,0:T(8,128)S(1)}, f32[2,4,4,3,32,256]{5,4,3,2,1,0:T(8,128)S(1)}) custom-call(s32[28]{0:T(128)S(1)} %concatenate.15.ints, f32[4]{0:T(128)S(1)} %bitcast.163, f32[256,256]{1,0:T(8,128)S(1)} %shard_map.85.refs_3_.refs_2_.refs_1_.refs_0_, ...), custom_call_target="tpu_custom_call", output_to_operand_aliasing={{0}: (8, {}), {1}: (9, {})} | custom-call | tf_op jit(solution)/shard_map/pallas_call | solution.py:142
  95.7 1.4 shard_map.99.refs_3_
  97.2 2.6 %shard_map.100 = (f32[2,4,4,3,32,256]{5,4,3,2,1,0:T(8,128)S(1)}, f32[2,4,4,3,32,256]{5,4,3,2,1,0:T(8,128)S(1)}) custom-call(s32[28]{0:T(128)S(1)} %concatenate.15.ints, f32[4]{0:T(128)S(1)} %bitcast.165, f32[256,256]{1,0:T(8,128)S(1)} %shard_map.87.refs_3_.refs_2_.refs_1_.refs_0_, ...), custom_call_target="tpu_custom_call", output_to_operand_aliasing={{0}: (8, {}), {1}: (9, {})} | custom-call | tf_op jit(solution)/shard_map/pallas_call | solution.py:142
  100.2 1.8 %collective-permute-done.14.arrived = f32[256,256]{1,0:T(8,128)S(1)} collective-permute-done((f32[256,256]{1,0:T(8,128)S(1)}, f32[256,256]{1,0:T(8,128)S(1)}, u32[]{:S(2)}, u32[]{:S(2)}) %collective-permute-start.14) | collective-permute-done | bytes 262176 | tf_op jit(solution)/shard_map/ppermute | solution.py:202
  102.1 1.4 shard_map.101.refs_3_
  103.5 1.5 %shard_map.102 = f32[2,4,4,3,32,256]{5,4,3,2,1,0:T(8,128)S(1)} custom-call(s32[28]{0:T(128)S(1)} %concatenate.15.ints, f32[4]{0:T(128)S(1)} %bitcast.167, f32[256,256]{1,0:T(8,128)S(1)} %shard_map.89.refs_3_.refs_2_.refs_1_.refs_0_, f32[256,256]{1,0:T(8,128)S(1)} %shard_map.93.refs_3_.refs_2_.refs_1_, ...), custom_call_target="tpu_custom_call", output_to_operand_aliasing={{}: (8, {})} | custom-call | tf_op jit(solution)/shard_map/pallas_call | solution.py:142
  106.2 2.3 %collective-permute-done.16 = f32[4,4,3,32,256]{4,3,2,1,0:T(8,128)S(1)} collective-permute-done((f32[4,4,3,32,256]{4,3,2,1,0:T(8,128)S(1)}, f32[4,4,3,32,256]{4,3,2,1,0:T(8,128)S(1)}, u32[]{:S(2)}, u32[]{:S(2)}) %collective-permute-start.16) | collective-permute-done | bytes 1572896 | tf_op jit(solution)/shard_map/ppermute | solution.py:170
  108.8 2.0 %collective-permute-done.17 = f32[4,4,3,32,256]{4,3,2,1,0:T(8,128)S(1)} collective-permute-done((f32[4,4,3,32,256]{4,3,2,1,0:T(8,128)S(1)}, f32[4,4,3,32,256]{4,3,2,1,0:T(8,128)S(1)}, u32[]{:S(2)}, u32[]{:S(2)}) %collective-permute-start.17) | collective-permute-done | bytes 1572896 | tf_op jit(solution)/shard_map/ppermute | solution.py:170
  111.2 1.6 %collective-permute-start.18 = (f32[2,96,256]{2,1,0:T(8,128)S(1)}, f32[2,96,256]{2,1,0:T(8,128)S(1)}, u32[]{:S(2)}, u32[]{:S(2)}) collective-permute-start(f32[2,96,256]{2,1,0:T(8,128)S(1)} %get-tuple-element.64), channel_id=1, source_target_pairs={{0,2},{2,4},{4,6},{6,0},{1,3},{3,5},{5,7},{7,1},{8,10},{10,12},{12... | collective-permute-start | bytes 589832 | tf_op jit(solution)/shard_map/ppermute | solution.py:154
  112.8 1.7 %collective-permute-start.20 = (f32[2,96,256]{2,1,0:T(8,128)S(1)}, f32[2,96,256]{2,1,0:T(8,128)S(1)}, u32[]{:S(2)}, u32[]{:S(2)}) collective-permute-start(f32[2,96,256]{2,1,0:T(8,128)S(1)} %get-tuple-element.65), channel_id=1, source_target_pairs={{0,6},{2,0},{4,2},{6,4},{1,7},{3,1},{5,3},{7,5},{8,14},{10,8},{12,... | collective-permute-start | bytes 589832 | tf_op jit(solution)/shard_map/ppermute | solution.py:154
  114.6 2.1 %collective-permute-start.25 = (f32[2,96,256]{2,1,0:T(8,128)S(1)}, f32[2,96,256]{2,1,0:T(8,128)S(1)}, u32[]{:S(2)}, u32[]{:S(2)}) collective-permute-start(f32[2,96,256]{2,1,0:T(8,128)S(1)} %get-tuple-element.57), channel_id=1, source_target_pairs={{0,8},{8,16},{16,24},{24,0},{1,9},{9,17},{17,25},{25,1},{2,10},{10... | collective-permute-start | bytes 589832 | tf_op jit(solution)/shard_map/ppermute | solution.py:154
  116.7 2.1 %collective-permute-start.27 = (f32[2,96,256]{2,1,0:T(8,128)S(1)}, f32[2,96,256]{2,1,0:T(8,128)S(1)}, u32[]{:S(2)}, u32[]{:S(2)}) collective-permute-start(f32[2,96,256]{2,1,0:T(8,128)S(1)} %get-tuple-element.58), channel_id=1, source_target_pairs={{0,24},{8,0},{16,8},{24,16},{1,25},{9,1},{17,9},{25,17},{2,26},{10... | collective-permute-start | bytes 589832 | tf_op jit(solution)/shard_map/ppermute | solution.py:154
  119.9 3.0 %collective-permute-start.21 = (f32[4,96,256]{2,1,0:T(8,128)S(1)}, f32[4,96,256]{2,1,0:T(8,128)S(1)}, u32[]{:S(2)}, u32[]{:S(2)}) collective-permute-start(f32[4,96,256]{2,1,0:T(8,128)S(1)} %pad_maximum_fusion.1), channel_id=1, source_target_pairs={{0,6},{2,0},{4,2},{6,4},{1,7},{3,1},{5,3},{7,5},{8,14},{10,8},{12,... | collective-permute-start | bytes 1179656 | tf_op jit(solution)/shard_map/ppermute | solution.py:154
  123.5 1.6 %collective-permute-start.26 = (f32[4,96,256]{2,1,0:T(8,128)S(1)}, f32[4,96,256]{2,1,0:T(8,128)S(1)}, u32[]{:S(2)}, u32[]{:S(2)}) collective-permute-start(f32[4,96,256]{2,1,0:T(8,128)S(1)} %pad_maximum_fusion.2), channel_id=1, source_target_pairs={{0,8},{8,16},{16,24},{24,0},{1,9},{9,17},{17,25},{25,1},{2,10},{10... | collective-permute-start | bytes 1179656 | tf_op jit(solution)/shard_map/ppermute | solution.py:154
  125.2 2.2 %collective-permute-start.28 = (f32[4,96,256]{2,1,0:T(8,128)S(1)}, f32[4,96,256]{2,1,0:T(8,128)S(1)}, u32[]{:S(2)}, u32[]{:S(2)}) collective-permute-start(f32[4,96,256]{2,1,0:T(8,128)S(1)} %pad_maximum_fusion.3), channel_id=1, source_target_pairs={{0,24},{8,0},{16,8},{24,16},{1,25},{9,1},{17,9},{25,17},{2,26},{10... | collective-permute-start | bytes 1179656 | tf_op jit(solution)/shard_map/ppermute | solution.py:154
  127.3 3.7 %collective-permute-done.19 = f32[4,96,256]{2,1,0:T(8,128)S(1)} collective-permute-done((f32[4,96,256]{2,1,0:T(8,128)S(1)}, f32[4,96,256]{2,1,0:T(8,128)S(1)}, u32[]{:S(2)}, u32[]{:S(2)}) %collective-permute-start.19) | collective-permute-done | bytes 393248 | tf_op jit(solution)/shard_map/ppermute | solution.py:154
  131.1 2.1 %collective-permute-start.22 = (f32[96,256]{1,0:T(8,128)S(1)}, f32[96,256]{1,0:T(8,128)S(1)}, u32[]{:S(2)}, u32[]{:S(2)}) collective-permute-start(f32[96,256]{1,0:T(8,128)S(1)} %get-tuple-element.75), channel_id=1, source_target_pairs={{0,8},{8,16},{16,24},{24,0},{1,9},{9,17},{17,25},{25,1},{2,10},{10... | collective-permute-start | bytes 294920 | tf_op jit(solution)/shard_map/ppermute | solution.py:154
  133.3 2.1 %collective-permute-start.23 = (f32[96,256]{1,0:T(8,128)S(1)}, f32[96,256]{1,0:T(8,128)S(1)}, u32[]{:S(2)}, u32[]{:S(2)}) collective-permute-start(f32[96,256]{1,0:T(8,128)S(1)} %get-tuple-element.74), channel_id=1, source_target_pairs={{0,24},{8,0},{16,8},{24,16},{1,25},{9,1},{17,9},{25,17},{2,26},{10... | collective-permute-start | bytes 294920 | tf_op jit(solution)/shard_map/ppermute | solution.py:154
  135.4 1.8 %collective-permute-start.24 = (f32[96,256]{1,0:T(8,128)S(1)}, f32[96,256]{1,0:T(8,128)S(1)}, u32[]{:S(2)}, u32[]{:S(2)}) collective-permute-start(f32[96,256]{1,0:T(8,128)S(1)} %get-tuple-element.73), channel_id=1, source_target_pairs={{0,16},{8,24},{16,0},{24,8},{1,17},{9,25},{17,1},{25,9},{2,18},{10... | collective-permute-start | bytes 294920 | tf_op jit(solution)/shard_map/ppermute | solution.py:154
  137.8 2.8 %collective-permute-start.30 = (f32[96,256]{1,0:T(8,128)S(1)}, f32[96,256]{1,0:T(8,128)S(1)}, u32[]{:S(2)}, u32[]{:S(2)}) collective-permute-start(f32[96,256]{1,0:T(8,128)S(1)} %get-tuple-element.77), channel_id=1, source_target_pairs={{0,6},{2,0},{4,2},{6,4},{1,7},{3,1},{5,3},{7,5},{8,14},{10,8},{12,... | collective-permute-start | bytes 294920 | tf_op jit(solution)/shard_map/ppermute | solution.py:154
  142.0 1.9 %collective-permute-done.29 = f32[96,256]{1,0:T(8,128)S(1)} collective-permute-done((f32[96,256]{1,0:T(8,128)S(1)}, f32[96,256]{1,0:T(8,128)S(1)}, u32[]{:S(2)}, u32[]{:S(2)}) %collective-permute-start.29) | collective-permute-done | bytes 98336 | tf_op jit(solution)/shard_map/ppermute | solution.py:154
  143.9 2.9 %collective-permute-done.31 = f32[96,256]{1,0:T(8,128)S(1)} collective-permute-done((f32[96,256]{1,0:T(8,128)S(1)}, f32[96,256]{1,0:T(8,128)S(1)}, u32[]{:S(2)}, u32[]{:S(2)}) %collective-permute-start.31) | collective-permute-done | bytes 98336 | tf_op jit(solution)/shard_map/ppermute | solution.py:154
  (92 shorter events, 37.9 us)
Async XLA Ops:
  0.7 0.7 copy-start.2
  1.4 2.2 %copy-start.3 = (f32[1,1,4]{2,1,0:T(1,128)S(1)}, f32[1,1,4]{2,1,0:T(1,128)}, u32[]{:S(2)}) copy-start(f32[1,1,4]{2,1,0:T(1,128)} %param.11) | copy-start | bytes 52
  1.4 12.0 %slice-start = ((s8[6291456]{0:T(1024)(128)(4,1)}), s8[4194304]{0:T(1024)(128)(4,1)S(1)}, s32[]{:S(2)}) async-start(s8[6291456]{0:T(1024)(128)(4,1)} %bitcast.76), calls=%async_computation | async-start | bytes 8388608
  2.0 11.4 %slice-start.1 = ((s8[6291456]{0:T(1024)(128)(4,1)}), s8[2097152]{0:T(1024)(128)(4,1)S(1)}, s32[]{:S(2)}) async-start(s8[6291456]{0:T(1024)(128)(4,1)} %bitcast.76), calls=%async_computation.1 | async-start | bytes 4194304
  2.0 11.4 %copy-start = (f32[1,12,256,256]{3,2,1,0:T(8,128)S(1)}, f32[1,12,256,256]{3,2,1,0:T(8,128)}, u32[]{:S(2)}) copy-start(f32[1,12,256,256]{3,2,1,0:T(8,128)} %param.7) | copy-start | bytes 9437188
  2.0 11.3 %collective-permute-start.1 = (f32[256,256]{1,0:T(8,128)S(1)}, f32[256,256]{1,0:T(8,128)S(1)}, u32[]{:S(2)}, u32[]{:S(2)}) collective-permute-start(f32[256,256]{1,0:T(8,128)S(1)} %shard_map.74.refs_0_), channel_id=1, source_target_pairs={{0,32},{32,64},{64,96},{1,33},{33,65},{65,97},{2,34},{34,66},{66,9... | collective-permute-start | bytes 786440 | tf_op jit(solution)/shard_map/ppermute | solution.py:202
  4.2 14.8 %collective-permute-start = (f32[256,256]{1,0:T(8,128)S(1)}, f32[256,256]{1,0:T(8,128)S(1)}, u32[]{:S(2)}, u32[]{:S(2)}) collective-permute-start(f32[256,256]{1,0:T(8,128)S(1)} %shard_map.73.refs_0_), channel_id=1, source_target_pairs={{0,32},{32,64},{64,96},{1,33},{33,65},{65,97},{2,34},{34,66},{66,9... | collective-permute-start | bytes 786440 | tf_op jit(solution)/shard_map/ppermute | solution.py:202
  14.0 11.1 %collective-permute-start.3 = (f32[256,256]{1,0:T(8,128)S(1)}, f32[256,256]{1,0:T(8,128)S(1)}, u32[]{:S(2)}, u32[]{:S(2)}) collective-permute-start(f32[256,256]{1,0:T(8,128)S(1)} %shard_map.76.refs_1_.refs_0_), channel_id=1, source_target_pairs={{0,32},{32,64},{64,96},{1,33},{33,65},{65,97},{2,34},{34,66},{66,9... | collective-permute-start | bytes 786440 | tf_op jit(solution)/shard_map/ppermute | solution.py:202
  19.5 11.1 %collective-permute-start.2 = (f32[256,256]{1,0:T(8,128)S(1)}, f32[256,256]{1,0:T(8,128)S(1)}, u32[]{:S(2)}, u32[]{:S(2)}) collective-permute-start(f32[256,256]{1,0:T(8,128)S(1)} %shard_map.75.refs_1_.refs_0_), channel_id=1, source_target_pairs={{0,32},{32,64},{64,96},{1,33},{33,65},{65,97},{2,34},{34,66},{66,9... | collective-permute-start | bytes 786440 | tf_op jit(solution)/shard_map/ppermute | solution.py:202
  25.6 10.8 %collective-permute-start.5 = (f32[256,256]{1,0:T(8,128)S(1)}, f32[256,256]{1,0:T(8,128)S(1)}, u32[]{:S(2)}, u32[]{:S(2)}) collective-permute-start(f32[256,256]{1,0:T(8,128)S(1)} %shard_map.78.refs_2_.refs_1_.refs_0_), channel_id=1, source_target_pairs={{0,32},{32,64},{64,96},{1,33},{33,65},{65,97},{2,34},{34,66},{66,9... | collective-permute-start | bytes 786440 | tf_op jit(solution)/shard_map/ppermute | solution.py:202
  30.7 8.5 %slice-start.2 = ((s8[6291456]{0:T(1024)(128)(4,1)}), s8[4194304]{0:T(1024)(128)(4,1)S(1)}, s32[]{:S(2)}) async-start(s8[6291456]{0:T(1024)(128)(4,1)} %bitcast.112), calls=%async_computation.2 | async-start | bytes 8388608
  31.2 8.0 %slice-start.3 = ((s8[6291456]{0:T(1024)(128)(4,1)}), s8[2097152]{0:T(1024)(128)(4,1)S(1)}, s32[]{:S(2)}) async-start(s8[6291456]{0:T(1024)(128)(4,1)} %bitcast.112), calls=%async_computation.3 | async-start | bytes 4194304
  31.2 8.0 %copy-start.1 = (f32[1,1,12,256,256]{4,3,2,1,0:T(8,128)S(1)}, f32[1,1,12,256,256]{4,3,2,1,0:T(8,128)}, u32[]{:S(2)}) copy-start(f32[1,1,12,256,256]{4,3,2,1,0:T(8,128)} %param.8) | copy-start | bytes 9437188
  31.3 10.6 %collective-permute-start.4 = (f32[256,256]{1,0:T(8,128)S(1)}, f32[256,256]{1,0:T(8,128)S(1)}, u32[]{:S(2)}, u32[]{:S(2)}) collective-permute-start(f32[256,256]{1,0:T(8,128)S(1)} %shard_map.77.refs_2_.refs_1_.refs_0_), channel_id=1, source_target_pairs={{0,32},{32,64},{64,96},{1,33},{33,65},{65,97},{2,34},{34,66},{66,9... | collective-permute-start | bytes 786440 | tf_op jit(solution)/shard_map/ppermute | solution.py:202
  37.9 10.0 %collective-permute-start.7 = (f32[256,256]{1,0:T(8,128)S(1)}, f32[256,256]{1,0:T(8,128)S(1)}, u32[]{:S(2)}, u32[]{:S(2)}) collective-permute-start(f32[256,256]{1,0:T(8,128)S(1)} %shard_map.79.refs_3_.refs_2_.refs_1_.refs_0_), channel_id=1, source_target_pairs={{0,32},{32,64},{64,96},{1,33},{33,65},{65,97},{2,34},{34,66},{66,9... | collective-permute-start | bytes 786440 | tf_op jit(solution)/shard_map/ppermute | solution.py:202
  43.3 10.3 %collective-permute-start.6 = (f32[256,256]{1,0:T(8,128)S(1)}, f32[256,256]{1,0:T(8,128)S(1)}, u32[]{:S(2)}, u32[]{:S(2)}) collective-permute-start(f32[256,256]{1,0:T(8,128)S(1)} %shard_map.81.refs_3_.refs_2_.refs_1_.refs_0_), channel_id=1, source_target_pairs={{0,32},{32,64},{64,96},{1,33},{33,65},{65,97},{2,34},{34,66},{66,9... | collective-permute-start | bytes 786440 | tf_op jit(solution)/shard_map/ppermute | solution.py:202
  49.3 10.0 %collective-permute-start.9 = (f32[256,256]{1,0:T(8,128)S(1)}, f32[256,256]{1,0:T(8,128)S(1)}, u32[]{:S(2)}, u32[]{:S(2)}) collective-permute-start(f32[256,256]{1,0:T(8,128)S(1)} %shard_map.83.refs_3_.refs_2_.refs_1_.refs_0_), channel_id=1, source_target_pairs={{0,32},{32,64},{64,96},{1,33},{33,65},{65,97},{2,34},{34,66},{66,9... | collective-permute-start | bytes 786440 | tf_op jit(solution)/shard_map/ppermute | solution.py:202
  55.0 10.7 %collective-permute-start.8 = (f32[256,256]{1,0:T(8,128)S(1)}, f32[256,256]{1,0:T(8,128)S(1)}, u32[]{:S(2)}, u32[]{:S(2)}) collective-permute-start(f32[256,256]{1,0:T(8,128)S(1)} %shard_map.85.refs_3_.refs_2_.refs_1_.refs_0_), channel_id=1, source_target_pairs={{0,32},{32,64},{64,96},{1,33},{33,65},{65,97},{2,34},{34,66},{66,9... | collective-permute-start | bytes 786440 | tf_op jit(solution)/shard_map/ppermute | solution.py:202
  60.8 10.4 %collective-permute-start.11 = (f32[256,256]{1,0:T(8,128)S(1)}, f32[256,256]{1,0:T(8,128)S(1)}, u32[]{:S(2)}, u32[]{:S(2)}) collective-permute-start(f32[256,256]{1,0:T(8,128)S(1)} %shard_map.87.refs_3_.refs_2_.refs_1_.refs_0_), channel_id=1, source_target_pairs={{0,32},{32,64},{64,96},{1,33},{33,65},{65,97},{2,34},{34,66},{66,9... | collective-permute-start | bytes 786440 | tf_op jit(solution)/shard_map/ppermute | solution.py:202
  67.2 11.3 %collective-permute-start.10 = (f32[256,256]{1,0:T(8,128)S(1)}, f32[256,256]{1,0:T(8,128)S(1)}, u32[]{:S(2)}, u32[]{:S(2)}) collective-permute-start(f32[256,256]{1,0:T(8,128)S(1)} %shard_map.89.refs_3_.refs_2_.refs_1_.refs_0_), channel_id=1, source_target_pairs={{0,32},{32,64},{64,96},{1,33},{33,65},{65,97},{2,34},{34,66},{66,9... | collective-permute-start | bytes 786440 | tf_op jit(solution)/shard_map/ppermute | solution.py:202
  72.6 11.6 %collective-permute-start.13 = (f32[256,256]{1,0:T(8,128)S(1)}, f32[256,256]{1,0:T(8,128)S(1)}, u32[]{:S(2)}, u32[]{:S(2)}) collective-permute-start(f32[256,256]{1,0:T(8,128)S(1)} %shard_map.91.refs_3_.refs_2_.refs_1_), channel_id=1, source_target_pairs={{0,32},{32,64},{64,96},{1,33},{33,65},{65,97},{2,34},{34,66},{66,9... | collective-permute-start | bytes 786440 | tf_op jit(solution)/shard_map/ppermute | solution.py:202
  79.9 10.2 %collective-permute-start.12 = (f32[256,256]{1,0:T(8,128)S(1)}, f32[256,256]{1,0:T(8,128)S(1)}, u32[]{:S(2)}, u32[]{:S(2)}) collective-permute-start(f32[256,256]{1,0:T(8,128)S(1)} %shard_map.93.refs_3_.refs_2_.refs_1_), channel_id=1, source_target_pairs={{0,32},{32,64},{64,96},{1,33},{33,65},{65,97},{2,34},{34,66},{66,9... | collective-permute-start | bytes 786440 | tf_op jit(solution)/shard_map/ppermute | solution.py:202
  85.7 10.0 %collective-permute-start.15 = (f32[256,256]{1,0:T(8,128)S(1)}, f32[256,256]{1,0:T(8,128)S(1)}, u32[]{:S(2)}, u32[]{:S(2)}) collective-permute-start(f32[256,256]{1,0:T(8,128)S(1)} %shard_map.95.refs_3_.refs_2_), channel_id=1, source_target_pairs={{0,32},{32,64},{64,96},{1,33},{33,65},{65,97},{2,34},{34,66},{66,9... | collective-permute-start | bytes 786440 | tf_op jit(solution)/shard_map/ppermute | solution.py:202
  93.8 8.3 %collective-permute-start.14 = (f32[256,256]{1,0:T(8,128)S(1)}, f32[256,256]{1,0:T(8,128)S(1)}, u32[]{:S(2)}, u32[]{:S(2)}) collective-permute-start(f32[256,256]{1,0:T(8,128)S(1)} %shard_map.97.refs_3_.refs_2_), channel_id=1, source_target_pairs={{0,32},{32,64},{64,96},{1,33},{33,65},{65,97},{2,34},{34,66},{66,9... | collective-permute-start | bytes 786440 | tf_op jit(solution)/shard_map/ppermute | solution.py:202
  105.0 3.5 %collective-permute-start.16 = (f32[4,4,3,32,256]{4,3,2,1,0:T(8,128)S(1)}, f32[4,4,3,32,256]{4,3,2,1,0:T(8,128)S(1)}, u32[]{:S(2)}, u32[]{:S(2)}) collective-permute-start(f32[4,4,3,32,256]{4,3,2,1,0:T(8,128)S(1)} %get-tuple-element.63), channel_id=1, source_target_pairs={{0,1},{1,0},{2,3},{3,2},{4,5},{5,4},{6,7},{7,6},{8,9},{9,8},{10,11... | collective-permute-start | bytes 4718600 | tf_op jit(solution)/shard_map/ppermute | solution.py:170
  105.3 5.5 %collective-permute-start.17 = (f32[4,4,3,32,256]{4,3,2,1,0:T(8,128)S(1)}, f32[4,4,3,32,256]{4,3,2,1,0:T(8,128)S(1)}, u32[]{:S(2)}, u32[]{:S(2)}) collective-permute-start(f32[4,4,3,32,256]{4,3,2,1,0:T(8,128)S(1)} %slice_bitcast_fusion), channel_id=1, source_target_pairs={{0,1},{1,0},{2,3},{3,2},{4,5},{5,4},{6,7},{7,6},{8,9},{9,8},{10,11... | collective-permute-start | bytes 4718600 | tf_op jit(solution)/shard_map/ppermute | solution.py:170
  111.2 8.2 %collective-permute-start.18 = (f32[2,96,256]{2,1,0:T(8,128)S(1)}, f32[2,96,256]{2,1,0:T(8,128)S(1)}, u32[]{:S(2)}, u32[]{:S(2)}) collective-permute-start(f32[2,96,256]{2,1,0:T(8,128)S(1)} %get-tuple-element.64), channel_id=1, source_target_pairs={{0,2},{2,4},{4,6},{6,0},{1,3},{3,5},{5,7},{7,1},{8,10},{10,12},{12... | collective-permute-start | bytes 589832 | tf_op jit(solution)/shard_map/ppermute | solution.py:154
  112.8 7.1 %collective-permute-start.20 = (f32[2,96,256]{2,1,0:T(8,128)S(1)}, f32[2,96,256]{2,1,0:T(8,128)S(1)}, u32[]{:S(2)}, u32[]{:S(2)}) collective-permute-start(f32[2,96,256]{2,1,0:T(8,128)S(1)} %get-tuple-element.65), channel_id=1, source_target_pairs={{0,6},{2,0},{4,2},{6,4},{1,7},{3,1},{5,3},{7,5},{8,14},{10,8},{12,... | collective-permute-start | bytes 589832 | tf_op jit(solution)/shard_map/ppermute | solution.py:154
  114.6 8.8 %collective-permute-start.25 = (f32[2,96,256]{2,1,0:T(8,128)S(1)}, f32[2,96,256]{2,1,0:T(8,128)S(1)}, u32[]{:S(2)}, u32[]{:S(2)}) collective-permute-start(f32[2,96,256]{2,1,0:T(8,128)S(1)} %get-tuple-element.57), channel_id=1, source_target_pairs={{0,8},{8,16},{16,24},{24,0},{1,9},{9,17},{17,25},{25,1},{2,10},{10... | collective-permute-start | bytes 589832 | tf_op jit(solution)/shard_map/ppermute | solution.py:154
  116.7 6.7 %collective-permute-start.27 = (f32[2,96,256]{2,1,0:T(8,128)S(1)}, f32[2,96,256]{2,1,0:T(8,128)S(1)}, u32[]{:S(2)}, u32[]{:S(2)}) collective-permute-start(f32[2,96,256]{2,1,0:T(8,128)S(1)} %get-tuple-element.58), channel_id=1, source_target_pairs={{0,24},{8,0},{16,8},{24,16},{1,25},{9,1},{17,9},{25,17},{2,26},{10... | collective-permute-start | bytes 589832 | tf_op jit(solution)/shard_map/ppermute | solution.py:154
  119.4 11.6 %collective-permute-start.19 = (f32[4,96,256]{2,1,0:T(8,128)S(1)}, f32[4,96,256]{2,1,0:T(8,128)S(1)}, u32[]{:S(2)}, u32[]{:S(2)}) collective-permute-start(f32[4,96,256]{2,1,0:T(8,128)S(1)} %pad_maximum_fusion), channel_id=1, source_target_pairs={{0,2},{2,4},{4,6},{6,0},{1,3},{3,5},{5,7},{7,1},{8,10},{10,12},{12... | collective-permute-start | bytes 1179656 | tf_op jit(solution)/shard_map/ppermute | solution.py:154
  119.9 11.1 %collective-permute-start.21 = (f32[4,96,256]{2,1,0:T(8,128)S(1)}, f32[4,96,256]{2,1,0:T(8,128)S(1)}, u32[]{:S(2)}, u32[]{:S(2)}) collective-permute-start(f32[4,96,256]{2,1,0:T(8,128)S(1)} %pad_maximum_fusion.1), channel_id=1, source_target_pairs={{0,6},{2,0},{4,2},{6,4},{1,7},{3,1},{5,3},{7,5},{8,14},{10,8},{12,... | collective-permute-start | bytes 1179656 | tf_op jit(solution)/shard_map/ppermute | solution.py:154
  123.5 13.7 %collective-permute-start.26 = (f32[4,96,256]{2,1,0:T(8,128)S(1)}, f32[4,96,256]{2,1,0:T(8,128)S(1)}, u32[]{:S(2)}, u32[]{:S(2)}) collective-permute-start(f32[4,96,256]{2,1,0:T(8,128)S(1)} %pad_maximum_fusion.2), channel_id=1, source_target_pairs={{0,8},{8,16},{16,24},{24,0},{1,9},{9,17},{17,25},{25,1},{2,10},{10... | collective-permute-start | bytes 1179656 | tf_op jit(solution)/shard_map/ppermute | solution.py:154
  125.2 12.1 %collective-permute-start.28 = (f32[4,96,256]{2,1,0:T(8,128)S(1)}, f32[4,96,256]{2,1,0:T(8,128)S(1)}, u32[]{:S(2)}, u32[]{:S(2)}) collective-permute-start(f32[4,96,256]{2,1,0:T(8,128)S(1)} %pad_maximum_fusion.3), channel_id=1, source_target_pairs={{0,24},{8,0},{16,8},{24,16},{1,25},{9,1},{17,9},{25,17},{2,26},{10... | collective-permute-start | bytes 1179656 | tf_op jit(solution)/shard_map/ppermute | solution.py:154
  131.1 9.5 %collective-permute-start.22 = (f32[96,256]{1,0:T(8,128)S(1)}, f32[96,256]{1,0:T(8,128)S(1)}, u32[]{:S(2)}, u32[]{:S(2)}) collective-permute-start(f32[96,256]{1,0:T(8,128)S(1)} %get-tuple-element.75), channel_id=1, source_target_pairs={{0,8},{8,16},{16,24},{24,0},{1,9},{9,17},{17,25},{25,1},{2,10},{10... | collective-permute-start | bytes 294920 | tf_op jit(solution)/shard_map/ppermute | solution.py:154
  133.3 8.7 %collective-permute-start.23 = (f32[96,256]{1,0:T(8,128)S(1)}, f32[96,256]{1,0:T(8,128)S(1)}, u32[]{:S(2)}, u32[]{:S(2)}) collective-permute-start(f32[96,256]{1,0:T(8,128)S(1)} %get-tuple-element.74), channel_id=1, source_target_pairs={{0,24},{8,0},{16,8},{24,16},{1,25},{9,1},{17,9},{25,17},{2,26},{10... | collective-permute-start | bytes 294920 | tf_op jit(solution)/shard_map/ppermute | solution.py:154
  135.4 6.6 %collective-permute-start.24 = (f32[96,256]{1,0:T(8,128)S(1)}, f32[96,256]{1,0:T(8,128)S(1)}, u32[]{:S(2)}, u32[]{:S(2)}) collective-permute-start(f32[96,256]{1,0:T(8,128)S(1)} %get-tuple-element.73), channel_id=1, source_target_pairs={{0,16},{8,24},{16,0},{24,8},{1,17},{9,25},{17,1},{25,9},{2,18},{10... | collective-permute-start | bytes 294920 | tf_op jit(solution)/shard_map/ppermute | solution.py:154
  137.3 6.5 %collective-permute-start.29 = (f32[96,256]{1,0:T(8,128)S(1)}, f32[96,256]{1,0:T(8,128)S(1)}, u32[]{:S(2)}, u32[]{:S(2)}) collective-permute-start(f32[96,256]{1,0:T(8,128)S(1)} %get-tuple-element.78), channel_id=1, source_target_pairs={{0,2},{2,4},{4,6},{6,0},{1,3},{3,5},{5,7},{7,1},{8,10},{10,12},{12... | collective-permute-start | bytes 294920 | tf_op jit(solution)/shard_map/ppermute | solution.py:154
  137.8 6.1 %collective-permute-start.30 = (f32[96,256]{1,0:T(8,128)S(1)}, f32[96,256]{1,0:T(8,128)S(1)}, u32[]{:S(2)}, u32[]{:S(2)}) collective-permute-start(f32[96,256]{1,0:T(8,128)S(1)} %get-tuple-element.77), channel_id=1, source_target_pairs={{0,6},{2,0},{4,2},{6,4},{1,7},{3,1},{5,3},{7,5},{8,14},{10,8},{12,... | collective-permute-start | bytes 294920 | tf_op jit(solution)/shard_map/ppermute | solution.py:154
  140.6 6.1 %collective-permute-start.31 = (f32[96,256]{1,0:T(8,128)S(1)}, f32[96,256]{1,0:T(8,128)S(1)}, u32[]{:S(2)}, u32[]{:S(2)}) collective-permute-start(f32[96,256]{1,0:T(8,128)S(1)} %get-tuple-element.76), channel_id=1, source_target_pairs={{0,4},{2,6},{4,0},{6,2},{1,5},{3,7},{5,1},{7,3},{8,12},{10,14},{12... | collective-permute-start | bytes 294920 | tf_op jit(solution)/shard_map/ppermute | solution.py:154
